TPU v7x, 32 devices: a whole 2x2x4 slice. The times are simulated.
32 devices in a mesh: shard: 2 (over y), tensor: 4 (over z), section: 4 (over x, core).
Axes of the slice: x: 2, y: 2, z: 4, core: 2. Of those that a mesh axis runs over, the one named last changes fastest.
Arguments:
- xin: bfloat16 [4, 16384, 768], P(None, ('shard', 'tensor', 'section')), may hold values from -6 to 6
- dout: bfloat16 [4, 16384, 768], P(None, ('shard', 'tensor', 'section')), may hold values from -6 to 6
- weights: bfloat16 [4, 768, 768], P(None, ('tensor', 'section')), may hold values from -0.21875 to 0.21875
- slot_block: int32 [8], replicated, may hold values from -1 to 3, as said below
- left_stat: float32 [8, 768, 768], P('shard', ('tensor', 'section')), may hold values from -1 to 10, as said below
- right_stat: float32 [8, 768, 768], P('shard', ('tensor', 'section')), may hold values from -1 to 10, as said below
- left_root: float32 [8, 768, 768], P('shard', ('tensor', 'section')), may hold values from -1 to 10, as said below
- right_root: float32 [8, 768, 768], P('shard', ('tensor', 'section')), may hold values from -1 to 10, as said below
- first_moment: float32 [8, 768, 768], P('shard', ('tensor', 'section')), may hold values from -0.3 to 0.3
- second_moment: float32 [8, 768, 768], P('shard', ('tensor', 'section')), may hold values from 0.001 to 0.01
Outputs:
- new_weights: bfloat16 [4, 768, 768], P(None, ('tensor', 'section'))
- new_left: float32 [8, 768, 768], P('shard', ('tensor', 'section'))
- new_right: float32 [8, 768, 768], P('shard', ('tensor', 'section'))
- new_first: float32 [8, 768, 768], P('shard', ('tensor', 'section'))
- new_second: float32 [8, 768, 768], P('shard', ('tensor', 'section'))
Inputs may be any that keep to these rules, and one draw needn't show every extreme that they name: `slot_block`: every block 0 to 3 stands in exactly one slot; slots 4 s to 4 s + 3 belong to shard index s; some shard index holds two blocks and none holds more; the other slots hold -1. `left_stat`: each slot is a symmetric positive definite matrix. `right_stat`: each slot is a symmetric positive definite matrix. `left_root`: each slot is a symmetric positive definite matrix. `right_root`: each slot is a symmetric positive definite matrix.
All inputs are finite; a program needn't handle non-finite values.
Results may differ from a plain program's by a relative error of at most 0.00045.
Values may be sent and summed in bfloat16 or wider, within the bound.
No kernel may reach another device: no remote copies, remote signals or barrier semaphores. Data moves between devices by JAX's collectives and lax.ppermute only.
A program may use at most 128 MiB of HBM per device.

v0:
```python
import math

import jax
import jax.numpy as jnp
from jax import lax
from jax.sharding import PartitionSpec as P


def spread(value, axis, source):
    kept = jnp.where(lax.axis_index(axis) == source, value, 0).astype(value.dtype)
    return lax.psum(kept, axis)


def absorb_slot(mine_rows, root_rows, portion, col_first):
    highest = lax.Precision.HIGHEST
    row_count = mine_rows.shape[0]
    block_part = jnp.dot(mine_rows, portion.T, precision=highest)
    own_cols = lax.dynamic_slice_in_dim(portion, col_first, row_count, 1)
    right_gram = jnp.dot(own_cols.T, portion, precision=highest)
    left_prod = jnp.dot(root_rows, portion, precision=highest)
    return (block_part, right_gram, left_prod)


def apply_slot(prod_rows, portion):
    return jnp.dot(prod_rows, portion, precision=lax.Precision.HIGHEST)


def on_device(
    xin,
    dout,
    weights,
    slot_block,
    left_stat,
    right_stat,
    left_root,
    right_root,
    first_moment,
    second_moment,
):
    block_count, tok_count, block_size = xin.shape
    slot_count, row_count = (left_stat.shape[0], left_stat.shape[1])
    group_count = lax.axis_size(("tensor", "section"))
    shard_count = lax.axis_size("shard")
    factor = 1.0 / math.sqrt(tok_count * shard_count * group_count * block_size)
    pieces_out = []
    for grad_member in range(block_count):
        cols = xin[grad_member]
        pieces_out.append(
            jnp.einsum("tr,tc->rc", cols, dout[grad_member], preferred_element_type=jnp.float32)
        )
    partial_rows = lax.psum_scatter(
        jnp.concatenate(pieces_out, axis=1) * factor,
        ("tensor", "section"),
        scatter_dimension=0,
        tiled=True,
    )
    grad_rows = lax.psum(partial_rows, "shard")
    shard_idx = lax.axis_index("shard")
    group_idx = lax.axis_index(("tensor", "section"))
    my_slots = lax.dynamic_slice_in_dim(slot_block, shard_idx * slot_count, slot_count)
    valid = my_slots >= 0
    picks = jnp.maximum(my_slots, 0)
    grad_three = grad_rows.reshape(row_count, block_count, block_size)
    mine = jnp.moveaxis(jnp.take(grad_three, picks, axis=1), 1, 0)
    col_first = group_idx * row_count
    zeros_rows = jnp.zeros((slot_count, row_count, block_size), jnp.float32)
    totals = (zeros_rows, zeros_rows, zeros_rows)
    portion = lax.all_gather(mine, ("tensor", "section"), axis=1, tiled=True)
    lefts = []
    rights = []
    prods = []
    for slot_pos in range(slot_count):
        current = (totals[0][slot_pos], totals[1][slot_pos], totals[2][slot_pos])
        result = lax.cond(
            valid[slot_pos],
            lambda values: absorb_slot(
                mine[slot_pos], left_root[slot_pos], portion[slot_pos], col_first
            ),
            lambda values: values,
            current,
        )
        lefts.append(result[0])
        rights.append(result[1])
        prods.append(result[2])
    left_gram = jnp.stack(lefts)
    right_gram = jnp.stack(rights)
    left_prod = jnp.stack(prods)
    apply_portion = lax.all_gather(right_root, ("tensor", "section"), axis=1, tiled=True)
    outputs = []
    for apply_slot_pos in range(slot_count):
        outputs.append(
            lax.cond(
                valid[apply_slot_pos],
                lambda values: apply_slot(left_prod[apply_slot_pos], apply_portion[apply_slot_pos]),
                lambda values: values,
                zeros_rows[apply_slot_pos],
            )
        )
    direction = jnp.stack(outputs)
    moment_one = 0.9 * first_moment + 0.1 * mine
    moment_two = 0.999 * second_moment + 0.001 * mine * mine
    adam = moment_one / (jnp.sqrt(moment_two) + 1e-08)
    adam_sq, dir_sq = lax.psum(
        (jnp.sum(adam * adam, axis=(1, 2)), jnp.sum(direction * direction, axis=(1, 2))),
        ("tensor", "section"),
    )
    graft = jnp.sqrt(adam_sq) / (jnp.sqrt(dir_sq) + 1e-06)
    mask = valid[:, None, None]
    new_left = jnp.where(mask, 0.5 * left_stat + 0.5 * left_gram, left_stat)
    new_right = jnp.where(mask, 0.5 * right_stat + 0.5 * right_gram, right_stat)
    new_first = jnp.where(mask, moment_one, first_moment)
    new_second = jnp.where(mask, moment_two, second_moment)
    my_weights = jnp.take(weights, picks, axis=0)
    new_rows = (my_weights.astype(jnp.float32) - 0.05 * graft[:, None, None] * direction).astype(
        jnp.bfloat16
    )
    slot_ids = jnp.arange(slot_block.shape[0], dtype=jnp.int32)
    holders = [
        jnp.sum(slot_ids * (slot_block == member).astype(jnp.int32))
        for member in range(block_count)
    ]
    published = []
    for member in range(block_count):
        owner = holders[member] // slot_count
        within = holders[member] % slot_count
        chosen = lax.dynamic_index_in_dim(new_rows, within, 0, keepdims=False)
        published.append(spread(chosen, "shard", owner))
    new_weights = jnp.stack(published)
    return (new_weights, new_left, new_right, new_first, new_second)


def solution(mesh):
    placed = (
        P(None, ("shard", "tensor", "section"), None),
        P(None, ("shard", "tensor", "section"), None),
        P(None, ("tensor", "section"), None),
        P(),
        P("shard", ("tensor", "section"), None),
        P("shard", ("tensor", "section"), None),
        P("shard", ("tensor", "section"), None),
        P("shard", ("tensor", "section"), None),
        P("shard", ("tensor", "section"), None),
        P("shard", ("tensor", "section"), None),
    )
    return jax.shard_map(
        on_device,
        mesh=mesh,
        in_specs=placed,
        out_specs=(
            P(None, ("tensor", "section"), None),
            P("shard", ("tensor", "section"), None),
            P("shard", ("tensor", "section"), None),
            P("shard", ("tensor", "section"), None),
            P("shard", ("tensor", "section"), None),
        ),
        check_vma=False,
    )
```

profile of v0, /device:TPU:0, one launch (start us, length us, event | category | flops | bytes accessed | tf_op | source)
XLA Modules:
  0.0 413.1 jit_solution(5907693126761822649)
XLA Ops:
  7.2 0.0 copy-start
  7.2 0.0 reduce-scatter.4.cloned.1.call-start
  7.2 2.4 fusion.108
  9.6 0.0 copy-done.3
  9.6 0.0 copy-start.4
  9.6 2.1 fusion.111
  11.8 0.8 fusion.114
  12.6 0.8 fusion.117
  13.4 4.1 maximum_multiply_fusion
  17.5 9.7 %copy.20 = f32[768,3072]{1,0:T(8,128)} copy(f32[768,3072]{0,1:T(8,128)} %maximum_multiply_fusion) | data formatting | bytes 18874368
  27.2 0.0 reduce-scatter.4.cloned.1.call-update
  27.2 0.0 copy-start.14
  27.2 0.0 all-reduce.5.cloned.1.call-start
  27.2 114.2 %reduce-scatter.4.cloned.1.call-done = f32[48,3072]{1,0:T(8,128)} async-done(((f32[768,3072]{1,0:T(8,128)}), f32[48,3072]{1,0:T(8,128)}) %reduce-scatter.4.cloned.1.call-update) | async-done | bytes 589840
  141.4 1.5 copy.21
  142.9 0.0 copy-start.5
  142.9 1.3 copy.17
  144.2 0.0 all-reduce.5.cloned.1.call-update
  144.2 0.0 all-gather.5.cloned.1.call-start
  144.3 0.1 broadcast_compare_fusion
  144.4 29.8 %all-reduce.5.cloned.1.call-done = f32[48,4,768]{2,0,1:T(8,128)} async-done(((f32[48,4,768]{2,0,1:T(8,128)}), f32[48,4,768]{2,0,1:T(8,128)}) %all-reduce.5.cloned.1.call-update) | async-done | bytes 589840 | tf_op jit(solution)/shard_map/psum | solution.py:57
  174.2 1.6 gather_fusion.1
  175.9 1.2 fusion.134
  177.1 0.0 all-gather.5.cloned.1.call-update
  177.1 0.0 all-gather.3.cloned.1.call-start
  177.1 0.5 all-gather.3.cloned.1.call-update
  177.7 0.0 all-reduce.7.cloned.1.call-start
  177.7 0.7 fusion.135
  188.8 0.6 fusion.140
  192.0 0.6 gather_fusion
  192.7 66.0 %all-gather.5.cloned.1.call-done = f32[4,768,768]{2,1,0:T(8,128)} async-done(((f32[4,48,768]{2,1,0:T(8,128)}), f32[4,768,768]{2,1,0:T(8,128)}) %all-gather.5.cloned.1.call-update) | async-done | bytes 9437200 | tf_op jit(solution)/shard_map/all_gather | solution.py:68
  258.7 0.1 conditional.8
  258.8 0.3 conditional.10
  259.1 0.6 copy-done.7
  259.7 10.9 %conditional.12 = (f32[48,768]{1,0:T(8,128)S(1)}, f32[1,48,768]{2,1,0:T(8,128)S(1)}, f32[1,48,768]{2,1,0:T(8,128)S(1)}) conditional(s32[]{:T(128)} %bitcast.43, () %tuple.96, (f32[4,48,768]{2,1,0:T(8,128)}, f32[4,768,768]{2,1,0:T(8,128)}, f32[4,48,768]{2,1,0:T(8,128)}, s32[]{:T(128)}) %tuple.90), branch_computations={%region_13.14_spmd, %region_14.15_spmd} | conditional | flops 1019215872 | bytes 12927038 | solution.py:74
  259.7 1.8 slice.69
  261.5 1.7 fusion.63
  263.2 3.3 fusion.58
  266.5 4.2 %fusion.60 = f32[1,48,768]{2,1,0:T(8,128)S(1)} fusion(f32[4,48,768]{2,1,0:T(8,128)} %get-tuple-element.86, f32[4,768,768]{2,1,0:T(8,128)} %get-tuple-element.85), kind=kOutput, calls=%fused_computation.50 | convolution fusion | flops 339738624 | bytes 2654208 | tf_op jit(solution)/shard_map/cond/branch_1_fun/dot_general | solution.py:17
  270.7 0.6 copy-done.8
  271.3 0.1 copy-done.9
  271.4 10.8 %conditional.14 = (f32[48,768]{1,0:T(8,128)S(1)}, f32[1,48,768]{2,1,0:T(8,128)S(1)}, f32[1,48,768]{2,1,0:T(8,128)S(1)}) conditional(s32[]{:T(128)} %bitcast.44, () %tuple.99, (f32[4,48,768]{2,1,0:T(8,128)}, f32[4,768,768]{2,1,0:T(8,128)}, f32[4,48,768]{2,1,0:T(8,128)}, s32[]{:T(128)}) %tuple.90), branch_computations={%region_17.18_spmd, %region_18.19_spmd} | conditional | flops 1019215872 | bytes 12927038 | solution.py:74
  271.4 1.8 slice.73
  273.2 1.7 fusion.90
  274.9 3.3 fusion.85
  278.2 4.1 fusion.87
  282.2 0.0 copy-start.12
  282.2 58.3 %all-gather.3.cloned.1.call-done = f32[4,768,768]{2,1,0:T(8,128)} async-done(((f32[4,48,768]{2,1,0:T(8,128)}), f32[4,768,768]{2,1,0:T(8,128)}) %all-gather.3.cloned.1.call-update) | async-done | bytes 9437200 | tf_op jit(solution)/shard_map/all_gather | solution.py:88
  340.6 3.2 conditional.13
  340.6 3.2 fusion.78
  343.8 0.0 copy-start.13
  343.9 0.0 copy-start.2
  343.9 0.0 copy-start.6
  343.9 0.8 copy-done.13
  344.7 3.2 conditional.15
  344.7 3.2 fusion.105
  347.9 0.2 multiply_reduce_fusion
  348.0 3.3 fusion.133
  351.4 30.8 %all-reduce = (f32[4]{0:T(128)S(1)}, f32[4]{0:T(128)S(1)}) all-reduce(f32[4]{0:T(128)S(1)} %multiply_reduce_fusion, f32[4]{0:T(128)S(1)} %get-tuple-element.140), channel_id=1, replica_groups=mesh['shard'=2,'tensor'=4,'section'=4] {'tensor','section'}, use_global_device_ids=true, to_apply=%region_22.23 | all-reduce | flops 8 | bytes 64 | tf_op jit(solution)/shard_map/psum | solution.py:103
  382.2 0.2 subtract_convert_fusion
  382.4 0.7 dynamic-slice_select_fusion.3
  383.1 0.0 all-reduce.7.cloned.1.call-update
  383.1 21.7 %all-reduce.7.cloned.1.call-done = (bf16[1,48,768]{2,1,0:T(8,128)(2,1)}, bf16[1,48,768]{2,1,0:T(8,128)(2,1)}, bf16[1,48,768]{2,1,0:T(8,128)(2,1)}, bf16[1,48,768]{2,1,0:T(8,128)(2,1)}) async-done(((bf16[1,48,768]{2,1,0:T(8,128)(2,1)}, bf16[1,48,768]{2,1,0:T(8,128)(2,1)}, bf16[1,48,768]{2,1,0:T(8,128)(2,1)}, bf16[1,48,768]{2,1,0:T(8,128)(2,1)}), (bf16[1,48,768]{2,1,0:T(8,128)(2,1)}, ...) | async-done | bytes 294928 | tf_op jit(solution)/shard_map/psum | solution.py:11
  404.8 1.7 pad_maximum_fusion.1
  (29 shorter events, 0.2 us)
Async XLA Ops:
  7.2 184.8 %copy-start = (bf16[4,48,768]{2,1,0:T(8,128)(2,1)S(1)}, bf16[4,48,768]{2,1,0:T(8,128)(2,1)}, u32[]{:S(2)}) copy-start(bf16[4,48,768]{2,1,0:T(8,128)(2,1)} %param.28) | copy-start | bytes 884740
  7.2 2.4 copy-start.3
  7.2 134.2 %reduce-scatter.4.cloned.1.call-start = ((), (), s32[]{:S(2)}) async-start(), calls=%async_computation.4 | async-start | bytes 10027008
  9.6 2.1 copy-start.4
  27.2 117.1 %copy-start.14 = (s32[8]{0:T(128)S(1)}, s32[8]{0:T(128)}, u32[]{:S(2)}) copy-start(s32[8]{0:T(128)} %param.29) | copy-start | bytes 100
  27.2 147.0 %all-reduce.5.cloned.1.call-start = ((), (), s32[]{:S(2)}) async-start(), calls=%async_computation.1 | async-start | bytes 1179648 | tf_op jit(solution)/shard_map/psum | solution.py:57
  142.9 32.9 %copy-start.5 = (f32[4,48,768]{2,1,0:T(8,128)S(1)}, f32[4,48,768]{2,1,0:T(8,128)}, u32[]{:S(2)}) copy-start(f32[4,48,768]{2,1,0:T(8,128)} %param.35) | copy-start | bytes 1769476
  144.2 114.5 %all-gather.5.cloned.1.call-start = ((), (), s32[]{:S(2)}) async-start(), calls=%async_computation.3 | async-start | bytes 10027008 | tf_op jit(solution)/shard_map/all_gather | solution.py:68
  177.1 163.5 %all-gather.3.cloned.1.call-start = ((), (), s32[]{:S(2)}) async-start(), calls=%async_computation.2 | async-start | bytes 10027008 | tf_op jit(solution)/shard_map/all_gather | solution.py:88
  177.7 227.1 %all-reduce.7.cloned.1.call-start = ((), (), s32[]{:S(2)}) async-start(), calls=%async_computation.5 | async-start | bytes 589824 | tf_op jit(solution)/shard_map/psum | solution.py:11
  259.0 0.7 copy-start.7
  270.6 0.7 copy-start.8
  270.6 0.7 copy-start.9
  282.2 58.4 %copy-start.10 = (f32[1,48,768]{2,1,0:T(8,128)}, f32[1,48,768]{2,1,0:T(8,128)S(1)}, u32[]{:S(2)}) copy-start(f32[1,48,768]{2,1,0:T(8,128)S(1)} %get-tuple-element.120) | copy-start | bytes 442372
  282.2 58.4 %copy-start.11 = (f32[1,48,768]{2,1,0:T(8,128)}, f32[1,48,768]{2,1,0:T(8,128)S(1)}, u32[]{:S(2)}) copy-start(f32[1,48,768]{2,1,0:T(8,128)S(1)} %get-tuple-element.124) | copy-start | bytes 442372
  282.2 58.4 %copy-start.12 = (f32[48,768]{1,0:T(8,128)}, f32[48,768]{1,0:T(8,128)S(1)}, u32[]{:S(2)}) copy-start(f32[48,768]{1,0:T(8,128)S(1)} %get-tuple-element.116) | copy-start | bytes 442372
  343.8 0.9 copy-start.13
  343.9 4.2 %copy-start.2 = (f32[4,48,768]{2,1,0:T(8,128)S(1)}, f32[4,48,768]{2,1,0:T(8,128)}, u32[]{:S(2)}) copy-start(f32[4,48,768]{2,1,0:T(8,128)} %get-tuple-element.136) | copy-start | bytes 1769476
  343.9 4.2 %copy-start.6 = (f32[4,48,768]{2,1,0:T(8,128)S(1)}, f32[4,48,768]{2,1,0:T(8,128)}, u32[]{:S(2)}) copy-start(f32[4,48,768]{2,1,0:T(8,128)} %param.34) | copy-start | bytes 1769476
  348.0 58.5 %copy-start.1 = (bf16[4,48,768]{2,1,0:T(8,128)(2,1)S(1)}, bf16[4,48,768]{2,1,0:T(8,128)(2,1)}, u32[]{:S(2)}) copy-start(bf16[4,48,768]{2,1,0:T(8,128)(2,1)} %param.28) | copy-start | bytes 884740
Sparse Core Ops, SparseCore 0:
  27.3 114.0 reduce-scatter.3
  144.4 29.7 all-reduce.4
  177.2 81.4 all-gather.4
  260.9 79.6 all-gather.2
  383.3 21.5 all-reduce.6
where the time goes:
time: 414 us; the launch traced here: 413 us
  waiting for transfers between devices  291 us (70%)
  blocking collectives  30.8 us (7%)
  matrix products  30.5 us (7%)
  between operations  27.2 us (7%)
  local copies, waits for them, and re-layouts  21.3 us (5%)
  other arithmetic  12.2 us (3%)
    unnamed x6, waiting for transfers between devices  115 us
    all_gather x1, waiting for transfers between devices, on_device(): portion = lax.all_gather(mine, ('tensor', 'section'), axis=1, tiled=True)  66 us
    all_gather x1, waiting for transfers between devices, on_device(): lax.all_gather(right_root, ('tensor', 'section'), axis=1, tiled=True)  58.3 us
    psum x1, blocking collectives, on_device(): lax.psum((jnp.sum(adam * adam, axis=(1, 2)), jnp.sum(direction * directio...  30.8 us
    psum x1, waiting for transfers between devices, on_device(): grad_rows = lax.psum(partial_rows, 'shard')  29.8 us
    psum x1, waiting for transfers between devices, spread(): return lax.psum(kept, axis)  21.7 us
    unnamed x32, local copies, waits for them, and re-layouts  13.4 us
  transfers between devices with their start and end apart: 5, of which 5 were waited for; matrix products, arithmetic and copies ran while one was open for 6% of the time, Pallas kernels for 0%

commit v1 on v0

--- a/solution.py
+++ b/solution.py
@@ -3,7 +3,13 @@
 import jax
 import jax.numpy as jnp
 from jax import lax
+from jax.experimental import pallas as pl
+from jax.experimental.pallas import tpu as pltpu
 from jax.sharding import PartitionSpec as P
+
+F32 = jnp.float32
+BF16 = jnp.bfloat16
+GROUP = ("tensor", "section")
 
 
 def spread(value, axis, source):
@@ -25,7 +31,7 @@
     return jnp.dot(prod_rows, portion, precision=lax.Precision.HIGHEST)
 
 
-def on_device(
+def any_mesh(
     xin,
     dout,
     weights,
@@ -39,7 +45,7 @@
 ):
     block_count, tok_count, block_size = xin.shape
     slot_count, row_count = (left_stat.shape[0], left_stat.shape[1])
-    group_count = lax.axis_size(("tensor", "section"))
+    group_count = lax.axis_size(GROUP)
     shard_count = lax.axis_size("shard")
     factor = 1.0 / math.sqrt(tok_count * shard_count * group_count * block_size)
     pieces_out = []
@@ -50,13 +56,13 @@
         )
     partial_rows = lax.psum_scatter(
         jnp.concatenate(pieces_out, axis=1) * factor,
-        ("tensor", "section"),
+        GROUP,
         scatter_dimension=0,
         tiled=True,
     )
     grad_rows = lax.psum(partial_rows, "shard")
     shard_idx = lax.axis_index("shard")
-    group_idx = lax.axis_index(("tensor", "section"))
+    group_idx = lax.axis_index(GROUP)
     my_slots = lax.dynamic_slice_in_dim(slot_block, shard_idx * slot_count, slot_count)
     valid = my_slots >= 0
     picks = jnp.maximum(my_slots, 0)
@@ -65,7 +71,7 @@
     col_first = group_idx * row_count
     zeros_rows = jnp.zeros((slot_count, row_count, block_size), jnp.float32)
     totals = (zeros_rows, zeros_rows, zeros_rows)
-    portion = lax.all_gather(mine, ("tensor", "section"), axis=1, tiled=True)
+    portion = lax.all_gather(mine, GROUP, axis=1, tiled=True)
     lefts = []
     rights = []
     prods = []
@@ -85,7 +91,7 @@
     left_gram = jnp.stack(lefts)
     right_gram = jnp.stack(rights)
     left_prod = jnp.stack(prods)
-    apply_portion = lax.all_gather(right_root, ("tensor", "section"), axis=1, tiled=True)
+    apply_portion = lax.all_gather(right_root, GROUP, axis=1, tiled=True)
     outputs = []
     for apply_slot_pos in range(slot_count):
         outputs.append(
@@ -102,7 +108,7 @@
     adam = moment_one / (jnp.sqrt(moment_two) + 1e-08)
     adam_sq, dir_sq = lax.psum(
         (jnp.sum(adam * adam, axis=(1, 2)), jnp.sum(direction * direction, axis=(1, 2))),
-        ("tensor", "section"),
+        GROUP,
     )
     graft = jnp.sqrt(adam_sq) / (jnp.sqrt(dir_sq) + 1e-06)
     mask = valid[:, None, None]
@@ -129,6 +135,280 @@
     return (new_weights, new_left, new_right, new_first, new_second)
 
 
+def to_core(value):
+    return lax.ppermute(value, "section", [(i, i ^ 1) for i in range(4)])
+
+
+def to_x(value):
+    return lax.ppermute(value, "section", [(i, i ^ 2) for i in range(4)])
+
+
+def to_y(value):
+    return lax.ppermute(value, "shard", [(0, 1), (1, 0)])
+
+
+def to_z(value, bits):
+    return lax.ppermute(value, "tensor", [(i, i ^ bits) for i in range(4)])
+
+
+def to_xz(value, bits):
+    pairs = [(4 * z + s, 4 * (z ^ bits) + (s ^ 2)) for z in range(4) for s in range(4)]
+    return lax.ppermute(value, GROUP, pairs)
+
+
+def to_cy(value):
+    pairs = [(4 * y + s, 4 * (1 - y) + (s ^ 1)) for y in range(2) for s in range(4)]
+    return lax.ppermute(value, ("shard", "section"), pairs)
+
+
+def row_dot(rows, full):
+    return lax.dot_general(rows, full, (((1,), (0,)), ((), ())), preferred_element_type=F32)
+
+
+def row_dot_t(rows, full):
+    return lax.dot_general(rows, full, (((1,), (1,)), ((), ())), preferred_element_type=F32)
+
+
+def halves(value):
+    high = value.astype(BF16)
+    return high, (value - high.astype(F32)).astype(BF16)
+
+
+def place_pieces(where, pieces, high_ref, low_ref):
+    rows = pieces[0].shape[0]
+    for step in range(4):
+        for side in range(2):
+            spot = 2 * (where[0] ^ step) + (where[1] ^ side)
+            first = pl.multiple_of(spot * rows, 32)
+            high, low = halves(pieces[2 * step + side][...])
+            high_ref[pl.ds(first, rows), :] = high
+            low_ref[pl.ds(first, rows), :] = low
+
+
+def root_kernel(where, *refs):
+    place_pieces(where, refs[:8], refs[8], refs[9])
+
+
+def join_root(where, pieces):
+    size = pieces[0].shape[1]
+    return pl.pallas_call(
+        root_kernel,
+        out_shape=[jax.ShapeDtypeStruct((size, size), BF16)] * 2,
+        in_specs=[pl.BlockSpec(memory_space=pltpu.SMEM)]
+        + [pl.BlockSpec(memory_space=pltpu.VMEM)] * 8,
+        out_specs=[pl.BlockSpec(memory_space=pltpu.VMEM)] * 2,
+        compiler_params=pltpu.CompilerParams(vmem_limit_bytes=40 << 20),
+    )(where, *pieces)
+
+
+def block_kernel(where, *refs):
+    pieces = refs[:8]
+    left_ref, root_high, root_low = refs[8:11]
+    left_out, right_out, dir_out, sum_out = refs[11:15]
+    high_ref, low_ref = refs[15:17]
+    place_pieces(where, pieces, high_ref, low_ref)
+    rows, size = left_ref.shape
+    first = (2 * where[0] + where[1]) * rows
+    high, low = high_ref[...], low_ref[...]
+    left_high, left_low = halves(left_ref[...])
+    prod = row_dot(left_high, high) + (row_dot(left_low, high) + row_dot(left_high, low))
+    prod_high, prod_low = halves(prod)
+    root_h, root_l = root_high[...], root_low[...]
+    direction = row_dot(prod_high, root_h) + (
+        row_dot(prod_low, root_h) + row_dot(prod_high, root_l)
+    )
+    dir_out[...] = direction
+    sum_out[...] = jnp.sum(direction * direction, axis=0, keepdims=True)
+    own_high, own_low = halves(pieces[0][...])
+    left_out[...] = row_dot_t(own_high, high) + (
+        row_dot_t(own_low, high) + row_dot_t(own_high, low)
+    )
+    row_ids = lax.broadcasted_iota(jnp.int32, (rows, size), 0) + first
+    col_ids = lax.broadcasted_iota(jnp.int32, (rows, size), 1)
+    pick = jnp.where(row_ids == col_ids, 1.0, 0.0).astype(BF16)
+    col_high = row_dot_t(pick, high).astype(BF16)
+    col_low = row_dot_t(pick, low).astype(BF16)
+    right_out[...] = row_dot(col_high, high) + (row_dot(col_low, high) + row_dot(col_high, low))
+
+
+def block_products(where, pieces, left_rows, root_high, root_low):
+    rows, size = left_rows.shape
+    tile = jax.ShapeDtypeStruct((rows, size), F32)
+    return pl.pallas_call(
+        block_kernel,
+        out_shape=[tile, tile, tile, jax.ShapeDtypeStruct((1, size), F32)],
+        in_specs=[pl.BlockSpec(memory_space=pltpu.SMEM)]
+        + [pl.BlockSpec(memory_space=pltpu.VMEM)] * 11,
+        out_specs=[pl.BlockSpec(memory_space=pltpu.VMEM)] * 4,
+        scratch_shapes=[pltpu.VMEM((size, size), BF16)] * 2,
+        compiler_params=pltpu.CompilerParams(vmem_limit_bytes=48 << 20),
+    )(where, *pieces, left_rows, root_high, root_low)
+
+
+def gather_chips(value):
+    column = [value] + [to_z(value, bits) for bits in (1, 2, 3)]
+    pieces = []
+    for piece in column:
+        pieces += [piece, to_x(piece)]
+    return pieces
+
+
+def pick_block(stack, index):
+    return lax.dynamic_index_in_dim(stack, index, 0, keepdims=False)
+
+
+def pick_rows(value, first, count):
+    return lax.dynamic_slice_in_dim(value, first, count, 0)
+
+
+def two_planes(
+    xin,
+    dout,
+    weights,
+    slot_block,
+    left_stat,
+    right_stat,
+    left_root,
+    right_root,
+    first_moment,
+    second_moment,
+):
+    block_count, tok_count, size = xin.shape
+    slot_count, rows = left_stat.shape[:2]
+    factor = 1.0 / math.sqrt(tok_count * lax.axis_size(("shard",) + GROUP) * size)
+    s = lax.axis_index("shard")
+    z = lax.axis_index("tensor")
+    section = lax.axis_index("section")
+    x, c = section // 2, section % 2
+    where = jnp.stack([z, x]).astype(jnp.int32)
+
+    table = slot_block.reshape(2, slot_count)
+    used = (table >= 0).astype(jnp.int32)
+    order = jnp.cumsum(used, axis=1) * used
+    spots = jnp.arange(slot_count, dtype=jnp.int32)
+    place = jnp.stack([jnp.sum(jnp.where(order == j + 1, spots, 0), axis=1) for j in (0, 1)], 1)
+    block = jnp.stack([jnp.sum(jnp.where(order == j + 1, table, 0), axis=1) for j in (0, 1)], 1)
+    mine, far = block[s, c], block[1 - s, c]
+    sib_mine, sib_far = block[s, 1 - c], block[1 - s, 1 - c]
+    my_place, sib_place = place[s, c], place[s, 1 - c]
+
+    def gradient(own, sibling):
+        other_in = to_core(pick_block(xin, sibling))
+        other_out = to_core(pick_block(dout, sibling))
+        first = jnp.einsum(
+            "tr,tc->rc", pick_block(xin, own), pick_block(dout, own), preferred_element_type=F32
+        )
+        return first + jnp.einsum("tr,tc->rc", other_in, other_out, preferred_element_type=F32)
+
+    grad_far = gradient(far, sib_far)
+    grad_mine = gradient(mine, sib_mine)
+
+    def chip_rows(stack):
+        other = to_core(pick_block(stack, sib_place))
+        own = pick_block(stack, my_place)
+        return jnp.concatenate(
+            [jnp.where(c == 0, own, other), jnp.where(c == 0, other, own)], axis=0
+        )
+
+    chip = 2 * rows
+    total = None
+    for bits in (3, 2, 1, 0):
+        start = (z ^ bits) * (2 * chip)
+        got = to_y(pick_rows(grad_far, start, 2 * chip))
+        both = got + pick_rows(grad_mine, start, 2 * chip)
+        got = to_x(pick_rows(both, (1 - x) * chip, chip))
+        both = got + pick_rows(both, x * chip, chip)
+        if bits:
+            both = to_z(both, bits)
+        total = both if total is None else total + both
+    grad = total * factor
+
+    root_high, root_low = join_root(where, gather_chips(chip_rows(right_root)))
+    left_rows = chip_rows(left_root)
+    pieces = gather_chips(grad)
+
+    def by_slot(own, other):
+        return jnp.where(c == 0, own, other), jnp.where(c == 0, other, own)
+
+    def swap_rows(value):
+        sent = to_core(pick_rows(value, (1 - c) * rows, rows))
+        return by_slot(pick_rows(value, c * rows, rows), sent)
+
+    grad_rows = swap_rows(grad)
+    places = [place[s, 0], place[s, 1]]
+    held = [jnp.arange(slot_count)[:, None, None] == places[j] for j in (0, 1)]
+    firsts = [
+        0.9 * pick_block(first_moment, places[j]) + 0.1 * grad_rows[j] for j in (0, 1)
+    ]
+    seconds = [
+        0.999 * pick_block(second_moment, places[j]) + 0.001 * grad_rows[j] * grad_rows[j]
+        for j in (0, 1)
+    ]
+    new_first = jnp.where(held[0], firsts[0], jnp.where(held[1], firsts[1], first_moment))
+    new_second = jnp.where(held[0], seconds[0], jnp.where(held[1], seconds[1], second_moment))
+
+    def device_sum(mine_sums):
+        near = mine_sums
+        near = jnp.concatenate([near, to_core(near), to_y(near), to_cy(near)], axis=0)
+        total = near
+        parts = [to_x(near)]
+        for bits in (1, 2, 3):
+            parts += [to_z(near, bits), to_xz(near, bits)]
+        for part in parts:
+            total = total + part
+        return total
+
+    adams = [firsts[j] / (jnp.sqrt(seconds[j]) + 1e-08) for j in (0, 1)]
+    adam_sums = [jnp.sum(value * value) for value in adams]
+    lanes = lax.broadcasted_iota(jnp.int32, (1, 128), 1)
+    adam_own = jnp.where(lanes == 0, adam_sums[0], jnp.where(lanes == 1, adam_sums[1], 0.0))
+    adam_all = device_sum(adam_own)
+    adam_near = adam_all[0] + adam_all[1]
+    adam_mirror = adam_all[2] + adam_all[3]
+
+    left_gram, right_gram, direction, dir_lanes = block_products(
+        where, pieces, left_rows, root_high, root_low
+    )
+    dir_own = jnp.where(lanes == 0, jnp.sum(dir_lanes), 0.0)
+    dir_all = device_sum(dir_own)[:, 0]
+
+    left_rows2 = swap_rows(left_gram)
+    right_rows2 = swap_rows(right_gram)
+    new_left = jnp.where(
+        held[0] | held[1],
+        0.5 * left_stat + 0.5 * jnp.where(held[0], left_rows2[0], left_rows2[1]),
+        left_stat,
+    )
+    new_right = jnp.where(
+        held[0] | held[1],
+        0.5 * right_stat + 0.5 * jnp.where(held[0], right_rows2[0], right_rows2[1]),
+        right_stat,
+    )
+
+    own_dir = pick_rows(direction, c * rows, rows)
+    out_dir = pick_rows(direction, (1 - c) * rows, rows)
+    near_dir = jnp.stack([own_dir, to_core(out_dir)])
+    dirs = jnp.concatenate([near_dir, to_y(near_dir)])
+    adam_near_own = jnp.where(c == 0, adam_near[0], adam_near[1])
+    adam_near_sib = jnp.where(c == 0, adam_near[1], adam_near[0])
+    adam_mir_own = jnp.where(c == 0, adam_mirror[0], adam_mirror[1])
+    adam_mir_sib = jnp.where(c == 0, adam_mirror[1], adam_mirror[0])
+    adam_four = jnp.stack([adam_near_own, adam_near_sib, adam_mir_own, adam_mir_sib])
+    graft = jnp.sqrt(adam_four) / (jnp.sqrt(dir_all) + 1e-06)
+    order_four = jnp.stack([mine, sib_mine, far, sib_far])
+    members = []
+    for member in range(block_count):
+        hit = order_four == member
+        value = jnp.zeros((rows, size), F32)
+        for j in range(4):
+            value = jnp.where(hit[j], dirs[j], value)
+        scale = jnp.sum(jnp.where(hit, graft, 0.0))
+        members.append(
+            (weights[member].astype(F32) - 0.05 * scale * value).astype(BF16)
+        )
+    return (jnp.stack(members), new_left, new_right, new_first, new_second)
+
+
 def solution(mesh):
     placed = (
         P(None, ("shard", "tensor", "section"), None),
@@ -142,8 +422,10 @@
         P("shard", ("tensor", "section"), None),
         P("shard", ("tensor", "section"), None),
     )
+    shape = mesh.shape
+    pair = (shape["shard"], shape["tensor"], shape["section"]) == (2, 4, 4)
     return jax.shard_map(
-        on_device,
+        two_planes if pair else any_mesh,
         mesh=mesh,
         in_specs=placed,
         out_specs=(

time: 414 us -> 249 us (0.60)
  waiting for transfers between devices: 291 us -> 89.9 us
  starting transfers between devices: 0.2 us -> 75.9 us
  blocking collectives: 30.8 us -> 0 us
  matrix products: 30.5 us -> 7.15 us
  other arithmetic: 12.2 us -> 31.1 us
  local copies, waits for them, and re-layouts: 21.3 us -> 14.1 us
  Pallas kernels: 0 us -> 5.58 us
    all_gather x2 -> x0, waiting for transfers between devices: 124 us -> none  [the longest x1 66 us: on_device(): portion = lax.all_gather(mine, ('tensor', 'section'), axis=1, tiled=True)]
    unnamed x6 -> x0, waiting for transfers between devices: 115 us -> none
    ppermute x0 -> x56, waiting for transfers between devices: none -> 89.9 us  [the longest x7 39.5 us: to_y(): return lax.ppermute(value, 'shard', [(0, 1), (1, 0)])]
    ppermute x0 -> x56, starting transfers between devices: none -> 75.9 us  [the longest x15 36.6 us: to_z(): return lax.ppermute(value, 'tensor', [(i, i ^ bits) for i in range(4)])]
    psum x2 -> x0, waiting for transfers between devices: 51.5 us -> none  [the longest x1 29.8 us: on_device(): grad_rows = lax.psum(partial_rows, 'shard')]
    psum x1 -> x0, blocking collectives: 30.8 us -> none  [on_device(): lax.psum((jnp.sum(adam * adam, axis=(1, 2)), jnp.sum(direction * directio...]
    dot_general x12 -> x4, matrix products: 30.5 us -> 7.15 us  [the longest x2 4.36 us: gradient(): jnp.einsum('tr,tc->rc', pick_block(xin, own), pick_block(dout, own), pref...]
    unnamed x32 -> x14, local copies, waits for them, and re-layouts: 13.4 us -> 0.21 us
  transfers between devices with their start and end apart: 5 -> 56, of which waited for: 5 -> 17; matrix products, arithmetic and copies ran while one was open for 6% -> 14% of each run, Pallas kernels for 0% -> 0%
where the time goes in v1:
time: 249 us; the launch traced here: 248 us
  waiting for transfers between devices  89.9 us (36%)
  starting transfers between devices  75.9 us (30%)
  other arithmetic  31.1 us (12%)
  between operations  24.2 us (10%)
  local copies, waits for them, and re-layouts  14.1 us (6%)
  matrix products  7.15 us (3%)
  Pallas kernels  5.58 us (2%)
    ppermute x7, waiting for transfers between devices, to_y(): return lax.ppermute(value, 'shard', [(0, 1), (1, 0)])  39.5 us
    ppermute x15, starting transfers between devices, to_z(): return lax.ppermute(value, 'tensor', [(i, i ^ bits) for i in range(4)])  36.6 us
    ppermute x14, waiting for transfers between devices, to_x(): return lax.ppermute(value, 'section', [(i, i ^ 2) for i in range(4)])  25.3 us
    ppermute x15, waiting for transfers between devices, to_z(): return lax.ppermute(value, 'tensor', [(i, i ^ bits) for i in range(4)])  21.7 us
    ppermute x14, starting transfers between devices, to_x(): return lax.ppermute(value, 'section', [(i, i ^ 2) for i in range(4)])  18.3 us
    another operation x3, other arithmetic, two_planes(): return (jnp.stack(members), new_left, new_right, new_first, new_second)  10.9 us
    ppermute x7, starting transfers between devices, to_y(): return lax.ppermute(value, 'shard', [(0, 1), (1, 0)])  9.37 us
    ppermute x6, starting transfers between devices, to_xz(): return lax.ppermute(value, GROUP, pairs)  8.75 us
  transfers between devices with their start and end apart: 56, of which 17 were waited for; matrix products, arithmetic and copies ran while one was open for 14% of the time, Pallas kernels for 0%

profile of v1, /device:TPU:0, one launch (start us, length us, event | category | flops | bytes accessed | tf_op | source)
XLA Modules:
  0.0 247.9 jit_solution(18037004264549186719)
XLA Ops:
  6.3 2.8 %dynamic-slice_bitcast_fusion.1 = (bf16[512,768]{1,0:T(8,128)(2,1)}, bf16[512,768]{1,0:T(8,128)(2,1)}) fusion(bf16[4,512,768]{2,1,0:T(8,128)(2,1)} %param.10, s32[]{:T(128)S(6)} %select_n.364, s32[]{:T(128)S(6)} %select_n.361), kind=kLoop, calls=%fused_computation.9 | loop fusion | bytes 3145736 | tf_op jit(solution)/shard_map/jit(dynamic_index_in_dim)/squeeze | solution.py:257
  9.6 1.0 dynamic-slice_bitcast_fusion
  19.1 2.7 %broadcast_compare_fusion.4 = (pred[4]{0:T(512)(128)(4,1)S(1)}, s32[4]{0:T(128)S(1)}) fusion(s32[1]{0:T(128)} %bitcast.6, s32[1]{0:T(128)} %bitcast.5, s32[1]{0:T(128)} %bitcast.4, s32[1]{0:T(128)} %bitcast.3), kind=kLoop, calls=%fused_computation.114 | loop fusion | flops 16 | bytes 36 | tf_op jit(solution)/shard_map/eq | solution.py:401
  25.8 2.2 fusion.3
  28.0 1.2 iota_compare_fusion.1
  29.2 2.2 fusion
  31.4 1.9 convolution_add_fusion.1
  33.6 2.6 %collective-permute-start.10 = (f32[192,768]{1,0:T(8,128)S(1)}, f32[192,768]{1,0:T(8,128)S(1)}, u32[]{:S(2)}, u32[]{:S(2)}) collective-permute-start(f32[192,768]{1,0:T(8,128)S(1)} %get-tuple-element.43), channel_id=1, source_target_pairs={{0,16},{16,0},{1,17},{17,1},{2,18},{18,2},{3,19},{19,3},{4,20},{20... | collective-permute-start | bytes 1769480 | tf_op jit(solution)/shard_map/ppermute | solution.py:147
  36.2 1.9 collective-permute-start.2
  39.2 2.1 collective-permute-start.36
  42.2 8.2 %collective-permute-done.10 = f32[192,768]{1,0:T(8,128)S(1)} collective-permute-done((f32[192,768]{1,0:T(8,128)S(1)}, f32[192,768]{1,0:T(8,128)S(1)}, u32[]{:S(2)}, u32[]{:S(2)}) %collective-permute-start.10) | collective-permute-done | bytes 589856 | tf_op jit(solution)/shard_map/ppermute | solution.py:147
  50.3 3.0 %collective-permute-start.38 = (f32[96,768]{1,0:T(8,128)S(1)}, f32[96,768]{1,0:T(8,128)S(1)}, u32[]{:S(2)}, u32[]{:S(2)}) collective-permute-start(f32[96,768]{1,0:T(8,128)S(1)} %pad_maximum_fusion.1.refs_0_), channel_id=1, source_target_pairs={{0,8},{4,12},{8,0},{12,4},{1,9},{5,13},{9,1},{13,5},{2,10},{6,14},... | collective-permute-start | bytes 884744 | tf_op jit(solution)/shard_map/ppermute | solution.py:151
  53.3 9.6 %collective-permute-done.13 = f32[192,768]{1,0:T(8,128)S(1)} collective-permute-done((f32[192,768]{1,0:T(8,128)S(1)}, f32[192,768]{1,0:T(8,128)S(1)}, u32[]{:S(2)}, u32[]{:S(2)}) %collective-permute-start.13) | collective-permute-done | bytes 589856 | tf_op jit(solution)/shard_map/ppermute | solution.py:147
  63.0 4.0 %collective-permute-start.40 = (f32[96,768]{1,0:T(8,128)S(1)}, f32[96,768]{1,0:T(8,128)S(1)}, u32[]{:S(2)}, u32[]{:S(2)}) collective-permute-start(f32[96,768]{1,0:T(8,128)S(1)} %pad_maximum_fusion.1.refs_0_), channel_id=1, source_target_pairs={{0,12},{4,8},{8,4},{12,0},{1,13},{5,9},{9,5},{13,1},{2,14},{6,10},... | collective-permute-start | bytes 884744 | tf_op jit(solution)/shard_map/ppermute | solution.py:151
  67.0 8.6 %collective-permute-done.2 = f32[192,768]{1,0:T(8,128)S(1)} collective-permute-done((f32[192,768]{1,0:T(8,128)S(1)}, f32[192,768]{1,0:T(8,128)S(1)}, u32[]{:S(2)}, u32[]{:S(2)}) %collective-permute-start.2) | collective-permute-done | bytes 589856 | tf_op jit(solution)/shard_map/ppermute | solution.py:147
  75.6 12.5 %collective-permute-done.7 = f32[192,768]{1,0:T(8,128)S(1)} collective-permute-done((f32[192,768]{1,0:T(8,128)S(1)}, f32[192,768]{1,0:T(8,128)S(1)}, u32[]{:S(2)}, u32[]{:S(2)}) %collective-permute-start.7) | collective-permute-done | bytes 589856 | tf_op jit(solution)/shard_map/ppermute | solution.py:147
  88.4 1.8 collective-permute-start.8
  90.6 7.7 %collective-permute-done.8 = f32[96,768]{1,0:T(8,128)S(1)} collective-permute-done((f32[96,768]{1,0:T(8,128)S(1)}, f32[96,768]{1,0:T(8,128)S(1)}, u32[]{:S(2)}, u32[]{:S(2)}) %collective-permute-start.8) | collective-permute-done | bytes 294944 | tf_op jit(solution)/shard_map/ppermute | solution.py:143
  98.3 1.7 collective-permute-start.11
  100.1 4.5 %collective-permute-done.5 = f32[96,768]{1,0:T(8,128)S(1)} collective-permute-done((f32[96,768]{1,0:T(8,128)S(1)}, f32[96,768]{1,0:T(8,128)S(1)}, u32[]{:S(2)}, u32[]{:S(2)}) %collective-permute-start.5) | collective-permute-done | bytes 294944 | tf_op jit(solution)/shard_map/ppermute | solution.py:143
  104.7 1.7 collective-permute-start.14
  106.4 4.5 %collective-permute-done.11 = f32[96,768]{1,0:T(8,128)S(1)} collective-permute-done((f32[96,768]{1,0:T(8,128)S(1)}, f32[96,768]{1,0:T(8,128)S(1)}, u32[]{:S(2)}, u32[]{:S(2)}) %collective-permute-start.11) | collective-permute-done | bytes 294944 | tf_op jit(solution)/shard_map/ppermute | solution.py:143
  111.0 2.8 %collective-permute-start.9 = (f32[96,768]{1,0:T(8,128)S(1)}, f32[96,768]{1,0:T(8,128)}, u32[]{:S(2)}, u32[]{:S(2)}) collective-permute-start(f32[96,768]{1,0:T(8,128)S(1)} %dynamic-slice_add_fusion.5), channel_id=1, source_target_pairs={{0,8},{4,12},{8,0},{12,4},{1,9},{5,13},{9,1},{13,5},{2,10},{6,14},... | collective-permute-start | bytes 884744 | tf_op jit(solution)/shard_map/ppermute | solution.py:151
  114.6 1.3 collective-permute-start.6
  116.2 1.2 iota_compare_fusion
  117.4 1.6 dynamic-slice_bitcast_fusion.5
  119.0 1.5 collective-permute-start.35
  125.0 7.6 %collective-permute-done.9 = f32[96,768]{1,0:T(8,128)} collective-permute-done((f32[96,768]{1,0:T(8,128)S(1)}, f32[96,768]{1,0:T(8,128)}, u32[]{:S(2)}, u32[]{:S(2)}) %collective-permute-start.9) | collective-permute-done | bytes 294944 | tf_op jit(solution)/shard_map/ppermute | solution.py:151
  132.5 1.5 collective-permute-start.39
  134.0 1.0 collective-permute-start.41
  135.1 1.1 add_multiply_fusion.refs_0_
  136.2 5.4 %collective-permute-start.27 = (f32[96,768]{1,0:T(8,128)S(1)}, f32[96,768]{1,0:T(8,128)S(1)}, u32[]{:S(2)}, u32[]{:S(2)}) collective-permute-start(f32[96,768]{1,0:T(8,128)S(1)} %add_multiply_fusion.refs_0_), channel_id=1, source_target_pairs={{0,4},{4,0},{8,12},{12,8},{1,5},{5,1},{9,13},{13,9},{2,6},{6,2},{1... | collective-permute-start | bytes 884744 | tf_op jit(solution)/shard_map/ppermute | solution.py:151
  141.6 1.9 collective-permute-start.29
  143.5 1.4 collective-permute-start.31
  146.0 2.3 collective-permute-done.41.refs_7_
  148.3 1.5 collective-permute-start.26
  149.8 4.1 %collective-permute-done.27.refs_2_ = f32[96,768]{1,0:T(8,128)S(1)} collective-permute-done((f32[96,768]{1,0:T(8,128)S(1)}, f32[96,768]{1,0:T(8,128)S(1)}, u32[]{:S(2)}, u32[]{:S(2)}) %collective-permute-start.27) | collective-permute-done | bytes 294944 | tf_op jit(solution)/shard_map/ppermute | solution.py:151
  153.9 1.5 collective-permute-start.28
  155.4 9.7 %collective-permute-done.29.refs_4_ = f32[96,768]{1,0:T(8,128)S(1)} collective-permute-done((f32[96,768]{1,0:T(8,128)S(1)}, f32[96,768]{1,0:T(8,128)S(1)}, u32[]{:S(2)}, u32[]{:S(2)}) %collective-permute-start.29) | collective-permute-done | bytes 294944 | tf_op jit(solution)/shard_map/ppermute | solution.py:151
  165.1 1.4 collective-permute-start.30
  168.1 1.5 multiply_reduce_fusion.1
  169.6 3.1 %collective-permute-done.30.refs_5_ = f32[96,768]{1,0:T(8,128)S(1)} collective-permute-done((f32[96,768]{1,0:T(8,128)S(1)}, f32[96,768]{1,0:T(8,128)S(1)}, u32[]{:S(2)}, u32[]{:S(2)}) %collective-permute-start.30) | collective-permute-done | bytes 294944 | tf_op jit(solution)/shard_map/ppermute | solution.py:143
  172.7 3.2 %collective-permute-done.32.refs_7_ = f32[96,768]{1,0:T(8,128)S(1)} collective-permute-done((f32[96,768]{1,0:T(8,128)S(1)}, f32[96,768]{1,0:T(8,128)S(1)}, u32[]{:S(2)}, u32[]{:S(2)}) %collective-permute-start.32) | collective-permute-done | bytes 294944 | tf_op jit(solution)/shard_map/ppermute | solution.py:143
  175.9 4.7 %shard_map.138 = (f32[96,768]{1,0:T(8,128)S(1)}, f32[96,768]{1,0:T(8,128)S(1)}, f32[96,768]{1,0:T(8,128)S(1)}, f32[1,768]{1,0:T(1,128)S(1)}) custom-call(s32[2]{0:T(128)S(1)} %pad_add_fusion.3.where, f32[96,768]{1,0:T(8,128)S(1)} %add_multiply_fusion.refs_0_, f32[96,768]{1,0:T(8,128)S(1)} %collective-permute-done.26.refs_1_, ...), custom_call_target="tpu_custom_call" | custom-call | tf_op jit(solution)/shard_map/pallas_call | solution.py:237
  181.1 1.9 compare_select_fusion.1
  183.2 1.6 collective-permute-start.17
  185.4 1.5 collective-permute-start.43
  188.3 1.6 collective-permute-start.19
  189.8 4.7 %collective-permute-start.20 = (f32[4,128]{1,0:T(4,128)S(1)}, f32[4,128]{1,0:T(4,128)S(1)}, u32[]{:S(2)}, u32[]{:S(2)}) collective-permute-start(f32[4,128]{1,0:T(4,128)S(1)} %pad_maximum_fusion.4), channel_id=1, source_target_pairs={{0,4},{4,0},{8,12},{12,8},{1,5},{5,1},{9,13},{13,9},{2,6},{6,2},{1... | collective-permute-start | bytes 6152 | tf_op jit(solution)/shard_map/ppermute | solution.py:151
  195.2 3.9 %collective-permute-start.22 = (f32[4,128]{1,0:T(4,128)S(1)}, f32[4,128]{1,0:T(4,128)S(1)}, u32[]{:S(2)}, u32[]{:S(2)}) collective-permute-start(f32[4,128]{1,0:T(4,128)S(1)} %pad_maximum_fusion.4), channel_id=1, source_target_pairs={{0,8},{4,12},{8,0},{12,4},{1,9},{5,13},{9,1},{13,5},{2,10},{6,14},... | collective-permute-start | bytes 6152 | tf_op jit(solution)/shard_map/ppermute | solution.py:151
  199.2 1.0 collective-permute-start.23
  200.2 2.3 collective-permute-start.24
  202.5 1.5 collective-permute-start.25
  204.0 1.5 collective-permute-start.45
  205.5 2.0 collective-permute-start.47
  207.6 1.0 collective-permute-start.48
  208.7 2.7 %collective-permute-start.49 = (f32[4,128]{1,0:T(4,128)S(1)}, f32[4,128]{1,0:T(4,128)S(1)}, u32[]{:S(2)}, u32[]{:S(2)}) collective-permute-start(f32[4,128]{1,0:T(4,128)S(1)} %pad_maximum_fusion.5), channel_id=1, source_target_pairs={{0,10},{1,11},{2,8},{3,9},{4,14},{5,15},{6,12},{7,13},{8,2},{9,3},... | collective-permute-start | bytes 6152 | tf_op jit(solution)/shard_map/ppermute | solution.py:156
  211.4 2.4 collective-permute-start.50
  213.8 1.5 collective-permute-start.51
  216.9 3.2 %collective-permute-done.51 = f32[4,128]{1,0:T(4,128)S(1)} collective-permute-done((f32[4,128]{1,0:T(4,128)S(1)}, f32[4,128]{1,0:T(4,128)S(1)}, u32[]{:S(2)}, u32[]{:S(2)}) %collective-permute-start.51) | collective-permute-done | bytes 2080 | tf_op jit(solution)/shard_map/ppermute | solution.py:156
  230.2 1.6 collective-permute-start.53
  233.7 2.6 %select_select_fusion = (f32[4,48,768]{2,1,0:T(8,128)}, f32[4,48,768]{2,1,0:T(8,128)}, f32[4,48,768]{2,1,0:T(8,128)}, f32[4,48,768]{2,1,0:T(8,128)}) fusion(f32[4,48,768]{2,1,0:T(8,128)S(1)} %copy-done, f32[48,768]{1,0:T(8,128)} %get-tuple-element.46, f32[48,768]{1,0:T(8,128)S(1)} %get-tuple-element.28, pred[4]{0:T(512)(128)(4,1)} %iota_compare_fusion, ...), kind=kLoop, calls=%fused_computation.16 | loop fusion | flops 1769472 | bytes 5898252 | tf_op jit(solution)/shard_map/jit(_where)/select_n | solution.py:348
  237.0 5.0 %fusion.17 = (bf16[1,48,768]{2,1,0:T(8,128)(2,1)S(1)}, bf16[1,48,768]{2,1,0:T(8,128)(2,1)S(1)}) fusion(f32[48,768]{1,0:T(8,128)S(1)} %collective-permute-done.52, f32[96,768]{1,0:T(8,128)S(1)} %get-tuple-element.14, s32[]{:T(128)S(6)} %select_n.371, f32[2,48,768]{2,1,0:T(8,128)S(1)} %collective-permute-done.53, f32[]{:T(128)S(6)} %mul.167, ...), kind=kLoop, calls=%fused_computation.64 | loop fusion | flops 589824 | bytes 884756 | tf_op jit(solution)/shard_map/stack | solution.py:409
  242.0 5.2 %fusion.16 = (bf16[1,48,768]{2,1,0:T(8,128)(2,1)S(1)}, bf16[1,48,768]{2,1,0:T(8,128)(2,1)S(1)}) fusion(f32[48,768]{1,0:T(8,128)S(1)} %collective-permute-done.52, f32[96,768]{1,0:T(8,128)S(1)} %get-tuple-element.14, s32[]{:T(128)S(6)} %select_n.371, f32[2,48,768]{2,1,0:T(8,128)S(1)} %collective-permute-done.53, f32[]{:T(128)S(6)} %mul.164, ...), kind=kLoop, calls=%fused_computation.63 | loop fusion | flops 589824 | bytes 884756 | tf_op jit(solution)/shard_map/stack | solution.py:409
  (125 shorter events, 25.2 us)
Async XLA Ops:
  6.3 3.3 %copy-start.2 = (bf16[4,512,768]{2,1,0:T(8,128)(2,1)S(1)}, bf16[4,512,768]{2,1,0:T(8,128)(2,1)}, u32[]{:S(2)}) copy-start(bf16[4,512,768]{2,1,0:T(8,128)(2,1)} %param.11) | copy-start | bytes 9437188
  9.1 22.3 %collective-permute-start = (bf16[512,768]{1,0:T(8,128)(2,1)}, bf16[512,768]{1,0:T(8,128)(2,1)S(1)}, u32[]{:S(2)}, u32[]{:S(2)}) collective-permute-start(bf16[512,768]{1,0:T(8,128)(2,1)} %get-tuple-element.36), channel_id=1, source_target_pairs={{0,1},{1,0},{2,3},{3,2},{4,5},{5,4},{6,7},{7,6},{8,9},{9,8},{10,11... | collective-permute-start | bytes 2359304 | tf_op jit(solution)/shard_map/ppermute | solution.py:139
  10.6 20.9 %collective-permute-start.1 = (bf16[512,768]{1,0:T(8,128)(2,1)}, bf16[512,768]{1,0:T(8,128)(2,1)}, u32[]{:S(2)}, u32[]{:S(2)}) collective-permute-start(bf16[512,768]{1,0:T(8,128)(2,1)} %get-tuple-element.34), channel_id=1, source_target_pairs={{0,1},{1,0},{2,3},{3,2},{4,5},{5,4},{6,7},{7,6},{8,9},{9,8},{10,11... | collective-permute-start | bytes 2359304 | tf_op jit(solution)/shard_map/ppermute | solution.py:139
  10.6 27.6 %collective-permute-start.3 = (bf16[512,768]{1,0:T(8,128)(2,1)}, bf16[512,768]{1,0:T(8,128)(2,1)S(1)}, u32[]{:S(2)}, u32[]{:S(2)}) collective-permute-start(bf16[512,768]{1,0:T(8,128)(2,1)} %get-tuple-element.35), channel_id=1, source_target_pairs={{0,1},{1,0},{2,3},{3,2},{4,5},{5,4},{6,7},{7,6},{8,9},{9,8},{10,11... | collective-permute-start | bytes 2359304 | tf_op jit(solution)/shard_map/ppermute | solution.py:139
  11.1 28.2 %collective-permute-start.4 = (bf16[512,768]{1,0:T(8,128)(2,1)S(1)}, bf16[512,768]{1,0:T(8,128)(2,1)S(1)}, u32[]{:S(2)}, u32[]{:S(2)}) collective-permute-start(bf16[512,768]{1,0:T(8,128)(2,1)S(1)} %get-tuple-element.33), channel_id=1, source_target_pairs={{0,1},{1,0},{2,3},{3,2},{4,5},{5,4},{6,7},{7,6},{8,9},{9,8},{10,11... | collective-permute-start | bytes 2359304 | tf_op jit(solution)/shard_map/ppermute | solution.py:139
  14.7 21.6 %collective-permute-start.34 = (f32[48,768]{1,0:T(8,128)S(1)}, f32[48,768]{1,0:T(8,128)S(1)}, u32[]{:S(2)}, u32[]{:S(2)}) collective-permute-start(f32[48,768]{1,0:T(8,128)S(1)} %dynamic-slice_bitcast_fusion.4), channel_id=1, source_target_pairs={{0,1},{1,0},{2,3},{3,2},{4,5},{5,4},{6,7},{7,6},{8,9},{9,8},{10,11... | collective-permute-start | bytes 442376 | tf_op jit(solution)/shard_map/ppermute | solution.py:139
  33.6 16.8 %collective-permute-start.10 = (f32[192,768]{1,0:T(8,128)S(1)}, f32[192,768]{1,0:T(8,128)S(1)}, u32[]{:S(2)}, u32[]{:S(2)}) collective-permute-start(f32[192,768]{1,0:T(8,128)S(1)} %get-tuple-element.43), channel_id=1, source_target_pairs={{0,16},{16,0},{1,17},{17,1},{2,18},{18,2},{3,19},{19,3},{4,20},{20... | collective-permute-start | bytes 1769480 | tf_op jit(solution)/shard_map/ppermute | solution.py:147
  36.1 26.8 %collective-permute-start.13 = (f32[192,768]{1,0:T(8,128)S(1)}, f32[192,768]{1,0:T(8,128)S(1)}, u32[]{:S(2)}, u32[]{:S(2)}) collective-permute-start(f32[192,768]{1,0:T(8,128)S(1)} %get-tuple-element.42), channel_id=1, source_target_pairs={{0,16},{16,0},{1,17},{17,1},{2,18},{18,2},{3,19},{19,3},{4,20},{20... | collective-permute-start | bytes 1769480 | tf_op jit(solution)/shard_map/ppermute | solution.py:147
  36.2 39.4 %collective-permute-start.2 = (f32[192,768]{1,0:T(8,128)S(1)}, f32[192,768]{1,0:T(8,128)S(1)}, u32[]{:S(2)}, u32[]{:S(2)}) collective-permute-start(f32[192,768]{1,0:T(8,128)S(1)} %get-tuple-element.44), channel_id=1, source_target_pairs={{0,16},{16,0},{1,17},{17,1},{2,18},{18,2},{3,19},{19,3},{4,20},{20... | collective-permute-start | bytes 1769480 | tf_op jit(solution)/shard_map/ppermute | solution.py:147
  38.2 49.9 %collective-permute-start.7 = (f32[192,768]{1,0:T(8,128)S(1)}, f32[192,768]{1,0:T(8,128)S(1)}, u32[]{:S(2)}, u32[]{:S(2)}) collective-permute-start(f32[192,768]{1,0:T(8,128)S(1)} %get-tuple-element.41), channel_id=1, source_target_pairs={{0,16},{16,0},{1,17},{17,1},{2,18},{18,2},{3,19},{19,3},{4,20},{20... | collective-permute-start | bytes 1769480 | tf_op jit(solution)/shard_map/ppermute | solution.py:147
  39.2 75.3 %collective-permute-start.36 = (f32[96,768]{1,0:T(8,128)S(1)}, f32[96,768]{1,0:T(8,128)S(1)}, u32[]{:S(2)}, u32[]{:S(2)}) collective-permute-start(f32[96,768]{1,0:T(8,128)S(1)} %pad_maximum_fusion.1.refs_0_), channel_id=1, source_target_pairs={{0,4},{4,0},{8,12},{12,8},{1,5},{5,1},{9,13},{13,9},{2,6},{6,2},{1... | collective-permute-start | bytes 884744 | tf_op jit(solution)/shard_map/ppermute | solution.py:151
  50.3 65.6 %collective-permute-start.38 = (f32[96,768]{1,0:T(8,128)S(1)}, f32[96,768]{1,0:T(8,128)S(1)}, u32[]{:S(2)}, u32[]{:S(2)}) collective-permute-start(f32[96,768]{1,0:T(8,128)S(1)} %pad_maximum_fusion.1.refs_0_), channel_id=1, source_target_pairs={{0,8},{4,12},{8,0},{12,4},{1,9},{5,13},{9,1},{13,5},{2,10},{6,14},... | collective-permute-start | bytes 884744 | tf_op jit(solution)/shard_map/ppermute | solution.py:151
  63.0 56.0 %collective-permute-start.40 = (f32[96,768]{1,0:T(8,128)S(1)}, f32[96,768]{1,0:T(8,128)S(1)}, u32[]{:S(2)}, u32[]{:S(2)}) collective-permute-start(f32[96,768]{1,0:T(8,128)S(1)} %pad_maximum_fusion.1.refs_0_), channel_id=1, source_target_pairs={{0,12},{4,8},{8,4},{12,0},{1,13},{5,9},{9,5},{13,1},{2,14},{6,10},... | collective-permute-start | bytes 884744 | tf_op jit(solution)/shard_map/ppermute | solution.py:151
  88.4 9.9 %collective-permute-start.8 = (f32[96,768]{1,0:T(8,128)S(1)}, f32[96,768]{1,0:T(8,128)S(1)}, u32[]{:S(2)}, u32[]{:S(2)}) collective-permute-start(f32[96,768]{1,0:T(8,128)S(1)} %constant_dynamic-slice_fusion.8), channel_id=1, source_target_pairs={{0,2},{1,3},{2,0},{3,1},{4,6},{5,7},{6,4},{7,5},{8,10},{9,11},{10,... | collective-permute-start | bytes 884744 | tf_op jit(solution)/shard_map/ppermute | solution.py:143
  90.2 14.5 %collective-permute-start.5 = (f32[96,768]{1,0:T(8,128)S(1)}, f32[96,768]{1,0:T(8,128)S(1)}, u32[]{:S(2)}, u32[]{:S(2)}) collective-permute-start(f32[96,768]{1,0:T(8,128)S(1)} %constant_dynamic-slice_fusion.10), channel_id=1, source_target_pairs={{0,2},{1,3},{2,0},{3,1},{4,6},{5,7},{6,4},{7,5},{8,10},{9,11},{10,... | collective-permute-start | bytes 884744 | tf_op jit(solution)/shard_map/ppermute | solution.py:143
  98.3 12.6 %collective-permute-start.11 = (f32[96,768]{1,0:T(8,128)S(1)}, f32[96,768]{1,0:T(8,128)S(1)}, u32[]{:S(2)}, u32[]{:S(2)}) collective-permute-start(f32[96,768]{1,0:T(8,128)S(1)} %constant_dynamic-slice_fusion.6), channel_id=1, source_target_pairs={{0,2},{1,3},{2,0},{3,1},{4,6},{5,7},{6,4},{7,5},{8,10},{9,11},{10,... | collective-permute-start | bytes 884744 | tf_op jit(solution)/shard_map/ppermute | solution.py:143
  104.7 15.8 %collective-permute-start.14 = (f32[96,768]{1,0:T(8,128)S(1)}, f32[96,768]{1,0:T(8,128)S(1)}, u32[]{:S(2)}, u32[]{:S(2)}) collective-permute-start(f32[96,768]{1,0:T(8,128)S(1)} %constant_dynamic-slice_fusion.4), channel_id=1, source_target_pairs={{0,2},{1,3},{2,0},{3,1},{4,6},{5,7},{6,4},{7,5},{8,10},{9,11},{10,... | collective-permute-start | bytes 884744 | tf_op jit(solution)/shard_map/ppermute | solution.py:143
  111.0 21.5 %collective-permute-start.9 = (f32[96,768]{1,0:T(8,128)S(1)}, f32[96,768]{1,0:T(8,128)}, u32[]{:S(2)}, u32[]{:S(2)}) collective-permute-start(f32[96,768]{1,0:T(8,128)S(1)} %dynamic-slice_add_fusion.5), channel_id=1, source_target_pairs={{0,8},{4,12},{8,0},{12,4},{1,9},{5,13},{9,1},{13,5},{2,10},{6,14},... | collective-permute-start | bytes 884744 | tf_op jit(solution)/shard_map/ppermute | solution.py:151
  114.6 17.9 %collective-permute-start.6 = (f32[96,768]{1,0:T(8,128)S(1)}, f32[96,768]{1,0:T(8,128)S(1)}, u32[]{:S(2)}, u32[]{:S(2)}) collective-permute-start(f32[96,768]{1,0:T(8,128)S(1)} %dynamic-slice_add_fusion.6), channel_id=1, source_target_pairs={{0,12},{4,8},{8,4},{12,0},{1,13},{5,9},{9,5},{13,1},{2,14},{6,10},... | collective-permute-start | bytes 884744 | tf_op jit(solution)/shard_map/ppermute | solution.py:151
  115.9 18.1 %collective-permute-start.12 = (f32[96,768]{1,0:T(8,128)}, f32[96,768]{1,0:T(8,128)S(1)}, u32[]{:S(2)}, u32[]{:S(2)}) collective-permute-start(f32[96,768]{1,0:T(8,128)} %dynamic-slice_add_fusion.4), channel_id=1, source_target_pairs={{0,4},{4,0},{8,12},{12,8},{1,5},{5,1},{9,13},{13,9},{2,6},{6,2},{1... | collective-permute-start | bytes 884744 | tf_op jit(solution)/shard_map/ppermute | solution.py:151
  119.0 22.6 %collective-permute-start.35 = (f32[96,768]{1,0:T(8,128)S(1)}, f32[96,768]{1,0:T(8,128)S(1)}, u32[]{:S(2)}, u32[]{:S(2)}) collective-permute-start(f32[96,768]{1,0:T(8,128)S(1)} %pad_maximum_fusion.1.refs_0_), channel_id=1, source_target_pairs={{0,2},{1,3},{2,0},{3,1},{4,6},{5,7},{6,4},{7,5},{8,10},{9,11},{10,... | collective-permute-start | bytes 884744 | tf_op jit(solution)/shard_map/ppermute | solution.py:143
  120.5 0.7 copy-start.5
  120.5 23.0 %collective-permute-start.37 = (f32[96,768]{1,0:T(8,128)S(1)}, f32[96,768]{1,0:T(8,128)S(1)}, u32[]{:S(2)}, u32[]{:S(2)}) collective-permute-start(f32[96,768]{1,0:T(8,128)S(1)} %collective-permute-done.36.refs_2_), channel_id=1, source_target_pairs={{0,2},{1,3},{2,0},{3,1},{4,6},{5,7},{6,4},{7,5},{8,10},{9,11},{10,... | collective-permute-start | bytes 884744 | tf_op jit(solution)/shard_map/ppermute | solution.py:143
  132.5 3.7 %collective-permute-start.33 = (f32[48,768]{1,0:T(8,128)}, f32[48,768]{1,0:T(8,128)S(1)}, u32[]{:S(2)}, u32[]{:S(2)}) collective-permute-start(f32[48,768]{1,0:T(8,128)} %dynamic-slice_bitcast_fusion.5), channel_id=1, source_target_pairs={{0,1},{1,0},{2,3},{3,2},{4,5},{5,4},{6,7},{7,6},{8,9},{9,8},{10,11... | collective-permute-start | bytes 442376 | tf_op jit(solution)/shard_map/ppermute | solution.py:139
  132.5 12.4 %collective-permute-start.39 = (f32[96,768]{1,0:T(8,128)S(1)}, f32[96,768]{1,0:T(8,128)S(1)}, u32[]{:S(2)}, u32[]{:S(2)}) collective-permute-start(f32[96,768]{1,0:T(8,128)S(1)} %collective-permute-done.38.refs_4_), channel_id=1, source_target_pairs={{0,2},{1,3},{2,0},{3,1},{4,6},{5,7},{6,4},{7,5},{8,10},{9,11},{10,... | collective-permute-start | bytes 884744 | tf_op jit(solution)/shard_map/ppermute | solution.py:143
  134.0 14.2 %collective-permute-start.41 = (f32[96,768]{1,0:T(8,128)S(1)}, f32[96,768]{1,0:T(8,128)S(1)}, u32[]{:S(2)}, u32[]{:S(2)}) collective-permute-start(f32[96,768]{1,0:T(8,128)S(1)} %collective-permute-done.40.refs_6_), channel_id=1, source_target_pairs={{0,2},{1,3},{2,0},{3,1},{4,6},{5,7},{6,4},{7,5},{8,10},{9,11},{10,... | collective-permute-start | bytes 884744 | tf_op jit(solution)/shard_map/ppermute | solution.py:143
  136.2 31.9 %copy-start = (f32[4,48,768]{2,1,0:T(8,128)S(1)}, f32[4,48,768]{2,1,0:T(8,128)}, u32[]{:S(2)}) copy-start(f32[4,48,768]{2,1,0:T(8,128)} %param.19) | copy-start | bytes 1769476
  136.2 31.9 %copy-start.1 = (f32[4,48,768]{2,1,0:T(8,128)S(1)}, f32[4,48,768]{2,1,0:T(8,128)}, u32[]{:S(2)}) copy-start(f32[4,48,768]{2,1,0:T(8,128)} %param.18) | copy-start | bytes 1769476
  136.2 17.7 %collective-permute-start.27 = (f32[96,768]{1,0:T(8,128)S(1)}, f32[96,768]{1,0:T(8,128)S(1)}, u32[]{:S(2)}, u32[]{:S(2)}) collective-permute-start(f32[96,768]{1,0:T(8,128)S(1)} %add_multiply_fusion.refs_0_), channel_id=1, source_target_pairs={{0,4},{4,0},{8,12},{12,8},{1,5},{5,1},{9,13},{13,9},{2,6},{6,2},{1... | collective-permute-start | bytes 884744 | tf_op jit(solution)/shard_map/ppermute | solution.py:151
  141.6 23.5 %collective-permute-start.29 = (f32[96,768]{1,0:T(8,128)S(1)}, f32[96,768]{1,0:T(8,128)S(1)}, u32[]{:S(2)}, u32[]{:S(2)}) collective-permute-start(f32[96,768]{1,0:T(8,128)S(1)} %add_multiply_fusion.refs_0_), channel_id=1, source_target_pairs={{0,8},{4,12},{8,0},{12,4},{1,9},{5,13},{9,1},{13,5},{2,10},{6,14},... | collective-permute-start | bytes 884744 | tf_op jit(solution)/shard_map/ppermute | solution.py:151
  143.5 23.0 %collective-permute-start.31 = (f32[96,768]{1,0:T(8,128)S(1)}, f32[96,768]{1,0:T(8,128)S(1)}, u32[]{:S(2)}, u32[]{:S(2)}) collective-permute-start(f32[96,768]{1,0:T(8,128)S(1)} %add_multiply_fusion.refs_0_), channel_id=1, source_target_pairs={{0,12},{4,8},{8,4},{12,0},{1,13},{5,9},{9,5},{13,1},{2,14},{6,10},... | collective-permute-start | bytes 884744 | tf_op jit(solution)/shard_map/ppermute | solution.py:151
  145.0 23.1 %collective-permute-start.15 = (f32[48,768]{1,0:T(8,128)S(1)}, f32[48,768]{1,0:T(8,128)S(1)}, u32[]{:S(2)}, u32[]{:S(2)}) collective-permute-start(f32[48,768]{1,0:T(8,128)S(1)} %constant_dynamic-slice_fusion.3), channel_id=1, source_target_pairs={{0,1},{1,0},{2,3},{3,2},{4,5},{5,4},{6,7},{7,6},{8,9},{9,8},{10,11... | collective-permute-start | bytes 442376 | tf_op jit(solution)/shard_map/ppermute | solution.py:139
  148.3 21.3 %collective-permute-start.26 = (f32[96,768]{1,0:T(8,128)S(1)}, f32[96,768]{1,0:T(8,128)S(1)}, u32[]{:S(2)}, u32[]{:S(2)}) collective-permute-start(f32[96,768]{1,0:T(8,128)S(1)} %add_multiply_fusion.refs_0_), channel_id=1, source_target_pairs={{0,2},{1,3},{2,0},{3,1},{4,6},{5,7},{6,4},{7,5},{8,10},{9,11},{10,... | collective-permute-start | bytes 884744 | tf_op jit(solution)/shard_map/ppermute | solution.py:143
  153.9 15.7 %collective-permute-start.28 = (f32[96,768]{1,0:T(8,128)S(1)}, f32[96,768]{1,0:T(8,128)S(1)}, u32[]{:S(2)}, u32[]{:S(2)}) collective-permute-start(f32[96,768]{1,0:T(8,128)S(1)} %collective-permute-done.27.refs_2_), channel_id=1, source_target_pairs={{0,2},{1,3},{2,0},{3,1},{4,6},{5,7},{6,4},{7,5},{8,10},{9,11},{10,... | collective-permute-start | bytes 884744 | tf_op jit(solution)/shard_map/ppermute | solution.py:143
  165.1 7.6 %collective-permute-start.30 = (f32[96,768]{1,0:T(8,128)S(1)}, f32[96,768]{1,0:T(8,128)S(1)}, u32[]{:S(2)}, u32[]{:S(2)}) collective-permute-start(f32[96,768]{1,0:T(8,128)S(1)} %collective-permute-done.29.refs_4_), channel_id=1, source_target_pairs={{0,2},{1,3},{2,0},{3,1},{4,6},{5,7},{6,4},{7,5},{8,10},{9,11},{10,... | collective-permute-start | bytes 884744 | tf_op jit(solution)/shard_map/ppermute | solution.py:143
  166.5 9.4 %collective-permute-start.32 = (f32[96,768]{1,0:T(8,128)S(1)}, f32[96,768]{1,0:T(8,128)S(1)}, u32[]{:S(2)}, u32[]{:S(2)}) collective-permute-start(f32[96,768]{1,0:T(8,128)S(1)} %collective-permute-done.31.refs_6_), channel_id=1, source_target_pairs={{0,2},{1,3},{2,0},{3,1},{4,6},{5,7},{6,4},{7,5},{8,10},{9,11},{10,... | collective-permute-start | bytes 884744 | tf_op jit(solution)/shard_map/ppermute | solution.py:143
  180.5 53.2 %copy-start.3 = (f32[4,48,768]{2,1,0:T(8,128)S(1)}, f32[4,48,768]{2,1,0:T(8,128)}, u32[]{:S(2)}) copy-start(f32[4,48,768]{2,1,0:T(8,128)} %param.14) | copy-start | bytes 1769476
  180.5 53.2 %copy-start.4 = (f32[4,48,768]{2,1,0:T(8,128)S(1)}, f32[4,48,768]{2,1,0:T(8,128)}, u32[]{:S(2)}) copy-start(f32[4,48,768]{2,1,0:T(8,128)} %param.15) | copy-start | bytes 1769476
  183.1 5.2 %collective-permute-start.16 = (f32[1,128]{1,0:T(1,128)S(1)}, f32[1,128]{1,0:T(1,128)S(1)}, u32[]{:S(2)}, u32[]{:S(2)}) collective-permute-start(f32[1,128]{1,0:T(1,128)S(1)} %get-tuple-element.102), channel_id=1, source_target_pairs={{0,1},{1,0},{2,3},{3,2},{4,5},{5,4},{6,7},{7,6},{8,9},{9,8},{10,11... | collective-permute-start | bytes 1544 | tf_op jit(solution)/shard_map/ppermute | solution.py:139
  183.2 5.1 %collective-permute-start.17 = (f32[1,128]{1,0:T(1,128)S(1)}, f32[1,128]{1,0:T(1,128)S(1)}, u32[]{:S(2)}, u32[]{:S(2)}) collective-permute-start(f32[1,128]{1,0:T(1,128)S(1)} %get-tuple-element.102), channel_id=1, source_target_pairs={{0,16},{16,0},{1,17},{17,1},{2,18},{18,2},{3,19},{19,3},{4,20},{20... | collective-permute-start | bytes 1544 | tf_op jit(solution)/shard_map/ppermute | solution.py:147
  184.8 3.5 %collective-permute-start.18 = (f32[1,128]{1,0:T(1,128)S(1)}, f32[1,128]{1,0:T(1,128)S(1)}, u32[]{:S(2)}, u32[]{:S(2)}) collective-permute-start(f32[1,128]{1,0:T(1,128)S(1)} %get-tuple-element.102), channel_id=1, source_target_pairs={{0,17},{1,16},{2,19},{3,18},{16,1},{17,0},{18,3},{19,2},{4,21},{5,... | collective-permute-start | bytes 1544 | tf_op jit(solution)/shard_map/ppermute | solution.py:161
  185.0 10.2 %collective-permute-start.42 = (f32[1,128]{1,0:T(1,128)S(1)}, f32[1,128]{1,0:T(1,128)S(1)}, u32[]{:S(2)}, u32[]{:S(2)}) collective-permute-start(f32[1,128]{1,0:T(1,128)S(1)} %get-tuple-element.101), channel_id=1, source_target_pairs={{0,1},{1,0},{2,3},{3,2},{4,5},{5,4},{6,7},{7,6},{8,9},{9,8},{10,11... | collective-permute-start | bytes 1544 | tf_op jit(solution)/shard_map/ppermute | solution.py:139
  185.4 9.9 %collective-permute-start.43 = (f32[1,128]{1,0:T(1,128)S(1)}, f32[1,128]{1,0:T(1,128)S(1)}, u32[]{:S(2)}, u32[]{:S(2)}) collective-permute-start(f32[1,128]{1,0:T(1,128)S(1)} %get-tuple-element.101), channel_id=1, source_target_pairs={{0,16},{16,0},{1,17},{17,1},{2,18},{18,2},{3,19},{19,3},{4,20},{20... | collective-permute-start | bytes 1544 | tf_op jit(solution)/shard_map/ppermute | solution.py:147
  188.2 10.9 %collective-permute-start.44 = (f32[1,128]{1,0:T(1,128)S(1)}, f32[1,128]{1,0:T(1,128)S(1)}, u32[]{:S(2)}, u32[]{:S(2)}) collective-permute-start(f32[1,128]{1,0:T(1,128)S(1)} %get-tuple-element.101), channel_id=1, source_target_pairs={{0,17},{1,16},{2,19},{3,18},{16,1},{17,0},{18,3},{19,2},{4,21},{5,... | collective-permute-start | bytes 1544 | tf_op jit(solution)/shard_map/ppermute | solution.py:161
  188.3 11.9 %collective-permute-start.19 = (f32[4,128]{1,0:T(4,128)S(1)}, f32[4,128]{1,0:T(4,128)S(1)}, u32[]{:S(2)}, u32[]{:S(2)}) collective-permute-start(f32[4,128]{1,0:T(4,128)S(1)} %pad_maximum_fusion.4), channel_id=1, source_target_pairs={{0,2},{1,3},{2,0},{3,1},{4,6},{5,7},{6,4},{7,5},{8,10},{9,11},{10,... | collective-permute-start | bytes 6152 | tf_op jit(solution)/shard_map/ppermute | solution.py:143
  189.8 12.6 %collective-permute-start.20 = (f32[4,128]{1,0:T(4,128)S(1)}, f32[4,128]{1,0:T(4,128)S(1)}, u32[]{:S(2)}, u32[]{:S(2)}) collective-permute-start(f32[4,128]{1,0:T(4,128)S(1)} %pad_maximum_fusion.4), channel_id=1, source_target_pairs={{0,4},{4,0},{8,12},{12,8},{1,5},{5,1},{9,13},{13,9},{2,6},{6,2},{1... | collective-permute-start | bytes 6152 | tf_op jit(solution)/shard_map/ppermute | solution.py:151
  195.2 8.8 %collective-permute-start.21 = (f32[4,128]{1,0:T(4,128)S(1)}, f32[4,128]{1,0:T(4,128)S(1)}, u32[]{:S(2)}, u32[]{:S(2)}) collective-permute-start(f32[4,128]{1,0:T(4,128)S(1)} %pad_maximum_fusion.4), channel_id=1, source_target_pairs={{0,6},{1,7},{2,4},{3,5},{4,2},{5,3},{6,0},{7,1},{8,14},{9,15},{10,... | collective-permute-start | bytes 6152 | tf_op jit(solution)/shard_map/ppermute | solution.py:156
  195.2 10.3 %collective-permute-start.22 = (f32[4,128]{1,0:T(4,128)S(1)}, f32[4,128]{1,0:T(4,128)S(1)}, u32[]{:S(2)}, u32[]{:S(2)}) collective-permute-start(f32[4,128]{1,0:T(4,128)S(1)} %pad_maximum_fusion.4), channel_id=1, source_target_pairs={{0,8},{4,12},{8,0},{12,4},{1,9},{5,13},{9,1},{13,5},{2,10},{6,14},... | collective-permute-start | bytes 6152 | tf_op jit(solution)/shard_map/ppermute | solution.py:151
  199.2 6.4 %collective-permute-start.23 = (f32[4,128]{1,0:T(4,128)S(1)}, f32[4,128]{1,0:T(4,128)S(1)}, u32[]{:S(2)}, u32[]{:S(2)}) collective-permute-start(f32[4,128]{1,0:T(4,128)S(1)} %pad_maximum_fusion.4), channel_id=1, source_target_pairs={{0,10},{1,11},{2,8},{3,9},{4,14},{5,15},{6,12},{7,13},{8,2},{9,3},... | collective-permute-start | bytes 6152 | tf_op jit(solution)/shard_map/ppermute | solution.py:156
  200.2 7.4 %collective-permute-start.24 = (f32[4,128]{1,0:T(4,128)S(1)}, f32[4,128]{1,0:T(4,128)S(1)}, u32[]{:S(2)}, u32[]{:S(2)}) collective-permute-start(f32[4,128]{1,0:T(4,128)S(1)} %pad_maximum_fusion.4), channel_id=1, source_target_pairs={{0,12},{4,8},{8,4},{12,0},{1,13},{5,9},{9,5},{13,1},{2,14},{6,10},... | collective-permute-start | bytes 6152 | tf_op jit(solution)/shard_map/ppermute | solution.py:151
  202.5 6.3 %collective-permute-start.25 = (f32[4,128]{1,0:T(4,128)S(1)}, f32[4,128]{1,0:T(4,128)S(1)}, u32[]{:S(2)}, u32[]{:S(2)}) collective-permute-start(f32[4,128]{1,0:T(4,128)S(1)} %pad_maximum_fusion.4), channel_id=1, source_target_pairs={{0,14},{1,15},{2,12},{3,13},{4,10},{5,11},{6,8},{7,9},{8,6},{9,7},... | collective-permute-start | bytes 6152 | tf_op jit(solution)/shard_map/ppermute | solution.py:156
  204.0 7.4 %collective-permute-start.45 = (f32[4,128]{1,0:T(4,128)S(1)}, f32[4,128]{1,0:T(4,128)S(1)}, u32[]{:S(2)}, u32[]{:S(2)}) collective-permute-start(f32[4,128]{1,0:T(4,128)S(1)} %pad_maximum_fusion.5), channel_id=1, source_target_pairs={{0,2},{1,3},{2,0},{3,1},{4,6},{5,7},{6,4},{7,5},{8,10},{9,11},{10,... | collective-permute-start | bytes 6152 | tf_op jit(solution)/shard_map/ppermute | solution.py:143
  205.5 8.3 %collective-permute-start.46 = (f32[4,128]{1,0:T(4,128)S(1)}, f32[4,128]{1,0:T(4,128)S(1)}, u32[]{:S(2)}, u32[]{:S(2)}) collective-permute-start(f32[4,128]{1,0:T(4,128)S(1)} %pad_maximum_fusion.5), channel_id=1, source_target_pairs={{0,4},{4,0},{8,12},{12,8},{1,5},{5,1},{9,13},{13,9},{2,6},{6,2},{1... | collective-permute-start | bytes 6152 | tf_op jit(solution)/shard_map/ppermute | solution.py:151
  205.5 10.4 %collective-permute-start.47 = (f32[4,128]{1,0:T(4,128)S(1)}, f32[4,128]{1,0:T(4,128)S(1)}, u32[]{:S(2)}, u32[]{:S(2)}) collective-permute-start(f32[4,128]{1,0:T(4,128)S(1)} %pad_maximum_fusion.5), channel_id=1, source_target_pairs={{0,6},{1,7},{2,4},{3,5},{4,2},{5,3},{6,0},{7,1},{8,14},{9,15},{10,... | collective-permute-start | bytes 6152 | tf_op jit(solution)/shard_map/ppermute | solution.py:156
  207.6 8.4 %collective-permute-start.48 = (f32[4,128]{1,0:T(4,128)S(1)}, f32[4,128]{1,0:T(4,128)S(1)}, u32[]{:S(2)}, u32[]{:S(2)}) collective-permute-start(f32[4,128]{1,0:T(4,128)S(1)} %pad_maximum_fusion.5), channel_id=1, source_target_pairs={{0,8},{4,12},{8,0},{12,4},{1,9},{5,13},{9,1},{13,5},{2,10},{6,14},... | collective-permute-start | bytes 6152 | tf_op jit(solution)/shard_map/ppermute | solution.py:151
  208.7 7.8 %collective-permute-start.49 = (f32[4,128]{1,0:T(4,128)S(1)}, f32[4,128]{1,0:T(4,128)S(1)}, u32[]{:S(2)}, u32[]{:S(2)}) collective-permute-start(f32[4,128]{1,0:T(4,128)S(1)} %pad_maximum_fusion.5), channel_id=1, source_target_pairs={{0,10},{1,11},{2,8},{3,9},{4,14},{5,15},{6,12},{7,13},{8,2},{9,3},... | collective-permute-start | bytes 6152 | tf_op jit(solution)/shard_map/ppermute | solution.py:156
  211.4 5.4 %collective-permute-start.50 = (f32[4,128]{1,0:T(4,128)S(1)}, f32[4,128]{1,0:T(4,128)S(1)}, u32[]{:S(2)}, u32[]{:S(2)}) collective-permute-start(f32[4,128]{1,0:T(4,128)S(1)} %pad_maximum_fusion.5), channel_id=1, source_target_pairs={{0,12},{4,8},{8,4},{12,0},{1,13},{5,9},{9,5},{13,1},{2,14},{6,10},... | collective-permute-start | bytes 6152 | tf_op jit(solution)/shard_map/ppermute | solution.py:151
  213.8 6.3 %collective-permute-start.51 = (f32[4,128]{1,0:T(4,128)S(1)}, f32[4,128]{1,0:T(4,128)S(1)}, u32[]{:S(2)}, u32[]{:S(2)}) collective-permute-start(f32[4,128]{1,0:T(4,128)S(1)} %pad_maximum_fusion.5), channel_id=1, source_target_pairs={{0,14},{1,15},{2,12},{3,13},{4,10},{5,11},{6,8},{7,9},{8,6},{9,7},... | collective-permute-start | bytes 6152 | tf_op jit(solution)/shard_map/ppermute | solution.py:156
  216.0 15.8 %collective-permute-start.55 = (f32[48,768]{1,0:T(8,128)}, f32[48,768]{1,0:T(8,128)}, u32[]{:S(2)}, u32[]{:S(2)}) collective-permute-start(f32[48,768]{1,0:T(8,128)} %constant_dynamic-slice_fusion), channel_id=1, source_target_pairs={{0,1},{1,0},{2,3},{3,2},{4,5},{5,4},{6,7},{7,6},{8,9},{9,8},{10,11... | collective-permute-start | bytes 442376 | tf_op jit(solution)/shard_map/ppermute | solution.py:139
  216.0 16.8 %collective-permute-start.54 = (f32[48,768]{1,0:T(8,128)}, f32[48,768]{1,0:T(8,128)}, u32[]{:S(2)}, u32[]{:S(2)}) collective-permute-start(f32[48,768]{1,0:T(8,128)} %constant_dynamic-slice_fusion.1), channel_id=1, source_target_pairs={{0,1},{1,0},{2,3},{3,2},{4,5},{5,4},{6,7},{7,6},{8,9},{9,8},{10,11... | collective-permute-start | bytes 442376 | tf_op jit(solution)/shard_map/ppermute | solution.py:139
  216.5 12.8 %collective-permute-start.52 = (f32[48,768]{1,0:T(8,128)}, f32[48,768]{1,0:T(8,128)S(1)}, u32[]{:S(2)}, u32[]{:S(2)}) collective-permute-start(f32[48,768]{1,0:T(8,128)} %get-tuple-element.61), channel_id=1, source_target_pairs={{0,1},{1,0},{2,3},{3,2},{4,5},{5,4},{6,7},{7,6},{8,9},{9,8},{10,11... | collective-permute-start | bytes 442376 | tf_op jit(solution)/shard_map/ppermute | solution.py:139
  230.2 6.8 %collective-permute-start.53 = (f32[2,48,768]{2,1,0:T(8,128)S(1)}, f32[2,48,768]{2,1,0:T(8,128)S(1)}, u32[]{:S(2)}, u32[]{:S(2)}) collective-permute-start(f32[2,48,768]{2,1,0:T(8,128)S(1)} %pad_maximum_fusion.2), channel_id=1, source_target_pairs={{0,16},{16,0},{1,17},{17,1},{2,18},{18,2},{3,19},{19,3},{4,20},{20... | collective-permute-start | bytes 884744 | tf_op jit(solution)/shard_map/ppermute | solution.py:147
  233.7 3.3 %copy-start.6 = (bf16[4,48,768]{2,1,0:T(8,128)(2,1)S(1)}, bf16[4,48,768]{2,1,0:T(8,128)(2,1)}, u32[]{:S(2)}) copy-start(bf16[4,48,768]{2,1,0:T(8,128)(2,1)} %param.12) | copy-start | bytes 884740

commit v2 on v0

--- a/solution.py
+++ b/solution.py
@@ -1,9 +1,16 @@
+import functools
 import math
 
 import jax
 import jax.numpy as jnp
 from jax import lax
+from jax.experimental import pallas as pl
+from jax.experimental.pallas import tpu as pltpu
 from jax.sharding import PartitionSpec as P
+
+F32 = jnp.float32
+BF16 = jnp.bfloat16
+GROUP = ("tensor", "section")
 
 
 def spread(value, axis, source):
@@ -25,7 +32,7 @@
     return jnp.dot(prod_rows, portion, precision=lax.Precision.HIGHEST)
 
 
-def on_device(
+def any_mesh(
     xin,
     dout,
     weights,
@@ -39,7 +46,7 @@
 ):
     block_count, tok_count, block_size = xin.shape
     slot_count, row_count = (left_stat.shape[0], left_stat.shape[1])
-    group_count = lax.axis_size(("tensor", "section"))
+    group_count = lax.axis_size(GROUP)
     shard_count = lax.axis_size("shard")
     factor = 1.0 / math.sqrt(tok_count * shard_count * group_count * block_size)
     pieces_out = []
@@ -50,13 +57,13 @@
         )
     partial_rows = lax.psum_scatter(
         jnp.concatenate(pieces_out, axis=1) * factor,
-        ("tensor", "section"),
+        GROUP,
         scatter_dimension=0,
         tiled=True,
     )
     grad_rows = lax.psum(partial_rows, "shard")
     shard_idx = lax.axis_index("shard")
-    group_idx = lax.axis_index(("tensor", "section"))
+    group_idx = lax.axis_index(GROUP)
     my_slots = lax.dynamic_slice_in_dim(slot_block, shard_idx * slot_count, slot_count)
     valid = my_slots >= 0
     picks = jnp.maximum(my_slots, 0)
@@ -65,7 +72,7 @@
     col_first = group_idx * row_count
     zeros_rows = jnp.zeros((slot_count, row_count, block_size), jnp.float32)
     totals = (zeros_rows, zeros_rows, zeros_rows)
-    portion = lax.all_gather(mine, ("tensor", "section"), axis=1, tiled=True)
+    portion = lax.all_gather(mine, GROUP, axis=1, tiled=True)
     lefts = []
     rights = []
     prods = []
@@ -85,7 +92,7 @@
     left_gram = jnp.stack(lefts)
     right_gram = jnp.stack(rights)
     left_prod = jnp.stack(prods)
-    apply_portion = lax.all_gather(right_root, ("tensor", "section"), axis=1, tiled=True)
+    apply_portion = lax.all_gather(right_root, GROUP, axis=1, tiled=True)
     outputs = []
     for apply_slot_pos in range(slot_count):
         outputs.append(
@@ -102,7 +109,7 @@
     adam = moment_one / (jnp.sqrt(moment_two) + 1e-08)
     adam_sq, dir_sq = lax.psum(
         (jnp.sum(adam * adam, axis=(1, 2)), jnp.sum(direction * direction, axis=(1, 2))),
-        ("tensor", "section"),
+        GROUP,
     )
     graft = jnp.sqrt(adam_sq) / (jnp.sqrt(dir_sq) + 1e-06)
     mask = valid[:, None, None]
@@ -129,6 +136,498 @@
     return (new_weights, new_left, new_right, new_first, new_second)
 
 
+def to_core(value):
+    return lax.ppermute(value, "section", [(i, i ^ 1) for i in range(4)])
+
+
+def to_x(value):
+    return lax.ppermute(value, "section", [(i, i ^ 2) for i in range(4)])
+
+
+def to_y(value):
+    return lax.ppermute(value, "shard", [(0, 1), (1, 0)])
+
+
+def to_z(value, bits):
+    return lax.ppermute(value, "tensor", [(i, i ^ bits) for i in range(4)])
+
+
+def to_cy(value):
+    pairs = [(4 * y + s, 4 * (1 - y) + (s ^ 1)) for y in range(2) for s in range(4)]
+    return lax.ppermute(value, ("shard", "section"), pairs)
+
+
+def row_dot(rows, full):
+    return lax.dot_general(rows, full, (((1,), (0,)), ((), ())), preferred_element_type=F32)
+
+
+def row_dot_t(rows, full):
+    return lax.dot_general(rows, full, (((1,), (1,)), ((), ())), preferred_element_type=F32)
+
+
+def token_dot(left, right):
+    return lax.dot_general(left, right, (((0,), (0,)), ((), ())), preferred_element_type=F32)
+
+
+def halves(value):
+    high = value.astype(BF16)
+    return high, (value - high.astype(F32)).astype(BF16)
+
+
+def coded_rows(rows):
+    return rows + rows // 3
+
+
+def encode(value):
+    rows = value.shape[0]
+    part = rows // 4
+    top = jnp.maximum(jnp.max(jnp.abs(value), axis=0, keepdims=True), 1e-30)
+    exponent = jnp.ceil(jnp.log2(top))
+    scaled = value * (jnp.exp2(-exponent) * 32760.0)
+    coarse = jnp.round(scaled)
+    fine = jnp.clip(jnp.floor((scaled - coarse) * 16.0), -8.0, 7.0) + 8.0
+    words = fine[:part] - 32768.0
+    for index in (1, 2, 3):
+        words = words + fine[index * part : (index + 1) * part] * float(16**index)
+    tail = jnp.broadcast_to(exponent, (rows // 3 - part, value.shape[1]))
+    both = jnp.concatenate([coarse, words, tail], axis=0)
+    return both.astype(jnp.int32).astype(jnp.int16)
+
+
+def decode(words):
+    rows = words.shape[0] // 4 * 3
+    part = rows // 4
+    wide = words.astype(jnp.int32)
+    coarse = wide[:rows].astype(F32)
+    fine = wide[rows : rows + part] + 32768
+    exponent = wide[rows + part : rows + part + 8].astype(F32)[:1]
+    parts = [(jnp.right_shift(fine, 4 * index) & 15).astype(F32) for index in range(4)]
+    low = jnp.concatenate(parts, axis=0)
+    return (coarse + (low - 7.5) * (1.0 / 16.0)) * (jnp.exp2(exponent) * (1.0 / 32760.0))
+
+
+def used_slot(meta, plane, nth):
+    seen = jnp.int32(0)
+    place = jnp.int32(0)
+    block = jnp.int32(0)
+    for spot in range(4):
+        entry = meta[4 * plane + spot]
+        used = entry >= 0
+        hit = jnp.logical_and(used, seen == nth)
+        place = jnp.where(hit, spot, place)
+        block = jnp.where(hit, entry, block)
+        seen = seen + jnp.where(used, 1, 0)
+    return place, block
+
+
+SMEM_SPEC = pl.BlockSpec(memory_space=pltpu.SMEM)
+VMEM_SPEC = pl.BlockSpec(memory_space=pltpu.VMEM)
+ANY_SPEC = pl.BlockSpec(memory_space=pl.ANY)
+
+
+def call(body, outs, ins, args, scratch=(), out_specs=None):
+    return pl.pallas_call(
+        body,
+        out_shape=outs,
+        in_specs=ins,
+        out_specs=[VMEM_SPEC] * len(outs) if out_specs is None else out_specs,
+        scratch_shapes=list(scratch),
+        compiler_params=pltpu.CompilerParams(vmem_limit_bytes=48 << 20),
+    )(*args)
+
+
+def pick_kernel(meta, xin, dout, left, right, x_far, d_far, x_mine, d_mine, roots, sems):
+    plane, core = meta[8], meta[11]
+    place, mine = used_slot(meta, plane, 1 - core)
+    _, far = used_slot(meta, 1 - plane, 1 - core)
+    copies = [
+        pltpu.make_async_copy(xin.at[far], x_far, sems.at[0]),
+        pltpu.make_async_copy(dout.at[far], d_far, sems.at[1]),
+        pltpu.make_async_copy(xin.at[mine], x_mine, sems.at[2]),
+        pltpu.make_async_copy(dout.at[mine], d_mine, sems.at[3]),
+        pltpu.make_async_copy(left.at[place], roots.at[0], sems.at[4]),
+        pltpu.make_async_copy(right.at[place], roots.at[1], sems.at[5]),
+    ]
+    for copy in copies:
+        copy.start()
+    for copy in copies:
+        copy.wait()
+
+
+def own_kernel(meta, x_ref, d_ref, out_ref):
+    out_ref[...] = token_dot(x_ref[...], d_ref[...])
+
+
+def own_part(meta, xin, dout, across):
+    _, tokens, size = xin.shape
+
+    def block_of(step, meta_ref):
+        plane = 1 - meta_ref[8] if across else meta_ref[8]
+        return (used_slot(meta_ref, plane, meta_ref[11])[1], 0, 0)
+
+    taken = pl.BlockSpec((None, tokens, size), block_of)
+    return pl.pallas_call(
+        own_kernel,
+        out_shape=jax.ShapeDtypeStruct((size, size), F32),
+        grid_spec=pltpu.PrefetchScalarGridSpec(
+            num_scalar_prefetch=1,
+            grid=(1,),
+            in_specs=[taken, taken],
+            out_specs=pl.BlockSpec((size, size), lambda step, meta_ref: (0, 0)),
+        ),
+        compiler_params=pltpu.CompilerParams(vmem_limit_bytes=48 << 20),
+    )(meta, xin, dout)
+
+
+def far_kernel(meta, x_ref, d_ref, own_ref, *refs):
+    outs, total = refs[:4], refs[4]
+    total[...] = own_ref[...] + token_dot(x_ref[...], d_ref[...])
+    span = total.shape[0] // 4
+    for out, bits in zip(outs, (3, 2, 1, 0)):
+        first = pl.multiple_of((meta[9] ^ bits) * span, 64)
+        out[...] = encode(total[pl.ds(first, span), :])
+
+
+def mine_kernel(x_ref, d_ref, own_ref, out_ref):
+    out_ref[...] = own_ref[...] + token_dot(x_ref[...], d_ref[...])
+
+
+def rows_kernel(meta, left, right, got, left_out, right_out):
+    core = meta[11]
+    place, _ = used_slot(meta, meta[8], core)
+    rows = left.shape[1]
+    own_first = pl.multiple_of(core * rows, 16)
+    sib_first = pl.multiple_of((1 - core) * rows, 16)
+    for index, (source, out) in enumerate(((left, left_out), (right, right_out))):
+        out[pl.ds(own_first, rows), :] = source[place]
+        out[pl.ds(sib_first, rows), :] = got[index]
+
+
+def y_kernel(meta, got, mine, coded, keep, both):
+    rows = keep.shape[0]
+    both[...] = decode(got[...]) + mine[...]
+    side = meta[10]
+    keep[...] = both[pl.ds(pl.multiple_of(side * rows, 32), rows), :]
+    coded[...] = encode(both[pl.ds(pl.multiple_of((1 - side) * rows, 32), rows), :])
+
+
+def after_y(meta, got, mine, bits):
+    size = mine.shape[1]
+    rows = size // 8
+    return pl.pallas_call(
+        y_kernel,
+        out_shape=[
+            jax.ShapeDtypeStruct((coded_rows(rows), size), jnp.int16),
+            jax.ShapeDtypeStruct((rows, size), F32),
+        ],
+        grid_spec=pltpu.PrefetchScalarGridSpec(
+            num_scalar_prefetch=1,
+            grid=(1,),
+            in_specs=[
+                pl.BlockSpec(got.shape, lambda step, meta_ref: (0, 0)),
+                pl.BlockSpec((2 * rows, size), lambda step, meta_ref: (meta_ref[9] ^ bits, 0)),
+            ],
+            out_specs=[
+                pl.BlockSpec((coded_rows(rows), size), lambda step, meta_ref: (0, 0)),
+                pl.BlockSpec((rows, size), lambda step, meta_ref: (0, 0)),
+            ],
+            scratch_shapes=[pltpu.VMEM((2 * rows, size), F32)],
+        ),
+        compiler_params=pltpu.CompilerParams(vmem_limit_bytes=48 << 20),
+    )(meta, got, mine)
+
+
+def x_kernel(got, keep, coded):
+    coded[...] = encode(decode(got[...]) + keep[...])
+
+
+def grad_kernel(factor, got, keep, one, two, three, grad, coded):
+    total = decode(got[...]) + keep[...]
+    for part in (one, two, three):
+        total = total + decode(part[...])
+    total = total * factor
+    grad[...] = total
+    coded[...] = encode(total)
+
+
+def put_rows(spot, value, high_ref, low_ref):
+    rows = value.shape[0]
+    first = pl.multiple_of(spot * rows, 32)
+    high, low = halves(value)
+    high_ref[pl.ds(first, rows), :] = high
+    low_ref[pl.ds(first, rows), :] = low
+
+
+def root_kernel(meta, *refs):
+    for step in range(4):
+        for side in range(2):
+            spot = 2 * (meta[9] ^ step) + (meta[10] ^ side)
+            put_rows(spot, refs[2 * step + side][...], refs[8], refs[9])
+
+
+def block_kernel(meta, *refs):
+    grad_ref, pieces = refs[0], refs[1:8]
+    left_ref, root_high, root_low, adam_ref = refs[8:12]
+    own_left, own_right, own_dir, sib_out, sib_dir, sums = refs[12:18]
+    high_ref, low_ref, whole = refs[18:21]
+    for index in range(8):
+        spot = 2 * (meta[9] ^ (index // 2)) + (meta[10] ^ (index % 2))
+        value = grad_ref[...] if index == 0 else decode(pieces[index - 1][...])
+        put_rows(spot, value, high_ref, low_ref)
+    rows, size = left_ref.shape
+    half = rows // 2
+    own = pl.ds(pl.multiple_of(meta[11] * half, 16), half)
+    sib = pl.ds(pl.multiple_of((1 - meta[11]) * half, 16), half)
+    first = (2 * meta[9] + meta[10]) * rows
+    high, low = high_ref[...], low_ref[...]
+    left_high, left_low = halves(left_ref[...])
+    prod = row_dot(left_high, high) + (row_dot(left_low, high) + row_dot(left_high, low))
+    prod_high, prod_low = halves(prod)
+    root_h, root_l = root_high[...], root_low[...]
+    direction = row_dot(prod_high, root_h) + (
+        row_dot(prod_low, root_h) + row_dot(prod_high, root_l)
+    )
+    whole[...] = direction
+    own_dir[...] = whole[own, :]
+    sib_dir[...] = whole[sib, :]
+    sib_out[2] = whole[sib, :]
+    lane = lax.broadcasted_iota(jnp.int32, (1, 128), 1)
+    line = jnp.where(lane == 2, jnp.sum(direction * direction), adam_ref[...])
+    sums[...] = jnp.broadcast_to(line.reshape(1, 1, 128), sums.shape)
+    own_high, own_low = halves(grad_ref[...])
+    whole[...] = row_dot_t(own_high, high) + (
+        row_dot_t(own_low, high) + row_dot_t(own_high, low)
+    )
+    own_left[...] = whole[own, :]
+    sib_out[0] = whole[sib, :]
+    row_ids = lax.broadcasted_iota(jnp.int32, (rows, size), 0) + first
+    col_ids = lax.broadcasted_iota(jnp.int32, (rows, size), 1)
+    pick = jnp.where(row_ids == col_ids, 1.0, 0.0).astype(BF16)
+    col_high = row_dot_t(pick, high).astype(BF16)
+    col_low = row_dot_t(pick, low).astype(BF16)
+    whole[...] = row_dot(col_high, high) + (row_dot(col_low, high) + row_dot(col_high, low))
+    own_right[...] = whole[own, :]
+    sib_out[1] = whole[sib, :]
+
+
+def moment_kernel(meta, grad, got, first, second, first_out, second_out, adam_out):
+    plane, core = meta[8], meta[11]
+    rows = got.shape[0]
+    first_out[...] = first[...]
+    second_out[...] = second[...]
+    lane = lax.broadcasted_iota(jnp.int32, (1, 128), 1)
+    line = jnp.zeros((1, 128), F32)
+    own = grad[pl.ds(pl.multiple_of(core * rows, 16), rows), :]
+    for slot, value in ((core, own), (1 - core, got[...])):
+        place, _ = used_slot(meta, plane, slot)
+        one = 0.9 * first[place] + 0.1 * value
+        two = 0.999 * second[place] + 0.001 * value * value
+        first_out[place] = one
+        second_out[place] = two
+        adam = one / (jnp.sqrt(two) + 1e-08)
+        line = line + jnp.where(lane == slot, jnp.sum(adam * adam), 0.0)
+    adam_out[...] = line
+
+
+def last_kernel(
+    meta,
+    sums,
+    own_left,
+    own_right,
+    own_dir,
+    got,
+    y_dir,
+    cy_dir,
+    weights,
+    left,
+    right,
+    weights_out,
+    left_out,
+    right_out,
+):
+    plane, core = meta[8], meta[11]
+    left_out[...] = left[...]
+    right_out[...] = right[...]
+    for slot, left_gram, right_gram in (
+        (core, own_left[...], own_right[...]),
+        (1 - core, got[0], got[1]),
+    ):
+        place, _ = used_slot(meta, plane, slot)
+        left_out[place] = 0.5 * left[place] + 0.5 * left_gram
+        right_out[place] = 0.5 * right[place] + 0.5 * right_gram
+    lane = lax.broadcasted_iota(jnp.int32, (1, 128), 1)
+
+    def graft(of_plane, slot):
+        line = jnp.zeros((1, 128), F32)
+        for device in range(16):
+            row = sums[of_plane * 16 + device]
+            kept = jnp.logical_or(lane == slot, jnp.logical_and(lane == 2, slot == device % 2))
+            line = line + jnp.where(kept, row, 0.0)
+        dir_sq = jnp.sum(jnp.where(lane == 2, line, 0.0), axis=1, keepdims=True)
+        adam_sq = jnp.sum(jnp.where(lane == 2, 0.0, line), axis=1, keepdims=True)
+        return jnp.sqrt(adam_sq) / (jnp.sqrt(dir_sq) + 1e-06)
+
+    for of_plane, slot, value in (
+        (plane, core, own_dir[...]),
+        (plane, 1 - core, got[2]),
+        (1 - plane, core, y_dir[...]),
+        (1 - plane, 1 - core, cy_dir[...]),
+    ):
+        _, block = used_slot(meta, of_plane, slot)
+        step = 0.05 * graft(of_plane, slot)
+        weights_out[block] = (weights[block].astype(F32) - step * value).astype(BF16)
+
+
+def two_planes(
+    xin,
+    dout,
+    weights,
+    slot_block,
+    left_stat,
+    right_stat,
+    left_root,
+    right_root,
+    first_moment,
+    second_moment,
+):
+    block_count, tokens, size = xin.shape
+    slot_count, rows = left_stat.shape[:2]
+    device_count = lax.axis_size(("shard",) + GROUP)
+    factor = 1.0 / math.sqrt(tokens * device_count * size)
+    section = lax.axis_index("section")
+    meta = jnp.concatenate(
+        [
+            slot_block,
+            jnp.stack(
+                [lax.axis_index("shard"), lax.axis_index("tensor"), section // 2, section % 2]
+            ).astype(jnp.int32),
+        ]
+    )
+
+    def shape(*dims, dtype=F32):
+        return jax.ShapeDtypeStruct(dims, dtype)
+
+    words = jnp.int16
+    rows_in = shape(tokens, size, dtype=BF16)
+    x_far, d_far, x_mine, d_mine, roots = call(
+        pick_kernel,
+        [rows_in] * 4 + [shape(2, rows, size)],
+        [SMEM_SPEC] + [ANY_SPEC] * 4,
+        (meta, xin, dout, left_root, right_root),
+        [pltpu.SemaphoreType.DMA((6,))],
+        [ANY_SPEC] * 5,
+    )
+    x_far, d_far = to_core(x_far), to_core(d_far)
+    x_mine, d_mine, roots = to_core(x_mine), to_core(d_mine), to_core(roots)
+    own_far = own_part(meta, xin, dout, True)
+    own_mine = own_part(meta, xin, dout, False)
+    chunk = coded_rows(size // 4)
+    coded = call(
+        far_kernel,
+        [shape(chunk, size, dtype=words)] * 4,
+        [SMEM_SPEC] + [VMEM_SPEC] * 3,
+        (meta, x_far, d_far, own_far),
+        [pltpu.VMEM((size, size), F32)],
+    )
+    got_y = [to_y(value) for value in coded]
+    (mine,) = call(
+        mine_kernel,
+        [shape(size, size)],
+        [VMEM_SPEC] * 3,
+        (x_mine, d_mine, own_mine),
+    )
+    left_rows, right_rows = call(
+        rows_kernel,
+        [shape(2 * rows, size)] * 2,
+        [SMEM_SPEC] + [VMEM_SPEC] * 3,
+        (meta, left_root, right_root, roots),
+    )
+    root_column = [right_rows] + [to_z(right_rows, bits) for bits in (1, 2, 3)]
+
+    piece = shape(coded_rows(2 * rows), size, dtype=words)
+    order = (3, 2, 1, 0)
+    got_x, keeps, got_z = [], [], []
+    for index, bits in enumerate(order):
+        arrived = got_y[index]
+        if index == 1:
+            arrived, got_x[0] = lax.optimization_barrier((arrived, got_x[0]))
+        if index == 2:
+            arrived, got_x[1] = lax.optimization_barrier((arrived, got_x[1]))
+        if index == 3:
+            arrived, got_x[2], got_z[0] = lax.optimization_barrier(
+                (arrived, got_x[2], got_z[0])
+            )
+        sent, keep = after_y(meta, arrived, mine, bits)
+        got_x.append(to_x(sent))
+        keeps.append(keep)
+        if index:
+            (sent,) = call(
+                x_kernel, [piece], [VMEM_SPEC] * 2, (got_x[index - 1], keeps[index - 1])
+            )
+            got_z.append(to_z(sent, order[index - 1]))
+    grad, coded = call(
+        functools.partial(grad_kernel, factor),
+        [shape(2 * rows, size), piece],
+        [VMEM_SPEC] * 5,
+        (got_x[3], keeps[3], *got_z),
+    )
+
+    column = [coded] + [to_z(coded, bits) for bits in (1, 2, 3)]
+    pieces = []
+    for part in column:
+        pieces += [part, to_x(part)]
+
+    root_pieces = []
+    for part in root_column:
+        root_pieces += [part, to_x(part)]
+    root_high, root_low = call(
+        root_kernel,
+        [shape(size, size, dtype=BF16)] * 2,
+        [SMEM_SPEC] + [VMEM_SPEC] * 8,
+        (meta, *root_pieces),
+    )
+
+    core = section % 2
+    grad_out = lax.dynamic_slice_in_dim(grad, (1 - core) * rows, rows, 0)
+    stack = shape(slot_count, rows, size)
+    new_first, new_second, adam = call(
+        moment_kernel,
+        [stack, stack, shape(1, 128)],
+        [SMEM_SPEC] + [VMEM_SPEC] * 4,
+        (meta, grad, to_core(grad_out), first_moment, second_moment),
+    )
+    tile = shape(rows, size)
+    own_left, own_right, own_dir, sib_out, sib_dir, sums = call(
+        block_kernel,
+        [tile, tile, tile, shape(3, rows, size), tile, shape(device_count, 1, 128)],
+        [SMEM_SPEC] + [VMEM_SPEC] * 12,
+        (meta, grad, *pieces[1:], left_rows, root_high, root_low, adam),
+        [pltpu.VMEM((size, size), BF16)] * 2 + [pltpu.VMEM((2 * rows, size), F32)],
+    )
+    got = to_core(sib_out)
+    y_dir = to_y(own_dir)
+    cy_dir = to_cy(sib_dir)
+    sums = lax.all_to_all(sums, ("shard",) + GROUP, 0, 0)
+    return tuple(call(
+        last_kernel,
+        [shape(block_count, rows, size, dtype=BF16), stack, stack],
+        [SMEM_SPEC] + [VMEM_SPEC] * 10,
+        (
+            meta,
+            sums,
+            own_left,
+            own_right,
+            own_dir,
+            got,
+            y_dir,
+            cy_dir,
+            weights,
+            left_stat,
+            right_stat,
+        ),
+    )) + (new_first, new_second)
+
+
 def solution(mesh):
     placed = (
         P(None, ("shard", "tensor", "section"), None),
@@ -142,8 +641,10 @@
         P("shard", ("tensor", "section"), None),
         P("shard", ("tensor", "section"), None),
     )
+    shape = mesh.shape
+    pair = (shape["shard"], shape["tensor"], shape["section"]) == (2, 4, 4)
     return jax.shard_map(
-        on_device,
+        two_planes if pair else any_mesh,
         mesh=mesh,
         in_specs=placed,
         out_specs=(

time: 414 us -> 137 us (0.33)
  waiting for transfers between devices: 291 us -> 40.8 us
  starting transfers between devices: 0.2 us -> 43.7 us
  Pallas kernels: 0 us -> 31.2 us
  matrix products: 30.5 us -> 0 us
  between operations: 27.2 us -> 0.93 us
  local copies, waits for them, and re-layouts: 21.3 us -> 4.31 us
  blocking collectives: 30.8 us -> 15.2 us
  other arithmetic: 12.2 us -> 0 us
    all_gather x2 -> x0, waiting for transfers between devices: 124 us -> none  [the longest x1 66 us: on_device(): portion = lax.all_gather(mine, ('tensor', 'section'), axis=1, tiled=True)]
    unnamed x6 -> x0, waiting for transfers between devices: 115 us -> none
    psum x2 -> x0, waiting for transfers between devices: 51.5 us -> none  [the longest x1 29.8 us: on_device(): grad_rows = lax.psum(partial_rows, 'shard')]
    ppermute x0 -> x34, starting transfers between devices: none -> 43.7 us  [the longest x9 18.8 us: to_z(): return lax.ppermute(value, 'tensor', [(i, i ^ bits) for i in range(4)])]
    ppermute x0 -> x34, waiting for transfers between devices: none -> 40.8 us  [the longest x9 29.1 us: to_z(): return lax.ppermute(value, 'tensor', [(i, i ^ bits) for i in range(4)])]
    pallas_call x0 -> x18, Pallas kernels: none -> 31.2 us  [the longest x12 21.8 us: call(): pl.pallas_call(body, out_shape=outs, in_specs=ins, out_specs=[VMEM_SPEC]...]
    psum x1 -> x0, blocking collectives: 30.8 us -> none  [on_device(): lax.psum((jnp.sum(adam * adam, axis=(1, 2)), jnp.sum(direction * directio...]
    dot_general x12 -> x0, matrix products: 30.5 us -> none  [the longest x2 8.22 us: absorb_slot(): block_part = jnp.dot(mine_rows, portion.T, precision=highest)]
  transfers between devices with their start and end apart: 5 -> 34, of which waited for: 5 -> 11; matrix products, arithmetic and copies ran while one was open for 6% -> 0% of each run, Pallas kernels for 0% -> 15%
where the time goes in v2:
time: 137 us; the launch traced here: 136 us
  starting transfers between devices  43.7 us (32%)
  waiting for transfers between devices  40.8 us (30%)
  Pallas kernels  31.2 us (23%)
  blocking collectives  15.2 us (11%)
  local copies, waits for them, and re-layouts  4.31 us (3%)
    ppermute x9, waiting for transfers between devices, to_z(): return lax.ppermute(value, 'tensor', [(i, i ^ bits) for i in range(4)])  29.1 us
    pallas_call x12, Pallas kernels, call(): pl.pallas_call(body, out_shape=outs, in_specs=ins, out_specs=[VMEM_SPEC]...  21.8 us
    ppermute x9, starting transfers between devices, to_z(): return lax.ppermute(value, 'tensor', [(i, i ^ bits) for i in range(4)])  18.8 us
    ppermute x12, starting transfers between devices, to_x(): return lax.ppermute(value, 'section', [(i, i ^ 2) for i in range(4)])  16.6 us
    all_to_all x1, blocking collectives, two_planes(): sums = lax.all_to_all(sums, ('shard',) + GROUP, 0, 0)  15.2 us
    ppermute x5, waiting for transfers between devices, to_y(): return lax.ppermute(value, 'shard', [(0, 1), (1, 0)])  7.57 us
    ppermute x5, starting transfers between devices, to_y(): return lax.ppermute(value, 'shard', [(0, 1), (1, 0)])  6.7 us
    pallas_call x2, Pallas kernels, own_part(): pl.pallas_call(own_kernel, out_shape=jax.ShapeDtypeStruct((size, size), F...  5.06 us
  transfers between devices with their start and end apart: 34, of which 11 were waited for; matrix products, arithmetic and copies ran while one was open for 0% of the time, Pallas kernels for 15%

profile of v2, /device:TPU:0, one launch (start us, length us, event | category | flops | bytes accessed | tf_op | source)
XLA Modules:
  0.0 136.1 jit_solution(1425240725094972483)
XLA Ops:
  0.7 0.7 concatenate.3.meta
  1.4 1.1 copy-done.2
  2.5 1.1 copy-done.4
  3.5 2.7 %shard_map.137 = (bf16[512,768]{1,0:T(8,128)(2,1)S(1)}, bf16[512,768]{1,0:T(8,128)(2,1)S(1)}, bf16[512,768]{1,0:T(8,128)(2,1)S(1)}, bf16[512,768]{1,0:T(8,128)(2,1)S(1)}, f32[2,48,768]{2,1,0:T(8,128)S(1)}) custom-call(s32[12]{0:T(128)S(1)} %concatenate.3.meta, bf16[4,512,768]{2,1,0:T(8,128)(2,1)} %x_ref.3, bf16[4,512,768]{2,1,0:T(8,128)(2,1)} %d_ref.3, ...), custom_call_target="tpu_custom_call" | custom-call | tf_op jit(solution)/shard_map/pallas_call | solution.py:229
  6.3 0.5 collective-permute-start
  6.8 0.1 collective-permute-start.1
  6.9 0.4 collective-permute-start.6
  7.3 0.1 collective-permute-start.7
  7.4 2.5 %shard_map.138.own_ref = f32[768,768]{1,0:T(8,128)S(1)} custom-call(s32[12]{0:T(128)S(1)} %concatenate.3.meta, bf16[4,512,768]{2,1,0:T(8,128)(2,1)S(1)} %copy-done, bf16[4,512,768]{2,1,0:T(8,128)(2,1)} %d_ref.3), custom_call_target="tpu_custom_call" | custom-call | tf_op jit(solution)/shard_map/pallas_call | solution.py:269
  9.9 2.5 %shard_map.139 = (s16[256,768]{1,0:T(8,128)(2,1)S(1)}, s16[256,768]{1,0:T(8,128)(2,1)S(1)}, s16[256,768]{1,0:T(8,128)(2,1)S(1)}, s16[256,768]{1,0:T(8,128)(2,1)S(1)}) custom-call(s32[12]{0:T(128)S(1)} %concatenate.3.meta, bf16[512,768]{1,0:T(8,128)(2,1)S(1)} %collective-permute-done.x_ref, bf16[512,768]{1,0:T(8,128)(2,1)S(1)} %collective-permute-done.1.d_ref, ...), custom_call_target="tpu_custom_call" | custom-call | tf_op jit(solution)/shard_map/pallas_call | solution.py:229
  12.4 3.0 %collective-permute-start.5 = (s16[256,768]{1,0:T(8,128)(2,1)S(1)}, s16[256,768]{1,0:T(8,128)(2,1)S(1)}, u32[]{:S(2)}, u32[]{:S(2)}) collective-permute-start(s16[256,768]{1,0:T(8,128)(2,1)S(1)} %get-tuple-element.52), channel_id=1, source_target_pairs={{0,16},{16,0},{1,17},{17,1},{2,18},{18,2},{3,19},{19,3},{4,20},{20... | collective-permute-start | bytes 1179656 | tf_op jit(solution)/shard_map/ppermute | solution.py:148
  15.4 0.1 collective-permute-start.4
  15.5 2.5 %shard_map.140.own_ref = f32[768,768]{1,0:T(8,128)S(1)} custom-call(s32[12]{0:T(128)S(1)} %concatenate.3.meta, bf16[4,512,768]{2,1,0:T(8,128)(2,1)S(1)} %copy-done, bf16[4,512,768]{2,1,0:T(8,128)(2,1)} %d_ref.3), custom_call_target="tpu_custom_call" | custom-call | tf_op jit(solution)/shard_map/pallas_call | solution.py:269
  18.0 1.4 %copy-done.1 = f32[768,768]{1,0:T(8,128)} copy-done((f32[768,768]{1,0:T(8,128)}, f32[768,768]{1,0:T(8,128)S(1)}, u32[]{:S(2)}) %copy-start.1) | copy-done | bytes 2359320
  19.4 2.5 %shard_map.141.mine = f32[768,768]{1,0:T(8,128)S(1)} custom-call(bf16[512,768]{1,0:T(8,128)(2,1)S(1)} %collective-permute-done.6.x_ref, bf16[512,768]{1,0:T(8,128)(2,1)S(1)} %collective-permute-done.7.d_ref, f32[768,768]{1,0:T(8,128)} %copy-done.1), custom_call_target="tpu_custom_call" | custom-call | tf_op jit(solution)/shard_map/pallas_call | solution.py:229
  22.0 3.4 %collective-permute-done.5.got = s16[256,768]{1,0:T(8,128)(2,1)S(1)} collective-permute-done((s16[256,768]{1,0:T(8,128)(2,1)S(1)}, s16[256,768]{1,0:T(8,128)(2,1)S(1)}, u32[]{:S(2)}, u32[]{:S(2)}) %collective-permute-start.5) | collective-permute-done | bytes 393248 | tf_op jit(solution)/shard_map/ppermute | solution.py:148
  25.3 1.1 shard_map.142
  26.4 2.1 %collective-permute-start.8 = (s16[128,768]{1,0:T(8,128)(2,1)S(1)}, s16[128,768]{1,0:T(8,128)(2,1)S(1)}, u32[]{:S(2)}, u32[]{:S(2)}) collective-permute-start(s16[128,768]{1,0:T(8,128)(2,1)S(1)} %get-tuple-element.55), channel_id=1, source_target_pairs={{0,2},{1,3},{2,0},{3,1},{4,6},{5,7},{6,4},{7,5},{8,10},{9,11},{10,... | collective-permute-start | bytes 589832 | tf_op jit(solution)/shard_map/ppermute | solution.py:144
  28.5 1.5 %collective-permute-start.3 = (s16[256,768]{1,0:T(8,128)(2,1)S(1)}, s16[256,768]{1,0:T(8,128)(2,1)S(1)}, u32[]{:S(2)}, u32[]{:S(2)}) collective-permute-start(s16[256,768]{1,0:T(8,128)(2,1)S(1)} %get-tuple-element.50), channel_id=1, source_target_pairs={{0,16},{16,0},{1,17},{17,1},{2,18},{18,2},{3,19},{19,3},{4,20},{20... | collective-permute-start | bytes 1179656 | tf_op jit(solution)/shard_map/ppermute | solution.py:148
  30.0 0.5 collective-permute-start.2
  30.5 3.2 %collective-permute-done.4.got = s16[256,768]{1,0:T(8,128)(2,1)S(1)} collective-permute-done((s16[256,768]{1,0:T(8,128)(2,1)S(1)}, s16[256,768]{1,0:T(8,128)(2,1)S(1)}, u32[]{:S(2)}, u32[]{:S(2)}) %collective-permute-start.4) | collective-permute-done | bytes 393248 | tf_op jit(solution)/shard_map/ppermute | solution.py:148
  33.8 1.1 shard_map.143
  34.8 2.1 %collective-permute-start.9 = (s16[128,768]{1,0:T(8,128)(2,1)S(1)}, s16[128,768]{1,0:T(8,128)(2,1)S(1)}, u32[]{:S(2)}, u32[]{:S(2)}) collective-permute-start(s16[128,768]{1,0:T(8,128)(2,1)S(1)} %get-tuple-element.57), channel_id=1, source_target_pairs={{0,2},{1,3},{2,0},{3,1},{4,6},{5,7},{6,4},{7,5},{8,10},{9,11},{10,... | collective-permute-start | bytes 589832 | tf_op jit(solution)/shard_map/ppermute | solution.py:144
  36.9 0.6 shard_map.150
  37.5 1.6 %collective-permute-start.24 = (f32[96,768]{1,0:T(8,128)S(1)}, f32[96,768]{1,0:T(8,128)S(1)}, u32[]{:S(2)}, u32[]{:S(2)}) collective-permute-start(f32[96,768]{1,0:T(8,128)S(1)} %get-tuple-element.74.refs_0_), channel_id=1, source_target_pairs={{0,4},{4,0},{8,12},{12,8},{1,5},{5,1},{9,13},{13,9},{2,6},{6,2},{1... | collective-permute-start | bytes 884744 | tf_op jit(solution)/shard_map/ppermute | solution.py:152
  39.2 2.6 %collective-permute-start.26 = (f32[96,768]{1,0:T(8,128)S(1)}, f32[96,768]{1,0:T(8,128)S(1)}, u32[]{:S(2)}, u32[]{:S(2)}) collective-permute-start(f32[96,768]{1,0:T(8,128)S(1)} %get-tuple-element.74.refs_0_), channel_id=1, source_target_pairs={{0,8},{4,12},{8,0},{12,4},{1,9},{5,13},{9,1},{13,5},{2,10},{6,14},... | collective-permute-start | bytes 884744 | tf_op jit(solution)/shard_map/ppermute | solution.py:152
  41.8 0.2 shard_map.145
  42.0 0.1 collective-permute-done.3.got
  42.2 4.1 %collective-permute-start.11 = (s16[128,768]{1,0:T(8,128)(2,1)S(1)}, s16[128,768]{1,0:T(8,128)(2,1)S(1)}, u32[]{:S(2)}, u32[]{:S(2)}) collective-permute-start(s16[128,768]{1,0:T(8,128)(2,1)S(1)} %shard_map.145), channel_id=1, source_target_pairs={{0,12},{4,8},{8,4},{12,0},{1,13},{5,9},{9,5},{13,1},{2,14},{6,10},... | collective-permute-start | bytes 589832 | tf_op jit(solution)/shard_map/ppermute | solution.py:152
  46.3 1.1 shard_map.144
  47.4 1.6 %collective-permute-start.10 = (s16[128,768]{1,0:T(8,128)(2,1)S(1)}, s16[128,768]{1,0:T(8,128)(2,1)S(1)}, u32[]{:S(2)}, u32[]{:S(2)}) collective-permute-start(s16[128,768]{1,0:T(8,128)(2,1)S(1)} %get-tuple-element.59), channel_id=1, source_target_pairs={{0,2},{1,3},{2,0},{3,1},{4,6},{5,7},{6,4},{7,5},{8,10},{9,11},{10,... | collective-permute-start | bytes 589832 | tf_op jit(solution)/shard_map/ppermute | solution.py:144
  49.0 0.2 shard_map.147
  49.2 0.8 collective-permute-done.2.got
  50.0 2.8 %collective-permute-start.13 = (s16[128,768]{1,0:T(8,128)(2,1)S(1)}, s16[128,768]{1,0:T(8,128)(2,1)S(1)}, u32[]{:S(2)}, u32[]{:S(2)}) collective-permute-start(s16[128,768]{1,0:T(8,128)(2,1)S(1)} %shard_map.147), channel_id=1, source_target_pairs={{0,8},{4,12},{8,0},{12,4},{1,9},{5,13},{9,1},{13,5},{2,10},{6,14},... | collective-permute-start | bytes 589832 | tf_op jit(solution)/shard_map/ppermute | solution.py:152
  52.9 6.5 %collective-permute-done.11.one = s16[128,768]{1,0:T(8,128)(2,1)S(1)} collective-permute-done((s16[128,768]{1,0:T(8,128)(2,1)S(1)}, s16[128,768]{1,0:T(8,128)(2,1)S(1)}, u32[]{:S(2)}, u32[]{:S(2)}) %collective-permute-start.11) | collective-permute-done | bytes 196640 | tf_op jit(solution)/shard_map/ppermute | solution.py:152
  59.4 1.1 shard_map.146
  60.5 0.6 collective-permute-start.12
  61.1 1.5 %collective-permute-start.23 = (f32[96,768]{1,0:T(8,128)S(1)}, f32[96,768]{1,0:T(8,128)S(1)}, u32[]{:S(2)}, u32[]{:S(2)}) collective-permute-start(f32[96,768]{1,0:T(8,128)S(1)} %get-tuple-element.74.refs_0_), channel_id=1, source_target_pairs={{0,2},{1,3},{2,0},{3,1},{4,6},{5,7},{6,4},{7,5},{8,10},{9,11},{10,... | collective-permute-start | bytes 884744 | tf_op jit(solution)/shard_map/ppermute | solution.py:144
  62.6 1.2 collective-permute-start.28
  63.8 3.6 %collective-permute-done.26.refs_4_ = f32[96,768]{1,0:T(8,128)S(1)} collective-permute-done((f32[96,768]{1,0:T(8,128)S(1)}, f32[96,768]{1,0:T(8,128)S(1)}, u32[]{:S(2)}, u32[]{:S(2)}) %collective-permute-start.26) | collective-permute-done | bytes 294944 | tf_op jit(solution)/shard_map/ppermute | solution.py:152
  67.4 0.2 shard_map.148
  67.7 11.3 %collective-permute-done.13.two = s16[128,768]{1,0:T(8,128)(2,1)S(1)} collective-permute-done((s16[128,768]{1,0:T(8,128)(2,1)S(1)}, s16[128,768]{1,0:T(8,128)(2,1)S(1)}, u32[]{:S(2)}, u32[]{:S(2)}) %collective-permute-start.13) | collective-permute-done | bytes 196640 | tf_op jit(solution)/shard_map/ppermute | solution.py:152
  79.0 2.0 %collective-permute-start.14 = (s16[128,768]{1,0:T(8,128)(2,1)S(1)}, s16[128,768]{1,0:T(8,128)(2,1)S(1)}, u32[]{:S(2)}, u32[]{:S(2)}) collective-permute-start(s16[128,768]{1,0:T(8,128)(2,1)S(1)} %shard_map.148), channel_id=1, source_target_pairs={{0,4},{4,0},{8,12},{12,8},{1,5},{5,1},{9,13},{13,9},{2,6},{6,2},{1... | collective-permute-start | bytes 589832 | tf_op jit(solution)/shard_map/ppermute | solution.py:152
  81.0 1.5 %collective-permute-start.27 = (f32[96,768]{1,0:T(8,128)S(1)}, f32[96,768]{1,0:T(8,128)}, u32[]{:S(2)}, u32[]{:S(2)}) collective-permute-start(f32[96,768]{1,0:T(8,128)S(1)} %collective-permute-done.26.refs_4_), channel_id=1, source_target_pairs={{0,2},{1,3},{2,0},{3,1},{4,6},{5,7},{6,4},{7,5},{8,10},{9,11},{10,... | collective-permute-start | bytes 884744 | tf_op jit(solution)/shard_map/ppermute | solution.py:144
  82.5 5.2 %collective-permute-done.14.three = s16[128,768]{1,0:T(8,128)(2,1)S(1)} collective-permute-done((s16[128,768]{1,0:T(8,128)(2,1)S(1)}, s16[128,768]{1,0:T(8,128)(2,1)S(1)}, u32[]{:S(2)}, u32[]{:S(2)}) %collective-permute-start.14) | collective-permute-done | bytes 196640 | tf_op jit(solution)/shard_map/ppermute | solution.py:152
  87.7 1.4 %shard_map.149 = (f32[96,768]{1,0:T(8,128)S(1)}, s16[128,768]{1,0:T(8,128)(2,1)}) custom-call(s16[128,768]{1,0:T(8,128)(2,1)S(1)} %collective-permute-done.12.got, f32[96,768]{1,0:T(8,128)S(1)} %get-tuple-element.64.keep, s16[128,768]{1,0:T(8,128)(2,1)S(1)} %collective-permute-done.11.one, s16[128,768]{1,0:T(8,128)(2,1)S(1)} %collective-permute-done.13.two, ...), custom_call_target="tpu_custom_call" | custom-call | tf_op jit(solution)/shard_map/pallas_call | solution.py:229
  89.1 1.0 collective-permute-start.16
  90.1 2.0 %collective-permute-start.18 = (s16[128,768]{1,0:T(8,128)(2,1)}, s16[128,768]{1,0:T(8,128)(2,1)}, u32[]{:S(2)}, u32[]{:S(2)}) collective-permute-start(s16[128,768]{1,0:T(8,128)(2,1)} %get-tuple-element.71), channel_id=1, source_target_pairs={{0,8},{4,12},{8,0},{12,4},{1,9},{5,13},{9,1},{13,5},{2,10},{6,14},... | collective-permute-start | bytes 589832 | tf_op jit(solution)/shard_map/ppermute | solution.py:152
  92.2 1.4 %collective-permute-start.20 = (s16[128,768]{1,0:T(8,128)(2,1)}, s16[128,768]{1,0:T(8,128)(2,1)}, u32[]{:S(2)}, u32[]{:S(2)}) collective-permute-start(s16[128,768]{1,0:T(8,128)(2,1)} %get-tuple-element.71), channel_id=1, source_target_pairs={{0,12},{4,8},{8,4},{12,0},{1,13},{5,9},{9,5},{13,1},{2,14},{6,10},... | collective-permute-start | bytes 589832 | tf_op jit(solution)/shard_map/ppermute | solution.py:152
  93.5 2.4 %collective-permute-start.29 = (f32[96,768]{1,0:T(8,128)S(1)}, f32[96,768]{1,0:T(8,128)}, u32[]{:S(2)}, u32[]{:S(2)}) collective-permute-start(f32[96,768]{1,0:T(8,128)S(1)} %collective-permute-done.28.refs_6_), channel_id=1, source_target_pairs={{0,2},{1,3},{2,0},{3,1},{4,6},{5,7},{6,4},{7,5},{8,10},{9,11},{10,... | collective-permute-start | bytes 884744 | tf_op jit(solution)/shard_map/ppermute | solution.py:144
  96.0 2.8 %collective-permute-start.17 = (s16[128,768]{1,0:T(8,128)(2,1)}, s16[128,768]{1,0:T(8,128)(2,1)S(1)}, u32[]{:S(2)}, u32[]{:S(2)}) collective-permute-start(s16[128,768]{1,0:T(8,128)(2,1)} %collective-permute-done.16.refs_2_), channel_id=1, source_target_pairs={{0,2},{1,3},{2,0},{3,1},{4,6},{5,7},{6,4},{7,5},{8,10},{9,11},{10,... | collective-permute-start | bytes 589832 | tf_op jit(solution)/shard_map/ppermute | solution.py:144
  98.8 2.4 %collective-permute-done.18.refs_4_ = s16[128,768]{1,0:T(8,128)(2,1)} collective-permute-done((s16[128,768]{1,0:T(8,128)(2,1)}, s16[128,768]{1,0:T(8,128)(2,1)}, u32[]{:S(2)}, u32[]{:S(2)}) %collective-permute-start.18) | collective-permute-done | bytes 196640 | tf_op jit(solution)/shard_map/ppermute | solution.py:152
  101.2 1.7 %collective-permute-start.19 = (s16[128,768]{1,0:T(8,128)(2,1)}, s16[128,768]{1,0:T(8,128)(2,1)S(1)}, u32[]{:S(2)}, u32[]{:S(2)}) collective-permute-start(s16[128,768]{1,0:T(8,128)(2,1)} %collective-permute-done.18.refs_4_), channel_id=1, source_target_pairs={{0,2},{1,3},{2,0},{3,1},{4,6},{5,7},{6,4},{7,5},{8,10},{9,11},{10,... | collective-permute-start | bytes 589832 | tf_op jit(solution)/shard_map/ppermute | solution.py:144
  102.9 0.4 collective-permute-start.21
  103.3 0.1 collective-permute-start.30
  103.4 1.4 %shard_map.151 = (bf16[768,768]{1,0:T(8,128)(2,1)S(1)}, bf16[768,768]{1,0:T(8,128)(2,1)S(1)}) custom-call(s32[12]{0:T(128)S(1)} %concatenate.3.meta, f32[96,768]{1,0:T(8,128)S(1)} %get-tuple-element.74.refs_0_, f32[96,768]{1,0:T(8,128)S(1)} %collective-permute-done.23.refs_1_, f32[96,768]{1,0:T(8,128)S(1)} %collective-permute-done.24.refs_2_, ...), custom_call_target="tpu_custom_call" | custom-call | tf_op jit(solution)/shard_map/pallas_call | solution.py:229
  104.9 1.9 %shard_map.152 = (f32[4,48,768]{2,1,0:T(8,128)}, f32[4,48,768]{2,1,0:T(8,128)}, f32[1,128]{1,0:T(1,128)S(1)}) custom-call(s32[12]{0:T(128)S(1)} %concatenate.3.meta, f32[96,768]{1,0:T(8,128)S(1)} %get-tuple-element.70.grad.refs_0_, f32[48,768]{1,0:T(8,128)S(1)} %collective-permute-done.30.got, f32[4,48,768]{2,1,0:T(8,128)S(1)} %copy-done.6, ...), custom_call_target="tpu_custom_call" | custom-call | tf_op jit(solution)/shard_map/pallas_call | solution.py:229
  106.7 2.0 %collective-permute-done.19.refs_5_ = s16[128,768]{1,0:T(8,128)(2,1)S(1)} collective-permute-done((s16[128,768]{1,0:T(8,128)(2,1)}, s16[128,768]{1,0:T(8,128)(2,1)S(1)}, u32[]{:S(2)}, u32[]{:S(2)}) %collective-permute-start.19) | collective-permute-done | bytes 196640 | tf_op jit(solution)/shard_map/ppermute | solution.py:144
  108.8 2.1 %collective-permute-done.21.refs_7_ = s16[128,768]{1,0:T(8,128)(2,1)S(1)} collective-permute-done((s16[128,768]{1,0:T(8,128)(2,1)}, s16[128,768]{1,0:T(8,128)(2,1)S(1)}, u32[]{:S(2)}, u32[]{:S(2)}) %collective-permute-start.21) | collective-permute-done | bytes 196640 | tf_op jit(solution)/shard_map/ppermute | solution.py:144
  110.9 6.2 %shard_map.153 = (f32[48,768]{1,0:T(8,128)S(1)}, f32[48,768]{1,0:T(8,128)S(1)}, f32[48,768]{1,0:T(8,128)S(1)}, f32[3,48,768]{2,1,0:T(8,128)S(1)}, f32[48,768]{1,0:T(8,128)S(1)}, /*index=5*/f32[32,1,128]{2,1,0:T(1,128)S(1)}) custom-call(s32[12]{0:T(128)S(1)} %concatenate.3.meta, f32[96,768]{1,0:T(8,128)S(1)} %get-tuple-element.70.grad.refs_0_, ...), custom_call_target="tpu_custom_call" | custom-call | tf_op jit(solution)/shard_map/pallas_call | solution.py:229
  117.2 1.6 %collective-permute-start.32 = (f32[48,768]{1,0:T(8,128)S(1)}, f32[48,768]{1,0:T(8,128)S(1)}, u32[]{:S(2)}, u32[]{:S(2)}) collective-permute-start(f32[48,768]{1,0:T(8,128)S(1)} %get-tuple-element.81.own_dir), channel_id=1, source_target_pairs={{0,16},{16,0},{1,17},{17,1},{2,18},{18,2},{3,19},{19,3},{4,20},{20... | collective-permute-start | bytes 442376 | tf_op jit(solution)/shard_map/ppermute | solution.py:148
  118.8 0.3 collective-permute-start.33
  119.1 15.2 %all_to_all.5.sums = f32[32,1,128]{2,1,0:T(1,128)S(1)} all-to-all(f32[32,1,128]{2,1,0:T(1,128)S(1)} %get-tuple-element.78), channel_id=1, replica_groups=mesh['shard'=2,'tensor'=4,'section'=4] {'shard','tensor','section'}, dimensions={0} | all-to-all | bytes 32768 | tf_op jit(solution)/shard_map/all_to_all | solution.py:610
  134.3 1.8 %shard_map.154 = (bf16[4,48,768]{2,1,0:T(8,128)(2,1)}, f32[4,48,768]{2,1,0:T(8,128)}, f32[4,48,768]{2,1,0:T(8,128)}) custom-call(s32[12]{0:T(128)S(1)} %concatenate.3.meta, f32[32,1,128]{2,1,0:T(1,128)S(1)} %all_to_all.5.sums, f32[48,768]{1,0:T(8,128)S(1)} %get-tuple-element.79.own_left, f32[48,768]{1,0:T(8,128)S(1)} %get-tuple-element.80.own_right, ...), custom_call_target="tpu_custom_call" | custom-call | tf_op jit(solution)/shard_map/pallas_call | solution.py:229
  (47 shorter events, 0.3 us)
Async XLA Ops:
  1.4 1.1 copy-start.2
  2.5 1.1 copy-start.4
  3.5 3.9 %copy-start = (bf16[4,512,768]{2,1,0:T(8,128)(2,1)S(1)}, bf16[4,512,768]{2,1,0:T(8,128)(2,1)}, u32[]{:S(2)}) copy-start(bf16[4,512,768]{2,1,0:T(8,128)(2,1)} %x_ref.3) | copy-start | bytes 9437188
  6.3 3.6 %collective-permute-start = (bf16[512,768]{1,0:T(8,128)(2,1)S(1)}, bf16[512,768]{1,0:T(8,128)(2,1)S(1)}, u32[]{:S(2)}, u32[]{:S(2)}) collective-permute-start(bf16[512,768]{1,0:T(8,128)(2,1)S(1)} %get-tuple-element.47), channel_id=1, source_target_pairs={{0,1},{1,0},{2,3},{3,2},{4,5},{5,4},{6,7},{7,6},{8,9},{9,8},{10,11... | collective-permute-start | bytes 2359304 | tf_op jit(solution)/shard_map/ppermute | solution.py:140
  6.8 3.1 %collective-permute-start.1 = (bf16[512,768]{1,0:T(8,128)(2,1)S(1)}, bf16[512,768]{1,0:T(8,128)(2,1)S(1)}, u32[]{:S(2)}, u32[]{:S(2)}) collective-permute-start(bf16[512,768]{1,0:T(8,128)(2,1)S(1)} %get-tuple-element.48), channel_id=1, source_target_pairs={{0,1},{1,0},{2,3},{3,2},{4,5},{5,4},{6,7},{7,6},{8,9},{9,8},{10,11... | collective-permute-start | bytes 2359304 | tf_op jit(solution)/shard_map/ppermute | solution.py:140
  6.9 12.6 %collective-permute-start.6 = (bf16[512,768]{1,0:T(8,128)(2,1)S(1)}, bf16[512,768]{1,0:T(8,128)(2,1)S(1)}, u32[]{:S(2)}, u32[]{:S(2)}) collective-permute-start(bf16[512,768]{1,0:T(8,128)(2,1)S(1)} %get-tuple-element.53), channel_id=1, source_target_pairs={{0,1},{1,0},{2,3},{3,2},{4,5},{5,4},{6,7},{7,6},{8,9},{9,8},{10,11... | collective-permute-start | bytes 2359304 | tf_op jit(solution)/shard_map/ppermute | solution.py:140
  7.3 12.2 %collective-permute-start.7 = (bf16[512,768]{1,0:T(8,128)(2,1)S(1)}, bf16[512,768]{1,0:T(8,128)(2,1)S(1)}, u32[]{:S(2)}, u32[]{:S(2)}) collective-permute-start(bf16[512,768]{1,0:T(8,128)(2,1)S(1)} %get-tuple-element.54), channel_id=1, source_target_pairs={{0,1},{1,0},{2,3},{3,2},{4,5},{5,4},{6,7},{7,6},{8,9},{9,8},{10,11... | collective-permute-start | bytes 2359304 | tf_op jit(solution)/shard_map/ppermute | solution.py:140
  12.4 12.9 %collective-permute-start.5 = (s16[256,768]{1,0:T(8,128)(2,1)S(1)}, s16[256,768]{1,0:T(8,128)(2,1)S(1)}, u32[]{:S(2)}, u32[]{:S(2)}) collective-permute-start(s16[256,768]{1,0:T(8,128)(2,1)S(1)} %get-tuple-element.52), channel_id=1, source_target_pairs={{0,16},{16,0},{1,17},{17,1},{2,18},{18,2},{3,19},{19,3},{4,20},{20... | collective-permute-start | bytes 1179656 | tf_op jit(solution)/shard_map/ppermute | solution.py:148
  15.4 18.3 %collective-permute-start.4 = (s16[256,768]{1,0:T(8,128)(2,1)S(1)}, s16[256,768]{1,0:T(8,128)(2,1)S(1)}, u32[]{:S(2)}, u32[]{:S(2)}) collective-permute-start(s16[256,768]{1,0:T(8,128)(2,1)S(1)} %get-tuple-element.51), channel_id=1, source_target_pairs={{0,16},{16,0},{1,17},{17,1},{2,18},{18,2},{3,19},{19,3},{4,20},{20... | collective-permute-start | bytes 1179656 | tf_op jit(solution)/shard_map/ppermute | solution.py:148
  18.0 1.4 %copy-start.1 = (f32[768,768]{1,0:T(8,128)}, f32[768,768]{1,0:T(8,128)S(1)}, u32[]{:S(2)}) copy-start(f32[768,768]{1,0:T(8,128)S(1)} %shard_map.140.own_ref) | copy-start | bytes 7077892
  21.9 15.0 %copy-start.3 = (f32[4,48,768]{2,1,0:T(8,128)S(1)}, f32[4,48,768]{2,1,0:T(8,128)}, u32[]{:S(2)}) copy-start(f32[4,48,768]{2,1,0:T(8,128)} %left.4) | copy-start | bytes 1769476
  21.9 15.0 %copy-start.5 = (f32[4,48,768]{2,1,0:T(8,128)S(1)}, f32[4,48,768]{2,1,0:T(8,128)}, u32[]{:S(2)}) copy-start(f32[4,48,768]{2,1,0:T(8,128)} %right.4) | copy-start | bytes 1769476
  26.4 7.3 %collective-permute-start.8 = (s16[128,768]{1,0:T(8,128)(2,1)S(1)}, s16[128,768]{1,0:T(8,128)(2,1)S(1)}, u32[]{:S(2)}, u32[]{:S(2)}) collective-permute-start(s16[128,768]{1,0:T(8,128)(2,1)S(1)} %get-tuple-element.55), channel_id=1, source_target_pairs={{0,2},{1,3},{2,0},{3,1},{4,6},{5,7},{6,4},{7,5},{8,10},{9,11},{10,... | collective-permute-start | bytes 589832 | tf_op jit(solution)/shard_map/ppermute | solution.py:144
  28.5 13.7 %collective-permute-start.3 = (s16[256,768]{1,0:T(8,128)(2,1)S(1)}, s16[256,768]{1,0:T(8,128)(2,1)S(1)}, u32[]{:S(2)}, u32[]{:S(2)}) collective-permute-start(s16[256,768]{1,0:T(8,128)(2,1)S(1)} %get-tuple-element.50), channel_id=1, source_target_pairs={{0,16},{16,0},{1,17},{17,1},{2,18},{18,2},{3,19},{19,3},{4,20},{20... | collective-permute-start | bytes 1179656 | tf_op jit(solution)/shard_map/ppermute | solution.py:148
  30.0 6.9 %collective-permute-start.22 = (f32[2,48,768]{2,1,0:T(8,128)S(1)}, f32[2,48,768]{2,1,0:T(8,128)S(1)}, u32[]{:S(2)}, u32[]{:S(2)}) collective-permute-start(f32[2,48,768]{2,1,0:T(8,128)S(1)} %get-tuple-element.72), channel_id=1, source_target_pairs={{0,1},{1,0},{2,3},{3,2},{4,5},{5,4},{6,7},{7,6},{8,9},{9,8},{10,11... | collective-permute-start | bytes 884744 | tf_op jit(solution)/shard_map/ppermute | solution.py:140
  30.0 20.0 %collective-permute-start.2 = (s16[256,768]{1,0:T(8,128)(2,1)S(1)}, s16[256,768]{1,0:T(8,128)(2,1)S(1)}, u32[]{:S(2)}, u32[]{:S(2)}) collective-permute-start(s16[256,768]{1,0:T(8,128)(2,1)S(1)} %get-tuple-element.49), channel_id=1, source_target_pairs={{0,16},{16,0},{1,17},{17,1},{2,18},{18,2},{3,19},{19,3},{4,20},{20... | collective-permute-start | bytes 1179656 | tf_op jit(solution)/shard_map/ppermute | solution.py:148
  34.8 11.5 %collective-permute-start.9 = (s16[128,768]{1,0:T(8,128)(2,1)S(1)}, s16[128,768]{1,0:T(8,128)(2,1)S(1)}, u32[]{:S(2)}, u32[]{:S(2)}) collective-permute-start(s16[128,768]{1,0:T(8,128)(2,1)S(1)} %get-tuple-element.57), channel_id=1, source_target_pairs={{0,2},{1,3},{2,0},{3,1},{4,6},{5,7},{6,4},{7,5},{8,10},{9,11},{10,... | collective-permute-start | bytes 589832 | tf_op jit(solution)/shard_map/ppermute | solution.py:144
  37.5 25.0 %collective-permute-start.24 = (f32[96,768]{1,0:T(8,128)S(1)}, f32[96,768]{1,0:T(8,128)S(1)}, u32[]{:S(2)}, u32[]{:S(2)}) collective-permute-start(f32[96,768]{1,0:T(8,128)S(1)} %get-tuple-element.74.refs_0_), channel_id=1, source_target_pairs={{0,4},{4,0},{8,12},{12,8},{1,5},{5,1},{9,13},{13,9},{2,6},{6,2},{1... | collective-permute-start | bytes 884744 | tf_op jit(solution)/shard_map/ppermute | solution.py:152
  39.2 28.2 %collective-permute-start.26 = (f32[96,768]{1,0:T(8,128)S(1)}, f32[96,768]{1,0:T(8,128)S(1)}, u32[]{:S(2)}, u32[]{:S(2)}) collective-permute-start(f32[96,768]{1,0:T(8,128)S(1)} %get-tuple-element.74.refs_0_), channel_id=1, source_target_pairs={{0,8},{4,12},{8,0},{12,4},{1,9},{5,13},{9,1},{13,5},{2,10},{6,14},... | collective-permute-start | bytes 884744 | tf_op jit(solution)/shard_map/ppermute | solution.py:152
  42.2 17.2 %collective-permute-start.11 = (s16[128,768]{1,0:T(8,128)(2,1)S(1)}, s16[128,768]{1,0:T(8,128)(2,1)S(1)}, u32[]{:S(2)}, u32[]{:S(2)}) collective-permute-start(s16[128,768]{1,0:T(8,128)(2,1)S(1)} %shard_map.145), channel_id=1, source_target_pairs={{0,12},{4,8},{8,4},{12,0},{1,13},{5,9},{9,5},{13,1},{2,14},{6,10},... | collective-permute-start | bytes 589832 | tf_op jit(solution)/shard_map/ppermute | solution.py:152
  47.4 12.0 %collective-permute-start.10 = (s16[128,768]{1,0:T(8,128)(2,1)S(1)}, s16[128,768]{1,0:T(8,128)(2,1)S(1)}, u32[]{:S(2)}, u32[]{:S(2)}) collective-permute-start(s16[128,768]{1,0:T(8,128)(2,1)S(1)} %get-tuple-element.59), channel_id=1, source_target_pairs={{0,2},{1,3},{2,0},{3,1},{4,6},{5,7},{6,4},{7,5},{8,10},{9,11},{10,... | collective-permute-start | bytes 589832 | tf_op jit(solution)/shard_map/ppermute | solution.py:144
  50.0 28.9 %collective-permute-start.13 = (s16[128,768]{1,0:T(8,128)(2,1)S(1)}, s16[128,768]{1,0:T(8,128)(2,1)S(1)}, u32[]{:S(2)}, u32[]{:S(2)}) collective-permute-start(s16[128,768]{1,0:T(8,128)(2,1)S(1)} %shard_map.147), channel_id=1, source_target_pairs={{0,8},{4,12},{8,0},{12,4},{1,9},{5,13},{9,1},{13,5},{2,10},{6,14},... | collective-permute-start | bytes 589832 | tf_op jit(solution)/shard_map/ppermute | solution.py:152
  60.5 44.4 %copy-start.6 = (f32[4,48,768]{2,1,0:T(8,128)S(1)}, f32[4,48,768]{2,1,0:T(8,128)}, u32[]{:S(2)}) copy-start(f32[4,48,768]{2,1,0:T(8,128)} %first.1) | copy-start | bytes 1769476
  60.5 44.4 %copy-start.7 = (f32[4,48,768]{2,1,0:T(8,128)S(1)}, f32[4,48,768]{2,1,0:T(8,128)}, u32[]{:S(2)}) copy-start(f32[4,48,768]{2,1,0:T(8,128)} %second.1) | copy-start | bytes 1769476
  60.5 20.5 %collective-permute-start.12 = (s16[128,768]{1,0:T(8,128)(2,1)S(1)}, s16[128,768]{1,0:T(8,128)(2,1)S(1)}, u32[]{:S(2)}, u32[]{:S(2)}) collective-permute-start(s16[128,768]{1,0:T(8,128)(2,1)S(1)} %get-tuple-element.63), channel_id=1, source_target_pairs={{0,2},{1,3},{2,0},{3,1},{4,6},{5,7},{6,4},{7,5},{8,10},{9,11},{10,... | collective-permute-start | bytes 589832 | tf_op jit(solution)/shard_map/ppermute | solution.py:144
  61.1 29.0 %collective-permute-start.23 = (f32[96,768]{1,0:T(8,128)S(1)}, f32[96,768]{1,0:T(8,128)S(1)}, u32[]{:S(2)}, u32[]{:S(2)}) collective-permute-start(f32[96,768]{1,0:T(8,128)S(1)} %get-tuple-element.74.refs_0_), channel_id=1, source_target_pairs={{0,2},{1,3},{2,0},{3,1},{4,6},{5,7},{6,4},{7,5},{8,10},{9,11},{10,... | collective-permute-start | bytes 884744 | tf_op jit(solution)/shard_map/ppermute | solution.py:144
  62.6 29.6 %collective-permute-start.28 = (f32[96,768]{1,0:T(8,128)S(1)}, f32[96,768]{1,0:T(8,128)S(1)}, u32[]{:S(2)}, u32[]{:S(2)}) collective-permute-start(f32[96,768]{1,0:T(8,128)S(1)} %get-tuple-element.74.refs_0_), channel_id=1, source_target_pairs={{0,12},{4,8},{8,4},{12,0},{1,13},{5,9},{9,5},{13,1},{2,14},{6,10},... | collective-permute-start | bytes 884744 | tf_op jit(solution)/shard_map/ppermute | solution.py:152
  67.4 26.1 %collective-permute-start.25 = (f32[96,768]{1,0:T(8,128)S(1)}, f32[96,768]{1,0:T(8,128)S(1)}, u32[]{:S(2)}, u32[]{:S(2)}) collective-permute-start(f32[96,768]{1,0:T(8,128)S(1)} %collective-permute-done.24.refs_2_), channel_id=1, source_target_pairs={{0,2},{1,3},{2,0},{3,1},{4,6},{5,7},{6,4},{7,5},{8,10},{9,11},{10,... | collective-permute-start | bytes 884744 | tf_op jit(solution)/shard_map/ppermute | solution.py:144
  79.0 8.7 %collective-permute-start.14 = (s16[128,768]{1,0:T(8,128)(2,1)S(1)}, s16[128,768]{1,0:T(8,128)(2,1)S(1)}, u32[]{:S(2)}, u32[]{:S(2)}) collective-permute-start(s16[128,768]{1,0:T(8,128)(2,1)S(1)} %shard_map.148), channel_id=1, source_target_pairs={{0,4},{4,0},{8,12},{12,8},{1,5},{5,1},{9,13},{13,9},{2,6},{6,2},{1... | collective-permute-start | bytes 589832 | tf_op jit(solution)/shard_map/ppermute | solution.py:152
  81.0 14.9 %collective-permute-start.27 = (f32[96,768]{1,0:T(8,128)S(1)}, f32[96,768]{1,0:T(8,128)}, u32[]{:S(2)}, u32[]{:S(2)}) collective-permute-start(f32[96,768]{1,0:T(8,128)S(1)} %collective-permute-done.26.refs_4_), channel_id=1, source_target_pairs={{0,2},{1,3},{2,0},{3,1},{4,6},{5,7},{6,4},{7,5},{8,10},{9,11},{10,... | collective-permute-start | bytes 884744 | tf_op jit(solution)/shard_map/ppermute | solution.py:144
  89.1 6.9 %collective-permute-start.16 = (s16[128,768]{1,0:T(8,128)(2,1)}, s16[128,768]{1,0:T(8,128)(2,1)}, u32[]{:S(2)}, u32[]{:S(2)}) collective-permute-start(s16[128,768]{1,0:T(8,128)(2,1)} %get-tuple-element.71), channel_id=1, source_target_pairs={{0,4},{4,0},{8,12},{12,8},{1,5},{5,1},{9,13},{13,9},{2,6},{6,2},{1... | collective-permute-start | bytes 589832 | tf_op jit(solution)/shard_map/ppermute | solution.py:152
  90.1 11.1 %collective-permute-start.18 = (s16[128,768]{1,0:T(8,128)(2,1)}, s16[128,768]{1,0:T(8,128)(2,1)}, u32[]{:S(2)}, u32[]{:S(2)}) collective-permute-start(s16[128,768]{1,0:T(8,128)(2,1)} %get-tuple-element.71), channel_id=1, source_target_pairs={{0,8},{4,12},{8,0},{12,4},{1,9},{5,13},{9,1},{13,5},{2,10},{6,14},... | collective-permute-start | bytes 589832 | tf_op jit(solution)/shard_map/ppermute | solution.py:152
  92.2 10.8 %collective-permute-start.20 = (s16[128,768]{1,0:T(8,128)(2,1)}, s16[128,768]{1,0:T(8,128)(2,1)}, u32[]{:S(2)}, u32[]{:S(2)}) collective-permute-start(s16[128,768]{1,0:T(8,128)(2,1)} %get-tuple-element.71), channel_id=1, source_target_pairs={{0,12},{4,8},{8,4},{12,0},{1,13},{5,9},{9,5},{13,1},{2,14},{6,10},... | collective-permute-start | bytes 589832 | tf_op jit(solution)/shard_map/ppermute | solution.py:152
  93.5 9.7 %collective-permute-start.29 = (f32[96,768]{1,0:T(8,128)S(1)}, f32[96,768]{1,0:T(8,128)}, u32[]{:S(2)}, u32[]{:S(2)}) collective-permute-start(f32[96,768]{1,0:T(8,128)S(1)} %collective-permute-done.28.refs_6_), channel_id=1, source_target_pairs={{0,2},{1,3},{2,0},{3,1},{4,6},{5,7},{6,4},{7,5},{8,10},{9,11},{10,... | collective-permute-start | bytes 884744 | tf_op jit(solution)/shard_map/ppermute | solution.py:144
  95.9 10.8 %collective-permute-start.15 = (s16[128,768]{1,0:T(8,128)(2,1)}, s16[128,768]{1,0:T(8,128)(2,1)S(1)}, u32[]{:S(2)}, u32[]{:S(2)}) collective-permute-start(s16[128,768]{1,0:T(8,128)(2,1)} %get-tuple-element.71), channel_id=1, source_target_pairs={{0,2},{1,3},{2,0},{3,1},{4,6},{5,7},{6,4},{7,5},{8,10},{9,11},{10,... | collective-permute-start | bytes 589832 | tf_op jit(solution)/shard_map/ppermute | solution.py:144
  96.0 10.7 %collective-permute-start.17 = (s16[128,768]{1,0:T(8,128)(2,1)}, s16[128,768]{1,0:T(8,128)(2,1)S(1)}, u32[]{:S(2)}, u32[]{:S(2)}) collective-permute-start(s16[128,768]{1,0:T(8,128)(2,1)} %collective-permute-done.16.refs_2_), channel_id=1, source_target_pairs={{0,2},{1,3},{2,0},{3,1},{4,6},{5,7},{6,4},{7,5},{8,10},{9,11},{10,... | collective-permute-start | bytes 589832 | tf_op jit(solution)/shard_map/ppermute | solution.py:144
  101.2 7.5 %collective-permute-start.19 = (s16[128,768]{1,0:T(8,128)(2,1)}, s16[128,768]{1,0:T(8,128)(2,1)S(1)}, u32[]{:S(2)}, u32[]{:S(2)}) collective-permute-start(s16[128,768]{1,0:T(8,128)(2,1)} %collective-permute-done.18.refs_4_), channel_id=1, source_target_pairs={{0,2},{1,3},{2,0},{3,1},{4,6},{5,7},{6,4},{7,5},{8,10},{9,11},{10,... | collective-permute-start | bytes 589832 | tf_op jit(solution)/shard_map/ppermute | solution.py:144
  102.9 8.0 %collective-permute-start.21 = (s16[128,768]{1,0:T(8,128)(2,1)}, s16[128,768]{1,0:T(8,128)(2,1)S(1)}, u32[]{:S(2)}, u32[]{:S(2)}) collective-permute-start(s16[128,768]{1,0:T(8,128)(2,1)} %collective-permute-done.20.refs_6_), channel_id=1, source_target_pairs={{0,2},{1,3},{2,0},{3,1},{4,6},{5,7},{6,4},{7,5},{8,10},{9,11},{10,... | collective-permute-start | bytes 589832 | tf_op jit(solution)/shard_map/ppermute | solution.py:144
  103.3 1.5 %collective-permute-start.30 = (f32[48,768]{1,0:T(8,128)S(1)}, f32[48,768]{1,0:T(8,128)S(1)}, u32[]{:S(2)}, u32[]{:S(2)}) collective-permute-start(f32[48,768]{1,0:T(8,128)S(1)} %constant_dynamic-slice_fusion), channel_id=1, source_target_pairs={{0,1},{1,0},{2,3},{3,2},{4,5},{5,4},{6,7},{7,6},{8,9},{9,8},{10,11... | collective-permute-start | bytes 442376 | tf_op jit(solution)/shard_map/ppermute | solution.py:140
  106.7 27.6 %copy-start.8 = (f32[4,48,768]{2,1,0:T(8,128)S(1)}, f32[4,48,768]{2,1,0:T(8,128)}, u32[]{:S(2)}) copy-start(f32[4,48,768]{2,1,0:T(8,128)} %left.5) | copy-start | bytes 1769476
  106.7 27.6 %copy-start.9 = (f32[4,48,768]{2,1,0:T(8,128)S(1)}, f32[4,48,768]{2,1,0:T(8,128)}, u32[]{:S(2)}) copy-start(f32[4,48,768]{2,1,0:T(8,128)} %right.5) | copy-start | bytes 1769476
  106.7 27.6 %copy-start.10 = (bf16[4,48,768]{2,1,0:T(8,128)(2,1)S(1)}, bf16[4,48,768]{2,1,0:T(8,128)(2,1)}, u32[]{:S(2)}) copy-start(bf16[4,48,768]{2,1,0:T(8,128)(2,1)} %weights.1) | copy-start | bytes 884740
  117.1 17.2 %collective-permute-start.31 = (f32[3,48,768]{2,1,0:T(8,128)S(1)}, f32[3,48,768]{2,1,0:T(8,128)S(1)}, u32[]{:S(2)}, u32[]{:S(2)}) collective-permute-start(f32[3,48,768]{2,1,0:T(8,128)S(1)} %get-tuple-element.82), channel_id=1, source_target_pairs={{0,1},{1,0},{2,3},{3,2},{4,5},{5,4},{6,7},{7,6},{8,9},{9,8},{10,11... | collective-permute-start | bytes 1327112 | tf_op jit(solution)/shard_map/ppermute | solution.py:140
  117.2 17.1 %collective-permute-start.32 = (f32[48,768]{1,0:T(8,128)S(1)}, f32[48,768]{1,0:T(8,128)S(1)}, u32[]{:S(2)}, u32[]{:S(2)}) collective-permute-start(f32[48,768]{1,0:T(8,128)S(1)} %get-tuple-element.81.own_dir), channel_id=1, source_target_pairs={{0,16},{16,0},{1,17},{17,1},{2,18},{18,2},{3,19},{19,3},{4,20},{20... | collective-permute-start | bytes 442376 | tf_op jit(solution)/shard_map/ppermute | solution.py:148
  118.8 15.5 %collective-permute-start.33 = (f32[48,768]{1,0:T(8,128)S(1)}, f32[48,768]{1,0:T(8,128)S(1)}, u32[]{:S(2)}, u32[]{:S(2)}) collective-permute-start(f32[48,768]{1,0:T(8,128)S(1)} %get-tuple-element.83), channel_id=1, source_target_pairs={{0,17},{1,16},{2,19},{3,18},{16,1},{17,0},{18,3},{19,2},{4,21},{5,... | collective-permute-start | bytes 442376 | tf_op jit(solution)/shard_map/ppermute | solution.py:157

commit v3 on v2

--- a/solution.py
+++ b/solution.py
@@ -152,11 +152,6 @@
     return lax.ppermute(value, "tensor", [(i, i ^ bits) for i in range(4)])
 
 
-def to_cy(value):
-    pairs = [(4 * y + s, 4 * (1 - y) + (s ^ 1)) for y in range(2) for s in range(4)]
-    return lax.ppermute(value, ("shard", "section"), pairs)
-
-
 def row_dot(rows, full):
     return lax.dot_general(rows, full, (((1,), (0,)), ((), ())), preferred_element_type=F32)
 
@@ -222,85 +217,100 @@
 
 SMEM_SPEC = pl.BlockSpec(memory_space=pltpu.SMEM)
 VMEM_SPEC = pl.BlockSpec(memory_space=pltpu.VMEM)
-ANY_SPEC = pl.BlockSpec(memory_space=pl.ANY)
-
-
-def call(body, outs, ins, args, scratch=(), out_specs=None):
+HBM_SPEC = pl.BlockSpec(memory_space=pltpu.HBM)
+
+
+def work(micros):
+    return pl.CostEstimate(
+        flops=int(micros * 10**6), transcendentals=0, bytes_accessed=int(micros * 3.6 * 10**6)
+    )
+
+
+def call(body, outs, ins, args, scratch=(), micros=1.0):
     return pl.pallas_call(
         body,
         out_shape=outs,
         in_specs=ins,
-        out_specs=[VMEM_SPEC] * len(outs) if out_specs is None else out_specs,
+        out_specs=[VMEM_SPEC] * len(outs),
+        cost_estimate=work(micros),
         scratch_shapes=list(scratch),
-        compiler_params=pltpu.CompilerParams(vmem_limit_bytes=48 << 20),
+        compiler_params=pltpu.CompilerParams(vmem_limit_bytes=24 << 20),
     )(*args)
 
 
-def pick_kernel(meta, xin, dout, left, right, x_far, d_far, x_mine, d_mine, roots, sems):
-    plane, core = meta[8], meta[11]
-    place, mine = used_slot(meta, plane, 1 - core)
-    _, far = used_slot(meta, 1 - plane, 1 - core)
+def start_copies(pairs, sems):
     copies = [
-        pltpu.make_async_copy(xin.at[far], x_far, sems.at[0]),
-        pltpu.make_async_copy(dout.at[far], d_far, sems.at[1]),
-        pltpu.make_async_copy(xin.at[mine], x_mine, sems.at[2]),
-        pltpu.make_async_copy(dout.at[mine], d_mine, sems.at[3]),
-        pltpu.make_async_copy(left.at[place], roots.at[0], sems.at[4]),
-        pltpu.make_async_copy(right.at[place], roots.at[1], sems.at[5]),
+        pltpu.make_async_copy(source, target, sems.at[index])
+        for index, (source, target) in enumerate(pairs)
     ]
     for copy in copies:
         copy.start()
-    for copy in copies:
+    return copies
+
+
+def in_parts(source, block, target, parts=4):
+    span = target.shape[0] // parts
+    rows = [pl.ds(part * span, span) for part in range(parts)]
+    return [(source.at[block, part], target.at[part]) for part in rows]
+
+
+def pick_far_kernel(meta, xin, dout, left, right, out, roots, sems):
+    _, block = used_slot(meta, 1 - meta[8], 1 - meta[11])
+    place, _ = used_slot(meta, meta[8], 1 - meta[11])
+    pairs = in_parts(xin, block, out.at[0]) + in_parts(dout, block, out.at[1])
+    pairs += [(left.at[place], roots.at[0]), (right.at[place], roots.at[1])]
+    for copy in start_copies(pairs, sems):
         copy.wait()
 
 
-def own_kernel(meta, x_ref, d_ref, out_ref):
-    out_ref[...] = token_dot(x_ref[...], d_ref[...])
-
-
-def own_part(meta, xin, dout, across):
-    _, tokens, size = xin.shape
-
-    def block_of(step, meta_ref):
-        plane = 1 - meta_ref[8] if across else meta_ref[8]
-        return (used_slot(meta_ref, plane, meta_ref[11])[1], 0, 0)
-
-    taken = pl.BlockSpec((None, tokens, size), block_of)
-    return pl.pallas_call(
-        own_kernel,
-        out_shape=jax.ShapeDtypeStruct((size, size), F32),
-        grid_spec=pltpu.PrefetchScalarGridSpec(
-            num_scalar_prefetch=1,
-            grid=(1,),
-            in_specs=[taken, taken],
-            out_specs=pl.BlockSpec((size, size), lambda step, meta_ref: (0, 0)),
-        ),
-        compiler_params=pltpu.CompilerParams(vmem_limit_bytes=48 << 20),
-    )(meta, xin, dout)
-
-
-def far_kernel(meta, x_ref, d_ref, own_ref, *refs):
+def pick_mine_kernel(meta, xin, dout, out, sems):
+    _, block = used_slot(meta, meta[8], 1 - meta[11])
+    pairs = in_parts(xin, block, out.at[0]) + in_parts(dout, block, out.at[1])
+    for copy in start_copies(pairs, sems):
+        copy.wait()
+
+
+def own_kernel(across, meta, xin, dout, out, taken, sems):
+    plane = 1 - meta[8] if across else meta[8]
+    _, block = used_slot(meta, plane, meta[11])
+    pairs = in_parts(xin, block, taken.at[0]) + in_parts(dout, block, taken.at[1])
+    copies = start_copies(pairs, sems)
+    half = taken.shape[1] // 2
+    for part in (0, 1):
+        for index in (0, 1):
+            copies[2 * part + index].wait()
+            copies[4 + 2 * part + index].wait()
+        rows = pl.ds(part * half, half)
+        value = token_dot(taken[0, rows, :], taken[1, rows, :])
+        out[...] = value if part == 0 else out[...] + value
+
+
+def far_kernel(meta, got, own_ref, *refs):
     outs, total = refs[:4], refs[4]
-    total[...] = own_ref[...] + token_dot(x_ref[...], d_ref[...])
+    total[...] = own_ref[...] + token_dot(got[0], got[1])
     span = total.shape[0] // 4
     for out, bits in zip(outs, (3, 2, 1, 0)):
         first = pl.multiple_of((meta[9] ^ bits) * span, 64)
         out[...] = encode(total[pl.ds(first, span), :])
 
 
-def mine_kernel(x_ref, d_ref, own_ref, out_ref):
-    out_ref[...] = own_ref[...] + token_dot(x_ref[...], d_ref[...])
-
-
-def rows_kernel(meta, left, right, got, left_out, right_out):
+def mine_kernel(got, own_ref, out_ref):
+    out_ref[...] = own_ref[...] + token_dot(got[0], got[1])
+
+
+def rows_kernel(meta, left, right, got, left_out, right_out, whole, sems):
     core = meta[11]
+    rows = got.shape[1]
     place, _ = used_slot(meta, meta[8], core)
-    rows = left.shape[1]
-    own_first = pl.multiple_of(core * rows, 16)
-    sib_first = pl.multiple_of((1 - core) * rows, 16)
-    for index, (source, out) in enumerate(((left, left_out), (right, right_out))):
-        out[pl.ds(own_first, rows), :] = source[place]
-        out[pl.ds(sib_first, rows), :] = got[index]
+    own = pl.ds(pl.multiple_of(core * rows, 16), rows)
+    sib = pl.ds(pl.multiple_of((1 - core) * rows, 16), rows)
+    pairs = [(left.at[place], left_out.at[own, :]), (right.at[place], whole.at[own, :])]
+    copies = start_copies(pairs, sems)
+    left_out[sib, :] = got[0]
+    whole[sib, :] = got[1]
+    for copy in copies:
+        copy.wait()
+    right_out[...] = encode(whole[...])
 
 
 def y_kernel(meta, got, mine, coded, keep, both):
@@ -333,7 +343,8 @@
             ],
             scratch_shapes=[pltpu.VMEM((2 * rows, size), F32)],
         ),
-        compiler_params=pltpu.CompilerParams(vmem_limit_bytes=48 << 20),
+        compiler_params=pltpu.CompilerParams(vmem_limit_bytes=24 << 20),
+        cost_estimate=work(1.1),
     )(meta, got, mine)
 
 
@@ -359,26 +370,20 @@
 
 
 def root_kernel(meta, *refs):
-    for step in range(4):
-        for side in range(2):
-            spot = 2 * (meta[9] ^ step) + (meta[10] ^ side)
-            put_rows(spot, refs[2 * step + side][...], refs[8], refs[9])
-
-
-def block_kernel(meta, *refs):
+    for index in range(8):
+        spot = 2 * (meta[9] ^ (index // 2)) + (meta[10] ^ (index % 2))
+        put_rows(spot, decode(refs[index][...]), refs[8], refs[9])
+
+
+def direction_kernel(meta, *refs):
     grad_ref, pieces = refs[0], refs[1:8]
     left_ref, root_high, root_low, adam_ref = refs[8:12]
-    own_left, own_right, own_dir, sib_out, sib_dir, sums = refs[12:18]
-    high_ref, low_ref, whole = refs[18:21]
+    own_dir, sib_dir, sums, high_ref, low_ref, whole = refs[12:18]
     for index in range(8):
         spot = 2 * (meta[9] ^ (index // 2)) + (meta[10] ^ (index % 2))
         value = grad_ref[...] if index == 0 else decode(pieces[index - 1][...])
         put_rows(spot, value, high_ref, low_ref)
-    rows, size = left_ref.shape
-    half = rows // 2
-    own = pl.ds(pl.multiple_of(meta[11] * half, 16), half)
-    sib = pl.ds(pl.multiple_of((1 - meta[11]) * half, 16), half)
-    first = (2 * meta[9] + meta[10]) * rows
+    half = left_ref.shape[0] // 2
     high, low = high_ref[...], low_ref[...]
     left_high, left_low = halves(left_ref[...])
     prod = row_dot(left_high, high) + (row_dot(left_low, high) + row_dot(left_high, low))
@@ -388,12 +393,19 @@
         row_dot(prod_low, root_h) + row_dot(prod_high, root_l)
     )
     whole[...] = direction
-    own_dir[...] = whole[own, :]
-    sib_dir[...] = whole[sib, :]
-    sib_out[2] = whole[sib, :]
+    own_dir[...] = whole[pl.ds(pl.multiple_of(meta[11] * half, 16), half), :]
+    sib_dir[...] = whole[pl.ds(pl.multiple_of((1 - meta[11]) * half, 16), half), :]
     lane = lax.broadcasted_iota(jnp.int32, (1, 128), 1)
-    line = jnp.where(lane == 2, jnp.sum(direction * direction), adam_ref[...])
-    sums[...] = jnp.broadcast_to(line.reshape(1, 1, 128), sums.shape)
+    sums[...] = jnp.where(lane == 2, jnp.sum(direction * direction), adam_ref[...])
+
+
+def gram_kernel(meta, grad_ref, high_ref, low_ref, own_left, own_right, sib_out, whole):
+    rows, size = grad_ref.shape
+    half = rows // 2
+    own = pl.ds(pl.multiple_of(meta[11] * half, 16), half)
+    sib = pl.ds(pl.multiple_of((1 - meta[11]) * half, 16), half)
+    first = (2 * meta[9] + meta[10]) * rows
+    high, low = high_ref[...], low_ref[...]
     own_high, own_low = halves(grad_ref[...])
     whole[...] = row_dot_t(own_high, high) + (
         row_dot_t(own_low, high) + row_dot_t(own_high, low)
@@ -429,22 +441,22 @@
     adam_out[...] = line
 
 
-def last_kernel(
-    meta,
-    sums,
-    own_left,
-    own_right,
-    own_dir,
-    got,
-    y_dir,
-    cy_dir,
-    weights,
-    left,
-    right,
-    weights_out,
-    left_out,
-    right_out,
-):
+def weight_kernel(meta, sums, own_dir, sib_dir, weights, out):
+    plane, core = meta[8], meta[11]
+    lane = lax.broadcasted_iota(jnp.int32, (1, 128), 1)
+    for slot, value in ((core, own_dir[...]), (1 - core, sib_dir[...])):
+        line = jnp.zeros((1, 128), F32)
+        for device in range(sums.shape[0]):
+            kept = jnp.logical_or(lane == slot, jnp.logical_and(lane == 2, slot == device % 2))
+            line = line + jnp.where(kept, sums[device], 0.0)
+        dir_sq = jnp.sum(jnp.where(lane == 2, line, 0.0), axis=1, keepdims=True)
+        adam_sq = jnp.sum(jnp.where(lane == 2, 0.0, line), axis=1, keepdims=True)
+        graft = jnp.sqrt(adam_sq) / (jnp.sqrt(dir_sq) + 1e-06)
+        _, block = used_slot(meta, plane, slot)
+        out[slot] = (weights[block].astype(F32) - 0.05 * graft * value).astype(BF16)
+
+
+def stat_kernel(meta, own_left, own_right, got, left, right, left_out, right_out):
     plane, core = meta[8], meta[11]
     left_out[...] = left[...]
     right_out[...] = right[...]
@@ -455,27 +467,15 @@
         place, _ = used_slot(meta, plane, slot)
         left_out[place] = 0.5 * left[place] + 0.5 * left_gram
         right_out[place] = 0.5 * right[place] + 0.5 * right_gram
-    lane = lax.broadcasted_iota(jnp.int32, (1, 128), 1)
-
-    def graft(of_plane, slot):
-        line = jnp.zeros((1, 128), F32)
-        for device in range(16):
-            row = sums[of_plane * 16 + device]
-            kept = jnp.logical_or(lane == slot, jnp.logical_and(lane == 2, slot == device % 2))
-            line = line + jnp.where(kept, row, 0.0)
-        dir_sq = jnp.sum(jnp.where(lane == 2, line, 0.0), axis=1, keepdims=True)
-        adam_sq = jnp.sum(jnp.where(lane == 2, 0.0, line), axis=1, keepdims=True)
-        return jnp.sqrt(adam_sq) / (jnp.sqrt(dir_sq) + 1e-06)
-
-    for of_plane, slot, value in (
-        (plane, core, own_dir[...]),
-        (plane, 1 - core, got[2]),
-        (1 - plane, core, y_dir[...]),
-        (1 - plane, 1 - core, cy_dir[...]),
-    ):
-        _, block = used_slot(meta, of_plane, slot)
-        step = 0.05 * graft(of_plane, slot)
-        weights_out[block] = (weights[block].astype(F32) - step * value).astype(BF16)
+
+
+def place_kernel(meta, near, mirror, out):
+    plane = meta[8]
+    for slot in (0, 1):
+        _, block = used_slot(meta, plane, slot)
+        out[block] = near[slot]
+        _, block = used_slot(meta, 1 - plane, slot)
+        out[block] = mirror[slot]
 
 
 def two_planes(
@@ -508,54 +508,92 @@
         return jax.ShapeDtypeStruct(dims, dtype)
 
     words = jnp.int16
-    rows_in = shape(tokens, size, dtype=BF16)
-    x_far, d_far, x_mine, d_mine, roots = call(
-        pick_kernel,
-        [rows_in] * 4 + [shape(2, rows, size)],
-        [SMEM_SPEC] + [ANY_SPEC] * 4,
+    tile = shape(rows, size)
+    tokens_in = shape(2, tokens, size, dtype=BF16)
+    piece = shape(coded_rows(2 * rows), size, dtype=words)
+
+    def dmas(count):
+        return pltpu.SemaphoreType.DMA((count,))
+
+    xin, dout, left_root, right_root = (
+        pltpu.with_memory_space_constraint(value, pltpu.HBM)
+        for value in (xin, dout, left_root, right_root)
+    )
+    far_in, roots = call(
+        pick_far_kernel,
+        [tokens_in, shape(2, rows, size)],
+        [SMEM_SPEC] + [HBM_SPEC] * 4,
         (meta, xin, dout, left_root, right_root),
-        [pltpu.SemaphoreType.DMA((6,))],
-        [ANY_SPEC] * 5,
-    )
-    x_far, d_far = to_core(x_far), to_core(d_far)
-    x_mine, d_mine, roots = to_core(x_mine), to_core(d_mine), to_core(roots)
-    own_far = own_part(meta, xin, dout, True)
-    own_mine = own_part(meta, xin, dout, False)
+        [dmas(10)],
+    )
+    roots = to_core(roots)
+    far_in = to_core(far_in)
+    def own_part(across, meta):
+        return call(
+            functools.partial(own_kernel, across),
+            [shape(size, size)],
+            [SMEM_SPEC] + [HBM_SPEC] * 2,
+            (meta, xin, dout),
+            [pltpu.VMEM((2, tokens, size), BF16), dmas(8)],
+        )[0]
+
+    own_far = own_part(True, meta)
     chunk = coded_rows(size // 4)
-    coded = call(
+    coded = list(call(
         far_kernel,
         [shape(chunk, size, dtype=words)] * 4,
-        [SMEM_SPEC] + [VMEM_SPEC] * 3,
-        (meta, x_far, d_far, own_far),
+        [SMEM_SPEC] + [VMEM_SPEC] * 2,
+        (meta, far_in, own_far),
         [pltpu.VMEM((size, size), F32)],
-    )
+    ))
+    coded[0], later, roots = lax.optimization_barrier((coded[0], meta, roots))
     got_y = [to_y(value) for value in coded]
+    left_rows, right_coded = call(
+        rows_kernel,
+        [shape(2 * rows, size), piece],
+        [SMEM_SPEC] + [HBM_SPEC] * 2 + [VMEM_SPEC],
+        (meta, left_root, right_root, roots),
+        [pltpu.VMEM((2 * rows, size), F32), dmas(2)],
+    )
+    root_z = [to_z(right_coded, bits) for bits in (1, 2, 3)]
+    root_x = [to_x(right_coded)]
+    (mine_in,) = call(
+        pick_mine_kernel,
+        [tokens_in],
+        [SMEM_SPEC] + [HBM_SPEC] * 2,
+        (later, xin, dout),
+        [dmas(8)],
+        2.1,
+    )
+    mine_in = to_core(mine_in)
+    own_mine = own_part(False, later)
     (mine,) = call(
         mine_kernel,
         [shape(size, size)],
-        [VMEM_SPEC] * 3,
-        (x_mine, d_mine, own_mine),
-    )
-    left_rows, right_rows = call(
-        rows_kernel,
-        [shape(2 * rows, size)] * 2,
-        [SMEM_SPEC] + [VMEM_SPEC] * 3,
-        (meta, left_root, right_root, roots),
-    )
-    root_column = [right_rows] + [to_z(right_rows, bits) for bits in (1, 2, 3)]
-
-    piece = shape(coded_rows(2 * rows), size, dtype=words)
+        [VMEM_SPEC] * 2,
+        (mine_in, own_mine),
+    )
     order = (3, 2, 1, 0)
     got_x, keeps, got_z = [], [], []
     for index, bits in enumerate(order):
         arrived = got_y[index]
+        if index == 0:
+            arrived, root_x[0], root_z[0] = lax.optimization_barrier(
+                (arrived, root_x[0], root_z[0])
+            )
+            root_x.append(to_x(root_z[0]))
         if index == 1:
-            arrived, got_x[0] = lax.optimization_barrier((arrived, got_x[0]))
+            arrived, got_x[0], root_x[1], *root_z[1:] = lax.optimization_barrier(
+                (arrived, got_x[0], root_x[1], *root_z[1:])
+            )
+            root_x += [to_x(root_z[1]), to_x(root_z[2])]
         if index == 2:
-            arrived, got_x[1] = lax.optimization_barrier((arrived, got_x[1]))
+            arrived, got_x[1], root_x[2] = lax.optimization_barrier(
+                (arrived, got_x[1], root_x[2])
+            )
         if index == 3:
-            arrived, got_x[2], got_z[0] = lax.optimization_barrier(
-                (arrived, got_x[2], got_z[0])
+            arrived, got_x[2], got_z[0], root_x[3] = lax.optimization_barrier(
+                (arrived, got_x[2], got_z[0], root_x[3])
             )
         sent, keep = after_y(meta, arrived, mine, bits)
         got_x.append(to_x(sent))
@@ -577,9 +615,9 @@
     for part in column:
         pieces += [part, to_x(part)]
 
-    root_pieces = []
-    for part in root_column:
-        root_pieces += [part, to_x(part)]
+    root_pieces = [right_coded, root_x[0]]
+    for near, across in zip(root_z, root_x[1:]):
+        root_pieces += [near, across]
     root_high, root_low = call(
         root_kernel,
         [shape(size, size, dtype=BF16)] * 2,
@@ -596,36 +634,46 @@
         [SMEM_SPEC] + [VMEM_SPEC] * 4,
         (meta, grad, to_core(grad_out), first_moment, second_moment),
     )
-    tile = shape(rows, size)
-    own_left, own_right, own_dir, sib_out, sib_dir, sums = call(
-        block_kernel,
-        [tile, tile, tile, shape(3, rows, size), tile, shape(device_count, 1, 128)],
+    own_dir, sib_dir, sums, high, low = call(
+        direction_kernel,
+        [tile, tile, shape(1, 128)] + [shape(size, size, dtype=BF16)] * 2,
         [SMEM_SPEC] + [VMEM_SPEC] * 12,
         (meta, grad, *pieces[1:], left_rows, root_high, root_low, adam),
-        [pltpu.VMEM((size, size), BF16)] * 2 + [pltpu.VMEM((2 * rows, size), F32)],
-    )
-    got = to_core(sib_out)
-    y_dir = to_y(own_dir)
-    cy_dir = to_cy(sib_dir)
-    sums = lax.all_to_all(sums, ("shard",) + GROUP, 0, 0)
-    return tuple(call(
-        last_kernel,
-        [shape(block_count, rows, size, dtype=BF16), stack, stack],
-        [SMEM_SPEC] + [VMEM_SPEC] * 10,
-        (
-            meta,
-            sums,
-            own_left,
-            own_right,
-            own_dir,
-            got,
-            y_dir,
-            cy_dir,
-            weights,
-            left_stat,
-            right_stat,
-        ),
-    )) + (new_first, new_second)
+        [pltpu.VMEM((2 * rows, size), F32)],
+    )
+    sib_dir = to_core(sib_dir)
+    sums = jnp.broadcast_to(sums[None], (device_count // 2, 1, 128))
+    sums = lax.all_to_all(sums, GROUP, 0, 0)
+    (near,) = call(
+        weight_kernel,
+        [shape(2, rows, size, dtype=BF16)],
+        [SMEM_SPEC] + [VMEM_SPEC] * 4,
+        (meta, sums, own_dir, sib_dir, weights),
+    )
+    mirror = to_y(near)
+    high, near = lax.optimization_barrier((high, near))
+    own_left, own_right, sib_out = call(
+        gram_kernel,
+        [tile, tile, shape(2, rows, size)],
+        [SMEM_SPEC] + [VMEM_SPEC] * 3,
+        (meta, grad, high, low),
+        [pltpu.VMEM((2 * rows, size), F32)],
+        3.1,
+    )
+    new_left, new_right = call(
+        stat_kernel,
+        [stack, stack],
+        [SMEM_SPEC] + [VMEM_SPEC] * 5,
+        (meta, own_left, own_right, to_core(sib_out), left_stat, right_stat),
+    )
+    new_left, mirror = lax.optimization_barrier((new_left, mirror))
+    (new_weights,) = call(
+        place_kernel,
+        [shape(block_count, rows, size, dtype=BF16)],
+        [SMEM_SPEC] + [VMEM_SPEC] * 2,
+        (meta, near, mirror),
+    )
+    return new_weights, new_left, new_right, new_first, new_second
 
 
 def solution(mesh):

time: 137 us -> 125 us (0.912)
  waiting for transfers between devices: 40.8 us -> 28.7 us
  Pallas kernels: 31.2 us -> 36.1 us
  blocking collectives: 15.2 us -> 10.9 us
  starting transfers between devices: 43.7 us -> 45.5 us
  local copies, waits for them, and re-layouts: 4.31 us -> 2.63 us
    ppermute x9, waiting for transfers between devices: 29.1 us -> 16.9 us  [to_z(): return lax.ppermute(value, 'tensor', [(i, i ^ bits) for i in range(4)])]
    pallas_call x12 -> x18, Pallas kernels: 21.8 us -> 31.9 us  [call(): pl.pallas_call(body, out_shape=outs, in_specs=ins, out_specs=[VMEM_SPEC]...]
    pallas_call x2 -> x0, Pallas kernels: 5.06 us -> none  [own_part(): pl.pallas_call(own_kernel, out_shape=jax.ShapeDtypeStruct((size, size), F...]
    all_to_all x1, blocking collectives: 15.2 us -> 10.9 us  [two_planes(): sums = lax.all_to_all(sums, GROUP, 0, 0)]
    ppermute x9, starting transfers between devices: 18.8 us -> 21.3 us  [to_z(): return lax.ppermute(value, 'tensor', [(i, i ^ bits) for i in range(4)])]
    unnamed x22 -> x18, local copies, waits for them, and re-layouts: 3.57 us -> 1.88 us
  transfers between devices with their start and end apart: 34 -> 32, of which waited for: 11 -> 11; matrix products, arithmetic and copies ran while one was open for 0% -> 0% of each run, Pallas kernels for 15% -> 17%
where the time goes in v3:
time: 125 us
  starting transfers between devices  45.5 us (36%)
  Pallas kernels  36.1 us (29%)
  waiting for transfers between devices  28.7 us (23%)
  blocking collectives  10.9 us (9%)
  local copies, waits for them, and re-layouts  2.63 us (2%)
    pallas_call x18, Pallas kernels, call(): pl.pallas_call(body, out_shape=outs, in_specs=ins, out_specs=[VMEM_SPEC]...  31.9 us
    ppermute x9, starting transfers between devices, to_z(): return lax.ppermute(value, 'tensor', [(i, i ^ bits) for i in range(4)])  21.3 us
    ppermute x9, waiting for transfers between devices, to_z(): return lax.ppermute(value, 'tensor', [(i, i ^ bits) for i in range(4)])  16.9 us
    ppermute x12, starting transfers between devices, to_x(): return lax.ppermute(value, 'section', [(i, i ^ 2) for i in range(4)])  16.8 us
    all_to_all x1, blocking collectives, two_planes(): sums = lax.all_to_all(sums, GROUP, 0, 0)  10.9 us
    ppermute x5, waiting for transfers between devices, to_y(): return lax.ppermute(value, 'shard', [(0, 1), (1, 0)])  7.12 us
    ppermute x5, starting transfers between devices, to_y(): return lax.ppermute(value, 'shard', [(0, 1), (1, 0)])  5.7 us
    pallas_call x4, Pallas kernels, after_y(): pl.pallas_call(y_kernel, out_shape=[jax.ShapeDtypeStruct((coded_rows(rows...  4.25 us
  transfers between devices with their start and end apart: 32, of which 11 were waited for; matrix products, arithmetic and copies ran while one was open for 0% of the time, Pallas kernels for 17%

profile of v3, /device:TPU:0, one launch (start us, length us, event | category | flops | bytes accessed | tf_op | source)
XLA Modules:
  0.0 124.8 jit_solution(9678724195029673768)
XLA Ops:
  0.7 0.7 concatenate.3.meta
  1.4 2.2 %shard_map.137 = (bf16[2,512,768]{2,1,0:T(8,128)(2,1)S(1)}, f32[2,48,768]{2,1,0:T(8,128)S(1)}) custom-call(s32[12]{0:T(128)S(1)} %concatenate.3.meta, bf16[4,512,768]{2,1,0:T(8,128)(2,1)} %xin.7, bf16[4,512,768]{2,1,0:T(8,128)(2,1)} %dout.7, f32[4,48,768]{2,1,0:T(8,128)} %left.4, f32[4,48,768]{2,1,0:T(8,128)} %right.4), custom_call_target="tpu_custom_call" | custom-call | flops 1000000 | bytes 3600000 | tf_op jit(solution)/shard_map/pallas_call | solution.py:230
  3.6 0.5 collective-permute-start
  4.2 3.1 %shard_map.138.own_ref = f32[768,768]{1,0:T(8,128)S(1)} custom-call(s32[12]{0:T(128)S(1)} %concatenate.3.meta, bf16[4,512,768]{2,1,0:T(8,128)(2,1)} %xin.7, bf16[4,512,768]{2,1,0:T(8,128)(2,1)} %dout.7), custom_call_target="tpu_custom_call" | custom-call | flops 1000000 | bytes 3600000 | tf_op jit(solution)/shard_map/pallas_call | solution.py:230
  7.2 2.5 %shard_map.139 = (s16[256,768]{1,0:T(8,128)(2,1)S(1)}, s16[256,768]{1,0:T(8,128)(2,1)S(1)}, s16[256,768]{1,0:T(8,128)(2,1)S(1)}, s16[256,768]{1,0:T(8,128)(2,1)S(1)}) custom-call(s32[12]{0:T(128)S(1)} %concatenate.3.meta, bf16[2,512,768]{2,1,0:T(8,128)(2,1)S(1)} %collective-permute-done.got, f32[768,768]{1,0:T(8,128)S(1)} %shard_map.138.own_ref), custom_call_target="tpu_custom_call" | custom-call | flops 1000000 | bytes 3600000 | tf_op jit(solution)/shard_map/pallas_call | solution.py:230
  9.7 2.1 %shard_map.141 = bf16[2,512,768]{2,1,0:T(8,128)(2,1)S(1)} custom-call(s32[12]{0:T(128)S(1)} %concatenate.3.meta, bf16[4,512,768]{2,1,0:T(8,128)(2,1)} %xin.7, bf16[4,512,768]{2,1,0:T(8,128)(2,1)} %dout.7), custom_call_target="tpu_custom_call" | custom-call | flops 2100000 | bytes 7560000 | tf_op jit(solution)/shard_map/pallas_call | solution.py:230
  11.8 0.5 collective-permute-start.8
  12.3 2.6 %collective-permute-start.5 = (s16[256,768]{1,0:T(8,128)(2,1)S(1)}, s16[256,768]{1,0:T(8,128)(2,1)S(1)}, u32[]{:S(2)}, u32[]{:S(2)}) collective-permute-start(s16[256,768]{1,0:T(8,128)(2,1)S(1)} %get-tuple-element.66), channel_id=1, source_target_pairs={{0,16},{16,0},{1,17},{17,1},{2,18},{18,2},{3,19},{19,3},{4,20},{20... | collective-permute-start | bytes 1179656 | tf_op jit(solution)/shard_map/ppermute | solution.py:148
  14.9 1.7 %shard_map.140 = (f32[96,768]{1,0:T(8,128)S(1)}, s16[128,768]{1,0:T(8,128)(2,1)S(1)}) custom-call(s32[12]{0:T(128)S(1)} %concatenate.3.meta, f32[4,48,768]{2,1,0:T(8,128)} %left.4, f32[4,48,768]{2,1,0:T(8,128)} %right.4, f32[2,48,768]{2,1,0:T(8,128)S(1)} %collective-permute-done.4.got), custom_call_target="tpu_custom_call" | custom-call | flops 1000000 | bytes 3600000 | tf_op jit(solution)/shard_map/pallas_call | solution.py:230
  16.6 1.6 %collective-permute-start.6 = (s16[128,768]{1,0:T(8,128)(2,1)S(1)}, s16[128,768]{1,0:T(8,128)(2,1)S(1)}, u32[]{:S(2)}, u32[]{:S(2)}) collective-permute-start(s16[128,768]{1,0:T(8,128)(2,1)S(1)} %get-tuple-element.68.refs_0_), channel_id=1, source_target_pairs={{0,2},{1,3},{2,0},{3,1},{4,6},{5,7},{6,4},{7,5},{8,10},{9,11},{10,... | collective-permute-start | bytes 589832 | tf_op jit(solution)/shard_map/ppermute | solution.py:144
  18.2 1.6 %collective-permute-start.7 = (s16[128,768]{1,0:T(8,128)(2,1)S(1)}, s16[128,768]{1,0:T(8,128)(2,1)S(1)}, u32[]{:S(2)}, u32[]{:S(2)}) collective-permute-start(s16[128,768]{1,0:T(8,128)(2,1)S(1)} %get-tuple-element.68.refs_0_), channel_id=1, source_target_pairs={{0,4},{4,0},{8,12},{12,8},{1,5},{5,1},{9,13},{13,9},{2,6},{6,2},{1... | collective-permute-start | bytes 589832 | tf_op jit(solution)/shard_map/ppermute | solution.py:152
  19.8 0.5 collective-permute-start.3
  20.3 3.4 %collective-permute-done.6.refs_1_ = s16[128,768]{1,0:T(8,128)(2,1)S(1)} collective-permute-done((s16[128,768]{1,0:T(8,128)(2,1)S(1)}, s16[128,768]{1,0:T(8,128)(2,1)S(1)}, u32[]{:S(2)}, u32[]{:S(2)}) %collective-permute-start.6) | collective-permute-done | bytes 196640 | tf_op jit(solution)/shard_map/ppermute | solution.py:144
  23.7 2.6 %collective-permute-start.11 = (s16[128,768]{1,0:T(8,128)(2,1)S(1)}, s16[128,768]{1,0:T(8,128)(2,1)S(1)}, u32[]{:S(2)}, u32[]{:S(2)}) collective-permute-start(s16[128,768]{1,0:T(8,128)(2,1)S(1)} %get-tuple-element.68.refs_0_), channel_id=1, source_target_pairs={{0,8},{4,12},{8,0},{12,4},{1,9},{5,13},{9,1},{13,5},{2,10},{6,14},... | collective-permute-start | bytes 589832 | tf_op jit(solution)/shard_map/ppermute | solution.py:152
  26.3 3.0 %shard_map.142.own_ref = f32[768,768]{1,0:T(8,128)S(1)} custom-call(s32[12]{0:T(128)S(1)} %concatenate.3.meta, bf16[4,512,768]{2,1,0:T(8,128)(2,1)} %xin.7, bf16[4,512,768]{2,1,0:T(8,128)(2,1)} %dout.7), custom_call_target="tpu_custom_call" | custom-call | flops 1000000 | bytes 3600000 | tf_op jit(solution)/shard_map/pallas_call | solution.py:230
  29.3 1.4 %collective-permute-start.12 = (s16[128,768]{1,0:T(8,128)(2,1)S(1)}, s16[128,768]{1,0:T(8,128)(2,1)S(1)}, u32[]{:S(2)}, u32[]{:S(2)}) collective-permute-start(s16[128,768]{1,0:T(8,128)(2,1)S(1)} %get-tuple-element.68.refs_0_), channel_id=1, source_target_pairs={{0,12},{4,8},{8,4},{12,0},{1,13},{5,9},{9,5},{13,1},{2,14},{6,10},... | collective-permute-start | bytes 589832 | tf_op jit(solution)/shard_map/ppermute | solution.py:152
  30.7 1.5 %collective-permute-start.10 = (s16[128,768]{1,0:T(8,128)(2,1)S(1)}, s16[128,768]{1,0:T(8,128)(2,1)S(1)}, u32[]{:S(2)}, u32[]{:S(2)}) collective-permute-start(s16[128,768]{1,0:T(8,128)(2,1)S(1)} %collective-permute-done.7.refs_2_), channel_id=1, source_target_pairs={{0,2},{1,3},{2,0},{3,1},{4,6},{5,7},{6,4},{7,5},{8,10},{9,11},{10,... | collective-permute-start | bytes 589832 | tf_op jit(solution)/shard_map/ppermute | solution.py:144
  32.2 0.8 shard_map.143.mine
  33.1 1.1 shard_map.144
  34.1 0.6 collective-permute-start.9
  34.7 5.6 %collective-permute-done.11.refs_4_ = s16[128,768]{1,0:T(8,128)(2,1)S(1)} collective-permute-done((s16[128,768]{1,0:T(8,128)(2,1)S(1)}, s16[128,768]{1,0:T(8,128)(2,1)S(1)}, u32[]{:S(2)}, u32[]{:S(2)}) %collective-permute-start.11) | collective-permute-done | bytes 196640 | tf_op jit(solution)/shard_map/ppermute | solution.py:152
  40.3 0.5 collective-permute-start.2
  40.8 1.1 shard_map.145
  41.9 1.6 %collective-permute-start.13 = (s16[128,768]{1,0:T(8,128)(2,1)S(1)}, s16[128,768]{1,0:T(8,128)(2,1)S(1)}, u32[]{:S(2)}, u32[]{:S(2)}) collective-permute-start(s16[128,768]{1,0:T(8,128)(2,1)S(1)} %get-tuple-element.74), channel_id=1, source_target_pairs={{0,2},{1,3},{2,0},{3,1},{4,6},{5,7},{6,4},{7,5},{8,10},{9,11},{10,... | collective-permute-start | bytes 589832 | tf_op jit(solution)/shard_map/ppermute | solution.py:144
  43.5 0.5 collective-permute-start.14
  44.0 1.5 %collective-permute-start.1 = (s16[256,768]{1,0:T(8,128)(2,1)S(1)}, s16[256,768]{1,0:T(8,128)(2,1)S(1)}, u32[]{:S(2)}, u32[]{:S(2)}) collective-permute-start(s16[256,768]{1,0:T(8,128)(2,1)S(1)} %get-tuple-element.61), channel_id=1, source_target_pairs={{0,16},{16,0},{1,17},{17,1},{2,18},{18,2},{3,19},{19,3},{4,20},{20... | collective-permute-start | bytes 1179656 | tf_op jit(solution)/shard_map/ppermute | solution.py:148
  45.5 0.2 shard_map.147
  45.8 2.5 %collective-permute-start.16 = (s16[128,768]{1,0:T(8,128)(2,1)S(1)}, s16[128,768]{1,0:T(8,128)(2,1)S(1)}, u32[]{:S(2)}, u32[]{:S(2)}) collective-permute-start(s16[128,768]{1,0:T(8,128)(2,1)S(1)} %shard_map.147), channel_id=1, source_target_pairs={{0,12},{4,8},{8,4},{12,0},{1,13},{5,9},{9,5},{13,1},{2,14},{6,10},... | collective-permute-start | bytes 589832 | tf_op jit(solution)/shard_map/ppermute | solution.py:152
  48.2 4.1 %collective-permute-done.2.got = s16[256,768]{1,0:T(8,128)(2,1)S(1)} collective-permute-done((s16[256,768]{1,0:T(8,128)(2,1)S(1)}, s16[256,768]{1,0:T(8,128)(2,1)S(1)}, u32[]{:S(2)}, u32[]{:S(2)}) %collective-permute-start.2) | collective-permute-done | bytes 393248 | tf_op jit(solution)/shard_map/ppermute | solution.py:148
  52.4 1.5 %collective-permute-start.17 = (s16[128,768]{1,0:T(8,128)(2,1)S(1)}, s16[128,768]{1,0:T(8,128)(2,1)S(1)}, u32[]{:S(2)}, u32[]{:S(2)}) collective-permute-start(s16[128,768]{1,0:T(8,128)(2,1)S(1)} %collective-permute-done.12.refs_6_), channel_id=1, source_target_pairs={{0,2},{1,3},{2,0},{3,1},{4,6},{5,7},{6,4},{7,5},{8,10},{9,11},{10,... | collective-permute-start | bytes 589832 | tf_op jit(solution)/shard_map/ppermute | solution.py:144
  53.9 1.1 shard_map.146
  54.9 0.6 collective-permute-start.15
  55.5 0.2 shard_map.149
  55.8 6.2 %collective-permute-start.19 = (s16[128,768]{1,0:T(8,128)(2,1)S(1)}, s16[128,768]{1,0:T(8,128)(2,1)S(1)}, u32[]{:S(2)}, u32[]{:S(2)}) collective-permute-start(s16[128,768]{1,0:T(8,128)(2,1)S(1)} %shard_map.149), channel_id=1, source_target_pairs={{0,8},{4,12},{8,0},{12,4},{1,9},{5,13},{9,1},{13,5},{2,10},{6,14},... | collective-permute-start | bytes 589832 | tf_op jit(solution)/shard_map/ppermute | solution.py:152
  62.0 0.2 shard_map.150
  62.3 2.6 %collective-permute-start.20 = (s16[128,768]{1,0:T(8,128)(2,1)S(1)}, s16[128,768]{1,0:T(8,128)(2,1)S(1)}, u32[]{:S(2)}, u32[]{:S(2)}) collective-permute-start(s16[128,768]{1,0:T(8,128)(2,1)S(1)} %shard_map.150), channel_id=1, source_target_pairs={{0,4},{4,0},{8,12},{12,8},{1,5},{5,1},{9,13},{13,9},{2,6},{6,2},{1... | collective-permute-start | bytes 589832 | tf_op jit(solution)/shard_map/ppermute | solution.py:152
  64.9 1.1 shard_map.148
  66.0 1.6 %collective-permute-start.18 = (s16[128,768]{1,0:T(8,128)(2,1)S(1)}, s16[128,768]{1,0:T(8,128)(2,1)S(1)}, u32[]{:S(2)}, u32[]{:S(2)}) collective-permute-start(s16[128,768]{1,0:T(8,128)(2,1)S(1)} %get-tuple-element.82), channel_id=1, source_target_pairs={{0,2},{1,3},{2,0},{3,1},{4,6},{5,7},{6,4},{7,5},{8,10},{9,11},{10,... | collective-permute-start | bytes 589832 | tf_op jit(solution)/shard_map/ppermute | solution.py:144
  67.6 1.7 %collective-permute-done.19.two = s16[128,768]{1,0:T(8,128)(2,1)S(1)} collective-permute-done((s16[128,768]{1,0:T(8,128)(2,1)S(1)}, s16[128,768]{1,0:T(8,128)(2,1)S(1)}, u32[]{:S(2)}, u32[]{:S(2)}) %collective-permute-start.19) | collective-permute-done | bytes 196640 | tf_op jit(solution)/shard_map/ppermute | solution.py:152
  69.4 2.3 %collective-permute-done.20.three = s16[128,768]{1,0:T(8,128)(2,1)S(1)} collective-permute-done((s16[128,768]{1,0:T(8,128)(2,1)S(1)}, s16[128,768]{1,0:T(8,128)(2,1)S(1)}, u32[]{:S(2)}, u32[]{:S(2)}) %collective-permute-start.20) | collective-permute-done | bytes 196640 | tf_op jit(solution)/shard_map/ppermute | solution.py:152
  71.8 1.4 %shard_map.151 = (f32[96,768]{1,0:T(8,128)S(1)}, s16[128,768]{1,0:T(8,128)(2,1)}) custom-call(s16[128,768]{1,0:T(8,128)(2,1)S(1)} %collective-permute-done.18.got, f32[96,768]{1,0:T(8,128)S(1)} %get-tuple-element.83.keep, s16[128,768]{1,0:T(8,128)(2,1)S(1)} %collective-permute-done.16.one, s16[128,768]{1,0:T(8,128)(2,1)S(1)} %collective-permute-done.19.two, ...), custom_call_target="tpu_custom_call" | custom-call | flops 1000000 | bytes 3600000 | tf_op jit(solution)/shard_map/pallas_call | solution.py:230
  73.3 3.8 %collective-permute-start.24 = (s16[128,768]{1,0:T(8,128)(2,1)}, s16[128,768]{1,0:T(8,128)(2,1)S(1)}, u32[]{:S(2)}, u32[]{:S(2)}) collective-permute-start(s16[128,768]{1,0:T(8,128)(2,1)} %get-tuple-element.90), channel_id=1, source_target_pairs={{0,8},{4,12},{8,0},{12,4},{1,9},{5,13},{9,1},{13,5},{2,10},{6,14},... | collective-permute-start | bytes 589832 | tf_op jit(solution)/shard_map/ppermute | solution.py:152
  77.2 0.4 collective-permute-start.26
  77.6 1.5 %collective-permute-start.21 = (s16[128,768]{1,0:T(8,128)(2,1)}, s16[128,768]{1,0:T(8,128)(2,1)S(1)}, u32[]{:S(2)}, u32[]{:S(2)}) collective-permute-start(s16[128,768]{1,0:T(8,128)(2,1)} %get-tuple-element.90), channel_id=1, source_target_pairs={{0,2},{1,3},{2,0},{3,1},{4,6},{5,7},{6,4},{7,5},{8,10},{9,11},{10,... | collective-permute-start | bytes 589832 | tf_op jit(solution)/shard_map/ppermute | solution.py:144
  79.1 2.6 %collective-permute-done.22.refs_2_ = s16[128,768]{1,0:T(8,128)(2,1)S(1)} collective-permute-done((s16[128,768]{1,0:T(8,128)(2,1)}, s16[128,768]{1,0:T(8,128)(2,1)S(1)}, u32[]{:S(2)}, u32[]{:S(2)}) %collective-permute-start.22) | collective-permute-done | bytes 196640 | tf_op jit(solution)/shard_map/ppermute | solution.py:152
  81.8 3.9 %collective-permute-start.23 = (s16[128,768]{1,0:T(8,128)(2,1)S(1)}, s16[128,768]{1,0:T(8,128)(2,1)S(1)}, u32[]{:S(2)}, u32[]{:S(2)}) collective-permute-start(s16[128,768]{1,0:T(8,128)(2,1)S(1)} %collective-permute-done.22.refs_2_), channel_id=1, source_target_pairs={{0,2},{1,3},{2,0},{3,1},{4,6},{5,7},{6,4},{7,5},{8,10},{9,11},{10,... | collective-permute-start | bytes 589832 | tf_op jit(solution)/shard_map/ppermute | solution.py:144
  85.6 4.6 %collective-permute-done.24.refs_4_ = s16[128,768]{1,0:T(8,128)(2,1)S(1)} collective-permute-done((s16[128,768]{1,0:T(8,128)(2,1)}, s16[128,768]{1,0:T(8,128)(2,1)S(1)}, u32[]{:S(2)}, u32[]{:S(2)}) %collective-permute-start.24) | collective-permute-done | bytes 196640 | tf_op jit(solution)/shard_map/ppermute | solution.py:152
  90.3 1.5 %collective-permute-start.25 = (s16[128,768]{1,0:T(8,128)(2,1)S(1)}, s16[128,768]{1,0:T(8,128)(2,1)S(1)}, u32[]{:S(2)}, u32[]{:S(2)}) collective-permute-start(s16[128,768]{1,0:T(8,128)(2,1)S(1)} %collective-permute-done.24.refs_4_), channel_id=1, source_target_pairs={{0,2},{1,3},{2,0},{3,1},{4,6},{5,7},{6,4},{7,5},{8,10},{9,11},{10,... | collective-permute-start | bytes 589832 | tf_op jit(solution)/shard_map/ppermute | solution.py:144
  91.8 0.5 collective-permute-start.27
  92.4 0.9 copy-done.6
  93.3 0.9 copy-done.8
  94.2 1.5 %shard_map.152 = (bf16[768,768]{1,0:T(8,128)(2,1)S(1)}, bf16[768,768]{1,0:T(8,128)(2,1)S(1)}) custom-call(s32[12]{0:T(128)S(1)} %concatenate.3.meta, s16[128,768]{1,0:T(8,128)(2,1)S(1)} %get-tuple-element.68.refs_0_, s16[128,768]{1,0:T(8,128)(2,1)S(1)} %collective-permute-done.6.refs_1_, s16[128,768]{1,0:T(8,128)(2,1)S(1)} %collective-permute-done.7.refs_2_, ...), custom_call_target="tpu_custom_call" | custom-call | flops 1000000 | bytes 3600000 | tf_op jit(solution)/shard_map/pallas_call | solution.py:230
  95.8 2.1 %shard_map.153 = (f32[4,48,768]{2,1,0:T(8,128)}, f32[4,48,768]{2,1,0:T(8,128)}, f32[1,128]{1,0:T(1,128)S(1)}) custom-call(s32[12]{0:T(128)S(1)} %concatenate.3.meta, f32[96,768]{1,0:T(8,128)S(1)} %get-tuple-element.89.grad.refs_0_.grad_ref, f32[48,768]{1,0:T(8,128)S(1)} %collective-permute-done.28.got, f32[4,48,768]{2,1,0:T(8,128)S(1)} %copy-done, ...), custom_call_target="tpu_custom_call" | custom-call | flops 1000000 | bytes 3600000 | tf_op jit(solution)/shard_map/pallas_call | solution.py:230
  97.9 0.2 collective-permute-done.27.refs_7_
  98.0 3.9 %shard_map.154 = (f32[48,768]{1,0:T(8,128)S(1)}, f32[48,768]{1,0:T(8,128)S(1)}, f32[1,128]{1,0:T(1,128)S(1)}, bf16[768,768]{1,0:T(8,128)(2,1)S(1)}, bf16[768,768]{1,0:T(8,128)(2,1)S(1)}) custom-call(s32[12]{0:T(128)S(1)} %concatenate.3.meta, f32[96,768]{1,0:T(8,128)S(1)} %get-tuple-element.89.grad.refs_0_.grad_ref, ...), custom_call_target="tpu_custom_call" | custom-call | flops 1000000 | bytes 3600000 | tf_op jit(solution)/shard_map/pallas_call | solution.py:230
  102.0 0.4 collective-permute-start.29
  102.4 10.9 %all_to_all.5.sums = f32[16,1,128]{2,1,0:T(1,128)S(1)} all-to-all(f32[16,1,128]{2,1,0:T(1,128)S(1)} %broadcast_in_dim.9), channel_id=1, replica_groups=mesh['shard'=2,'tensor'=4,'section'=4] {'tensor','section'}, dimensions={0} | all-to-all | bytes 16384 | tf_op jit(solution)/shard_map/all_to_all | solution.py:646
  113.3 0.7 shard_map.155.near
  114.0 3.1 %shard_map.156 = (f32[48,768]{1,0:T(8,128)S(1)}, f32[48,768]{1,0:T(8,128)S(1)}, f32[2,48,768]{2,1,0:T(8,128)S(1)}) custom-call(s32[12]{0:T(128)S(1)} %concatenate.3.meta, f32[96,768]{1,0:T(8,128)S(1)} %get-tuple-element.89.grad.refs_0_.grad_ref, bf16[768,768]{1,0:T(8,128)(2,1)S(1)} %get-tuple-element.104.high_ref, ...), custom_call_target="tpu_custom_call" | custom-call | flops 3100000 | bytes 11160000 | tf_op jit(solution)/shard_map/pallas_call | solution.py:230
  117.2 0.6 collective-permute-start.31
  117.8 1.0 collective-permute-done.30.got
  118.8 1.7 %shard_map.157 = (f32[4,48,768]{2,1,0:T(8,128)}, f32[4,48,768]{2,1,0:T(8,128)}) custom-call(s32[12]{0:T(128)S(1)} %concatenate.3.meta, f32[48,768]{1,0:T(8,128)S(1)} %get-tuple-element.106.own_left, f32[48,768]{1,0:T(8,128)S(1)} %get-tuple-element.107.own_right, f32[2,48,768]{2,1,0:T(8,128)S(1)} %collective-permute-done.30.got, f32[4,48,768]{2,1,0:T(8,128)S(1)} %copy-done.2, ...), custom_call_target="tpu_custom_call" | custom-call | flops 1000000 | bytes 3600000 | tf_op jit(solution)/shard_map/pallas_call | solution.py:230
  120.5 3.0 %collective-permute-done.31.mirror = bf16[2,48,768]{2,1,0:T(8,128)(2,1)S(1)} collective-permute-done((bf16[2,48,768]{2,1,0:T(8,128)(2,1)S(1)}, bf16[2,48,768]{2,1,0:T(8,128)(2,1)S(1)}, u32[]{:S(2)}, u32[]{:S(2)}) %collective-permute-start.31) | collective-permute-done | bytes 147488 | tf_op jit(solution)/shard_map/ppermute | solution.py:148
  123.5 1.3 %shard_map.158 = bf16[4,48,768]{2,1,0:T(8,128)(2,1)} custom-call(s32[12]{0:T(128)S(1)} %concatenate.3.meta, bf16[2,48,768]{2,1,0:T(8,128)(2,1)S(1)} %shard_map.155.near, bf16[2,48,768]{2,1,0:T(8,128)(2,1)S(1)} %collective-permute-done.31.mirror), custom_call_target="tpu_custom_call" | custom-call | flops 1000000 | bytes 3600000 | tf_op jit(solution)/shard_map/pallas_call | solution.py:230
  (44 shorter events, 0.6 us)
Async XLA Ops:
  3.6 3.7 %collective-permute-start = (bf16[2,512,768]{2,1,0:T(8,128)(2,1)S(1)}, bf16[2,512,768]{2,1,0:T(8,128)(2,1)S(1)}, u32[]{:S(2)}, u32[]{:S(2)}) collective-permute-start(bf16[2,512,768]{2,1,0:T(8,128)(2,1)S(1)} %get-tuple-element.60), channel_id=1, source_target_pairs={{0,1},{1,0},{2,3},{3,2},{4,5},{5,4},{6,7},{7,6},{8,9},{9,8},{10,11... | collective-permute-start | bytes 4718600 | tf_op jit(solution)/shard_map/ppermute | solution.py:140
  4.1 5.6 %collective-permute-start.4 = (f32[2,48,768]{2,1,0:T(8,128)S(1)}, f32[2,48,768]{2,1,0:T(8,128)S(1)}, u32[]{:S(2)}, u32[]{:S(2)}) collective-permute-start(f32[2,48,768]{2,1,0:T(8,128)S(1)} %get-tuple-element.65), channel_id=1, source_target_pairs={{0,1},{1,0},{2,3},{3,2},{4,5},{5,4},{6,7},{7,6},{8,9},{9,8},{10,11... | collective-permute-start | bytes 884744 | tf_op jit(solution)/shard_map/ppermute | solution.py:140
  11.8 20.4 %collective-permute-start.8 = (bf16[2,512,768]{2,1,0:T(8,128)(2,1)S(1)}, bf16[2,512,768]{2,1,0:T(8,128)(2,1)S(1)}, u32[]{:S(2)}, u32[]{:S(2)}) collective-permute-start(bf16[2,512,768]{2,1,0:T(8,128)(2,1)S(1)} %shard_map.141), channel_id=1, source_target_pairs={{0,1},{1,0},{2,3},{3,2},{4,5},{5,4},{6,7},{7,6},{8,9},{9,8},{10,11... | collective-permute-start | bytes 4718600 | tf_op jit(solution)/shard_map/ppermute | solution.py:140
  12.3 18.4 %collective-permute-start.5 = (s16[256,768]{1,0:T(8,128)(2,1)S(1)}, s16[256,768]{1,0:T(8,128)(2,1)S(1)}, u32[]{:S(2)}, u32[]{:S(2)}) collective-permute-start(s16[256,768]{1,0:T(8,128)(2,1)S(1)} %get-tuple-element.66), channel_id=1, source_target_pairs={{0,16},{16,0},{1,17},{17,1},{2,18},{18,2},{3,19},{19,3},{4,20},{20... | collective-permute-start | bytes 1179656 | tf_op jit(solution)/shard_map/ppermute | solution.py:148
  16.6 7.0 %collective-permute-start.6 = (s16[128,768]{1,0:T(8,128)(2,1)S(1)}, s16[128,768]{1,0:T(8,128)(2,1)S(1)}, u32[]{:S(2)}, u32[]{:S(2)}) collective-permute-start(s16[128,768]{1,0:T(8,128)(2,1)S(1)} %get-tuple-element.68.refs_0_), channel_id=1, source_target_pairs={{0,2},{1,3},{2,0},{3,1},{4,6},{5,7},{6,4},{7,5},{8,10},{9,11},{10,... | collective-permute-start | bytes 589832 | tf_op jit(solution)/shard_map/ppermute | solution.py:144
  18.2 11.1 %collective-permute-start.7 = (s16[128,768]{1,0:T(8,128)(2,1)S(1)}, s16[128,768]{1,0:T(8,128)(2,1)S(1)}, u32[]{:S(2)}, u32[]{:S(2)}) collective-permute-start(s16[128,768]{1,0:T(8,128)(2,1)S(1)} %get-tuple-element.68.refs_0_), channel_id=1, source_target_pairs={{0,4},{4,0},{8,12},{12,8},{1,5},{5,1},{9,13},{13,9},{2,6},{6,2},{1... | collective-permute-start | bytes 589832 | tf_op jit(solution)/shard_map/ppermute | solution.py:152
  19.8 21.0 %collective-permute-start.3 = (s16[256,768]{1,0:T(8,128)(2,1)S(1)}, s16[256,768]{1,0:T(8,128)(2,1)S(1)}, u32[]{:S(2)}, u32[]{:S(2)}) collective-permute-start(s16[256,768]{1,0:T(8,128)(2,1)S(1)} %get-tuple-element.63), channel_id=1, source_target_pairs={{0,16},{16,0},{1,17},{17,1},{2,18},{18,2},{3,19},{19,3},{4,20},{20... | collective-permute-start | bytes 1179656 | tf_op jit(solution)/shard_map/ppermute | solution.py:148
  23.7 16.6 %collective-permute-start.11 = (s16[128,768]{1,0:T(8,128)(2,1)S(1)}, s16[128,768]{1,0:T(8,128)(2,1)S(1)}, u32[]{:S(2)}, u32[]{:S(2)}) collective-permute-start(s16[128,768]{1,0:T(8,128)(2,1)S(1)} %get-tuple-element.68.refs_0_), channel_id=1, source_target_pairs={{0,8},{4,12},{8,0},{12,4},{1,9},{5,13},{9,1},{13,5},{2,10},{6,14},... | collective-permute-start | bytes 589832 | tf_op jit(solution)/shard_map/ppermute | solution.py:152
  29.3 11.5 %collective-permute-start.12 = (s16[128,768]{1,0:T(8,128)(2,1)S(1)}, s16[128,768]{1,0:T(8,128)(2,1)S(1)}, u32[]{:S(2)}, u32[]{:S(2)}) collective-permute-start(s16[128,768]{1,0:T(8,128)(2,1)S(1)} %get-tuple-element.68.refs_0_), channel_id=1, source_target_pairs={{0,12},{4,8},{8,4},{12,0},{1,13},{5,9},{9,5},{13,1},{2,14},{6,10},... | collective-permute-start | bytes 589832 | tf_op jit(solution)/shard_map/ppermute | solution.py:152
  30.7 10.1 %collective-permute-start.10 = (s16[128,768]{1,0:T(8,128)(2,1)S(1)}, s16[128,768]{1,0:T(8,128)(2,1)S(1)}, u32[]{:S(2)}, u32[]{:S(2)}) collective-permute-start(s16[128,768]{1,0:T(8,128)(2,1)S(1)} %collective-permute-done.7.refs_2_), channel_id=1, source_target_pairs={{0,2},{1,3},{2,0},{3,1},{4,6},{5,7},{6,4},{7,5},{8,10},{9,11},{10,... | collective-permute-start | bytes 589832 | tf_op jit(solution)/shard_map/ppermute | solution.py:144
  34.1 6.7 %collective-permute-start.9 = (s16[128,768]{1,0:T(8,128)(2,1)S(1)}, s16[128,768]{1,0:T(8,128)(2,1)S(1)}, u32[]{:S(2)}, u32[]{:S(2)}) collective-permute-start(s16[128,768]{1,0:T(8,128)(2,1)S(1)} %get-tuple-element.71), channel_id=1, source_target_pairs={{0,2},{1,3},{2,0},{3,1},{4,6},{5,7},{6,4},{7,5},{8,10},{9,11},{10,... | collective-permute-start | bytes 589832 | tf_op jit(solution)/shard_map/ppermute | solution.py:144
  40.3 12.1 %collective-permute-start.2 = (s16[256,768]{1,0:T(8,128)(2,1)S(1)}, s16[256,768]{1,0:T(8,128)(2,1)S(1)}, u32[]{:S(2)}, u32[]{:S(2)}) collective-permute-start(s16[256,768]{1,0:T(8,128)(2,1)S(1)} %get-tuple-element.62), channel_id=1, source_target_pairs={{0,16},{16,0},{1,17},{17,1},{2,18},{18,2},{3,19},{19,3},{4,20},{20... | collective-permute-start | bytes 1179656 | tf_op jit(solution)/shard_map/ppermute | solution.py:148
  41.9 12.0 %collective-permute-start.13 = (s16[128,768]{1,0:T(8,128)(2,1)S(1)}, s16[128,768]{1,0:T(8,128)(2,1)S(1)}, u32[]{:S(2)}, u32[]{:S(2)}) collective-permute-start(s16[128,768]{1,0:T(8,128)(2,1)S(1)} %get-tuple-element.74), channel_id=1, source_target_pairs={{0,2},{1,3},{2,0},{3,1},{4,6},{5,7},{6,4},{7,5},{8,10},{9,11},{10,... | collective-permute-start | bytes 589832 | tf_op jit(solution)/shard_map/ppermute | solution.py:144
  43.5 10.4 %collective-permute-start.14 = (s16[128,768]{1,0:T(8,128)(2,1)S(1)}, s16[128,768]{1,0:T(8,128)(2,1)S(1)}, u32[]{:S(2)}, u32[]{:S(2)}) collective-permute-start(s16[128,768]{1,0:T(8,128)(2,1)S(1)} %collective-permute-done.11.refs_4_), channel_id=1, source_target_pairs={{0,2},{1,3},{2,0},{3,1},{4,6},{5,7},{6,4},{7,5},{8,10},{9,11},{10,... | collective-permute-start | bytes 589832 | tf_op jit(solution)/shard_map/ppermute | solution.py:144
  44.0 18.0 %collective-permute-start.1 = (s16[256,768]{1,0:T(8,128)(2,1)S(1)}, s16[256,768]{1,0:T(8,128)(2,1)S(1)}, u32[]{:S(2)}, u32[]{:S(2)}) collective-permute-start(s16[256,768]{1,0:T(8,128)(2,1)S(1)} %get-tuple-element.61), channel_id=1, source_target_pairs={{0,16},{16,0},{1,17},{17,1},{2,18},{18,2},{3,19},{19,3},{4,20},{20... | collective-permute-start | bytes 1179656 | tf_op jit(solution)/shard_map/ppermute | solution.py:148
  45.8 16.3 %collective-permute-start.16 = (s16[128,768]{1,0:T(8,128)(2,1)S(1)}, s16[128,768]{1,0:T(8,128)(2,1)S(1)}, u32[]{:S(2)}, u32[]{:S(2)}) collective-permute-start(s16[128,768]{1,0:T(8,128)(2,1)S(1)} %shard_map.147), channel_id=1, source_target_pairs={{0,12},{4,8},{8,4},{12,0},{1,13},{5,9},{9,5},{13,1},{2,14},{6,10},... | collective-permute-start | bytes 589832 | tf_op jit(solution)/shard_map/ppermute | solution.py:152
  52.4 9.7 %collective-permute-start.17 = (s16[128,768]{1,0:T(8,128)(2,1)S(1)}, s16[128,768]{1,0:T(8,128)(2,1)S(1)}, u32[]{:S(2)}, u32[]{:S(2)}) collective-permute-start(s16[128,768]{1,0:T(8,128)(2,1)S(1)} %collective-permute-done.12.refs_6_), channel_id=1, source_target_pairs={{0,2},{1,3},{2,0},{3,1},{4,6},{5,7},{6,4},{7,5},{8,10},{9,11},{10,... | collective-permute-start | bytes 589832 | tf_op jit(solution)/shard_map/ppermute | solution.py:144
  53.9 1.9 %copy-start.5 = (s16[128,768]{1,0:T(8,128)(2,1)}, s16[128,768]{1,0:T(8,128)(2,1)S(1)}, u32[]{:S(2)}) copy-start(s16[128,768]{1,0:T(8,128)(2,1)S(1)} %collective-permute-done.14.refs_5_) | copy-start | bytes 589828
  54.9 7.1 %collective-permute-start.15 = (s16[128,768]{1,0:T(8,128)(2,1)S(1)}, s16[128,768]{1,0:T(8,128)(2,1)S(1)}, u32[]{:S(2)}, u32[]{:S(2)}) collective-permute-start(s16[128,768]{1,0:T(8,128)(2,1)S(1)} %get-tuple-element.77), channel_id=1, source_target_pairs={{0,2},{1,3},{2,0},{3,1},{4,6},{5,7},{6,4},{7,5},{8,10},{9,11},{10,... | collective-permute-start | bytes 589832 | tf_op jit(solution)/shard_map/ppermute | solution.py:144
  55.8 13.6 %collective-permute-start.19 = (s16[128,768]{1,0:T(8,128)(2,1)S(1)}, s16[128,768]{1,0:T(8,128)(2,1)S(1)}, u32[]{:S(2)}, u32[]{:S(2)}) collective-permute-start(s16[128,768]{1,0:T(8,128)(2,1)S(1)} %shard_map.149), channel_id=1, source_target_pairs={{0,8},{4,12},{8,0},{12,4},{1,9},{5,13},{9,1},{13,5},{2,10},{6,14},... | collective-permute-start | bytes 589832 | tf_op jit(solution)/shard_map/ppermute | solution.py:152
  62.0 4.0 %copy-start.7 = (s16[128,768]{1,0:T(8,128)(2,1)}, s16[128,768]{1,0:T(8,128)(2,1)S(1)}, u32[]{:S(2)}) copy-start(s16[128,768]{1,0:T(8,128)(2,1)S(1)} %collective-permute-done.17.refs_7_) | copy-start | bytes 589828
  62.3 9.4 %collective-permute-start.20 = (s16[128,768]{1,0:T(8,128)(2,1)S(1)}, s16[128,768]{1,0:T(8,128)(2,1)S(1)}, u32[]{:S(2)}, u32[]{:S(2)}) collective-permute-start(s16[128,768]{1,0:T(8,128)(2,1)S(1)} %shard_map.150), channel_id=1, source_target_pairs={{0,4},{4,0},{8,12},{12,8},{1,5},{5,1},{9,13},{13,9},{2,6},{6,2},{1... | collective-permute-start | bytes 589832 | tf_op jit(solution)/shard_map/ppermute | solution.py:152
  66.0 29.8 %copy-start = (f32[4,48,768]{2,1,0:T(8,128)S(1)}, f32[4,48,768]{2,1,0:T(8,128)}, u32[]{:S(2)}) copy-start(f32[4,48,768]{2,1,0:T(8,128)} %first.1) | copy-start | bytes 1769476
  66.0 29.8 %copy-start.1 = (f32[4,48,768]{2,1,0:T(8,128)S(1)}, f32[4,48,768]{2,1,0:T(8,128)}, u32[]{:S(2)}) copy-start(f32[4,48,768]{2,1,0:T(8,128)} %second.1) | copy-start | bytes 1769476
  66.0 5.7 %collective-permute-start.18 = (s16[128,768]{1,0:T(8,128)(2,1)S(1)}, s16[128,768]{1,0:T(8,128)(2,1)S(1)}, u32[]{:S(2)}, u32[]{:S(2)}) collective-permute-start(s16[128,768]{1,0:T(8,128)(2,1)S(1)} %get-tuple-element.82), channel_id=1, source_target_pairs={{0,2},{1,3},{2,0},{3,1},{4,6},{5,7},{6,4},{7,5},{8,10},{9,11},{10,... | collective-permute-start | bytes 589832 | tf_op jit(solution)/shard_map/ppermute | solution.py:144
  73.2 8.5 %collective-permute-start.22 = (s16[128,768]{1,0:T(8,128)(2,1)}, s16[128,768]{1,0:T(8,128)(2,1)S(1)}, u32[]{:S(2)}, u32[]{:S(2)}) collective-permute-start(s16[128,768]{1,0:T(8,128)(2,1)} %get-tuple-element.90), channel_id=1, source_target_pairs={{0,4},{4,0},{8,12},{12,8},{1,5},{5,1},{9,13},{13,9},{2,6},{6,2},{1... | collective-permute-start | bytes 589832 | tf_op jit(solution)/shard_map/ppermute | solution.py:152
  73.3 16.9 %collective-permute-start.24 = (s16[128,768]{1,0:T(8,128)(2,1)}, s16[128,768]{1,0:T(8,128)(2,1)S(1)}, u32[]{:S(2)}, u32[]{:S(2)}) collective-permute-start(s16[128,768]{1,0:T(8,128)(2,1)} %get-tuple-element.90), channel_id=1, source_target_pairs={{0,8},{4,12},{8,0},{12,4},{1,9},{5,13},{9,1},{13,5},{2,10},{6,14},... | collective-permute-start | bytes 589832 | tf_op jit(solution)/shard_map/ppermute | solution.py:152
  77.2 14.6 %collective-permute-start.26 = (s16[128,768]{1,0:T(8,128)(2,1)}, s16[128,768]{1,0:T(8,128)(2,1)S(1)}, u32[]{:S(2)}, u32[]{:S(2)}) collective-permute-start(s16[128,768]{1,0:T(8,128)(2,1)} %get-tuple-element.90), channel_id=1, source_target_pairs={{0,12},{4,8},{8,4},{12,0},{1,13},{5,9},{9,5},{13,1},{2,14},{6,10},... | collective-permute-start | bytes 589832 | tf_op jit(solution)/shard_map/ppermute | solution.py:152
  77.6 20.3 %collective-permute-start.21 = (s16[128,768]{1,0:T(8,128)(2,1)}, s16[128,768]{1,0:T(8,128)(2,1)S(1)}, u32[]{:S(2)}, u32[]{:S(2)}) collective-permute-start(s16[128,768]{1,0:T(8,128)(2,1)} %get-tuple-element.90), channel_id=1, source_target_pairs={{0,2},{1,3},{2,0},{3,1},{4,6},{5,7},{6,4},{7,5},{8,10},{9,11},{10,... | collective-permute-start | bytes 589832 | tf_op jit(solution)/shard_map/ppermute | solution.py:144
  81.8 16.1 %collective-permute-start.23 = (s16[128,768]{1,0:T(8,128)(2,1)S(1)}, s16[128,768]{1,0:T(8,128)(2,1)S(1)}, u32[]{:S(2)}, u32[]{:S(2)}) collective-permute-start(s16[128,768]{1,0:T(8,128)(2,1)S(1)} %collective-permute-done.22.refs_2_), channel_id=1, source_target_pairs={{0,2},{1,3},{2,0},{3,1},{4,6},{5,7},{6,4},{7,5},{8,10},{9,11},{10,... | collective-permute-start | bytes 589832 | tf_op jit(solution)/shard_map/ppermute | solution.py:144
  90.3 7.6 %collective-permute-start.25 = (s16[128,768]{1,0:T(8,128)(2,1)S(1)}, s16[128,768]{1,0:T(8,128)(2,1)S(1)}, u32[]{:S(2)}, u32[]{:S(2)}) collective-permute-start(s16[128,768]{1,0:T(8,128)(2,1)S(1)} %collective-permute-done.24.refs_4_), channel_id=1, source_target_pairs={{0,2},{1,3},{2,0},{3,1},{4,6},{5,7},{6,4},{7,5},{8,10},{9,11},{10,... | collective-permute-start | bytes 589832 | tf_op jit(solution)/shard_map/ppermute | solution.py:144
  91.8 6.3 %collective-permute-start.27 = (s16[128,768]{1,0:T(8,128)(2,1)S(1)}, s16[128,768]{1,0:T(8,128)(2,1)S(1)}, u32[]{:S(2)}, u32[]{:S(2)}) collective-permute-start(s16[128,768]{1,0:T(8,128)(2,1)S(1)} %collective-permute-done.26.refs_6_), channel_id=1, source_target_pairs={{0,2},{1,3},{2,0},{3,1},{4,6},{5,7},{6,4},{7,5},{8,10},{9,11},{10,... | collective-permute-start | bytes 589832 | tf_op jit(solution)/shard_map/ppermute | solution.py:144
  92.3 3.5 %collective-permute-start.28 = (f32[48,768]{1,0:T(8,128)S(1)}, f32[48,768]{1,0:T(8,128)S(1)}, u32[]{:S(2)}, u32[]{:S(2)}) collective-permute-start(f32[48,768]{1,0:T(8,128)S(1)} %constant_dynamic-slice_fusion), channel_id=1, source_target_pairs={{0,1},{1,0},{2,3},{3,2},{4,5},{5,4},{6,7},{7,6},{8,9},{9,8},{10,11... | collective-permute-start | bytes 442376 | tf_op jit(solution)/shard_map/ppermute | solution.py:140
  92.4 0.9 copy-start.6
  93.3 0.9 copy-start.8
  98.0 15.2 %copy-start.4 = (bf16[4,48,768]{2,1,0:T(8,128)(2,1)S(1)}, bf16[4,48,768]{2,1,0:T(8,128)(2,1)}, u32[]{:S(2)}) copy-start(bf16[4,48,768]{2,1,0:T(8,128)(2,1)} %weights.1) | copy-start | bytes 884740
  102.0 11.3 %collective-permute-start.29 = (f32[48,768]{1,0:T(8,128)S(1)}, f32[48,768]{1,0:T(8,128)S(1)}, u32[]{:S(2)}, u32[]{:S(2)}) collective-permute-start(f32[48,768]{1,0:T(8,128)S(1)} %get-tuple-element.102), channel_id=1, source_target_pairs={{0,1},{1,0},{2,3},{3,2},{4,5},{5,4},{6,7},{7,6},{8,9},{9,8},{10,11... | collective-permute-start | bytes 442376 | tf_op jit(solution)/shard_map/ppermute | solution.py:140
  113.3 5.5 %copy-start.2 = (f32[4,48,768]{2,1,0:T(8,128)S(1)}, f32[4,48,768]{2,1,0:T(8,128)}, u32[]{:S(2)}) copy-start(f32[4,48,768]{2,1,0:T(8,128)} %left.5) | copy-start | bytes 1769476
  113.3 5.5 %copy-start.3 = (f32[4,48,768]{2,1,0:T(8,128)S(1)}, f32[4,48,768]{2,1,0:T(8,128)}, u32[]{:S(2)}) copy-start(f32[4,48,768]{2,1,0:T(8,128)} %right.5) | copy-start | bytes 1769476
  117.1 1.6 %collective-permute-start.30 = (f32[2,48,768]{2,1,0:T(8,128)S(1)}, f32[2,48,768]{2,1,0:T(8,128)S(1)}, u32[]{:S(2)}, u32[]{:S(2)}) collective-permute-start(f32[2,48,768]{2,1,0:T(8,128)S(1)} %get-tuple-element.108), channel_id=1, source_target_pairs={{0,1},{1,0},{2,3},{3,2},{4,5},{5,4},{6,7},{7,6},{8,9},{9,8},{10,11... | collective-permute-start | bytes 884744 | tf_op jit(solution)/shard_map/ppermute | solution.py:140
  117.2 6.3 %collective-permute-start.31 = (bf16[2,48,768]{2,1,0:T(8,128)(2,1)S(1)}, bf16[2,48,768]{2,1,0:T(8,128)(2,1)S(1)}, u32[]{:S(2)}, u32[]{:S(2)}) collective-permute-start(bf16[2,48,768]{2,1,0:T(8,128)(2,1)S(1)} %shard_map.155.near), channel_id=1, source_target_pairs={{0,16},{16,0},{1,17},{17,1},{2,18},{18,2},{3,19},{19,3},{4,20},{20... | collective-permute-start | bytes 442376 | tf_op jit(solution)/shard_map/ppermute | solution.py:148

commit v4 on v3

--- a/solution.py
+++ b/solution.py
@@ -215,6 +215,9 @@
     return place, block
 
 
+ORDER = (2, 3, 1, 0)
+
+
 SMEM_SPEC = pl.BlockSpec(memory_space=pltpu.SMEM)
 VMEM_SPEC = pl.BlockSpec(memory_space=pltpu.VMEM)
 HBM_SPEC = pl.BlockSpec(memory_space=pltpu.HBM)
@@ -222,7 +225,7 @@
 
 def work(micros):
     return pl.CostEstimate(
-        flops=int(micros * 10**6), transcendentals=0, bytes_accessed=int(micros * 3.6 * 10**6)
+        flops=int(micros * 10**9), transcendentals=0, bytes_accessed=int(micros * 36 * 10**6)
     )
 
 
@@ -254,18 +257,12 @@
     return [(source.at[block, part], target.at[part]) for part in rows]
 
 
-def pick_far_kernel(meta, xin, dout, left, right, out, roots, sems):
+def pick_kernel(meta, xin, dout, left, right, far, mine, roots, sems):
     _, block = used_slot(meta, 1 - meta[8], 1 - meta[11])
-    place, _ = used_slot(meta, meta[8], 1 - meta[11])
-    pairs = in_parts(xin, block, out.at[0]) + in_parts(dout, block, out.at[1])
+    pairs = in_parts(xin, block, far.at[0]) + in_parts(dout, block, far.at[1])
+    place, block = used_slot(meta, meta[8], 1 - meta[11])
     pairs += [(left.at[place], roots.at[0]), (right.at[place], roots.at[1])]
-    for copy in start_copies(pairs, sems):
-        copy.wait()
-
-
-def pick_mine_kernel(meta, xin, dout, out, sems):
-    _, block = used_slot(meta, meta[8], 1 - meta[11])
-    pairs = in_parts(xin, block, out.at[0]) + in_parts(dout, block, out.at[1])
+    pairs += in_parts(xin, block, mine.at[0]) + in_parts(dout, block, mine.at[1])
     for copy in start_copies(pairs, sems):
         copy.wait()
 
@@ -289,7 +286,7 @@
     outs, total = refs[:4], refs[4]
     total[...] = own_ref[...] + token_dot(got[0], got[1])
     span = total.shape[0] // 4
-    for out, bits in zip(outs, (3, 2, 1, 0)):
+    for out, bits in zip(outs, ORDER):
         first = pl.multiple_of((meta[9] ^ bits) * span, 64)
         out[...] = encode(total[pl.ds(first, span), :])
 
@@ -348,13 +345,16 @@
     )(meta, got, mine)
 
 
-def x_kernel(got, keep, coded):
-    coded[...] = encode(decode(got[...]) + keep[...])
-
-
-def grad_kernel(factor, got, keep, one, two, three, grad, coded):
-    total = decode(got[...]) + keep[...]
-    for part in (one, two, three):
+def x_kernel(keep, *refs):
+    total = keep[...]
+    for part in refs[:-1]:
+        total = total + decode(part[...])
+    refs[-1][...] = encode(total)
+
+
+def grad_kernel(factor, keep, got, far, near, grad, coded):
+    total = keep[...]
+    for part in (got, far, near):
         total = total + decode(part[...])
     total = total * factor
     grad[...] = total
@@ -399,27 +399,30 @@
     sums[...] = jnp.where(lane == 2, jnp.sum(direction * direction), adam_ref[...])
 
 
-def gram_kernel(meta, grad_ref, high_ref, low_ref, own_left, own_right, sib_out, whole):
-    rows, size = grad_ref.shape
-    half = rows // 2
-    own = pl.ds(pl.multiple_of(meta[11] * half, 16), half)
-    sib = pl.ds(pl.multiple_of((1 - meta[11]) * half, 16), half)
-    first = (2 * meta[9] + meta[10]) * rows
+def left_kernel(meta, grad_ref, high_ref, low_ref, own_out, sib_out, whole):
+    half = own_out.shape[0]
     high, low = high_ref[...], low_ref[...]
     own_high, own_low = halves(grad_ref[...])
     whole[...] = row_dot_t(own_high, high) + (
         row_dot_t(own_low, high) + row_dot_t(own_high, low)
     )
-    own_left[...] = whole[own, :]
-    sib_out[0] = whole[sib, :]
+    own_out[...] = whole[pl.ds(pl.multiple_of(meta[11] * half, 16), half), :]
+    sib_out[...] = whole[pl.ds(pl.multiple_of((1 - meta[11]) * half, 16), half), :]
+
+
+def right_kernel(meta, high_ref, low_ref, own_out, sib_out, whole):
+    half, size = own_out.shape
+    rows = 2 * half
+    first = (2 * meta[9] + meta[10]) * rows
+    high, low = high_ref[...], low_ref[...]
     row_ids = lax.broadcasted_iota(jnp.int32, (rows, size), 0) + first
     col_ids = lax.broadcasted_iota(jnp.int32, (rows, size), 1)
     pick = jnp.where(row_ids == col_ids, 1.0, 0.0).astype(BF16)
     col_high = row_dot_t(pick, high).astype(BF16)
     col_low = row_dot_t(pick, low).astype(BF16)
     whole[...] = row_dot(col_high, high) + (row_dot(col_low, high) + row_dot(col_high, low))
-    own_right[...] = whole[own, :]
-    sib_out[1] = whole[sib, :]
+    own_out[...] = whole[pl.ds(pl.multiple_of(meta[11] * half, 16), half), :]
+    sib_out[...] = whole[pl.ds(pl.multiple_of((1 - meta[11]) * half, 16), half), :]
 
 
 def moment_kernel(meta, grad, got, first, second, first_out, second_out, adam_out):
@@ -456,17 +459,11 @@
         out[slot] = (weights[block].astype(F32) - 0.05 * graft * value).astype(BF16)
 
 
-def stat_kernel(meta, own_left, own_right, got, left, right, left_out, right_out):
-    plane, core = meta[8], meta[11]
-    left_out[...] = left[...]
-    right_out[...] = right[...]
-    for slot, left_gram, right_gram in (
-        (core, own_left[...], own_right[...]),
-        (1 - core, got[0], got[1]),
-    ):
-        place, _ = used_slot(meta, plane, slot)
-        left_out[place] = 0.5 * left[place] + 0.5 * left_gram
-        right_out[place] = 0.5 * right[place] + 0.5 * right_gram
+def stat_kernel(meta, own, got, stat, out):
+    out[...] = stat[...]
+    for slot, gram in ((meta[11], own), (1 - meta[11], got)):
+        place, _ = used_slot(meta, meta[8], slot)
+        out[place] = 0.5 * stat[place] + 0.5 * gram[...]
 
 
 def place_kernel(meta, near, mirror, out):
@@ -519,15 +516,16 @@
         pltpu.with_memory_space_constraint(value, pltpu.HBM)
         for value in (xin, dout, left_root, right_root)
     )
-    far_in, roots = call(
-        pick_far_kernel,
-        [tokens_in, shape(2, rows, size)],
+    far_in, mine_in, roots = call(
+        pick_kernel,
+        [tokens_in, tokens_in, shape(2, rows, size)],
         [SMEM_SPEC] + [HBM_SPEC] * 4,
         (meta, xin, dout, left_root, right_root),
-        [dmas(10)],
+        [dmas(18)],
     )
     roots = to_core(roots)
     far_in = to_core(far_in)
+    mine_in = to_core(mine_in)
     def own_part(across, meta):
         return call(
             functools.partial(own_kernel, across),
@@ -546,7 +544,7 @@
         (meta, far_in, own_far),
         [pltpu.VMEM((size, size), F32)],
     ))
-    coded[0], later, roots = lax.optimization_barrier((coded[0], meta, roots))
+    coded[0], roots = lax.optimization_barrier((coded[0], roots))
     got_y = [to_y(value) for value in coded]
     left_rows, right_coded = call(
         rows_kernel,
@@ -555,69 +553,71 @@
         (meta, left_root, right_root, roots),
         [pltpu.VMEM((2 * rows, size), F32), dmas(2)],
     )
-    root_z = [to_z(right_coded, bits) for bits in (1, 2, 3)]
-    root_x = [to_x(right_coded)]
-    (mine_in,) = call(
-        pick_mine_kernel,
-        [tokens_in],
-        [SMEM_SPEC] + [HBM_SPEC] * 2,
-        (later, xin, dout),
-        [dmas(8)],
-        2.1,
-    )
-    mine_in = to_core(mine_in)
-    own_mine = own_part(False, later)
+    own_mine = own_part(False, meta)
+    root_z = {3: to_z(right_coded, 3), 1: to_z(right_coded, 1)}
+    mine_in, sent = lax.optimization_barrier((mine_in, right_coded))
+    root_x = {0: to_x(sent)}
+    sent, root_z[1] = lax.optimization_barrier((root_z[3], root_z[1]))
+    root_z[2] = to_z(sent, 1)
+    sent, root_x[0] = lax.optimization_barrier((root_z[1], root_x[0]))
+    root_x[1] = to_x(sent)
+
     (mine,) = call(
         mine_kernel,
         [shape(size, size)],
         [VMEM_SPEC] * 2,
         (mine_in, own_mine),
     )
-    order = (3, 2, 1, 0)
     got_x, keeps, got_z = [], [], []
-    for index, bits in enumerate(order):
+    for index, bits in enumerate(ORDER):
         arrived = got_y[index]
-        if index == 0:
-            arrived, root_x[0], root_z[0] = lax.optimization_barrier(
-                (arrived, root_x[0], root_z[0])
+        if index == 1:
+            arrived, got_x[0], root_x[0], root_z[3] = lax.optimization_barrier(
+                (arrived, got_x[0], root_x[0], root_z[3])
             )
-            root_x.append(to_x(root_z[0]))
-        if index == 1:
-            arrived, got_x[0], root_x[1], *root_z[1:] = lax.optimization_barrier(
-                (arrived, got_x[0], root_x[1], *root_z[1:])
-            )
-            root_x += [to_x(root_z[1]), to_x(root_z[2])]
+            root_x[3] = to_x(root_z[3])
         if index == 2:
-            arrived, got_x[1], root_x[2] = lax.optimization_barrier(
-                (arrived, got_x[1], root_x[2])
+            arrived, got_x[1], root_x[1], root_z[2] = lax.optimization_barrier(
+                (arrived, got_x[1], root_x[1], root_z[2])
             )
         if index == 3:
-            arrived, got_x[2], got_z[0], root_x[3] = lax.optimization_barrier(
-                (arrived, got_x[2], got_z[0], root_x[3])
+            arrived, got_x[2], root_x[3] = lax.optimization_barrier(
+                (arrived, got_x[2], root_x[3])
             )
         sent, keep = after_y(meta, arrived, mine, bits)
         got_x.append(to_x(sent))
         keeps.append(keep)
         if index:
+            carried = got_z if index == 2 else []
             (sent,) = call(
-                x_kernel, [piece], [VMEM_SPEC] * 2, (got_x[index - 1], keeps[index - 1])
+                x_kernel,
+                [piece],
+                [VMEM_SPEC] * (2 + len(carried)),
+                (keeps[index - 1], got_x[index - 1], *carried),
             )
-            got_z.append(to_z(sent, order[index - 1]))
+            got_z.append(to_z(sent, (1, 3, 1)[index - 1]))
     grad, coded = call(
         functools.partial(grad_kernel, factor),
         [shape(2 * rows, size), piece],
-        [VMEM_SPEC] * 5,
-        (got_x[3], keeps[3], *got_z),
-    )
-
-    column = [coded] + [to_z(coded, bits) for bits in (1, 2, 3)]
-    pieces = []
-    for part in column:
-        pieces += [part, to_x(part)]
-
-    root_pieces = [right_coded, root_x[0]]
-    for near, across in zip(root_z, root_x[1:]):
-        root_pieces += [near, across]
+        [VMEM_SPEC] * 4,
+        (keeps[3], got_x[3], got_z[1], got_z[2]),
+    )
+
+    across = {0: to_x(coded)}
+    column = {bits: to_z(coded, bits) for bits in (1, 2, 3)}
+    coded, sent = lax.optimization_barrier((coded, root_z[2]))
+    root_x[2] = to_x(sent)
+    column[1], across[0] = lax.optimization_barrier((column[1], across[0]))
+    for bits in (1, 2, 3):
+        across[bits] = to_x(column[bits])
+    pieces = [across[0]]
+    for bits in (1, 2, 3):
+        pieces += [column[bits], across[bits]]
+
+    root_z[0] = right_coded
+    root_pieces = []
+    for index in range(4):
+        root_pieces += [root_z[index], root_x[index]]
     root_high, root_low = call(
         root_kernel,
         [shape(size, size, dtype=BF16)] * 2,
@@ -638,7 +638,7 @@
         direction_kernel,
         [tile, tile, shape(1, 128)] + [shape(size, size, dtype=BF16)] * 2,
         [SMEM_SPEC] + [VMEM_SPEC] * 12,
-        (meta, grad, *pieces[1:], left_rows, root_high, root_low, adam),
+        (meta, grad, *pieces, left_rows, root_high, root_low, adam),
         [pltpu.VMEM((2 * rows, size), F32)],
     )
     sib_dir = to_core(sib_dir)
@@ -652,27 +652,39 @@
     )
     mirror = to_y(near)
     high, near = lax.optimization_barrier((high, near))
-    own_left, own_right, sib_out = call(
-        gram_kernel,
-        [tile, tile, shape(2, rows, size)],
+    whole = [pltpu.VMEM((2 * rows, size), F32)]
+    own_right, sib_right = call(
+        right_kernel,
+        [tile, tile],
+        [SMEM_SPEC] + [VMEM_SPEC] * 2,
+        (meta, high, low),
+        whole,
+        1.8,
+    )
+    got_right = to_core(sib_right)
+    own_left, sib_left = call(
+        left_kernel,
+        [tile, tile],
         [SMEM_SPEC] + [VMEM_SPEC] * 3,
         (meta, grad, high, low),
-        [pltpu.VMEM((2 * rows, size), F32)],
-        3.1,
-    )
-    new_left, new_right = call(
-        stat_kernel,
-        [stack, stack],
-        [SMEM_SPEC] + [VMEM_SPEC] * 5,
-        (meta, own_left, own_right, to_core(sib_out), left_stat, right_stat),
-    )
-    new_left, mirror = lax.optimization_barrier((new_left, mirror))
+        whole,
+        1.4,
+    )
+    got_left = to_core(sib_left)
     (new_weights,) = call(
         place_kernel,
         [shape(block_count, rows, size, dtype=BF16)],
         [SMEM_SPEC] + [VMEM_SPEC] * 2,
         (meta, near, mirror),
     )
+
+    def update(own, got, stat):
+        return call(
+            stat_kernel, [stack], [SMEM_SPEC] + [VMEM_SPEC] * 3, (meta, own, got, stat), (), 1.0
+        )[0]
+
+    new_right = update(own_right, got_right, right_stat)
+    new_left = update(own_left, got_left, left_stat)
     return new_weights, new_left, new_right, new_first, new_second
 
 

time: 125 us -> 114 us (0.912)
  starting transfers between devices: 45.5 us -> 34.9 us
  local copies, waits for them, and re-layouts: 2.63 us -> 0.77 us
    ppermute x9, starting transfers between devices: 21.3 us -> 15.4 us  [to_z(): return lax.ppermute(value, 'tensor', [(i, i ^ bits) for i in range(4)])]
    ppermute x12, starting transfers between devices: 16.8 us -> 11.9 us  [to_x(): return lax.ppermute(value, 'section', [(i, i ^ 2) for i in range(4)])]
    ppermute x9, waiting for transfers between devices: 16.9 us -> 20.9 us  [to_z(): return lax.ppermute(value, 'tensor', [(i, i ^ bits) for i in range(4)])]
    ppermute x5, waiting for transfers between devices: 7.12 us -> 4.91 us  [to_y(): return lax.ppermute(value, 'shard', [(0, 1), (1, 0)])]
    unnamed x18 -> x10, local copies, waits for them, and re-layouts: 1.88 us -> 0.02 us
    pallas_call x18 -> x19, Pallas kernels: 31.9 us -> 31.5 us  [call(): pl.pallas_call(body, out_shape=outs, in_specs=ins, out_specs=[VMEM_SPEC]...]
  transfers between devices with their start and end apart: 32 -> 33, of which waited for: 11 -> 11; matrix products, arithmetic and copies ran while one was open for 0% -> 0% of each run, Pallas kernels for 17% -> 23%
where the time goes in v4:
time: 114 us; the launch traced here: 113 us
  Pallas kernels  35.8 us (31%)
  starting transfers between devices  34.9 us (31%)
  waiting for transfers between devices  29.9 us (26%)
  blocking collectives  11.1 us (10%)
    pallas_call x19, Pallas kernels, call(): pl.pallas_call(body, out_shape=outs, in_specs=ins, out_specs=[VMEM_SPEC]...  31.5 us
    ppermute x9, waiting for transfers between devices, to_z(): return lax.ppermute(value, 'tensor', [(i, i ^ bits) for i in range(4)])  20.9 us
    ppermute x9, starting transfers between devices, to_z(): return lax.ppermute(value, 'tensor', [(i, i ^ bits) for i in range(4)])  15.4 us
    ppermute x12, starting transfers between devices, to_x(): return lax.ppermute(value, 'section', [(i, i ^ 2) for i in range(4)])  11.9 us
    all_to_all x1, blocking collectives, two_planes(): sums = lax.all_to_all(sums, GROUP, 0, 0)  11.1 us
    ppermute x5, starting transfers between devices, to_y(): return lax.ppermute(value, 'shard', [(0, 1), (1, 0)])  5.82 us
    ppermute x5, waiting for transfers between devices, to_y(): return lax.ppermute(value, 'shard', [(0, 1), (1, 0)])  4.91 us
    pallas_call x4, Pallas kernels, after_y(): pl.pallas_call(y_kernel, out_shape=[jax.ShapeDtypeStruct((coded_rows(rows...  4.25 us
  transfers between devices with their start and end apart: 33, of which 11 were waited for; matrix products, arithmetic and copies ran while one was open for 0% of the time, Pallas kernels for 23%

profile of v4, /device:TPU:0, one launch (start us, length us, event | category | flops | bytes accessed | tf_op | source)
XLA Modules:
  0.0 113.4 jit_solution(17605773639273352504)
XLA Ops:
  0.7 0.7 concatenate.3.meta
  1.4 2.7 %shard_map.137 = (bf16[2,512,768]{2,1,0:T(8,128)(2,1)S(1)}, bf16[2,512,768]{2,1,0:T(8,128)(2,1)S(1)}, f32[2,48,768]{2,1,0:T(8,128)S(1)}) custom-call(s32[12]{0:T(128)S(1)} %concatenate.3.meta, bf16[4,512,768]{2,1,0:T(8,128)(2,1)} %xin.5, bf16[4,512,768]{2,1,0:T(8,128)(2,1)} %dout.5, f32[4,48,768]{2,1,0:T(8,128)} %left.3, f32[4,48,768]{2,1,0:T(8,128)} %right.3), custom_call_target="tpu_custom_call" | custom-call | flops 1000000000 | bytes 36000000 | tf_op jit(solution)/shard_map/pallas_call | solution.py:233
  4.1 0.5 collective-permute-start
  4.7 0.4 collective-permute-start.4
  5.2 3.1 %shard_map.138.own_ref = f32[768,768]{1,0:T(8,128)S(1)} custom-call(s32[12]{0:T(128)S(1)} %concatenate.3.meta, bf16[4,512,768]{2,1,0:T(8,128)(2,1)} %xin.5, bf16[4,512,768]{2,1,0:T(8,128)(2,1)} %dout.5), custom_call_target="tpu_custom_call" | custom-call | flops 1000000000 | bytes 36000000 | tf_op jit(solution)/shard_map/pallas_call | solution.py:233
  8.2 2.5 %shard_map.139 = (s16[256,768]{1,0:T(8,128)(2,1)S(1)}, s16[256,768]{1,0:T(8,128)(2,1)S(1)}, s16[256,768]{1,0:T(8,128)(2,1)S(1)}, s16[256,768]{1,0:T(8,128)(2,1)S(1)}) custom-call(s32[12]{0:T(128)S(1)} %concatenate.3.meta, bf16[2,512,768]{2,1,0:T(8,128)(2,1)S(1)} %collective-permute-done.got, f32[768,768]{1,0:T(8,128)S(1)} %shard_map.138.own_ref), custom_call_target="tpu_custom_call" | custom-call | flops 1000000000 | bytes 36000000 | tf_op jit(solution)/shard_map/pallas_call | solution.py:233
  10.7 2.7 %collective-permute-start.5 = (s16[256,768]{1,0:T(8,128)(2,1)S(1)}, s16[256,768]{1,0:T(8,128)(2,1)S(1)}, u32[]{:S(2)}, u32[]{:S(2)}) collective-permute-start(s16[256,768]{1,0:T(8,128)(2,1)S(1)} %get-tuple-element.68), channel_id=1, source_target_pairs={{0,16},{16,0},{1,17},{17,1},{2,18},{18,2},{3,19},{19,3},{4,20},{20... | collective-permute-start | bytes 1179656 | tf_op jit(solution)/shard_map/ppermute | solution.py:148
  13.4 3.0 %shard_map.141.own_ref = f32[768,768]{1,0:T(8,128)S(1)} custom-call(s32[12]{0:T(128)S(1)} %concatenate.3.meta, bf16[4,512,768]{2,1,0:T(8,128)(2,1)} %xin.5, bf16[4,512,768]{2,1,0:T(8,128)(2,1)} %dout.5), custom_call_target="tpu_custom_call" | custom-call | flops 1000000000 | bytes 36000000 | tf_op jit(solution)/shard_map/pallas_call | solution.py:233
  16.4 1.7 %shard_map.140 = (f32[96,768]{1,0:T(8,128)S(1)}, s16[128,768]{1,0:T(8,128)(2,1)S(1)}) custom-call(s32[12]{0:T(128)S(1)} %concatenate.3.meta, f32[4,48,768]{2,1,0:T(8,128)} %left.3, f32[4,48,768]{2,1,0:T(8,128)} %right.3, f32[2,48,768]{2,1,0:T(8,128)S(1)} %collective-permute-done.4.got), custom_call_target="tpu_custom_call" | custom-call | flops 1000000000 | bytes 36000000 | tf_op jit(solution)/shard_map/pallas_call | solution.py:233
  18.1 3.7 %collective-permute-start.8 = (s16[128,768]{1,0:T(8,128)(2,1)S(1)}, s16[128,768]{1,0:T(8,128)(2,1)S(1)}, u32[]{:S(2)}, u32[]{:S(2)}) collective-permute-start(s16[128,768]{1,0:T(8,128)(2,1)S(1)} %get-tuple-element.75.refs_0_), channel_id=1, source_target_pairs={{0,12},{4,8},{8,4},{12,0},{1,13},{5,9},{9,5},{13,1},{2,14},{6,10},... | collective-permute-start | bytes 589832 | tf_op jit(solution)/shard_map/ppermute | solution.py:152
  21.8 0.5 collective-permute-start.3
  22.3 1.5 %collective-permute-start.10 = (s16[128,768]{1,0:T(8,128)(2,1)S(1)}, s16[128,768]{1,0:T(8,128)(2,1)S(1)}, u32[]{:S(2)}, u32[]{:S(2)}) collective-permute-start(s16[128,768]{1,0:T(8,128)(2,1)S(1)} %get-tuple-element.75.refs_0_), channel_id=1, source_target_pairs={{0,2},{1,3},{2,0},{3,1},{4,6},{5,7},{6,4},{7,5},{8,10},{9,11},{10,... | collective-permute-start | bytes 589832 | tf_op jit(solution)/shard_map/ppermute | solution.py:144
  23.8 0.8 shard_map.142.mine
  24.7 1.1 shard_map.143
  25.7 0.6 collective-permute-start.7
  26.3 1.5 %collective-permute-done.8.refs_6_ = s16[128,768]{1,0:T(8,128)(2,1)S(1)} collective-permute-done((s16[128,768]{1,0:T(8,128)(2,1)S(1)}, s16[128,768]{1,0:T(8,128)(2,1)S(1)}, u32[]{:S(2)}, u32[]{:S(2)}) %collective-permute-start.8) | collective-permute-done | bytes 196640 | tf_op jit(solution)/shard_map/ppermute | solution.py:152
  27.8 0.3 collective-permute-start.2
  28.1 3.3 %collective-permute-done.9.refs_2_ = s16[128,768]{1,0:T(8,128)(2,1)S(1)} collective-permute-done((s16[128,768]{1,0:T(8,128)(2,1)S(1)}, s16[128,768]{1,0:T(8,128)(2,1)S(1)}, u32[]{:S(2)}, u32[]{:S(2)}) %collective-permute-start.9) | collective-permute-done | bytes 196640 | tf_op jit(solution)/shard_map/ppermute | solution.py:152
  31.4 1.5 %collective-permute-start.12 = (s16[128,768]{1,0:T(8,128)(2,1)S(1)}, s16[128,768]{1,0:T(8,128)(2,1)S(1)}, u32[]{:S(2)}, u32[]{:S(2)}) collective-permute-start(s16[128,768]{1,0:T(8,128)(2,1)S(1)} %collective-permute-done.9.refs_2_), channel_id=1, source_target_pairs={{0,2},{1,3},{2,0},{3,1},{4,6},{5,7},{6,4},{7,5},{8,10},{9,11},{10,... | collective-permute-start | bytes 589832 | tf_op jit(solution)/shard_map/ppermute | solution.py:144
  32.9 1.7 %collective-permute-start.13 = (s16[128,768]{1,0:T(8,128)(2,1)S(1)}, s16[128,768]{1,0:T(8,128)(2,1)S(1)}, u32[]{:S(2)}, u32[]{:S(2)}) collective-permute-start(s16[128,768]{1,0:T(8,128)(2,1)S(1)} %collective-permute-done.8.refs_6_), channel_id=1, source_target_pairs={{0,4},{4,0},{8,12},{12,8},{1,5},{5,1},{9,13},{13,9},{2,6},{6,2},{1... | collective-permute-start | bytes 589832 | tf_op jit(solution)/shard_map/ppermute | solution.py:152
  34.6 1.1 shard_map.144
  35.6 0.8 collective-permute-start.11
  36.4 0.7 collective-permute-start.1
  37.1 0.2 shard_map.147
  37.3 4.9 %collective-permute-done.2.got = s16[256,768]{1,0:T(8,128)(2,1)S(1)} collective-permute-done((s16[256,768]{1,0:T(8,128)(2,1)S(1)}, s16[256,768]{1,0:T(8,128)(2,1)S(1)}, u32[]{:S(2)}, u32[]{:S(2)}) %collective-permute-start.2) | collective-permute-done | bytes 393248 | tf_op jit(solution)/shard_map/ppermute | solution.py:148
  42.2 1.5 %collective-permute-start.15 = (s16[128,768]{1,0:T(8,128)(2,1)S(1)}, s16[128,768]{1,0:T(8,128)(2,1)S(1)}, u32[]{:S(2)}, u32[]{:S(2)}) collective-permute-start(s16[128,768]{1,0:T(8,128)(2,1)S(1)} %collective-permute-done.8.refs_6_), channel_id=1, source_target_pairs={{0,2},{1,3},{2,0},{3,1},{4,6},{5,7},{6,4},{7,5},{8,10},{9,11},{10,... | collective-permute-start | bytes 589832 | tf_op jit(solution)/shard_map/ppermute | solution.py:144
  43.7 2.1 %collective-permute-start.17 = (s16[128,768]{1,0:T(8,128)(2,1)S(1)}, s16[128,768]{1,0:T(8,128)(2,1)S(1)}, u32[]{:S(2)}, u32[]{:S(2)}) collective-permute-start(s16[128,768]{1,0:T(8,128)(2,1)S(1)} %shard_map.147), channel_id=1, source_target_pairs={{0,4},{4,0},{8,12},{12,8},{1,5},{5,1},{9,13},{13,9},{2,6},{6,2},{1... | collective-permute-start | bytes 589832 | tf_op jit(solution)/shard_map/ppermute | solution.py:152
  45.8 1.1 shard_map.145
  46.9 0.6 collective-permute-start.14
  47.5 2.0 %collective-permute-done.17.refs_1_ = s16[128,768]{1,0:T(8,128)(2,1)S(1)} collective-permute-done((s16[128,768]{1,0:T(8,128)(2,1)S(1)}, s16[128,768]{1,0:T(8,128)(2,1)S(1)}, u32[]{:S(2)}, u32[]{:S(2)}) %collective-permute-start.17) | collective-permute-done | bytes 196640 | tf_op jit(solution)/shard_map/ppermute | solution.py:152
  49.4 0.4 shard_map.148
  49.9 2.1 %collective-permute-start.18 = (s16[128,768]{1,0:T(8,128)(2,1)S(1)}, s16[128,768]{1,0:T(8,128)(2,1)S(1)}, u32[]{:S(2)}, u32[]{:S(2)}) collective-permute-start(s16[128,768]{1,0:T(8,128)(2,1)S(1)} %shard_map.148), channel_id=1, source_target_pairs={{0,12},{4,8},{8,4},{12,0},{1,13},{5,9},{9,5},{13,1},{2,14},{6,10},... | collective-permute-start | bytes 589832 | tf_op jit(solution)/shard_map/ppermute | solution.py:152
  52.0 0.6 collective-permute-done.14.refs_0_
  52.6 1.1 shard_map.146
  53.7 0.6 collective-permute-start.16
  54.3 0.2 shard_map.149
  54.5 1.0 collective-permute-start.19
  55.6 2.6 %collective-permute-done.18.far = s16[128,768]{1,0:T(8,128)(2,1)S(1)} collective-permute-done((s16[128,768]{1,0:T(8,128)(2,1)S(1)}, s16[128,768]{1,0:T(8,128)(2,1)S(1)}, u32[]{:S(2)}, u32[]{:S(2)}) %collective-permute-start.18) | collective-permute-done | bytes 196640 | tf_op jit(solution)/shard_map/ppermute | solution.py:152
  58.2 1.2 %collective-permute-done.16.got = s16[128,768]{1,0:T(8,128)(2,1)S(1)} collective-permute-done((s16[128,768]{1,0:T(8,128)(2,1)S(1)}, s16[128,768]{1,0:T(8,128)(2,1)S(1)}, u32[]{:S(2)}, u32[]{:S(2)}) %collective-permute-start.16) | collective-permute-done | bytes 196640 | tf_op jit(solution)/shard_map/ppermute | solution.py:144
  59.4 1.4 %collective-permute-done.19.near = s16[128,768]{1,0:T(8,128)(2,1)S(1)} collective-permute-done((s16[128,768]{1,0:T(8,128)(2,1)S(1)}, s16[128,768]{1,0:T(8,128)(2,1)S(1)}, u32[]{:S(2)}, u32[]{:S(2)}) %collective-permute-start.19) | collective-permute-done | bytes 196640 | tf_op jit(solution)/shard_map/ppermute | solution.py:152
  60.8 0.6 shard_map.150
  61.4 0.9 collective-permute-start.20
  62.3 0.7 collective-permute-start.21
  63.0 2.8 %collective-permute-start.23 = (s16[128,768]{1,0:T(8,128)(2,1)S(1)}, s16[128,768]{1,0:T(8,128)(2,1)S(1)}, u32[]{:S(2)}, u32[]{:S(2)}) collective-permute-start(s16[128,768]{1,0:T(8,128)(2,1)S(1)} %get-tuple-element.94), channel_id=1, source_target_pairs={{0,8},{4,12},{8,0},{12,4},{1,9},{5,13},{9,1},{13,5},{2,10},{6,14},... | collective-permute-start | bytes 589832 | tf_op jit(solution)/shard_map/ppermute | solution.py:152
  65.8 1.2 %collective-permute-start.25 = (s16[128,768]{1,0:T(8,128)(2,1)S(1)}, s16[128,768]{1,0:T(8,128)(2,1)S(1)}, u32[]{:S(2)}, u32[]{:S(2)}) collective-permute-start(s16[128,768]{1,0:T(8,128)(2,1)S(1)} %get-tuple-element.94), channel_id=1, source_target_pairs={{0,12},{4,8},{8,4},{12,0},{1,13},{5,9},{9,5},{13,1},{2,14},{6,10},... | collective-permute-start | bytes 589832 | tf_op jit(solution)/shard_map/ppermute | solution.py:152
  67.1 2.1 %collective-permute-done.20.refs_2_ = s16[128,768]{1,0:T(8,128)(2,1)S(1)} collective-permute-done((s16[128,768]{1,0:T(8,128)(2,1)S(1)}, s16[128,768]{1,0:T(8,128)(2,1)S(1)}, u32[]{:S(2)}, u32[]{:S(2)}) %collective-permute-start.20) | collective-permute-done | bytes 196640 | tf_op jit(solution)/shard_map/ppermute | solution.py:152
  69.3 1.5 %collective-permute-start.27 = (s16[128,768]{1,0:T(8,128)(2,1)S(1)}, s16[128,768]{1,0:T(8,128)(2,1)S(1)}, u32[]{:S(2)}, u32[]{:S(2)}) collective-permute-start(s16[128,768]{1,0:T(8,128)(2,1)S(1)} %collective-permute-done.13.refs_4_), channel_id=1, source_target_pairs={{0,2},{1,3},{2,0},{3,1},{4,6},{5,7},{6,4},{7,5},{8,10},{9,11},{10,... | collective-permute-start | bytes 589832 | tf_op jit(solution)/shard_map/ppermute | solution.py:144
  70.8 0.5 collective-permute-start.22
  71.3 8.1 %collective-permute-done.23.refs_4_ = s16[128,768]{1,0:T(8,128)(2,1)S(1)} collective-permute-done((s16[128,768]{1,0:T(8,128)(2,1)S(1)}, s16[128,768]{1,0:T(8,128)(2,1)S(1)}, u32[]{:S(2)}, u32[]{:S(2)}) %collective-permute-start.23) | collective-permute-done | bytes 196640 | tf_op jit(solution)/shard_map/ppermute | solution.py:152
  79.4 1.1 collective-permute-start.24
  80.5 1.0 collective-permute-start.26
  81.4 1.9 %shard_map.152 = (f32[4,48,768]{2,1,0:T(8,128)}, f32[4,48,768]{2,1,0:T(8,128)}, f32[1,128]{1,0:T(1,128)S(1)}) custom-call(s32[12]{0:T(128)S(1)} %concatenate.3.meta, f32[96,768]{1,0:T(8,128)S(1)} %get-tuple-element.93.grad.refs_0_.grad_ref, f32[48,768]{1,0:T(8,128)S(1)} %collective-permute-done.28.got, f32[4,48,768]{2,1,0:T(8,128)S(1)} %copy-done, ...), custom_call_target="tpu_custom_call" | custom-call | flops 1000000000 | bytes 36000000 | tf_op jit(solution)/shard_map/pallas_call | solution.py:233
  83.3 1.7 %shard_map.151 = (bf16[768,768]{1,0:T(8,128)(2,1)S(1)}, bf16[768,768]{1,0:T(8,128)(2,1)S(1)}) custom-call(s32[12]{0:T(128)S(1)} %concatenate.3.meta, s16[128,768]{1,0:T(8,128)(2,1)S(1)} %get-tuple-element.75.refs_0_, s16[128,768]{1,0:T(8,128)(2,1)S(1)} %collective-permute-done.10.refs_1_, s16[128,768]{1,0:T(8,128)(2,1)S(1)} %collective-permute-done.9.refs_2_, ...), custom_call_target="tpu_custom_call" | custom-call | flops 1000000000 | bytes 36000000 | tf_op jit(solution)/shard_map/pallas_call | solution.py:233
  85.1 2.1 %collective-permute-done.26.refs_7_ = s16[128,768]{1,0:T(8,128)(2,1)S(1)} collective-permute-done((s16[128,768]{1,0:T(8,128)(2,1)S(1)}, s16[128,768]{1,0:T(8,128)(2,1)S(1)}, u32[]{:S(2)}, u32[]{:S(2)}) %collective-permute-start.26) | collective-permute-done | bytes 196640 | tf_op jit(solution)/shard_map/ppermute | solution.py:144
  87.2 3.9 %shard_map.153 = (f32[48,768]{1,0:T(8,128)S(1)}, f32[48,768]{1,0:T(8,128)S(1)}, f32[1,128]{1,0:T(1,128)S(1)}, bf16[768,768]{1,0:T(8,128)(2,1)S(1)}, bf16[768,768]{1,0:T(8,128)(2,1)S(1)}) custom-call(s32[12]{0:T(128)S(1)} %concatenate.3.meta, f32[96,768]{1,0:T(8,128)S(1)} %get-tuple-element.93.grad.refs_0_.grad_ref, ...), custom_call_target="tpu_custom_call" | custom-call | flops 1000000000 | bytes 36000000 | tf_op jit(solution)/shard_map/pallas_call | solution.py:233
  91.2 11.1 %all_to_all.5.sums = f32[16,1,128]{2,1,0:T(1,128)S(1)} all-to-all(f32[16,1,128]{2,1,0:T(1,128)S(1)} %broadcast_in_dim.9), channel_id=1, replica_groups=mesh['shard'=2,'tensor'=4,'section'=4] {'tensor','section'}, dimensions={0} | all-to-all | bytes 16384 | tf_op jit(solution)/shard_map/all_to_all | solution.py:646
  102.3 0.7 shard_map.154.near
  103.0 1.7 %collective-permute-start.30 = (bf16[2,48,768]{2,1,0:T(8,128)(2,1)S(1)}, bf16[2,48,768]{2,1,0:T(8,128)(2,1)S(1)}, u32[]{:S(2)}, u32[]{:S(2)}) collective-permute-start(bf16[2,48,768]{2,1,0:T(8,128)(2,1)S(1)} %shard_map.154.near), channel_id=1, source_target_pairs={{0,16},{16,0},{1,17},{17,1},{2,18},{18,2},{3,19},{19,3},{4,20},{20... | collective-permute-start | bytes 442376 | tf_op jit(solution)/shard_map/ppermute | solution.py:148
  104.8 1.8 %shard_map.156 = (f32[48,768]{1,0:T(8,128)S(1)}, f32[48,768]{1,0:T(8,128)S(1)}) custom-call(s32[12]{0:T(128)S(1)} %concatenate.3.meta, f32[96,768]{1,0:T(8,128)S(1)} %get-tuple-element.93.grad.refs_0_.grad_ref, bf16[768,768]{1,0:T(8,128)(2,1)S(1)} %get-tuple-element.111.high_ref, bf16[768,768]{1,0:T(8,128)(2,1)S(1)} %get-tuple-element.112.low_ref), custom_call_target="tpu_custom_call" | custom-call | flops 1400000000 | bytes 50400000 | tf_op jit(solution)/shard_map/pallas_call | solution.py:233
  106.6 2.0 %shard_map.158 = (f32[48,768]{1,0:T(8,128)S(1)}, f32[48,768]{1,0:T(8,128)S(1)}) custom-call(s32[12]{0:T(128)S(1)} %concatenate.3.meta, bf16[768,768]{1,0:T(8,128)(2,1)S(1)} %get-tuple-element.111.high_ref, bf16[768,768]{1,0:T(8,128)(2,1)S(1)} %get-tuple-element.112.low_ref), custom_call_target="tpu_custom_call" | custom-call | flops 1800000000 | bytes 64800000 | tf_op jit(solution)/shard_map/pallas_call | solution.py:233
  108.6 0.6 collective-permute-start.32
  109.2 1.3 %shard_map.155 = bf16[4,48,768]{2,1,0:T(8,128)(2,1)} custom-call(s32[12]{0:T(128)S(1)} %concatenate.3.meta, bf16[2,48,768]{2,1,0:T(8,128)(2,1)S(1)} %shard_map.154.near, bf16[2,48,768]{2,1,0:T(8,128)(2,1)S(1)} %collective-permute-done.30.mirror), custom_call_target="tpu_custom_call" | custom-call | flops 1000000000 | bytes 36000000 | tf_op jit(solution)/shard_map/pallas_call | solution.py:233
  110.5 1.4 %shard_map.157 = f32[4,48,768]{2,1,0:T(8,128)} custom-call(s32[12]{0:T(128)S(1)} %concatenate.3.meta, f32[48,768]{1,0:T(8,128)S(1)} %get-tuple-element.113.own, f32[48,768]{1,0:T(8,128)S(1)} %collective-permute-done.31.got, f32[4,48,768]{2,1,0:T(8,128)S(1)} %copy-done.2), custom_call_target="tpu_custom_call" | custom-call | flops 1000000000 | bytes 36000000 | tf_op jit(solution)/shard_map/pallas_call | solution.py:233
  111.9 1.4 %shard_map.159 = f32[4,48,768]{2,1,0:T(8,128)} custom-call(s32[12]{0:T(128)S(1)} %concatenate.3.meta, f32[48,768]{1,0:T(8,128)S(1)} %get-tuple-element.115.own, f32[48,768]{1,0:T(8,128)S(1)} %collective-permute-done.32.got, f32[4,48,768]{2,1,0:T(8,128)S(1)} %copy-done.3), custom_call_target="tpu_custom_call" | custom-call | flops 1000000000 | bytes 36000000 | tf_op jit(solution)/shard_map/pallas_call | solution.py:233
  (39 shorter events, 0.4 us)
Async XLA Ops:
  4.1 4.1 %collective-permute-start = (bf16[2,512,768]{2,1,0:T(8,128)(2,1)S(1)}, bf16[2,512,768]{2,1,0:T(8,128)(2,1)S(1)}, u32[]{:S(2)}, u32[]{:S(2)}) collective-permute-start(bf16[2,512,768]{2,1,0:T(8,128)(2,1)S(1)} %get-tuple-element.62), channel_id=1, source_target_pairs={{0,1},{1,0},{2,3},{3,2},{4,5},{5,4},{6,7},{7,6},{8,9},{9,8},{10,11... | collective-permute-start | bytes 4718600 | tf_op jit(solution)/shard_map/ppermute | solution.py:140
  4.7 17.7 %collective-permute-start.6 = (bf16[2,512,768]{2,1,0:T(8,128)(2,1)S(1)}, bf16[2,512,768]{2,1,0:T(8,128)(2,1)S(1)}, u32[]{:S(2)}, u32[]{:S(2)}) collective-permute-start(bf16[2,512,768]{2,1,0:T(8,128)(2,1)S(1)} %get-tuple-element.69), channel_id=1, source_target_pairs={{0,1},{1,0},{2,3},{3,2},{4,5},{5,4},{6,7},{7,6},{8,9},{9,8},{10,11... | collective-permute-start | bytes 4718600 | tf_op jit(solution)/shard_map/ppermute | solution.py:140
  4.7 6.0 %collective-permute-start.4 = (f32[2,48,768]{2,1,0:T(8,128)S(1)}, f32[2,48,768]{2,1,0:T(8,128)S(1)}, u32[]{:S(2)}, u32[]{:S(2)}) collective-permute-start(f32[2,48,768]{2,1,0:T(8,128)S(1)} %get-tuple-element.67), channel_id=1, source_target_pairs={{0,1},{1,0},{2,3},{3,2},{4,5},{5,4},{6,7},{7,6},{8,9},{9,8},{10,11... | collective-permute-start | bytes 884744 | tf_op jit(solution)/shard_map/ppermute | solution.py:140
  10.7 13.9 %collective-permute-start.5 = (s16[256,768]{1,0:T(8,128)(2,1)S(1)}, s16[256,768]{1,0:T(8,128)(2,1)S(1)}, u32[]{:S(2)}, u32[]{:S(2)}) collective-permute-start(s16[256,768]{1,0:T(8,128)(2,1)S(1)} %get-tuple-element.68), channel_id=1, source_target_pairs={{0,16},{16,0},{1,17},{17,1},{2,18},{18,2},{3,19},{19,3},{4,20},{20... | collective-permute-start | bytes 1179656 | tf_op jit(solution)/shard_map/ppermute | solution.py:148
  18.1 9.6 %collective-permute-start.8 = (s16[128,768]{1,0:T(8,128)(2,1)S(1)}, s16[128,768]{1,0:T(8,128)(2,1)S(1)}, u32[]{:S(2)}, u32[]{:S(2)}) collective-permute-start(s16[128,768]{1,0:T(8,128)(2,1)S(1)} %get-tuple-element.75.refs_0_), channel_id=1, source_target_pairs={{0,12},{4,8},{8,4},{12,0},{1,13},{5,9},{9,5},{13,1},{2,14},{6,10},... | collective-permute-start | bytes 589832 | tf_op jit(solution)/shard_map/ppermute | solution.py:152
  21.8 9.5 %collective-permute-start.9 = (s16[128,768]{1,0:T(8,128)(2,1)S(1)}, s16[128,768]{1,0:T(8,128)(2,1)S(1)}, u32[]{:S(2)}, u32[]{:S(2)}) collective-permute-start(s16[128,768]{1,0:T(8,128)(2,1)S(1)} %get-tuple-element.75.refs_0_), channel_id=1, source_target_pairs={{0,4},{4,0},{8,12},{12,8},{1,5},{5,1},{9,13},{13,9},{2,6},{6,2},{1... | collective-permute-start | bytes 589832 | tf_op jit(solution)/shard_map/ppermute | solution.py:152
  21.8 12.7 %collective-permute-start.3 = (s16[256,768]{1,0:T(8,128)(2,1)S(1)}, s16[256,768]{1,0:T(8,128)(2,1)S(1)}, u32[]{:S(2)}, u32[]{:S(2)}) collective-permute-start(s16[256,768]{1,0:T(8,128)(2,1)S(1)} %get-tuple-element.65), channel_id=1, source_target_pairs={{0,16},{16,0},{1,17},{17,1},{2,18},{18,2},{3,19},{19,3},{4,20},{20... | collective-permute-start | bytes 1179656 | tf_op jit(solution)/shard_map/ppermute | solution.py:148
  22.3 9.0 %collective-permute-start.10 = (s16[128,768]{1,0:T(8,128)(2,1)S(1)}, s16[128,768]{1,0:T(8,128)(2,1)S(1)}, u32[]{:S(2)}, u32[]{:S(2)}) collective-permute-start(s16[128,768]{1,0:T(8,128)(2,1)S(1)} %get-tuple-element.75.refs_0_), channel_id=1, source_target_pairs={{0,2},{1,3},{2,0},{3,1},{4,6},{5,7},{6,4},{7,5},{8,10},{9,11},{10,... | collective-permute-start | bytes 589832 | tf_op jit(solution)/shard_map/ppermute | solution.py:144
  25.7 8.8 %collective-permute-start.7 = (s16[128,768]{1,0:T(8,128)(2,1)S(1)}, s16[128,768]{1,0:T(8,128)(2,1)S(1)}, u32[]{:S(2)}, u32[]{:S(2)}) collective-permute-start(s16[128,768]{1,0:T(8,128)(2,1)S(1)} %get-tuple-element.73), channel_id=1, source_target_pairs={{0,2},{1,3},{2,0},{3,1},{4,6},{5,7},{6,4},{7,5},{8,10},{9,11},{10,... | collective-permute-start | bytes 589832 | tf_op jit(solution)/shard_map/ppermute | solution.py:144
  27.8 14.5 %collective-permute-start.2 = (s16[256,768]{1,0:T(8,128)(2,1)S(1)}, s16[256,768]{1,0:T(8,128)(2,1)S(1)}, u32[]{:S(2)}, u32[]{:S(2)}) collective-permute-start(s16[256,768]{1,0:T(8,128)(2,1)S(1)} %get-tuple-element.64), channel_id=1, source_target_pairs={{0,16},{16,0},{1,17},{17,1},{2,18},{18,2},{3,19},{19,3},{4,20},{20... | collective-permute-start | bytes 1179656 | tf_op jit(solution)/shard_map/ppermute | solution.py:148
  31.4 12.4 %collective-permute-start.12 = (s16[128,768]{1,0:T(8,128)(2,1)S(1)}, s16[128,768]{1,0:T(8,128)(2,1)S(1)}, u32[]{:S(2)}, u32[]{:S(2)}) collective-permute-start(s16[128,768]{1,0:T(8,128)(2,1)S(1)} %collective-permute-done.9.refs_2_), channel_id=1, source_target_pairs={{0,2},{1,3},{2,0},{3,1},{4,6},{5,7},{6,4},{7,5},{8,10},{9,11},{10,... | collective-permute-start | bytes 589832 | tf_op jit(solution)/shard_map/ppermute | solution.py:144
  32.9 12.9 %collective-permute-start.13 = (s16[128,768]{1,0:T(8,128)(2,1)S(1)}, s16[128,768]{1,0:T(8,128)(2,1)S(1)}, u32[]{:S(2)}, u32[]{:S(2)}) collective-permute-start(s16[128,768]{1,0:T(8,128)(2,1)S(1)} %collective-permute-done.8.refs_6_), channel_id=1, source_target_pairs={{0,4},{4,0},{8,12},{12,8},{1,5},{5,1},{9,13},{13,9},{2,6},{6,2},{1... | collective-permute-start | bytes 589832 | tf_op jit(solution)/shard_map/ppermute | solution.py:152
  35.6 10.2 %collective-permute-start.11 = (s16[128,768]{1,0:T(8,128)(2,1)S(1)}, s16[128,768]{1,0:T(8,128)(2,1)S(1)}, u32[]{:S(2)}, u32[]{:S(2)}) collective-permute-start(s16[128,768]{1,0:T(8,128)(2,1)S(1)} %get-tuple-element.78), channel_id=1, source_target_pairs={{0,2},{1,3},{2,0},{3,1},{4,6},{5,7},{6,4},{7,5},{8,10},{9,11},{10,... | collective-permute-start | bytes 589832 | tf_op jit(solution)/shard_map/ppermute | solution.py:144
  36.4 15.5 %collective-permute-start.1 = (s16[256,768]{1,0:T(8,128)(2,1)S(1)}, s16[256,768]{1,0:T(8,128)(2,1)S(1)}, u32[]{:S(2)}, u32[]{:S(2)}) collective-permute-start(s16[256,768]{1,0:T(8,128)(2,1)S(1)} %get-tuple-element.63), channel_id=1, source_target_pairs={{0,16},{16,0},{1,17},{17,1},{2,18},{18,2},{3,19},{19,3},{4,20},{20... | collective-permute-start | bytes 1179656 | tf_op jit(solution)/shard_map/ppermute | solution.py:148
  42.2 9.7 %collective-permute-start.15 = (s16[128,768]{1,0:T(8,128)(2,1)S(1)}, s16[128,768]{1,0:T(8,128)(2,1)S(1)}, u32[]{:S(2)}, u32[]{:S(2)}) collective-permute-start(s16[128,768]{1,0:T(8,128)(2,1)S(1)} %collective-permute-done.8.refs_6_), channel_id=1, source_target_pairs={{0,2},{1,3},{2,0},{3,1},{4,6},{5,7},{6,4},{7,5},{8,10},{9,11},{10,... | collective-permute-start | bytes 589832 | tf_op jit(solution)/shard_map/ppermute | solution.py:144
  43.7 5.7 %collective-permute-start.17 = (s16[128,768]{1,0:T(8,128)(2,1)S(1)}, s16[128,768]{1,0:T(8,128)(2,1)S(1)}, u32[]{:S(2)}, u32[]{:S(2)}) collective-permute-start(s16[128,768]{1,0:T(8,128)(2,1)S(1)} %shard_map.147), channel_id=1, source_target_pairs={{0,4},{4,0},{8,12},{12,8},{1,5},{5,1},{9,13},{13,9},{2,6},{6,2},{1... | collective-permute-start | bytes 589832 | tf_op jit(solution)/shard_map/ppermute | solution.py:152
  46.9 5.7 %collective-permute-start.14 = (s16[128,768]{1,0:T(8,128)(2,1)S(1)}, s16[128,768]{1,0:T(8,128)(2,1)S(1)}, u32[]{:S(2)}, u32[]{:S(2)}) collective-permute-start(s16[128,768]{1,0:T(8,128)(2,1)S(1)} %get-tuple-element.82), channel_id=1, source_target_pairs={{0,2},{1,3},{2,0},{3,1},{4,6},{5,7},{6,4},{7,5},{8,10},{9,11},{10,... | collective-permute-start | bytes 589832 | tf_op jit(solution)/shard_map/ppermute | solution.py:144
  49.9 8.3 %collective-permute-start.18 = (s16[128,768]{1,0:T(8,128)(2,1)S(1)}, s16[128,768]{1,0:T(8,128)(2,1)S(1)}, u32[]{:S(2)}, u32[]{:S(2)}) collective-permute-start(s16[128,768]{1,0:T(8,128)(2,1)S(1)} %shard_map.148), channel_id=1, source_target_pairs={{0,12},{4,8},{8,4},{12,0},{1,13},{5,9},{9,5},{13,1},{2,14},{6,10},... | collective-permute-start | bytes 589832 | tf_op jit(solution)/shard_map/ppermute | solution.py:152
  53.7 5.7 %collective-permute-start.16 = (s16[128,768]{1,0:T(8,128)(2,1)S(1)}, s16[128,768]{1,0:T(8,128)(2,1)S(1)}, u32[]{:S(2)}, u32[]{:S(2)}) collective-permute-start(s16[128,768]{1,0:T(8,128)(2,1)S(1)} %get-tuple-element.86), channel_id=1, source_target_pairs={{0,2},{1,3},{2,0},{3,1},{4,6},{5,7},{6,4},{7,5},{8,10},{9,11},{10,... | collective-permute-start | bytes 589832 | tf_op jit(solution)/shard_map/ppermute | solution.py:144
  54.5 6.2 %collective-permute-start.19 = (s16[128,768]{1,0:T(8,128)(2,1)S(1)}, s16[128,768]{1,0:T(8,128)(2,1)S(1)}, u32[]{:S(2)}, u32[]{:S(2)}) collective-permute-start(s16[128,768]{1,0:T(8,128)(2,1)S(1)} %shard_map.149), channel_id=1, source_target_pairs={{0,4},{4,0},{8,12},{12,8},{1,5},{5,1},{9,13},{13,9},{2,6},{6,2},{1... | collective-permute-start | bytes 589832 | tf_op jit(solution)/shard_map/ppermute | solution.py:152
  60.8 20.7 %copy-start = (f32[4,48,768]{2,1,0:T(8,128)S(1)}, f32[4,48,768]{2,1,0:T(8,128)}, u32[]{:S(2)}) copy-start(f32[4,48,768]{2,1,0:T(8,128)} %first.1) | copy-start | bytes 1769476
  60.8 20.7 %copy-start.1 = (f32[4,48,768]{2,1,0:T(8,128)S(1)}, f32[4,48,768]{2,1,0:T(8,128)}, u32[]{:S(2)}) copy-start(f32[4,48,768]{2,1,0:T(8,128)} %second.1) | copy-start | bytes 1769476
  61.4 7.9 %collective-permute-start.20 = (s16[128,768]{1,0:T(8,128)(2,1)S(1)}, s16[128,768]{1,0:T(8,128)(2,1)S(1)}, u32[]{:S(2)}, u32[]{:S(2)}) collective-permute-start(s16[128,768]{1,0:T(8,128)(2,1)S(1)} %get-tuple-element.94), channel_id=1, source_target_pairs={{0,4},{4,0},{8,12},{12,8},{1,5},{5,1},{9,13},{13,9},{2,6},{6,2},{1... | collective-permute-start | bytes 589832 | tf_op jit(solution)/shard_map/ppermute | solution.py:152
  62.3 8.5 %collective-permute-start.21 = (s16[128,768]{1,0:T(8,128)(2,1)S(1)}, s16[128,768]{1,0:T(8,128)(2,1)S(1)}, u32[]{:S(2)}, u32[]{:S(2)}) collective-permute-start(s16[128,768]{1,0:T(8,128)(2,1)S(1)} %get-tuple-element.94), channel_id=1, source_target_pairs={{0,2},{1,3},{2,0},{3,1},{4,6},{5,7},{6,4},{7,5},{8,10},{9,11},{10,... | collective-permute-start | bytes 589832 | tf_op jit(solution)/shard_map/ppermute | solution.py:144
  63.0 16.4 %collective-permute-start.23 = (s16[128,768]{1,0:T(8,128)(2,1)S(1)}, s16[128,768]{1,0:T(8,128)(2,1)S(1)}, u32[]{:S(2)}, u32[]{:S(2)}) collective-permute-start(s16[128,768]{1,0:T(8,128)(2,1)S(1)} %get-tuple-element.94), channel_id=1, source_target_pairs={{0,8},{4,12},{8,0},{12,4},{1,9},{5,13},{9,1},{13,5},{2,10},{6,14},... | collective-permute-start | bytes 589832 | tf_op jit(solution)/shard_map/ppermute | solution.py:152
  65.8 14.7 %collective-permute-start.25 = (s16[128,768]{1,0:T(8,128)(2,1)S(1)}, s16[128,768]{1,0:T(8,128)(2,1)S(1)}, u32[]{:S(2)}, u32[]{:S(2)}) collective-permute-start(s16[128,768]{1,0:T(8,128)(2,1)S(1)} %get-tuple-element.94), channel_id=1, source_target_pairs={{0,12},{4,8},{8,4},{12,0},{1,13},{5,9},{9,5},{13,1},{2,14},{6,10},... | collective-permute-start | bytes 589832 | tf_op jit(solution)/shard_map/ppermute | solution.py:152
  67.0 14.4 %collective-permute-start.28 = (f32[48,768]{1,0:T(8,128)S(1)}, f32[48,768]{1,0:T(8,128)S(1)}, u32[]{:S(2)}, u32[]{:S(2)}) collective-permute-start(f32[48,768]{1,0:T(8,128)S(1)} %constant_dynamic-slice_fusion), channel_id=1, source_target_pairs={{0,1},{1,0},{2,3},{3,2},{4,5},{5,4},{6,7},{7,6},{8,9},{9,8},{10,11... | collective-permute-start | bytes 442376 | tf_op jit(solution)/shard_map/ppermute | solution.py:140
  69.3 14.0 %collective-permute-start.27 = (s16[128,768]{1,0:T(8,128)(2,1)S(1)}, s16[128,768]{1,0:T(8,128)(2,1)S(1)}, u32[]{:S(2)}, u32[]{:S(2)}) collective-permute-start(s16[128,768]{1,0:T(8,128)(2,1)S(1)} %collective-permute-done.13.refs_4_), channel_id=1, source_target_pairs={{0,2},{1,3},{2,0},{3,1},{4,6},{5,7},{6,4},{7,5},{8,10},{9,11},{10,... | collective-permute-start | bytes 589832 | tf_op jit(solution)/shard_map/ppermute | solution.py:144
  70.8 14.2 %collective-permute-start.22 = (s16[128,768]{1,0:T(8,128)(2,1)S(1)}, s16[128,768]{1,0:T(8,128)(2,1)S(1)}, u32[]{:S(2)}, u32[]{:S(2)}) collective-permute-start(s16[128,768]{1,0:T(8,128)(2,1)S(1)} %collective-permute-done.20.refs_2_), channel_id=1, source_target_pairs={{0,2},{1,3},{2,0},{3,1},{4,6},{5,7},{6,4},{7,5},{8,10},{9,11},{10,... | collective-permute-start | bytes 589832 | tf_op jit(solution)/shard_map/ppermute | solution.py:144
  79.4 5.7 %collective-permute-start.24 = (s16[128,768]{1,0:T(8,128)(2,1)S(1)}, s16[128,768]{1,0:T(8,128)(2,1)S(1)}, u32[]{:S(2)}, u32[]{:S(2)}) collective-permute-start(s16[128,768]{1,0:T(8,128)(2,1)S(1)} %collective-permute-done.23.refs_4_), channel_id=1, source_target_pairs={{0,2},{1,3},{2,0},{3,1},{4,6},{5,7},{6,4},{7,5},{8,10},{9,11},{10,... | collective-permute-start | bytes 589832 | tf_op jit(solution)/shard_map/ppermute | solution.py:144
  80.5 6.7 %collective-permute-start.26 = (s16[128,768]{1,0:T(8,128)(2,1)S(1)}, s16[128,768]{1,0:T(8,128)(2,1)S(1)}, u32[]{:S(2)}, u32[]{:S(2)}) collective-permute-start(s16[128,768]{1,0:T(8,128)(2,1)S(1)} %collective-permute-done.25.refs_6_), channel_id=1, source_target_pairs={{0,2},{1,3},{2,0},{3,1},{4,6},{5,7},{6,4},{7,5},{8,10},{9,11},{10,... | collective-permute-start | bytes 589832 | tf_op jit(solution)/shard_map/ppermute | solution.py:144
  87.2 15.1 %copy-start.4 = (bf16[4,48,768]{2,1,0:T(8,128)(2,1)S(1)}, bf16[4,48,768]{2,1,0:T(8,128)(2,1)}, u32[]{:S(2)}) copy-start(bf16[4,48,768]{2,1,0:T(8,128)(2,1)} %weights.1) | copy-start | bytes 884740
  91.1 11.2 %collective-permute-start.29 = (f32[48,768]{1,0:T(8,128)S(1)}, f32[48,768]{1,0:T(8,128)S(1)}, u32[]{:S(2)}, u32[]{:S(2)}) collective-permute-start(f32[48,768]{1,0:T(8,128)S(1)} %get-tuple-element.109), channel_id=1, source_target_pairs={{0,1},{1,0},{2,3},{3,2},{4,5},{5,4},{6,7},{7,6},{8,9},{9,8},{10,11... | collective-permute-start | bytes 442376 | tf_op jit(solution)/shard_map/ppermute | solution.py:140
  103.0 6.2 %collective-permute-start.30 = (bf16[2,48,768]{2,1,0:T(8,128)(2,1)S(1)}, bf16[2,48,768]{2,1,0:T(8,128)(2,1)S(1)}, u32[]{:S(2)}, u32[]{:S(2)}) collective-permute-start(bf16[2,48,768]{2,1,0:T(8,128)(2,1)S(1)} %shard_map.154.near), channel_id=1, source_target_pairs={{0,16},{16,0},{1,17},{17,1},{2,18},{18,2},{3,19},{19,3},{4,20},{20... | collective-permute-start | bytes 442376 | tf_op jit(solution)/shard_map/ppermute | solution.py:148
  106.5 3.9 %collective-permute-start.31 = (f32[48,768]{1,0:T(8,128)S(1)}, f32[48,768]{1,0:T(8,128)S(1)}, u32[]{:S(2)}, u32[]{:S(2)}) collective-permute-start(f32[48,768]{1,0:T(8,128)S(1)} %get-tuple-element.114), channel_id=1, source_target_pairs={{0,1},{1,0},{2,3},{3,2},{4,5},{5,4},{6,7},{7,6},{8,9},{9,8},{10,11... | collective-permute-start | bytes 442376 | tf_op jit(solution)/shard_map/ppermute | solution.py:140
  108.6 1.9 %copy-start.2 = (f32[4,48,768]{2,1,0:T(8,128)S(1)}, f32[4,48,768]{2,1,0:T(8,128)}, u32[]{:S(2)}) copy-start(f32[4,48,768]{2,1,0:T(8,128)} %stat.2) | copy-start | bytes 1769476
  108.6 3.3 %collective-permute-start.32 = (f32[48,768]{1,0:T(8,128)S(1)}, f32[48,768]{1,0:T(8,128)S(1)}, u32[]{:S(2)}, u32[]{:S(2)}) collective-permute-start(f32[48,768]{1,0:T(8,128)S(1)} %get-tuple-element.116), channel_id=1, source_target_pairs={{0,1},{1,0},{2,3},{3,2},{4,5},{5,4},{6,7},{7,6},{8,9},{9,8},{10,11... | collective-permute-start | bytes 442376 | tf_op jit(solution)/shard_map/ppermute | solution.py:140
  110.5 1.4 %copy-start.3 = (f32[4,48,768]{2,1,0:T(8,128)S(1)}, f32[4,48,768]{2,1,0:T(8,128)}, u32[]{:S(2)}) copy-start(f32[4,48,768]{2,1,0:T(8,128)} %stat.3) | copy-start | bytes 1769476

commit v5 on v4

--- a/solution.py
+++ b/solution.py
@@ -170,15 +170,55 @@
 
 
 def coded_rows(rows):
+    return rows + rows // 6
+
+
+def scaling(value):
+    top = jnp.maximum(jnp.max(jnp.abs(value), axis=0, keepdims=True), 1e-30)
+    exponent = jnp.ceil(jnp.log2(top))
+    return exponent, value * (jnp.exp2(-exponent) * 32760.0)
+
+
+def encode(value):
+    exponent, scaled = scaling(value)
+    coarse = jnp.round(scaled)
+    fine = jnp.clip(jnp.floor((scaled - coarse) * 4.0), -2.0, 1.0) + 2.0
+    tiles = value.shape[0] // 8
+    parts = [coarse]
+    for first in range(0, tiles + 1, 8):
+        full = first + 8 <= tiles
+        word = -32768.0 if full else jnp.broadcast_to(exponent * 256.0, (8, value.shape[1]))
+        for index in range(first, min(first + 8, tiles)):
+            word = word + fine[8 * index : 8 * index + 8] * float(4 ** (index - first))
+        parts.append(word)
+    return jnp.concatenate(parts, axis=0).astype(jnp.int32).astype(jnp.int16)
+
+
+def decode(words):
+    rows = words.shape[0] // 7 * 6
+    tiles = rows // 8
+    wide = words.astype(jnp.int32)
+    coarse = wide[:rows].astype(F32)
+    low = []
+    for first in range(0, tiles + 1, 8):
+        word = wide[rows + first : rows + first + 8]
+        if first + 8 <= tiles:
+            word = word + 32768
+        for index in range(first, min(first + 8, tiles)):
+            low.append((jnp.right_shift(word, 2 * (index - first)) & 3).astype(F32))
+    exponent = jnp.right_shift(word, 8).astype(F32)[:1]
+    fine = jnp.concatenate(low, axis=0)
+    return (coarse + (fine - 1.5) * 0.25) * (jnp.exp2(exponent) * (1.0 / 32760.0))
+
+
+def root_rows(rows):
     return rows + rows // 3
 
 
-def encode(value):
+def encode_root(value):
     rows = value.shape[0]
     part = rows // 4
-    top = jnp.maximum(jnp.max(jnp.abs(value), axis=0, keepdims=True), 1e-30)
-    exponent = jnp.ceil(jnp.log2(top))
-    scaled = value * (jnp.exp2(-exponent) * 32760.0)
+    exponent, scaled = scaling(value)
     coarse = jnp.round(scaled)
     fine = jnp.clip(jnp.floor((scaled - coarse) * 16.0), -8.0, 7.0) + 8.0
     words = fine[:part] - 32768.0
@@ -189,7 +229,7 @@
     return both.astype(jnp.int32).astype(jnp.int16)
 
 
-def decode(words):
+def decode_root(words):
     rows = words.shape[0] // 4 * 3
     part = rows // 4
     wide = words.astype(jnp.int32)
@@ -257,9 +297,11 @@
     return [(source.at[block, part], target.at[part]) for part in rows]
 
 
-def pick_kernel(meta, xin, dout, left, right, far, mine, roots, sems):
+def pick_kernel(meta, xin, dout, left, right, far, mine, roots, own, sems):
     _, block = used_slot(meta, 1 - meta[8], 1 - meta[11])
     pairs = in_parts(xin, block, far.at[0]) + in_parts(dout, block, far.at[1])
+    _, block = used_slot(meta, 1 - meta[8], meta[11])
+    pairs += in_parts(xin, block, own.at[0]) + in_parts(dout, block, own.at[1])
     place, block = used_slot(meta, meta[8], 1 - meta[11])
     pairs += [(left.at[place], roots.at[0]), (right.at[place], roots.at[1])]
     pairs += in_parts(xin, block, mine.at[0]) + in_parts(dout, block, mine.at[1])
@@ -267,9 +309,12 @@
         copy.wait()
 
 
-def own_kernel(across, meta, xin, dout, out, taken, sems):
-    plane = 1 - meta[8] if across else meta[8]
-    _, block = used_slot(meta, plane, meta[11])
+def own_far_kernel(taken, out):
+    out[...] = token_dot(taken[0], taken[1])
+
+
+def own_mine_kernel(meta, xin, dout, out, taken, sems):
+    _, block = used_slot(meta, meta[8], meta[11])
     pairs = in_parts(xin, block, taken.at[0]) + in_parts(dout, block, taken.at[1])
     copies = start_copies(pairs, sems)
     half = taken.shape[1] // 2
@@ -307,7 +352,7 @@
     whole[sib, :] = got[1]
     for copy in copies:
         copy.wait()
-    right_out[...] = encode(whole[...])
+    right_out[...] = encode_root(whole[...])
 
 
 def y_kernel(meta, got, mine, coded, keep, both):
@@ -372,17 +417,26 @@
 def root_kernel(meta, *refs):
     for index in range(8):
         spot = 2 * (meta[9] ^ (index // 2)) + (meta[10] ^ (index % 2))
-        put_rows(spot, decode(refs[index][...]), refs[8], refs[9])
-
-
-def direction_kernel(meta, *refs):
-    grad_ref, pieces = refs[0], refs[1:8]
-    left_ref, root_high, root_low, adam_ref = refs[8:12]
-    own_dir, sib_dir, sums, high_ref, low_ref, whole = refs[12:18]
-    for index in range(8):
-        spot = 2 * (meta[9] ^ (index // 2)) + (meta[10] ^ (index % 2))
-        value = grad_ref[...] if index == 0 else decode(pieces[index - 1][...])
-        put_rows(spot, value, high_ref, low_ref)
+        put_rows(spot, decode_root(refs[index][...]), refs[8], refs[9])
+
+
+def column_kernel(meta, grad_ref, one, two, three, high_ref, low_ref):
+    for step, ref in enumerate((grad_ref, one, two, three)):
+        value = decode(ref[...]) if step else ref[...]
+        put_rows(2 * (meta[9] ^ step) + meta[10], value, high_ref, low_ref)
+
+
+def direction_kernel(meta, high_in, low_in, *refs):
+    pieces = refs[:4]
+    left_ref, root_high, root_low, adam_ref = refs[4:8]
+    own_dir, sib_dir, sums, high_ref, low_ref, whole = refs[8:14]
+    for step in range(4):
+        spot = 2 * (meta[9] ^ step)
+        put_rows(spot + 1 - meta[10], decode(pieces[step][...]), high_ref, low_ref)
+        rows = left_ref.shape[0]
+        held = pl.ds(pl.multiple_of((spot + meta[10]) * rows, 32), rows)
+        high_ref[held, :] = high_in[held, :]
+        low_ref[held, :] = low_in[held, :]
     half = left_ref.shape[0] // 2
     high, low = high_ref[...], low_ref[...]
     left_high, left_low = halves(left_ref[...])
@@ -459,13 +513,6 @@
         out[slot] = (weights[block].astype(F32) - 0.05 * graft * value).astype(BF16)
 
 
-def stat_kernel(meta, own, got, stat, out):
-    out[...] = stat[...]
-    for slot, gram in ((meta[11], own), (1 - meta[11], got)):
-        place, _ = used_slot(meta, meta[8], slot)
-        out[place] = 0.5 * stat[place] + 0.5 * gram[...]
-
-
 def place_kernel(meta, near, mirror, out):
     plane = meta[8]
     for slot in (0, 1):
@@ -473,6 +520,19 @@
         out[block] = near[slot]
         _, block = used_slot(meta, 1 - plane, slot)
         out[block] = mirror[slot]
+
+
+def stat_kernel(
+    meta, own_right, got_right, own_left, got_left, right, left, right_out, left_out
+):
+    for own, got, stat, out in (
+        (own_right, got_right, right, right_out),
+        (own_left, got_left, left, left_out),
+    ):
+        out[...] = stat[...]
+        for slot, gram in ((meta[11], own), (1 - meta[11], got)):
+            place, _ = used_slot(meta, meta[8], slot)
+            out[place] = 0.5 * stat[place] + 0.5 * gram[...]
 
 
 def two_planes(
@@ -516,26 +576,17 @@
         pltpu.with_memory_space_constraint(value, pltpu.HBM)
         for value in (xin, dout, left_root, right_root)
     )
-    far_in, mine_in, roots = call(
+    far_in, mine_in, roots, own_in = call(
         pick_kernel,
-        [tokens_in, tokens_in, shape(2, rows, size)],
+        [tokens_in, tokens_in, shape(2, rows, size), tokens_in],
         [SMEM_SPEC] + [HBM_SPEC] * 4,
         (meta, xin, dout, left_root, right_root),
-        [dmas(18)],
+        [dmas(26)],
     )
     roots = to_core(roots)
     far_in = to_core(far_in)
     mine_in = to_core(mine_in)
-    def own_part(across, meta):
-        return call(
-            functools.partial(own_kernel, across),
-            [shape(size, size)],
-            [SMEM_SPEC] + [HBM_SPEC] * 2,
-            (meta, xin, dout),
-            [pltpu.VMEM((2, tokens, size), BF16), dmas(8)],
-        )[0]
-
-    own_far = own_part(True, meta)
+    (own_far,) = call(own_far_kernel, [shape(size, size)], [VMEM_SPEC], (own_in,))
     chunk = coded_rows(size // 4)
     coded = list(call(
         far_kernel,
@@ -548,12 +599,19 @@
     got_y = [to_y(value) for value in coded]
     left_rows, right_coded = call(
         rows_kernel,
-        [shape(2 * rows, size), piece],
+        [shape(2 * rows, size), shape(root_rows(2 * rows), size, dtype=words)],
         [SMEM_SPEC] + [HBM_SPEC] * 2 + [VMEM_SPEC],
         (meta, left_root, right_root, roots),
         [pltpu.VMEM((2 * rows, size), F32), dmas(2)],
     )
-    own_mine = own_part(False, meta)
+    right_coded, later = lax.optimization_barrier((right_coded, meta))
+    (own_mine,) = call(
+        own_mine_kernel,
+        [shape(size, size)],
+        [SMEM_SPEC] + [HBM_SPEC] * 2,
+        (later, xin, dout),
+        [pltpu.VMEM((2, tokens, size), BF16), dmas(8)],
+    )
     root_z = {3: to_z(right_coded, 3), 1: to_z(right_coded, 1)}
     mine_in, sent = lax.optimization_barrier((mine_in, right_coded))
     root_x = {0: to_x(sent)}
@@ -610,10 +668,6 @@
     column[1], across[0] = lax.optimization_barrier((column[1], across[0]))
     for bits in (1, 2, 3):
         across[bits] = to_x(column[bits])
-    pieces = [across[0]]
-    for bits in (1, 2, 3):
-        pieces += [column[bits], across[bits]]
-
     root_z[0] = right_coded
     root_pieces = []
     for index in range(4):
@@ -634,12 +688,20 @@
         [SMEM_SPEC] + [VMEM_SPEC] * 4,
         (meta, grad, to_core(grad_out), first_moment, second_moment),
     )
+    split = [shape(size, size, dtype=BF16)] * 2
+    high, low = call(
+        column_kernel,
+        split,
+        [SMEM_SPEC] + [VMEM_SPEC] * 4,
+        (meta, grad, column[1], column[2], column[3]),
+    )
     own_dir, sib_dir, sums, high, low = call(
         direction_kernel,
-        [tile, tile, shape(1, 128)] + [shape(size, size, dtype=BF16)] * 2,
-        [SMEM_SPEC] + [VMEM_SPEC] * 12,
-        (meta, grad, *pieces, left_rows, root_high, root_low, adam),
+        [tile, tile, shape(1, 128)] + split,
+        [SMEM_SPEC] + [VMEM_SPEC] * 10,
+        (meta, high, low, *across.values(), left_rows, root_high, root_low, adam),
         [pltpu.VMEM((2 * rows, size), F32)],
+        4.0,
     )
     sib_dir = to_core(sib_dir)
     sums = jnp.broadcast_to(sums[None], (device_count // 2, 1, 128))
@@ -677,14 +739,13 @@
         [SMEM_SPEC] + [VMEM_SPEC] * 2,
         (meta, near, mirror),
     )
-
-    def update(own, got, stat):
-        return call(
-            stat_kernel, [stack], [SMEM_SPEC] + [VMEM_SPEC] * 3, (meta, own, got, stat), (), 1.0
-        )[0]
-
-    new_right = update(own_right, got_right, right_stat)
-    new_left = update(own_left, got_left, left_stat)
+    got_left, new_weights = lax.optimization_barrier((got_left, new_weights))
+    new_right, new_left = call(
+        stat_kernel,
+        [stack, stack],
+        [SMEM_SPEC] + [VMEM_SPEC] * 6,
+        (meta, own_right, got_right, own_left, got_left, right_stat, left_stat),
+    )
     return new_weights, new_left, new_right, new_first, new_second
 
 

time: 114 us -> 107 us (0.939)
  waiting for transfers between devices: 29.9 us -> 24.2 us
  Pallas kernels: 35.8 us -> 33.2 us
  starting transfers between devices: 34.9 us -> 36.8 us
    ppermute x9, waiting for transfers between devices: 20.9 us -> 12.7 us  [to_z(): return lax.ppermute(value, 'tensor', [(i, i ^ bits) for i in range(4)])]
    ppermute x12, waiting for transfers between devices: 3.99 us -> 8.73 us  [to_x(): return lax.ppermute(value, 'section', [(i, i ^ 2) for i in range(4)])]
    ppermute x5, waiting for transfers between devices: 4.91 us -> 0.89 us  [to_y(): return lax.ppermute(value, 'shard', [(0, 1), (1, 0)])]
    ppermute x5, starting transfers between devices: 5.82 us -> 8.53 us  [to_y(): return lax.ppermute(value, 'shard', [(0, 1), (1, 0)])]
    pallas_call x19, Pallas kernels: 31.5 us -> 29 us  [call(): pl.pallas_call(body, out_shape=outs, in_specs=ins, out_specs=[VMEM_SPEC]...]
    ppermute x7, waiting for transfers between devices: 0.02 us -> 1.95 us  [to_core(): return lax.ppermute(value, 'section', [(i, i ^ 1) for i in range(4)])]
    ppermute x9, starting transfers between devices: 15.4 us -> 14 us  [to_z(): return lax.ppermute(value, 'tensor', [(i, i ^ bits) for i in range(4)])]
  transfers between devices with their start and end apart: 33 -> 33, of which waited for: 11 -> 12; matrix products, arithmetic and copies ran while one was open for 0% -> 0% of each run, Pallas kernels for 23% -> 22%
where the time goes in v5:
time: 107 us; the launch traced here: 106 us
  starting transfers between devices  36.8 us (34%)
  Pallas kernels  33.2 us (31%)
  waiting for transfers between devices  24.2 us (23%)
  blocking collectives  10.4 us (10%)
    pallas_call x19, Pallas kernels, call(): pl.pallas_call(body, out_shape=outs, in_specs=ins, out_specs=[VMEM_SPEC]...  29 us
    ppermute x9, starting transfers between devices, to_z(): return lax.ppermute(value, 'tensor', [(i, i ^ bits) for i in range(4)])  14 us
    ppermute x9, waiting for transfers between devices, to_z(): return lax.ppermute(value, 'tensor', [(i, i ^ bits) for i in range(4)])  12.7 us
    ppermute x12, starting transfers between devices, to_x(): return lax.ppermute(value, 'section', [(i, i ^ 2) for i in range(4)])  12.5 us
    all_to_all x1, blocking collectives, two_planes(): sums = lax.all_to_all(sums, GROUP, 0, 0)  10.4 us
    ppermute x12, waiting for transfers between devices, to_x(): return lax.ppermute(value, 'section', [(i, i ^ 2) for i in range(4)])  8.73 us
    ppermute x5, starting transfers between devices, to_y(): return lax.ppermute(value, 'shard', [(0, 1), (1, 0)])  8.53 us
    pallas_call x4, Pallas kernels, after_y(): pl.pallas_call(y_kernel, out_shape=[jax.ShapeDtypeStruct((coded_rows(rows...  4.15 us
  transfers between devices with their start and end apart: 33, of which 12 were waited for; matrix products, arithmetic and copies ran while one was open for 0% of the time, Pallas kernels for 22%

profile of v5, /device:TPU:0, one launch (start us, length us, event | category | flops | bytes accessed | tf_op | source)
XLA Modules:
  0.0 106.3 jit_solution(14993618656484379063)
XLA Ops:
  0.7 0.7 concatenate.3.meta
  1.4 3.3 %shard_map.137 = (bf16[2,512,768]{2,1,0:T(8,128)(2,1)S(1)}, bf16[2,512,768]{2,1,0:T(8,128)(2,1)S(1)}, f32[2,48,768]{2,1,0:T(8,128)S(1)}, bf16[2,512,768]{2,1,0:T(8,128)(2,1)S(1)}) custom-call(s32[12]{0:T(128)S(1)} %concatenate.3.meta, bf16[4,512,768]{2,1,0:T(8,128)(2,1)} %xin.3, bf16[4,512,768]{2,1,0:T(8,128)(2,1)} %dout.3, f32[4,48,768]{2,1,0:T(8,128)} %left.4, ...), custom_call_target="tpu_custom_call" | custom-call | flops 1000000000 | bytes 36000000 | tf_op jit(solution)/shard_map/pallas_call | solution.py:273
  4.7 0.5 collective-permute-start
  5.3 0.4 collective-permute-start.4
  5.7 0.8 shard_map.138.own_ref
  6.5 1.7 %collective-permute-done.got = bf16[2,512,768]{2,1,0:T(8,128)(2,1)S(1)} collective-permute-done((bf16[2,512,768]{2,1,0:T(8,128)(2,1)S(1)}, bf16[2,512,768]{2,1,0:T(8,128)(2,1)S(1)}, u32[]{:S(2)}, u32[]{:S(2)}) %collective-permute-start) | collective-permute-done | bytes 1572896 | tf_op jit(solution)/shard_map/ppermute | solution.py:140
  8.2 2.4 %shard_map.139 = (s16[224,768]{1,0:T(8,128)(2,1)S(1)}, s16[224,768]{1,0:T(8,128)(2,1)S(1)}, s16[224,768]{1,0:T(8,128)(2,1)S(1)}, s16[224,768]{1,0:T(8,128)(2,1)S(1)}) custom-call(s32[12]{0:T(128)S(1)} %concatenate.3.meta, bf16[2,512,768]{2,1,0:T(8,128)(2,1)S(1)} %collective-permute-done.got, f32[768,768]{1,0:T(8,128)S(1)} %shard_map.138.own_ref), custom_call_target="tpu_custom_call" | custom-call | flops 1000000000 | bytes 36000000 | tf_op jit(solution)/shard_map/pallas_call | solution.py:273
  10.7 0.2 collective-permute-done.4.got
  10.9 2.9 %collective-permute-start.5 = (s16[224,768]{1,0:T(8,128)(2,1)S(1)}, s16[224,768]{1,0:T(8,128)(2,1)S(1)}, u32[]{:S(2)}, u32[]{:S(2)}) collective-permute-start(s16[224,768]{1,0:T(8,128)(2,1)S(1)} %get-tuple-element.78), channel_id=1, source_target_pairs={{0,16},{16,0},{1,17},{17,1},{2,18},{18,2},{3,19},{19,3},{4,20},{20... | collective-permute-start | bytes 1032200 | tf_op jit(solution)/shard_map/ppermute | solution.py:148
  13.8 1.7 %shard_map.140 = (f32[96,768]{1,0:T(8,128)S(1)}, s16[128,768]{1,0:T(8,128)(2,1)S(1)}) custom-call(s32[12]{0:T(128)S(1)} %concatenate.3.meta, f32[4,48,768]{2,1,0:T(8,128)} %left.4, f32[4,48,768]{2,1,0:T(8,128)} %right.4, f32[2,48,768]{2,1,0:T(8,128)S(1)} %collective-permute-done.4.got), custom_call_target="tpu_custom_call" | custom-call | flops 1000000000 | bytes 36000000 | tf_op jit(solution)/shard_map/pallas_call | solution.py:273
  15.5 1.6 %collective-permute-start.9 = (s16[128,768]{1,0:T(8,128)(2,1)S(1)}, s16[128,768]{1,0:T(8,128)(2,1)S(1)}, u32[]{:S(2)}, u32[]{:S(2)}) collective-permute-start(s16[128,768]{1,0:T(8,128)(2,1)S(1)} %get-tuple-element.87.refs_0_), channel_id=1, source_target_pairs={{0,4},{4,0},{8,12},{12,8},{1,5},{5,1},{9,13},{13,9},{2,6},{6,2},{1... | collective-permute-start | bytes 589832 | tf_op jit(solution)/shard_map/ppermute | solution.py:152
  17.1 2.5 %collective-permute-start.8 = (s16[128,768]{1,0:T(8,128)(2,1)S(1)}, s16[128,768]{1,0:T(8,128)(2,1)S(1)}, u32[]{:S(2)}, u32[]{:S(2)}) collective-permute-start(s16[128,768]{1,0:T(8,128)(2,1)S(1)} %get-tuple-element.87.refs_0_), channel_id=1, source_target_pairs={{0,12},{4,8},{8,4},{12,0},{1,13},{5,9},{9,5},{13,1},{2,14},{6,10},... | collective-permute-start | bytes 589832 | tf_op jit(solution)/shard_map/ppermute | solution.py:152
  19.6 0.5 collective-permute-start.3
  20.1 1.5 %collective-permute-start.10 = (s16[128,768]{1,0:T(8,128)(2,1)S(1)}, s16[128,768]{1,0:T(8,128)(2,1)S(1)}, u32[]{:S(2)}, u32[]{:S(2)}) collective-permute-start(s16[128,768]{1,0:T(8,128)(2,1)S(1)} %get-tuple-element.87.refs_0_), channel_id=1, source_target_pairs={{0,2},{1,3},{2,0},{3,1},{4,6},{5,7},{6,4},{7,5},{8,10},{9,11},{10,... | collective-permute-start | bytes 589832 | tf_op jit(solution)/shard_map/ppermute | solution.py:144
  21.6 3.1 %shard_map.141.own_ref = f32[768,768]{1,0:T(8,128)S(1)} custom-call(s32[12]{0:T(128)S(1)} %concatenate.3.meta, bf16[4,512,768]{2,1,0:T(8,128)(2,1)} %xin.3, bf16[4,512,768]{2,1,0:T(8,128)(2,1)} %dout.3), custom_call_target="tpu_custom_call" | custom-call | flops 1000000000 | bytes 36000000 | tf_op jit(solution)/shard_map/pallas_call | solution.py:273
  24.7 0.8 shard_map.142.mine
  25.5 1.0 shard_map.143
  26.6 0.6 collective-permute-start.7
  27.2 1.5 %collective-permute-start.2 = (s16[224,768]{1,0:T(8,128)(2,1)S(1)}, s16[224,768]{1,0:T(8,128)(2,1)S(1)}, u32[]{:S(2)}, u32[]{:S(2)}) collective-permute-start(s16[224,768]{1,0:T(8,128)(2,1)S(1)} %get-tuple-element.74), channel_id=1, source_target_pairs={{0,16},{16,0},{1,17},{17,1},{2,18},{18,2},{3,19},{19,3},{4,20},{20... | collective-permute-start | bytes 1032200 | tf_op jit(solution)/shard_map/ppermute | solution.py:148
  28.7 1.5 %collective-permute-start.12 = (s16[128,768]{1,0:T(8,128)(2,1)S(1)}, s16[128,768]{1,0:T(8,128)(2,1)S(1)}, u32[]{:S(2)}, u32[]{:S(2)}) collective-permute-start(s16[128,768]{1,0:T(8,128)(2,1)S(1)} %collective-permute-done.9.refs_2_), channel_id=1, source_target_pairs={{0,2},{1,3},{2,0},{3,1},{4,6},{5,7},{6,4},{7,5},{8,10},{9,11},{10,... | collective-permute-start | bytes 589832 | tf_op jit(solution)/shard_map/ppermute | solution.py:144
  30.2 0.7 collective-permute-start.13
  30.9 3.0 %collective-permute-done.7.refs_0_ = s16[112,768]{1,0:T(8,128)(2,1)S(1)} collective-permute-done((s16[112,768]{1,0:T(8,128)(2,1)S(1)}, s16[112,768]{1,0:T(8,128)(2,1)S(1)}, u32[]{:S(2)}, u32[]{:S(2)}) %collective-permute-start.7) | collective-permute-done | bytes 172064 | tf_op jit(solution)/shard_map/ppermute | solution.py:144
  33.9 1.0 shard_map.144
  35.0 2.0 %collective-permute-start.1 = (s16[224,768]{1,0:T(8,128)(2,1)S(1)}, s16[224,768]{1,0:T(8,128)(2,1)S(1)}, u32[]{:S(2)}, u32[]{:S(2)}) collective-permute-start(s16[224,768]{1,0:T(8,128)(2,1)S(1)} %get-tuple-element.73), channel_id=1, source_target_pairs={{0,16},{16,0},{1,17},{17,1},{2,18},{18,2},{3,19},{19,3},{4,20},{20... | collective-permute-start | bytes 1032200 | tf_op jit(solution)/shard_map/ppermute | solution.py:148
  37.0 0.2 shard_map.147
  37.3 0.9 collective-permute-done.2.got
  38.2 1.3 %collective-permute-start.17 = (s16[112,768]{1,0:T(8,128)(2,1)S(1)}, s16[112,768]{1,0:T(8,128)(2,1)S(1)}, u32[]{:S(2)}, u32[]{:S(2)}) collective-permute-start(s16[112,768]{1,0:T(8,128)(2,1)S(1)} %shard_map.147), channel_id=1, source_target_pairs={{0,4},{4,0},{8,12},{12,8},{1,5},{5,1},{9,13},{13,9},{2,6},{6,2},{1... | collective-permute-start | bytes 516104 | tf_op jit(solution)/shard_map/ppermute | solution.py:152
  39.5 1.5 %collective-permute-start.15 = (s16[128,768]{1,0:T(8,128)(2,1)S(1)}, s16[128,768]{1,0:T(8,128)(2,1)S(1)}, u32[]{:S(2)}, u32[]{:S(2)}) collective-permute-start(s16[128,768]{1,0:T(8,128)(2,1)S(1)} %collective-permute-done.8.refs_6_), channel_id=1, source_target_pairs={{0,2},{1,3},{2,0},{3,1},{4,6},{5,7},{6,4},{7,5},{8,10},{9,11},{10,... | collective-permute-start | bytes 589832 | tf_op jit(solution)/shard_map/ppermute | solution.py:144
  41.0 1.0 shard_map.145
  42.0 0.6 collective-permute-start.14
  42.6 0.9 collective-permute-done.17.refs_1_
  43.6 0.4 shard_map.148
  44.0 3.4 %collective-permute-start.18 = (s16[112,768]{1,0:T(8,128)(2,1)S(1)}, s16[112,768]{1,0:T(8,128)(2,1)S(1)}, u32[]{:S(2)}, u32[]{:S(2)}) collective-permute-start(s16[112,768]{1,0:T(8,128)(2,1)S(1)} %shard_map.148), channel_id=1, source_target_pairs={{0,12},{4,8},{8,4},{12,0},{1,13},{5,9},{9,5},{13,1},{2,14},{6,10},... | collective-permute-start | bytes 516104 | tf_op jit(solution)/shard_map/ppermute | solution.py:152
  47.4 1.0 collective-permute-done.14.refs_0_
  48.4 1.0 shard_map.146
  49.5 1.3 %collective-permute-start.16 = (s16[112,768]{1,0:T(8,128)(2,1)S(1)}, s16[112,768]{1,0:T(8,128)(2,1)S(1)}, u32[]{:S(2)}, u32[]{:S(2)}) collective-permute-start(s16[112,768]{1,0:T(8,128)(2,1)S(1)} %get-tuple-element.98), channel_id=1, source_target_pairs={{0,2},{1,3},{2,0},{3,1},{4,6},{5,7},{6,4},{7,5},{8,10},{9,11},{10,... | collective-permute-start | bytes 516104 | tf_op jit(solution)/shard_map/ppermute | solution.py:144
  50.8 0.2 shard_map.149
  51.1 0.3 collective-permute-start.19
  51.4 0.7 collective-permute-done.18.far
  52.1 2.8 %collective-permute-done.16.got = s16[112,768]{1,0:T(8,128)(2,1)S(1)} collective-permute-done((s16[112,768]{1,0:T(8,128)(2,1)S(1)}, s16[112,768]{1,0:T(8,128)(2,1)S(1)}, u32[]{:S(2)}, u32[]{:S(2)}) %collective-permute-start.16) | collective-permute-done | bytes 172064 | tf_op jit(solution)/shard_map/ppermute | solution.py:144
  55.0 1.6 %collective-permute-done.19.near = s16[112,768]{1,0:T(8,128)(2,1)S(1)} collective-permute-done((s16[112,768]{1,0:T(8,128)(2,1)S(1)}, s16[112,768]{1,0:T(8,128)(2,1)S(1)}, u32[]{:S(2)}, u32[]{:S(2)}) %collective-permute-start.19) | collective-permute-done | bytes 172064 | tf_op jit(solution)/shard_map/ppermute | solution.py:152
  56.5 0.6 shard_map.150
  57.3 0.8 collective-permute-start.21
  58.1 0.4 collective-permute-start.20
  58.5 3.6 %collective-permute-start.23 = (s16[112,768]{1,0:T(8,128)(2,1)S(1)}, s16[112,768]{1,0:T(8,128)(2,1)S(1)}, u32[]{:S(2)}, u32[]{:S(2)}) collective-permute-start(s16[112,768]{1,0:T(8,128)(2,1)S(1)} %get-tuple-element.106), channel_id=1, source_target_pairs={{0,12},{4,8},{8,4},{12,0},{1,13},{5,9},{9,5},{13,1},{2,14},{6,10},... | collective-permute-start | bytes 516104 | tf_op jit(solution)/shard_map/ppermute | solution.py:152
  62.1 1.3 %collective-permute-start.27 = (s16[128,768]{1,0:T(8,128)(2,1)S(1)}, s16[128,768]{1,0:T(8,128)(2,1)S(1)}, u32[]{:S(2)}, u32[]{:S(2)}) collective-permute-start(s16[128,768]{1,0:T(8,128)(2,1)S(1)} %collective-permute-done.13.refs_4_), channel_id=1, source_target_pairs={{0,2},{1,3},{2,0},{3,1},{4,6},{5,7},{6,4},{7,5},{8,10},{9,11},{10,... | collective-permute-start | bytes 589832 | tf_op jit(solution)/shard_map/ppermute | solution.py:144
  63.4 1.9 %shard_map.153 = (f32[4,48,768]{2,1,0:T(8,128)}, f32[4,48,768]{2,1,0:T(8,128)}, f32[1,128]{1,0:T(1,128)S(1)}) custom-call(s32[12]{0:T(128)S(1)} %concatenate.3.meta, f32[96,768]{1,0:T(8,128)S(1)} %get-tuple-element.105.grad_ref.grad, f32[48,768]{1,0:T(8,128)S(1)} %collective-permute-done.28.got, f32[4,48,768]{2,1,0:T(8,128)S(1)} %copy-done, ...), custom_call_target="tpu_custom_call" | custom-call | flops 1000000000 | bytes 36000000 | tf_op jit(solution)/shard_map/pallas_call | solution.py:273
  65.3 0.8 collective-permute-start.24
  66.1 5.0 %collective-permute-done.23.three = s16[112,768]{1,0:T(8,128)(2,1)S(1)} collective-permute-done((s16[112,768]{1,0:T(8,128)(2,1)S(1)}, s16[112,768]{1,0:T(8,128)(2,1)S(1)}, u32[]{:S(2)}, u32[]{:S(2)}) %collective-permute-start.23) | collective-permute-done | bytes 172064 | tf_op jit(solution)/shard_map/ppermute | solution.py:152
  71.1 1.3 %collective-permute-start.26 = (s16[112,768]{1,0:T(8,128)(2,1)S(1)}, s16[112,768]{1,0:T(8,128)(2,1)S(1)}, u32[]{:S(2)}, u32[]{:S(2)}) collective-permute-start(s16[112,768]{1,0:T(8,128)(2,1)S(1)} %collective-permute-done.23.three), channel_id=1, source_target_pairs={{0,2},{1,3},{2,0},{3,1},{4,6},{5,7},{6,4},{7,5},{8,10},{9,11},{10,... | collective-permute-start | bytes 516104 | tf_op jit(solution)/shard_map/ppermute | solution.py:144
  72.4 4.4 %collective-permute-done.22.two = s16[112,768]{1,0:T(8,128)(2,1)S(1)} collective-permute-done((s16[112,768]{1,0:T(8,128)(2,1)S(1)}, s16[112,768]{1,0:T(8,128)(2,1)S(1)}, u32[]{:S(2)}, u32[]{:S(2)}) %collective-permute-start.22) | collective-permute-done | bytes 172064 | tf_op jit(solution)/shard_map/ppermute | solution.py:152
  76.8 1.3 %collective-permute-start.25 = (s16[112,768]{1,0:T(8,128)(2,1)S(1)}, s16[112,768]{1,0:T(8,128)(2,1)S(1)}, u32[]{:S(2)}, u32[]{:S(2)}) collective-permute-start(s16[112,768]{1,0:T(8,128)(2,1)S(1)} %collective-permute-done.22.two), channel_id=1, source_target_pairs={{0,2},{1,3},{2,0},{3,1},{4,6},{5,7},{6,4},{7,5},{8,10},{9,11},{10,... | collective-permute-start | bytes 516104 | tf_op jit(solution)/shard_map/ppermute | solution.py:144
  78.0 1.0 shard_map.151
  79.0 1.7 %shard_map.152 = (bf16[768,768]{1,0:T(8,128)(2,1)S(1)}, bf16[768,768]{1,0:T(8,128)(2,1)S(1)}) custom-call(s32[12]{0:T(128)S(1)} %concatenate.3.meta, s16[128,768]{1,0:T(8,128)(2,1)S(1)} %get-tuple-element.87.refs_0_, s16[128,768]{1,0:T(8,128)(2,1)S(1)} %collective-permute-done.10.refs_1_, s16[128,768]{1,0:T(8,128)(2,1)S(1)} %collective-permute-done.9.refs_2_, ...), custom_call_target="tpu_custom_call" | custom-call | flops 1000000000 | bytes 36000000 | tf_op jit(solution)/shard_map/pallas_call | solution.py:273
  80.8 1.9 %collective-permute-done.25.refs_2_ = s16[112,768]{1,0:T(8,128)(2,1)S(1)} collective-permute-done((s16[112,768]{1,0:T(8,128)(2,1)S(1)}, s16[112,768]{1,0:T(8,128)(2,1)S(1)}, u32[]{:S(2)}, u32[]{:S(2)}) %collective-permute-start.25) | collective-permute-done | bytes 172064 | tf_op jit(solution)/shard_map/ppermute | solution.py:144
  82.6 3.4 %shard_map.154 = (f32[48,768]{1,0:T(8,128)S(1)}, f32[48,768]{1,0:T(8,128)S(1)}, f32[1,128]{1,0:T(1,128)S(1)}, bf16[768,768]{1,0:T(8,128)(2,1)S(1)}, bf16[768,768]{1,0:T(8,128)(2,1)S(1)}) custom-call(s32[12]{0:T(128)S(1)} %concatenate.3.meta, bf16[768,768]{1,0:T(8,128)(2,1)S(1)} %get-tuple-element.108.high_in, ...), custom_call_target="tpu_custom_call" | custom-call | flops 4000000000 | bytes 144000000 | tf_op jit(solution)/shard_map/pallas_call | solution.py:273
  86.2 10.4 %all_to_all.5.sums = f32[16,1,128]{2,1,0:T(1,128)S(1)} all-to-all(f32[16,1,128]{2,1,0:T(1,128)S(1)} %broadcast_in_dim.9), channel_id=1, replica_groups=mesh['shard'=2,'tensor'=4,'section'=4] {'tensor','section'}, dimensions={0} | all-to-all | bytes 16384 | tf_op jit(solution)/shard_map/all_to_all | solution.py:708
  96.6 0.7 shard_map.155.near
  97.3 1.6 %collective-permute-start.31 = (bf16[2,48,768]{2,1,0:T(8,128)(2,1)S(1)}, bf16[2,48,768]{2,1,0:T(8,128)(2,1)S(1)}, u32[]{:S(2)}, u32[]{:S(2)}) collective-permute-start(bf16[2,48,768]{2,1,0:T(8,128)(2,1)S(1)} %shard_map.155.near), channel_id=1, source_target_pairs={{0,16},{16,0},{1,17},{17,1},{2,18},{18,2},{3,19},{19,3},{4,20},{20... | collective-permute-start | bytes 442376 | tf_op jit(solution)/shard_map/ppermute | solution.py:148
  98.8 1.8 %shard_map.156 = (f32[48,768]{1,0:T(8,128)S(1)}, f32[48,768]{1,0:T(8,128)S(1)}) custom-call(s32[12]{0:T(128)S(1)} %concatenate.3.meta, f32[96,768]{1,0:T(8,128)S(1)} %get-tuple-element.105.grad_ref.grad, bf16[768,768]{1,0:T(8,128)(2,1)S(1)} %get-tuple-element.124.high_ref, bf16[768,768]{1,0:T(8,128)(2,1)S(1)} %get-tuple-element.125.low_ref), custom_call_target="tpu_custom_call" | custom-call | flops 1400000000 | bytes 50400000 | tf_op jit(solution)/shard_map/pallas_call | solution.py:273
  100.7 2.0 %shard_map.158 = (f32[48,768]{1,0:T(8,128)S(1)}, f32[48,768]{1,0:T(8,128)S(1)}) custom-call(s32[12]{0:T(128)S(1)} %concatenate.3.meta, bf16[768,768]{1,0:T(8,128)(2,1)S(1)} %get-tuple-element.124.high_ref, bf16[768,768]{1,0:T(8,128)(2,1)S(1)} %get-tuple-element.125.low_ref), custom_call_target="tpu_custom_call" | custom-call | flops 1800000000 | bytes 64800000 | tf_op jit(solution)/shard_map/pallas_call | solution.py:273
  102.7 0.6 collective-permute-start.32
  103.3 1.3 %shard_map.157 = bf16[4,48,768]{2,1,0:T(8,128)(2,1)} custom-call(s32[12]{0:T(128)S(1)} %concatenate.3.meta, bf16[2,48,768]{2,1,0:T(8,128)(2,1)S(1)} %shard_map.155.near, bf16[2,48,768]{2,1,0:T(8,128)(2,1)S(1)} %collective-permute-done.31.mirror), custom_call_target="tpu_custom_call" | custom-call | flops 1000000000 | bytes 36000000 | tf_op jit(solution)/shard_map/pallas_call | solution.py:273
  104.6 1.7 %shard_map.159 = (f32[4,48,768]{2,1,0:T(8,128)}, f32[4,48,768]{2,1,0:T(8,128)}) custom-call(s32[12]{0:T(128)S(1)} %concatenate.3.meta, f32[48,768]{1,0:T(8,128)S(1)} %get-tuple-element.129.own_right, f32[48,768]{1,0:T(8,128)S(1)} %collective-permute-done.32.got_right, f32[48,768]{1,0:T(8,128)S(1)} %get-tuple-element.131.own_left, ...), custom_call_target="tpu_custom_call" | custom-call | flops 1000000000 | bytes 36000000 | tf_op jit(solution)/shard_map/pallas_call | solution.py:273
  (39 shorter events, 0.5 us)
Async XLA Ops:
  4.7 3.6 %collective-permute-start = (bf16[2,512,768]{2,1,0:T(8,128)(2,1)S(1)}, bf16[2,512,768]{2,1,0:T(8,128)(2,1)S(1)}, u32[]{:S(2)}, u32[]{:S(2)}) collective-permute-start(bf16[2,512,768]{2,1,0:T(8,128)(2,1)S(1)} %get-tuple-element.71), channel_id=1, source_target_pairs={{0,1},{1,0},{2,3},{3,2},{4,5},{5,4},{6,7},{7,6},{8,9},{9,8},{10,11... | collective-permute-start | bytes 4718600 | tf_op jit(solution)/shard_map/ppermute | solution.py:140
  5.2 14.9 %collective-permute-start.6 = (bf16[2,512,768]{2,1,0:T(8,128)(2,1)S(1)}, bf16[2,512,768]{2,1,0:T(8,128)(2,1)S(1)}, u32[]{:S(2)}, u32[]{:S(2)}) collective-permute-start(bf16[2,512,768]{2,1,0:T(8,128)(2,1)S(1)} %get-tuple-element.79), channel_id=1, source_target_pairs={{0,1},{1,0},{2,3},{3,2},{4,5},{5,4},{6,7},{7,6},{8,9},{9,8},{10,11... | collective-permute-start | bytes 4718600 | tf_op jit(solution)/shard_map/ppermute | solution.py:140
  5.3 5.6 %collective-permute-start.4 = (f32[2,48,768]{2,1,0:T(8,128)S(1)}, f32[2,48,768]{2,1,0:T(8,128)S(1)}, u32[]{:S(2)}, u32[]{:S(2)}) collective-permute-start(f32[2,48,768]{2,1,0:T(8,128)S(1)} %get-tuple-element.77), channel_id=1, source_target_pairs={{0,1},{1,0},{2,3},{3,2},{4,5},{5,4},{6,7},{7,6},{8,9},{9,8},{10,11... | collective-permute-start | bytes 884744 | tf_op jit(solution)/shard_map/ppermute | solution.py:140
  10.9 14.6 %collective-permute-start.5 = (s16[224,768]{1,0:T(8,128)(2,1)S(1)}, s16[224,768]{1,0:T(8,128)(2,1)S(1)}, u32[]{:S(2)}, u32[]{:S(2)}) collective-permute-start(s16[224,768]{1,0:T(8,128)(2,1)S(1)} %get-tuple-element.78), channel_id=1, source_target_pairs={{0,16},{16,0},{1,17},{17,1},{2,18},{18,2},{3,19},{19,3},{4,20},{20... | collective-permute-start | bytes 1032200 | tf_op jit(solution)/shard_map/ppermute | solution.py:148
  15.5 11.7 %collective-permute-start.9 = (s16[128,768]{1,0:T(8,128)(2,1)S(1)}, s16[128,768]{1,0:T(8,128)(2,1)S(1)}, u32[]{:S(2)}, u32[]{:S(2)}) collective-permute-start(s16[128,768]{1,0:T(8,128)(2,1)S(1)} %get-tuple-element.87.refs_0_), channel_id=1, source_target_pairs={{0,4},{4,0},{8,12},{12,8},{1,5},{5,1},{9,13},{13,9},{2,6},{6,2},{1... | collective-permute-start | bytes 589832 | tf_op jit(solution)/shard_map/ppermute | solution.py:152
  17.1 11.5 %collective-permute-start.8 = (s16[128,768]{1,0:T(8,128)(2,1)S(1)}, s16[128,768]{1,0:T(8,128)(2,1)S(1)}, u32[]{:S(2)}, u32[]{:S(2)}) collective-permute-start(s16[128,768]{1,0:T(8,128)(2,1)S(1)} %get-tuple-element.87.refs_0_), channel_id=1, source_target_pairs={{0,12},{4,8},{8,4},{12,0},{1,13},{5,9},{9,5},{13,1},{2,14},{6,10},... | collective-permute-start | bytes 589832 | tf_op jit(solution)/shard_map/ppermute | solution.py:152
  19.6 11.3 %collective-permute-start.3 = (s16[224,768]{1,0:T(8,128)(2,1)S(1)}, s16[224,768]{1,0:T(8,128)(2,1)S(1)}, u32[]{:S(2)}, u32[]{:S(2)}) collective-permute-start(s16[224,768]{1,0:T(8,128)(2,1)S(1)} %get-tuple-element.75), channel_id=1, source_target_pairs={{0,16},{16,0},{1,17},{17,1},{2,18},{18,2},{3,19},{19,3},{4,20},{20... | collective-permute-start | bytes 1032200 | tf_op jit(solution)/shard_map/ppermute | solution.py:148
  20.1 8.6 %collective-permute-start.10 = (s16[128,768]{1,0:T(8,128)(2,1)S(1)}, s16[128,768]{1,0:T(8,128)(2,1)S(1)}, u32[]{:S(2)}, u32[]{:S(2)}) collective-permute-start(s16[128,768]{1,0:T(8,128)(2,1)S(1)} %get-tuple-element.87.refs_0_), channel_id=1, source_target_pairs={{0,2},{1,3},{2,0},{3,1},{4,6},{5,7},{6,4},{7,5},{8,10},{9,11},{10,... | collective-permute-start | bytes 589832 | tf_op jit(solution)/shard_map/ppermute | solution.py:144
  26.6 7.3 %collective-permute-start.7 = (s16[112,768]{1,0:T(8,128)(2,1)S(1)}, s16[112,768]{1,0:T(8,128)(2,1)S(1)}, u32[]{:S(2)}, u32[]{:S(2)}) collective-permute-start(s16[112,768]{1,0:T(8,128)(2,1)S(1)} %get-tuple-element.85), channel_id=1, source_target_pairs={{0,2},{1,3},{2,0},{3,1},{4,6},{5,7},{6,4},{7,5},{8,10},{9,11},{10,... | collective-permute-start | bytes 516104 | tf_op jit(solution)/shard_map/ppermute | solution.py:144
  27.2 11.0 %collective-permute-start.2 = (s16[224,768]{1,0:T(8,128)(2,1)S(1)}, s16[224,768]{1,0:T(8,128)(2,1)S(1)}, u32[]{:S(2)}, u32[]{:S(2)}) collective-permute-start(s16[224,768]{1,0:T(8,128)(2,1)S(1)} %get-tuple-element.74), channel_id=1, source_target_pairs={{0,16},{16,0},{1,17},{17,1},{2,18},{18,2},{3,19},{19,3},{4,20},{20... | collective-permute-start | bytes 1032200 | tf_op jit(solution)/shard_map/ppermute | solution.py:148
  28.7 10.8 %collective-permute-start.12 = (s16[128,768]{1,0:T(8,128)(2,1)S(1)}, s16[128,768]{1,0:T(8,128)(2,1)S(1)}, u32[]{:S(2)}, u32[]{:S(2)}) collective-permute-start(s16[128,768]{1,0:T(8,128)(2,1)S(1)} %collective-permute-done.9.refs_2_), channel_id=1, source_target_pairs={{0,2},{1,3},{2,0},{3,1},{4,6},{5,7},{6,4},{7,5},{8,10},{9,11},{10,... | collective-permute-start | bytes 589832 | tf_op jit(solution)/shard_map/ppermute | solution.py:144
  30.2 10.8 %collective-permute-start.13 = (s16[128,768]{1,0:T(8,128)(2,1)S(1)}, s16[128,768]{1,0:T(8,128)(2,1)S(1)}, u32[]{:S(2)}, u32[]{:S(2)}) collective-permute-start(s16[128,768]{1,0:T(8,128)(2,1)S(1)} %collective-permute-done.8.refs_6_), channel_id=1, source_target_pairs={{0,4},{4,0},{8,12},{12,8},{1,5},{5,1},{9,13},{13,9},{2,6},{6,2},{1... | collective-permute-start | bytes 589832 | tf_op jit(solution)/shard_map/ppermute | solution.py:152
  34.9 6.1 %collective-permute-start.11 = (s16[112,768]{1,0:T(8,128)(2,1)S(1)}, s16[112,768]{1,0:T(8,128)(2,1)S(1)}, u32[]{:S(2)}, u32[]{:S(2)}) collective-permute-start(s16[112,768]{1,0:T(8,128)(2,1)S(1)} %get-tuple-element.90), channel_id=1, source_target_pairs={{0,2},{1,3},{2,0},{3,1},{4,6},{5,7},{6,4},{7,5},{8,10},{9,11},{10,... | collective-permute-start | bytes 516104 | tf_op jit(solution)/shard_map/ppermute | solution.py:144
  35.0 12.4 %collective-permute-start.1 = (s16[224,768]{1,0:T(8,128)(2,1)S(1)}, s16[224,768]{1,0:T(8,128)(2,1)S(1)}, u32[]{:S(2)}, u32[]{:S(2)}) collective-permute-start(s16[224,768]{1,0:T(8,128)(2,1)S(1)} %get-tuple-element.73), channel_id=1, source_target_pairs={{0,16},{16,0},{1,17},{17,1},{2,18},{18,2},{3,19},{19,3},{4,20},{20... | collective-permute-start | bytes 1032200 | tf_op jit(solution)/shard_map/ppermute | solution.py:148
  38.2 5.4 %collective-permute-start.17 = (s16[112,768]{1,0:T(8,128)(2,1)S(1)}, s16[112,768]{1,0:T(8,128)(2,1)S(1)}, u32[]{:S(2)}, u32[]{:S(2)}) collective-permute-start(s16[112,768]{1,0:T(8,128)(2,1)S(1)} %shard_map.147), channel_id=1, source_target_pairs={{0,4},{4,0},{8,12},{12,8},{1,5},{5,1},{9,13},{13,9},{2,6},{6,2},{1... | collective-permute-start | bytes 516104 | tf_op jit(solution)/shard_map/ppermute | solution.py:152
  39.5 7.9 %collective-permute-start.15 = (s16[128,768]{1,0:T(8,128)(2,1)S(1)}, s16[128,768]{1,0:T(8,128)(2,1)S(1)}, u32[]{:S(2)}, u32[]{:S(2)}) collective-permute-start(s16[128,768]{1,0:T(8,128)(2,1)S(1)} %collective-permute-done.8.refs_6_), channel_id=1, source_target_pairs={{0,2},{1,3},{2,0},{3,1},{4,6},{5,7},{6,4},{7,5},{8,10},{9,11},{10,... | collective-permute-start | bytes 589832 | tf_op jit(solution)/shard_map/ppermute | solution.py:144
  42.0 6.4 %collective-permute-start.14 = (s16[112,768]{1,0:T(8,128)(2,1)S(1)}, s16[112,768]{1,0:T(8,128)(2,1)S(1)}, u32[]{:S(2)}, u32[]{:S(2)}) collective-permute-start(s16[112,768]{1,0:T(8,128)(2,1)S(1)} %get-tuple-element.94), channel_id=1, source_target_pairs={{0,2},{1,3},{2,0},{3,1},{4,6},{5,7},{6,4},{7,5},{8,10},{9,11},{10,... | collective-permute-start | bytes 516104 | tf_op jit(solution)/shard_map/ppermute | solution.py:144
  44.0 8.1 %collective-permute-start.18 = (s16[112,768]{1,0:T(8,128)(2,1)S(1)}, s16[112,768]{1,0:T(8,128)(2,1)S(1)}, u32[]{:S(2)}, u32[]{:S(2)}) collective-permute-start(s16[112,768]{1,0:T(8,128)(2,1)S(1)} %shard_map.148), channel_id=1, source_target_pairs={{0,12},{4,8},{8,4},{12,0},{1,13},{5,9},{9,5},{13,1},{2,14},{6,10},... | collective-permute-start | bytes 516104 | tf_op jit(solution)/shard_map/ppermute | solution.py:152
  49.5 5.5 %collective-permute-start.16 = (s16[112,768]{1,0:T(8,128)(2,1)S(1)}, s16[112,768]{1,0:T(8,128)(2,1)S(1)}, u32[]{:S(2)}, u32[]{:S(2)}) collective-permute-start(s16[112,768]{1,0:T(8,128)(2,1)S(1)} %get-tuple-element.98), channel_id=1, source_target_pairs={{0,2},{1,3},{2,0},{3,1},{4,6},{5,7},{6,4},{7,5},{8,10},{9,11},{10,... | collective-permute-start | bytes 516104 | tf_op jit(solution)/shard_map/ppermute | solution.py:144
  51.1 5.5 %collective-permute-start.19 = (s16[112,768]{1,0:T(8,128)(2,1)S(1)}, s16[112,768]{1,0:T(8,128)(2,1)S(1)}, u32[]{:S(2)}, u32[]{:S(2)}) collective-permute-start(s16[112,768]{1,0:T(8,128)(2,1)S(1)} %shard_map.149), channel_id=1, source_target_pairs={{0,4},{4,0},{8,12},{12,8},{1,5},{5,1},{9,13},{13,9},{2,6},{6,2},{1... | collective-permute-start | bytes 516104 | tf_op jit(solution)/shard_map/ppermute | solution.py:152
  56.5 6.9 %copy-start = (f32[4,48,768]{2,1,0:T(8,128)S(1)}, f32[4,48,768]{2,1,0:T(8,128)}, u32[]{:S(2)}) copy-start(f32[4,48,768]{2,1,0:T(8,128)} %first.1) | copy-start | bytes 1769476
  56.5 6.9 %copy-start.1 = (f32[4,48,768]{2,1,0:T(8,128)S(1)}, f32[4,48,768]{2,1,0:T(8,128)}, u32[]{:S(2)}) copy-start(f32[4,48,768]{2,1,0:T(8,128)} %second.1) | copy-start | bytes 1769476
  57.2 5.0 %collective-permute-start.28 = (f32[48,768]{1,0:T(8,128)S(1)}, f32[48,768]{1,0:T(8,128)S(1)}, u32[]{:S(2)}, u32[]{:S(2)}) collective-permute-start(f32[48,768]{1,0:T(8,128)S(1)} %constant_dynamic-slice_fusion), channel_id=1, source_target_pairs={{0,1},{1,0},{2,3},{3,2},{4,5},{5,4},{6,7},{7,6},{8,9},{9,8},{10,11... | collective-permute-start | bytes 442376 | tf_op jit(solution)/shard_map/ppermute | solution.py:140
  57.3 8.0 %collective-permute-start.21 = (s16[112,768]{1,0:T(8,128)(2,1)S(1)}, s16[112,768]{1,0:T(8,128)(2,1)S(1)}, u32[]{:S(2)}, u32[]{:S(2)}) collective-permute-start(s16[112,768]{1,0:T(8,128)(2,1)S(1)} %get-tuple-element.106), channel_id=1, source_target_pairs={{0,2},{1,3},{2,0},{3,1},{4,6},{5,7},{6,4},{7,5},{8,10},{9,11},{10,... | collective-permute-start | bytes 516104 | tf_op jit(solution)/shard_map/ppermute | solution.py:144
  58.1 7.2 %collective-permute-start.20 = (s16[112,768]{1,0:T(8,128)(2,1)S(1)}, s16[112,768]{1,0:T(8,128)(2,1)S(1)}, u32[]{:S(2)}, u32[]{:S(2)}) collective-permute-start(s16[112,768]{1,0:T(8,128)(2,1)S(1)} %get-tuple-element.106), channel_id=1, source_target_pairs={{0,4},{4,0},{8,12},{12,8},{1,5},{5,1},{9,13},{13,9},{2,6},{6,2},{1... | collective-permute-start | bytes 516104 | tf_op jit(solution)/shard_map/ppermute | solution.py:152
  58.5 12.6 %collective-permute-start.23 = (s16[112,768]{1,0:T(8,128)(2,1)S(1)}, s16[112,768]{1,0:T(8,128)(2,1)S(1)}, u32[]{:S(2)}, u32[]{:S(2)}) collective-permute-start(s16[112,768]{1,0:T(8,128)(2,1)S(1)} %get-tuple-element.106), channel_id=1, source_target_pairs={{0,12},{4,8},{8,4},{12,0},{1,13},{5,9},{9,5},{13,1},{2,14},{6,10},... | collective-permute-start | bytes 516104 | tf_op jit(solution)/shard_map/ppermute | solution.py:152
  62.1 14.6 %collective-permute-start.22 = (s16[112,768]{1,0:T(8,128)(2,1)S(1)}, s16[112,768]{1,0:T(8,128)(2,1)S(1)}, u32[]{:S(2)}, u32[]{:S(2)}) collective-permute-start(s16[112,768]{1,0:T(8,128)(2,1)S(1)} %get-tuple-element.106), channel_id=1, source_target_pairs={{0,8},{4,12},{8,0},{12,4},{1,9},{5,13},{9,1},{13,5},{2,10},{6,14},... | collective-permute-start | bytes 516104 | tf_op jit(solution)/shard_map/ppermute | solution.py:152
  62.1 16.9 %collective-permute-start.27 = (s16[128,768]{1,0:T(8,128)(2,1)S(1)}, s16[128,768]{1,0:T(8,128)(2,1)S(1)}, u32[]{:S(2)}, u32[]{:S(2)}) collective-permute-start(s16[128,768]{1,0:T(8,128)(2,1)S(1)} %collective-permute-done.13.refs_4_), channel_id=1, source_target_pairs={{0,2},{1,3},{2,0},{3,1},{4,6},{5,7},{6,4},{7,5},{8,10},{9,11},{10,... | collective-permute-start | bytes 589832 | tf_op jit(solution)/shard_map/ppermute | solution.py:144
  65.3 17.3 %collective-permute-start.24 = (s16[112,768]{1,0:T(8,128)(2,1)S(1)}, s16[112,768]{1,0:T(8,128)(2,1)S(1)}, u32[]{:S(2)}, u32[]{:S(2)}) collective-permute-start(s16[112,768]{1,0:T(8,128)(2,1)S(1)} %collective-permute-done.20.one), channel_id=1, source_target_pairs={{0,2},{1,3},{2,0},{3,1},{4,6},{5,7},{6,4},{7,5},{8,10},{9,11},{10,... | collective-permute-start | bytes 516104 | tf_op jit(solution)/shard_map/ppermute | solution.py:144
  71.1 9.6 %collective-permute-start.26 = (s16[112,768]{1,0:T(8,128)(2,1)S(1)}, s16[112,768]{1,0:T(8,128)(2,1)S(1)}, u32[]{:S(2)}, u32[]{:S(2)}) collective-permute-start(s16[112,768]{1,0:T(8,128)(2,1)S(1)} %collective-permute-done.23.three), channel_id=1, source_target_pairs={{0,2},{1,3},{2,0},{3,1},{4,6},{5,7},{6,4},{7,5},{8,10},{9,11},{10,... | collective-permute-start | bytes 516104 | tf_op jit(solution)/shard_map/ppermute | solution.py:144
  76.8 5.9 %collective-permute-start.25 = (s16[112,768]{1,0:T(8,128)(2,1)S(1)}, s16[112,768]{1,0:T(8,128)(2,1)S(1)}, u32[]{:S(2)}, u32[]{:S(2)}) collective-permute-start(s16[112,768]{1,0:T(8,128)(2,1)S(1)} %collective-permute-done.22.two), channel_id=1, source_target_pairs={{0,2},{1,3},{2,0},{3,1},{4,6},{5,7},{6,4},{7,5},{8,10},{9,11},{10,... | collective-permute-start | bytes 516104 | tf_op jit(solution)/shard_map/ppermute | solution.py:144
  82.6 13.9 %copy-start.4 = (bf16[4,48,768]{2,1,0:T(8,128)(2,1)S(1)}, bf16[4,48,768]{2,1,0:T(8,128)(2,1)}, u32[]{:S(2)}) copy-start(bf16[4,48,768]{2,1,0:T(8,128)(2,1)} %weights.1) | copy-start | bytes 884740
  86.1 10.5 %collective-permute-start.29 = (f32[48,768]{1,0:T(8,128)S(1)}, f32[48,768]{1,0:T(8,128)S(1)}, u32[]{:S(2)}, u32[]{:S(2)}) collective-permute-start(f32[48,768]{1,0:T(8,128)S(1)} %get-tuple-element.123), channel_id=1, source_target_pairs={{0,1},{1,0},{2,3},{3,2},{4,5},{5,4},{6,7},{7,6},{8,9},{9,8},{10,11... | collective-permute-start | bytes 442376 | tf_op jit(solution)/shard_map/ppermute | solution.py:140
  97.3 6.0 %collective-permute-start.31 = (bf16[2,48,768]{2,1,0:T(8,128)(2,1)S(1)}, bf16[2,48,768]{2,1,0:T(8,128)(2,1)S(1)}, u32[]{:S(2)}, u32[]{:S(2)}) collective-permute-start(bf16[2,48,768]{2,1,0:T(8,128)(2,1)S(1)} %shard_map.155.near), channel_id=1, source_target_pairs={{0,16},{16,0},{1,17},{17,1},{2,18},{18,2},{3,19},{19,3},{4,20},{20... | collective-permute-start | bytes 442376 | tf_op jit(solution)/shard_map/ppermute | solution.py:148
  100.6 4.0 %collective-permute-start.30 = (f32[48,768]{1,0:T(8,128)S(1)}, f32[48,768]{1,0:T(8,128)S(1)}, u32[]{:S(2)}, u32[]{:S(2)}) collective-permute-start(f32[48,768]{1,0:T(8,128)S(1)} %get-tuple-element.126), channel_id=1, source_target_pairs={{0,1},{1,0},{2,3},{3,2},{4,5},{5,4},{6,7},{7,6},{8,9},{9,8},{10,11... | collective-permute-start | bytes 442376 | tf_op jit(solution)/shard_map/ppermute | solution.py:140
  102.7 1.9 %copy-start.2 = (f32[4,48,768]{2,1,0:T(8,128)S(1)}, f32[4,48,768]{2,1,0:T(8,128)}, u32[]{:S(2)}) copy-start(f32[4,48,768]{2,1,0:T(8,128)} %right.5) | copy-start | bytes 1769476
  102.7 1.9 %copy-start.3 = (f32[4,48,768]{2,1,0:T(8,128)S(1)}, f32[4,48,768]{2,1,0:T(8,128)}, u32[]{:S(2)}) copy-start(f32[4,48,768]{2,1,0:T(8,128)} %left.5) | copy-start | bytes 1769476
  102.7 1.9 %collective-permute-start.32 = (f32[48,768]{1,0:T(8,128)S(1)}, f32[48,768]{1,0:T(8,128)S(1)}, u32[]{:S(2)}, u32[]{:S(2)}) collective-permute-start(f32[48,768]{1,0:T(8,128)S(1)} %get-tuple-element.130), channel_id=1, source_target_pairs={{0,1},{1,0},{2,3},{3,2},{4,5},{5,4},{6,7},{7,6},{8,9},{9,8},{10,11... | collective-permute-start | bytes 442376 | tf_op jit(solution)/shard_map/ppermute | solution.py:140

commit v6 on v5

--- a/solution.py
+++ b/solution.py
@@ -662,12 +662,14 @@
     )
 
     across = {0: to_x(coded)}
-    column = {bits: to_z(coded, bits) for bits in (1, 2, 3)}
+    column = {bits: to_z(coded, bits) for bits in (3, 1)}
     coded, sent = lax.optimization_barrier((coded, root_z[2]))
     root_x[2] = to_x(sent)
-    column[1], across[0] = lax.optimization_barrier((column[1], across[0]))
-    for bits in (1, 2, 3):
+    column[3], across[0] = lax.optimization_barrier((column[3], across[0]))
+    column[2] = to_z(column[3], 1)
+    for bits in (1, 3, 2):
         across[bits] = to_x(column[bits])
+
     root_z[0] = right_coded
     root_pieces = []
     for index in range(4):
@@ -699,7 +701,7 @@
         direction_kernel,
         [tile, tile, shape(1, 128)] + split,
         [SMEM_SPEC] + [VMEM_SPEC] * 10,
-        (meta, high, low, *across.values(), left_rows, root_high, root_low, adam),
+        (meta, high, low, *(across[step] for step in range(4)), left_rows, root_high, root_low, adam),
         [pltpu.VMEM((2 * rows, size), F32)],
         4.0,
     )

time: 107 us -> 104 us (0.972)
  waiting for transfers between devices: 24.2 us -> 22.3 us
    ppermute x9, waiting for transfers between devices: 12.7 us -> 8.72 us  [to_z(): return lax.ppermute(value, 'tensor', [(i, i ^ bits) for i in range(4)])]
    ppermute x12, waiting for transfers between devices: 8.73 us -> 10.7 us  [to_x(): return lax.ppermute(value, 'section', [(i, i ^ 2) for i in range(4)])]
  transfers between devices with their start and end apart: 33 -> 33, of which waited for: 12 -> 14; matrix products, arithmetic and copies ran while one was open for 0% -> 0% of each run, Pallas kernels for 22% -> 23%
where the time goes in v6:
time: 104 us
  starting transfers between devices  36.7 us (35%)
  Pallas kernels  33.2 us (32%)
  waiting for transfers between devices  22.3 us (21%)
  blocking collectives  10.4 us (10%)
    pallas_call x19, Pallas kernels, call(): pl.pallas_call(body, out_shape=outs, in_specs=ins, out_specs=[VMEM_SPEC]...  29 us
    ppermute x12, starting transfers between devices, to_x(): return lax.ppermute(value, 'section', [(i, i ^ 2) for i in range(4)])  13.2 us
    ppermute x9, starting transfers between devices, to_z(): return lax.ppermute(value, 'tensor', [(i, i ^ bits) for i in range(4)])  13.1 us
    ppermute x12, waiting for transfers between devices, to_x(): return lax.ppermute(value, 'section', [(i, i ^ 2) for i in range(4)])  10.7 us
    all_to_all x1, blocking collectives, two_planes(): sums = lax.all_to_all(sums, GROUP, 0, 0)  10.4 us
    ppermute x9, waiting for transfers between devices, to_z(): return lax.ppermute(value, 'tensor', [(i, i ^ bits) for i in range(4)])  8.72 us
    ppermute x5, starting transfers between devices, to_y(): return lax.ppermute(value, 'shard', [(0, 1), (1, 0)])  8.53 us
    pallas_call x4, Pallas kernels, after_y(): pl.pallas_call(y_kernel, out_shape=[jax.ShapeDtypeStruct((coded_rows(rows...  4.15 us
  transfers between devices with their start and end apart: 33, of which 14 were waited for; matrix products, arithmetic and copies ran while one was open for 0% of the time, Pallas kernels for 23%

profile of v6, /device:TPU:0, one launch (start us, length us, event | category | flops | bytes accessed | tf_op | source)
XLA Modules:
  0.0 104.2 jit_solution(161299609152372507)
XLA Ops:
  0.7 0.7 concatenate.3.meta
  1.4 3.3 %shard_map.137 = (bf16[2,512,768]{2,1,0:T(8,128)(2,1)S(1)}, bf16[2,512,768]{2,1,0:T(8,128)(2,1)S(1)}, f32[2,48,768]{2,1,0:T(8,128)S(1)}, bf16[2,512,768]{2,1,0:T(8,128)(2,1)S(1)}) custom-call(s32[12]{0:T(128)S(1)} %concatenate.3.meta, bf16[4,512,768]{2,1,0:T(8,128)(2,1)} %xin.3, bf16[4,512,768]{2,1,0:T(8,128)(2,1)} %dout.3, f32[4,48,768]{2,1,0:T(8,128)} %left.4, ...), custom_call_target="tpu_custom_call" | custom-call | flops 1000000000 | bytes 36000000 | tf_op jit(solution)/shard_map/pallas_call | solution.py:273
  4.7 0.5 collective-permute-start
  5.3 0.4 collective-permute-start.4
  5.7 0.8 shard_map.138.own_ref
  6.5 1.7 %collective-permute-done.got = bf16[2,512,768]{2,1,0:T(8,128)(2,1)S(1)} collective-permute-done((bf16[2,512,768]{2,1,0:T(8,128)(2,1)S(1)}, bf16[2,512,768]{2,1,0:T(8,128)(2,1)S(1)}, u32[]{:S(2)}, u32[]{:S(2)}) %collective-permute-start) | collective-permute-done | bytes 1572896 | tf_op jit(solution)/shard_map/ppermute | solution.py:140
  8.2 2.4 %shard_map.139 = (s16[224,768]{1,0:T(8,128)(2,1)S(1)}, s16[224,768]{1,0:T(8,128)(2,1)S(1)}, s16[224,768]{1,0:T(8,128)(2,1)S(1)}, s16[224,768]{1,0:T(8,128)(2,1)S(1)}) custom-call(s32[12]{0:T(128)S(1)} %concatenate.3.meta, bf16[2,512,768]{2,1,0:T(8,128)(2,1)S(1)} %collective-permute-done.got, f32[768,768]{1,0:T(8,128)S(1)} %shard_map.138.own_ref), custom_call_target="tpu_custom_call" | custom-call | flops 1000000000 | bytes 36000000 | tf_op jit(solution)/shard_map/pallas_call | solution.py:273
  10.9 2.9 %collective-permute-start.5 = (s16[224,768]{1,0:T(8,128)(2,1)S(1)}, s16[224,768]{1,0:T(8,128)(2,1)S(1)}, u32[]{:S(2)}, u32[]{:S(2)}) collective-permute-start(s16[224,768]{1,0:T(8,128)(2,1)S(1)} %get-tuple-element.78), channel_id=1, source_target_pairs={{0,16},{16,0},{1,17},{17,1},{2,18},{18,2},{3,19},{19,3},{4,20},{20... | collective-permute-start | bytes 1032200 | tf_op jit(solution)/shard_map/ppermute | solution.py:148
  13.8 1.7 %shard_map.140 = (f32[96,768]{1,0:T(8,128)S(1)}, s16[128,768]{1,0:T(8,128)(2,1)S(1)}) custom-call(s32[12]{0:T(128)S(1)} %concatenate.3.meta, f32[4,48,768]{2,1,0:T(8,128)} %left.4, f32[4,48,768]{2,1,0:T(8,128)} %right.4, f32[2,48,768]{2,1,0:T(8,128)S(1)} %collective-permute-done.4.got), custom_call_target="tpu_custom_call" | custom-call | flops 1000000000 | bytes 36000000 | tf_op jit(solution)/shard_map/pallas_call | solution.py:273
  15.5 1.6 %collective-permute-start.9 = (s16[128,768]{1,0:T(8,128)(2,1)S(1)}, s16[128,768]{1,0:T(8,128)(2,1)S(1)}, u32[]{:S(2)}, u32[]{:S(2)}) collective-permute-start(s16[128,768]{1,0:T(8,128)(2,1)S(1)} %get-tuple-element.87.refs_0_), channel_id=1, source_target_pairs={{0,4},{4,0},{8,12},{12,8},{1,5},{5,1},{9,13},{13,9},{2,6},{6,2},{1... | collective-permute-start | bytes 589832 | tf_op jit(solution)/shard_map/ppermute | solution.py:152
  17.1 2.5 %collective-permute-start.8 = (s16[128,768]{1,0:T(8,128)(2,1)S(1)}, s16[128,768]{1,0:T(8,128)(2,1)S(1)}, u32[]{:S(2)}, u32[]{:S(2)}) collective-permute-start(s16[128,768]{1,0:T(8,128)(2,1)S(1)} %get-tuple-element.87.refs_0_), channel_id=1, source_target_pairs={{0,12},{4,8},{8,4},{12,0},{1,13},{5,9},{9,5},{13,1},{2,14},{6,10},... | collective-permute-start | bytes 589832 | tf_op jit(solution)/shard_map/ppermute | solution.py:152
  19.6 0.5 collective-permute-start.3
  20.1 1.5 %collective-permute-start.10 = (s16[128,768]{1,0:T(8,128)(2,1)S(1)}, s16[128,768]{1,0:T(8,128)(2,1)S(1)}, u32[]{:S(2)}, u32[]{:S(2)}) collective-permute-start(s16[128,768]{1,0:T(8,128)(2,1)S(1)} %get-tuple-element.87.refs_0_), channel_id=1, source_target_pairs={{0,2},{1,3},{2,0},{3,1},{4,6},{5,7},{6,4},{7,5},{8,10},{9,11},{10,... | collective-permute-start | bytes 589832 | tf_op jit(solution)/shard_map/ppermute | solution.py:144
  21.6 3.1 %shard_map.141.own_ref = f32[768,768]{1,0:T(8,128)S(1)} custom-call(s32[12]{0:T(128)S(1)} %concatenate.3.meta, bf16[4,512,768]{2,1,0:T(8,128)(2,1)} %xin.3, bf16[4,512,768]{2,1,0:T(8,128)(2,1)} %dout.3), custom_call_target="tpu_custom_call" | custom-call | flops 1000000000 | bytes 36000000 | tf_op jit(solution)/shard_map/pallas_call | solution.py:273
  24.7 0.8 shard_map.142.mine
  25.5 1.0 shard_map.143
  26.6 0.6 collective-permute-start.7
  27.2 1.5 %collective-permute-start.2 = (s16[224,768]{1,0:T(8,128)(2,1)S(1)}, s16[224,768]{1,0:T(8,128)(2,1)S(1)}, u32[]{:S(2)}, u32[]{:S(2)}) collective-permute-start(s16[224,768]{1,0:T(8,128)(2,1)S(1)} %get-tuple-element.74), channel_id=1, source_target_pairs={{0,16},{16,0},{1,17},{17,1},{2,18},{18,2},{3,19},{19,3},{4,20},{20... | collective-permute-start | bytes 1032200 | tf_op jit(solution)/shard_map/ppermute | solution.py:148
  28.7 1.5 %collective-permute-start.12 = (s16[128,768]{1,0:T(8,128)(2,1)S(1)}, s16[128,768]{1,0:T(8,128)(2,1)S(1)}, u32[]{:S(2)}, u32[]{:S(2)}) collective-permute-start(s16[128,768]{1,0:T(8,128)(2,1)S(1)} %collective-permute-done.9.refs_2_), channel_id=1, source_target_pairs={{0,2},{1,3},{2,0},{3,1},{4,6},{5,7},{6,4},{7,5},{8,10},{9,11},{10,... | collective-permute-start | bytes 589832 | tf_op jit(solution)/shard_map/ppermute | solution.py:144
  30.2 0.7 collective-permute-start.13
  30.9 3.0 %collective-permute-done.7.refs_0_ = s16[112,768]{1,0:T(8,128)(2,1)S(1)} collective-permute-done((s16[112,768]{1,0:T(8,128)(2,1)S(1)}, s16[112,768]{1,0:T(8,128)(2,1)S(1)}, u32[]{:S(2)}, u32[]{:S(2)}) %collective-permute-start.7) | collective-permute-done | bytes 172064 | tf_op jit(solution)/shard_map/ppermute | solution.py:144
  33.9 1.0 shard_map.144
  35.0 2.0 %collective-permute-start.1 = (s16[224,768]{1,0:T(8,128)(2,1)S(1)}, s16[224,768]{1,0:T(8,128)(2,1)S(1)}, u32[]{:S(2)}, u32[]{:S(2)}) collective-permute-start(s16[224,768]{1,0:T(8,128)(2,1)S(1)} %get-tuple-element.73), channel_id=1, source_target_pairs={{0,16},{16,0},{1,17},{17,1},{2,18},{18,2},{3,19},{19,3},{4,20},{20... | collective-permute-start | bytes 1032200 | tf_op jit(solution)/shard_map/ppermute | solution.py:148
  37.0 0.2 shard_map.147
  37.3 0.9 collective-permute-done.2.got
  38.2 1.3 %collective-permute-start.17 = (s16[112,768]{1,0:T(8,128)(2,1)S(1)}, s16[112,768]{1,0:T(8,128)(2,1)S(1)}, u32[]{:S(2)}, u32[]{:S(2)}) collective-permute-start(s16[112,768]{1,0:T(8,128)(2,1)S(1)} %shard_map.147), channel_id=1, source_target_pairs={{0,4},{4,0},{8,12},{12,8},{1,5},{5,1},{9,13},{13,9},{2,6},{6,2},{1... | collective-permute-start | bytes 516104 | tf_op jit(solution)/shard_map/ppermute | solution.py:152
  39.5 1.5 %collective-permute-start.15 = (s16[128,768]{1,0:T(8,128)(2,1)S(1)}, s16[128,768]{1,0:T(8,128)(2,1)S(1)}, u32[]{:S(2)}, u32[]{:S(2)}) collective-permute-start(s16[128,768]{1,0:T(8,128)(2,1)S(1)} %collective-permute-done.8.refs_6_), channel_id=1, source_target_pairs={{0,2},{1,3},{2,0},{3,1},{4,6},{5,7},{6,4},{7,5},{8,10},{9,11},{10,... | collective-permute-start | bytes 589832 | tf_op jit(solution)/shard_map/ppermute | solution.py:144
  41.0 1.0 shard_map.145
  42.0 0.6 collective-permute-start.14
  42.6 0.9 collective-permute-done.17.refs_1_
  43.6 0.4 shard_map.148
  44.0 3.4 %collective-permute-start.18 = (s16[112,768]{1,0:T(8,128)(2,1)S(1)}, s16[112,768]{1,0:T(8,128)(2,1)S(1)}, u32[]{:S(2)}, u32[]{:S(2)}) collective-permute-start(s16[112,768]{1,0:T(8,128)(2,1)S(1)} %shard_map.148), channel_id=1, source_target_pairs={{0,12},{4,8},{8,4},{12,0},{1,13},{5,9},{9,5},{13,1},{2,14},{6,10},... | collective-permute-start | bytes 516104 | tf_op jit(solution)/shard_map/ppermute | solution.py:152
  47.4 1.0 collective-permute-done.14.refs_0_
  48.4 1.0 shard_map.146
  49.5 1.3 %collective-permute-start.16 = (s16[112,768]{1,0:T(8,128)(2,1)S(1)}, s16[112,768]{1,0:T(8,128)(2,1)S(1)}, u32[]{:S(2)}, u32[]{:S(2)}) collective-permute-start(s16[112,768]{1,0:T(8,128)(2,1)S(1)} %get-tuple-element.98), channel_id=1, source_target_pairs={{0,2},{1,3},{2,0},{3,1},{4,6},{5,7},{6,4},{7,5},{8,10},{9,11},{10,... | collective-permute-start | bytes 516104 | tf_op jit(solution)/shard_map/ppermute | solution.py:144
  50.8 0.2 shard_map.149
  51.1 0.3 collective-permute-start.19
  51.4 0.7 collective-permute-done.18.far
  52.1 2.8 %collective-permute-done.16.got = s16[112,768]{1,0:T(8,128)(2,1)S(1)} collective-permute-done((s16[112,768]{1,0:T(8,128)(2,1)S(1)}, s16[112,768]{1,0:T(8,128)(2,1)S(1)}, u32[]{:S(2)}, u32[]{:S(2)}) %collective-permute-start.16) | collective-permute-done | bytes 172064 | tf_op jit(solution)/shard_map/ppermute | solution.py:144
  55.0 1.6 %collective-permute-done.19.near = s16[112,768]{1,0:T(8,128)(2,1)S(1)} collective-permute-done((s16[112,768]{1,0:T(8,128)(2,1)S(1)}, s16[112,768]{1,0:T(8,128)(2,1)S(1)}, u32[]{:S(2)}, u32[]{:S(2)}) %collective-permute-start.19) | collective-permute-done | bytes 172064 | tf_op jit(solution)/shard_map/ppermute | solution.py:152
  56.5 0.6 shard_map.150
  57.1 0.8 collective-permute-start.22
  58.0 2.6 %collective-permute-start.21 = (s16[112,768]{1,0:T(8,128)(2,1)S(1)}, s16[112,768]{1,0:T(8,128)(2,1)S(1)}, u32[]{:S(2)}, u32[]{:S(2)}) collective-permute-start(s16[112,768]{1,0:T(8,128)(2,1)S(1)} %get-tuple-element.106), channel_id=1, source_target_pairs={{0,12},{4,8},{8,4},{12,0},{1,13},{5,9},{9,5},{13,1},{2,14},{6,10},... | collective-permute-start | bytes 516104 | tf_op jit(solution)/shard_map/ppermute | solution.py:152
  60.6 1.3 %collective-permute-start.27 = (s16[128,768]{1,0:T(8,128)(2,1)S(1)}, s16[128,768]{1,0:T(8,128)(2,1)S(1)}, u32[]{:S(2)}, u32[]{:S(2)}) collective-permute-start(s16[128,768]{1,0:T(8,128)(2,1)S(1)} %collective-permute-done.13.refs_4_), channel_id=1, source_target_pairs={{0,2},{1,3},{2,0},{3,1},{4,6},{5,7},{6,4},{7,5},{8,10},{9,11},{10,... | collective-permute-start | bytes 589832 | tf_op jit(solution)/shard_map/ppermute | solution.py:144
  61.9 0.7 collective-permute-start.20
  62.6 3.5 %collective-permute-done.21.three = s16[112,768]{1,0:T(8,128)(2,1)S(1)} collective-permute-done((s16[112,768]{1,0:T(8,128)(2,1)S(1)}, s16[112,768]{1,0:T(8,128)(2,1)S(1)}, u32[]{:S(2)}, u32[]{:S(2)}) %collective-permute-start.21) | collective-permute-done | bytes 172064 | tf_op jit(solution)/shard_map/ppermute | solution.py:152
  66.1 1.9 %shard_map.153 = (f32[4,48,768]{2,1,0:T(8,128)}, f32[4,48,768]{2,1,0:T(8,128)}, f32[1,128]{1,0:T(1,128)S(1)}) custom-call(s32[12]{0:T(128)S(1)} %concatenate.3.meta, f32[96,768]{1,0:T(8,128)S(1)} %get-tuple-element.105.grad_ref.grad, f32[48,768]{1,0:T(8,128)S(1)} %collective-permute-done.28.got, f32[4,48,768]{2,1,0:T(8,128)S(1)} %copy-done, ...), custom_call_target="tpu_custom_call" | custom-call | flops 1000000000 | bytes 36000000 | tf_op jit(solution)/shard_map/pallas_call | solution.py:273
  68.0 1.9 %collective-permute-start.26 = (s16[112,768]{1,0:T(8,128)(2,1)S(1)}, s16[112,768]{1,0:T(8,128)(2,1)S(1)}, u32[]{:S(2)}, u32[]{:S(2)}) collective-permute-start(s16[112,768]{1,0:T(8,128)(2,1)S(1)} %collective-permute-done.21.three), channel_id=1, source_target_pairs={{0,2},{1,3},{2,0},{3,1},{4,6},{5,7},{6,4},{7,5},{8,10},{9,11},{10,... | collective-permute-start | bytes 516104 | tf_op jit(solution)/shard_map/ppermute | solution.py:144
  69.9 0.9 collective-permute-start.24
  70.8 2.0 %collective-permute-done.23.two = s16[112,768]{1,0:T(8,128)(2,1)S(1)} collective-permute-done((s16[112,768]{1,0:T(8,128)(2,1)S(1)}, s16[112,768]{1,0:T(8,128)(2,1)S(1)}, u32[]{:S(2)}, u32[]{:S(2)}) %collective-permute-start.23) | collective-permute-done | bytes 172064 | tf_op jit(solution)/shard_map/ppermute | solution.py:152
  72.7 1.3 %collective-permute-start.25 = (s16[112,768]{1,0:T(8,128)(2,1)S(1)}, s16[112,768]{1,0:T(8,128)(2,1)S(1)}, u32[]{:S(2)}, u32[]{:S(2)}) collective-permute-start(s16[112,768]{1,0:T(8,128)(2,1)S(1)} %collective-permute-done.23.two), channel_id=1, source_target_pairs={{0,2},{1,3},{2,0},{3,1},{4,6},{5,7},{6,4},{7,5},{8,10},{9,11},{10,... | collective-permute-start | bytes 516104 | tf_op jit(solution)/shard_map/ppermute | solution.py:144
  74.1 1.5 %shard_map.152 = (bf16[768,768]{1,0:T(8,128)(2,1)S(1)}, bf16[768,768]{1,0:T(8,128)(2,1)S(1)}) custom-call(s32[12]{0:T(128)S(1)} %concatenate.3.meta, s16[128,768]{1,0:T(8,128)(2,1)S(1)} %get-tuple-element.87.refs_0_, s16[128,768]{1,0:T(8,128)(2,1)S(1)} %collective-permute-done.10.refs_1_, s16[128,768]{1,0:T(8,128)(2,1)S(1)} %collective-permute-done.9.refs_2_, ...), custom_call_target="tpu_custom_call" | custom-call | flops 1000000000 | bytes 36000000 | tf_op jit(solution)/shard_map/pallas_call | solution.py:273
  75.6 1.1 %shard_map.151 = (bf16[768,768]{1,0:T(8,128)(2,1)S(1)}, bf16[768,768]{1,0:T(8,128)(2,1)S(1)}) custom-call(s32[12]{0:T(128)S(1)} %concatenate.3.meta, f32[96,768]{1,0:T(8,128)S(1)} %get-tuple-element.105.grad_ref.grad, s16[112,768]{1,0:T(8,128)(2,1)S(1)} %collective-permute-done.20.one, s16[112,768]{1,0:T(8,128)(2,1)S(1)} %collective-permute-done.23.two, ...), custom_call_target="tpu_custom_call" | custom-call | flops 1000000000 | bytes 36000000 | tf_op jit(solution)/shard_map/pallas_call | solution.py:273
  76.8 2.0 %collective-permute-done.24.refs_1_ = s16[112,768]{1,0:T(8,128)(2,1)S(1)} collective-permute-done((s16[112,768]{1,0:T(8,128)(2,1)S(1)}, s16[112,768]{1,0:T(8,128)(2,1)S(1)}, u32[]{:S(2)}, u32[]{:S(2)}) %collective-permute-start.24) | collective-permute-done | bytes 172064 | tf_op jit(solution)/shard_map/ppermute | solution.py:144
  78.8 1.8 %collective-permute-done.25.refs_2_ = s16[112,768]{1,0:T(8,128)(2,1)S(1)} collective-permute-done((s16[112,768]{1,0:T(8,128)(2,1)S(1)}, s16[112,768]{1,0:T(8,128)(2,1)S(1)}, u32[]{:S(2)}, u32[]{:S(2)}) %collective-permute-start.25) | collective-permute-done | bytes 172064 | tf_op jit(solution)/shard_map/ppermute | solution.py:144
  80.6 3.4 %shard_map.154 = (f32[48,768]{1,0:T(8,128)S(1)}, f32[48,768]{1,0:T(8,128)S(1)}, f32[1,128]{1,0:T(1,128)S(1)}, bf16[768,768]{1,0:T(8,128)(2,1)S(1)}, bf16[768,768]{1,0:T(8,128)(2,1)S(1)}) custom-call(s32[12]{0:T(128)S(1)} %concatenate.3.meta, bf16[768,768]{1,0:T(8,128)(2,1)S(1)} %get-tuple-element.108.high_in, ...), custom_call_target="tpu_custom_call" | custom-call | flops 4000000000 | bytes 144000000 | tf_op jit(solution)/shard_map/pallas_call | solution.py:273
  84.1 10.4 %all_to_all.5.sums = f32[16,1,128]{2,1,0:T(1,128)S(1)} all-to-all(f32[16,1,128]{2,1,0:T(1,128)S(1)} %broadcast_in_dim.9), channel_id=1, replica_groups=mesh['shard'=2,'tensor'=4,'section'=4] {'tensor','section'}, dimensions={0} | all-to-all | bytes 16384 | tf_op jit(solution)/shard_map/all_to_all | solution.py:710
  94.5 0.7 shard_map.155.near
  95.2 1.6 %collective-permute-start.31 = (bf16[2,48,768]{2,1,0:T(8,128)(2,1)S(1)}, bf16[2,48,768]{2,1,0:T(8,128)(2,1)S(1)}, u32[]{:S(2)}, u32[]{:S(2)}) collective-permute-start(bf16[2,48,768]{2,1,0:T(8,128)(2,1)S(1)} %shard_map.155.near), channel_id=1, source_target_pairs={{0,16},{16,0},{1,17},{17,1},{2,18},{18,2},{3,19},{19,3},{4,20},{20... | collective-permute-start | bytes 442376 | tf_op jit(solution)/shard_map/ppermute | solution.py:148
  96.8 1.8 %shard_map.156 = (f32[48,768]{1,0:T(8,128)S(1)}, f32[48,768]{1,0:T(8,128)S(1)}) custom-call(s32[12]{0:T(128)S(1)} %concatenate.3.meta, f32[96,768]{1,0:T(8,128)S(1)} %get-tuple-element.105.grad_ref.grad, bf16[768,768]{1,0:T(8,128)(2,1)S(1)} %get-tuple-element.124.high_ref, bf16[768,768]{1,0:T(8,128)(2,1)S(1)} %get-tuple-element.125.low_ref), custom_call_target="tpu_custom_call" | custom-call | flops 1400000000 | bytes 50400000 | tf_op jit(solution)/shard_map/pallas_call | solution.py:273
  98.7 2.0 %shard_map.158 = (f32[48,768]{1,0:T(8,128)S(1)}, f32[48,768]{1,0:T(8,128)S(1)}) custom-call(s32[12]{0:T(128)S(1)} %concatenate.3.meta, bf16[768,768]{1,0:T(8,128)(2,1)S(1)} %get-tuple-element.124.high_ref, bf16[768,768]{1,0:T(8,128)(2,1)S(1)} %get-tuple-element.125.low_ref), custom_call_target="tpu_custom_call" | custom-call | flops 1800000000 | bytes 64800000 | tf_op jit(solution)/shard_map/pallas_call | solution.py:273
  100.7 0.6 collective-permute-start.32
  101.2 1.3 %shard_map.157 = bf16[4,48,768]{2,1,0:T(8,128)(2,1)} custom-call(s32[12]{0:T(128)S(1)} %concatenate.3.meta, bf16[2,48,768]{2,1,0:T(8,128)(2,1)S(1)} %shard_map.155.near, bf16[2,48,768]{2,1,0:T(8,128)(2,1)S(1)} %collective-permute-done.31.mirror), custom_call_target="tpu_custom_call" | custom-call | flops 1000000000 | bytes 36000000 | tf_op jit(solution)/shard_map/pallas_call | solution.py:273
  102.6 1.7 %shard_map.159 = (f32[4,48,768]{2,1,0:T(8,128)}, f32[4,48,768]{2,1,0:T(8,128)}) custom-call(s32[12]{0:T(128)S(1)} %concatenate.3.meta, f32[48,768]{1,0:T(8,128)S(1)} %get-tuple-element.129.own_right, f32[48,768]{1,0:T(8,128)S(1)} %collective-permute-done.32.got_right, f32[48,768]{1,0:T(8,128)S(1)} %get-tuple-element.131.own_left, ...), custom_call_target="tpu_custom_call" | custom-call | flops 1000000000 | bytes 36000000 | tf_op jit(solution)/shard_map/pallas_call | solution.py:273
  (39 shorter events, 0.8 us)
Async XLA Ops:
  4.7 3.6 %collective-permute-start = (bf16[2,512,768]{2,1,0:T(8,128)(2,1)S(1)}, bf16[2,512,768]{2,1,0:T(8,128)(2,1)S(1)}, u32[]{:S(2)}, u32[]{:S(2)}) collective-permute-start(bf16[2,512,768]{2,1,0:T(8,128)(2,1)S(1)} %get-tuple-element.71), channel_id=1, source_target_pairs={{0,1},{1,0},{2,3},{3,2},{4,5},{5,4},{6,7},{7,6},{8,9},{9,8},{10,11... | collective-permute-start | bytes 4718600 | tf_op jit(solution)/shard_map/ppermute | solution.py:140
  5.2 14.9 %collective-permute-start.6 = (bf16[2,512,768]{2,1,0:T(8,128)(2,1)S(1)}, bf16[2,512,768]{2,1,0:T(8,128)(2,1)S(1)}, u32[]{:S(2)}, u32[]{:S(2)}) collective-permute-start(bf16[2,512,768]{2,1,0:T(8,128)(2,1)S(1)} %get-tuple-element.79), channel_id=1, source_target_pairs={{0,1},{1,0},{2,3},{3,2},{4,5},{5,4},{6,7},{7,6},{8,9},{9,8},{10,11... | collective-permute-start | bytes 4718600 | tf_op jit(solution)/shard_map/ppermute | solution.py:140
  5.3 5.6 %collective-permute-start.4 = (f32[2,48,768]{2,1,0:T(8,128)S(1)}, f32[2,48,768]{2,1,0:T(8,128)S(1)}, u32[]{:S(2)}, u32[]{:S(2)}) collective-permute-start(f32[2,48,768]{2,1,0:T(8,128)S(1)} %get-tuple-element.77), channel_id=1, source_target_pairs={{0,1},{1,0},{2,3},{3,2},{4,5},{5,4},{6,7},{7,6},{8,9},{9,8},{10,11... | collective-permute-start | bytes 884744 | tf_op jit(solution)/shard_map/ppermute | solution.py:140
  10.9 14.6 %collective-permute-start.5 = (s16[224,768]{1,0:T(8,128)(2,1)S(1)}, s16[224,768]{1,0:T(8,128)(2,1)S(1)}, u32[]{:S(2)}, u32[]{:S(2)}) collective-permute-start(s16[224,768]{1,0:T(8,128)(2,1)S(1)} %get-tuple-element.78), channel_id=1, source_target_pairs={{0,16},{16,0},{1,17},{17,1},{2,18},{18,2},{3,19},{19,3},{4,20},{20... | collective-permute-start | bytes 1032200 | tf_op jit(solution)/shard_map/ppermute | solution.py:148
  15.5 11.7 %collective-permute-start.9 = (s16[128,768]{1,0:T(8,128)(2,1)S(1)}, s16[128,768]{1,0:T(8,128)(2,1)S(1)}, u32[]{:S(2)}, u32[]{:S(2)}) collective-permute-start(s16[128,768]{1,0:T(8,128)(2,1)S(1)} %get-tuple-element.87.refs_0_), channel_id=1, source_target_pairs={{0,4},{4,0},{8,12},{12,8},{1,5},{5,1},{9,13},{13,9},{2,6},{6,2},{1... | collective-permute-start | bytes 589832 | tf_op jit(solution)/shard_map/ppermute | solution.py:152
  17.1 11.5 %collective-permute-start.8 = (s16[128,768]{1,0:T(8,128)(2,1)S(1)}, s16[128,768]{1,0:T(8,128)(2,1)S(1)}, u32[]{:S(2)}, u32[]{:S(2)}) collective-permute-start(s16[128,768]{1,0:T(8,128)(2,1)S(1)} %get-tuple-element.87.refs_0_), channel_id=1, source_target_pairs={{0,12},{4,8},{8,4},{12,0},{1,13},{5,9},{9,5},{13,1},{2,14},{6,10},... | collective-permute-start | bytes 589832 | tf_op jit(solution)/shard_map/ppermute | solution.py:152
  19.6 11.3 %collective-permute-start.3 = (s16[224,768]{1,0:T(8,128)(2,1)S(1)}, s16[224,768]{1,0:T(8,128)(2,1)S(1)}, u32[]{:S(2)}, u32[]{:S(2)}) collective-permute-start(s16[224,768]{1,0:T(8,128)(2,1)S(1)} %get-tuple-element.75), channel_id=1, source_target_pairs={{0,16},{16,0},{1,17},{17,1},{2,18},{18,2},{3,19},{19,3},{4,20},{20... | collective-permute-start | bytes 1032200 | tf_op jit(solution)/shard_map/ppermute | solution.py:148
  20.1 8.6 %collective-permute-start.10 = (s16[128,768]{1,0:T(8,128)(2,1)S(1)}, s16[128,768]{1,0:T(8,128)(2,1)S(1)}, u32[]{:S(2)}, u32[]{:S(2)}) collective-permute-start(s16[128,768]{1,0:T(8,128)(2,1)S(1)} %get-tuple-element.87.refs_0_), channel_id=1, source_target_pairs={{0,2},{1,3},{2,0},{3,1},{4,6},{5,7},{6,4},{7,5},{8,10},{9,11},{10,... | collective-permute-start | bytes 589832 | tf_op jit(solution)/shard_map/ppermute | solution.py:144
  26.6 7.3 %collective-permute-start.7 = (s16[112,768]{1,0:T(8,128)(2,1)S(1)}, s16[112,768]{1,0:T(8,128)(2,1)S(1)}, u32[]{:S(2)}, u32[]{:S(2)}) collective-permute-start(s16[112,768]{1,0:T(8,128)(2,1)S(1)} %get-tuple-element.85), channel_id=1, source_target_pairs={{0,2},{1,3},{2,0},{3,1},{4,6},{5,7},{6,4},{7,5},{8,10},{9,11},{10,... | collective-permute-start | bytes 516104 | tf_op jit(solution)/shard_map/ppermute | solution.py:144
  27.2 11.0 %collective-permute-start.2 = (s16[224,768]{1,0:T(8,128)(2,1)S(1)}, s16[224,768]{1,0:T(8,128)(2,1)S(1)}, u32[]{:S(2)}, u32[]{:S(2)}) collective-permute-start(s16[224,768]{1,0:T(8,128)(2,1)S(1)} %get-tuple-element.74), channel_id=1, source_target_pairs={{0,16},{16,0},{1,17},{17,1},{2,18},{18,2},{3,19},{19,3},{4,20},{20... | collective-permute-start | bytes 1032200 | tf_op jit(solution)/shard_map/ppermute | solution.py:148
  28.7 10.8 %collective-permute-start.12 = (s16[128,768]{1,0:T(8,128)(2,1)S(1)}, s16[128,768]{1,0:T(8,128)(2,1)S(1)}, u32[]{:S(2)}, u32[]{:S(2)}) collective-permute-start(s16[128,768]{1,0:T(8,128)(2,1)S(1)} %collective-permute-done.9.refs_2_), channel_id=1, source_target_pairs={{0,2},{1,3},{2,0},{3,1},{4,6},{5,7},{6,4},{7,5},{8,10},{9,11},{10,... | collective-permute-start | bytes 589832 | tf_op jit(solution)/shard_map/ppermute | solution.py:144
  30.2 10.8 %collective-permute-start.13 = (s16[128,768]{1,0:T(8,128)(2,1)S(1)}, s16[128,768]{1,0:T(8,128)(2,1)S(1)}, u32[]{:S(2)}, u32[]{:S(2)}) collective-permute-start(s16[128,768]{1,0:T(8,128)(2,1)S(1)} %collective-permute-done.8.refs_6_), channel_id=1, source_target_pairs={{0,4},{4,0},{8,12},{12,8},{1,5},{5,1},{9,13},{13,9},{2,6},{6,2},{1... | collective-permute-start | bytes 589832 | tf_op jit(solution)/shard_map/ppermute | solution.py:152
  34.9 6.1 %collective-permute-start.11 = (s16[112,768]{1,0:T(8,128)(2,1)S(1)}, s16[112,768]{1,0:T(8,128)(2,1)S(1)}, u32[]{:S(2)}, u32[]{:S(2)}) collective-permute-start(s16[112,768]{1,0:T(8,128)(2,1)S(1)} %get-tuple-element.90), channel_id=1, source_target_pairs={{0,2},{1,3},{2,0},{3,1},{4,6},{5,7},{6,4},{7,5},{8,10},{9,11},{10,... | collective-permute-start | bytes 516104 | tf_op jit(solution)/shard_map/ppermute | solution.py:144
  35.0 12.4 %collective-permute-start.1 = (s16[224,768]{1,0:T(8,128)(2,1)S(1)}, s16[224,768]{1,0:T(8,128)(2,1)S(1)}, u32[]{:S(2)}, u32[]{:S(2)}) collective-permute-start(s16[224,768]{1,0:T(8,128)(2,1)S(1)} %get-tuple-element.73), channel_id=1, source_target_pairs={{0,16},{16,0},{1,17},{17,1},{2,18},{18,2},{3,19},{19,3},{4,20},{20... | collective-permute-start | bytes 1032200 | tf_op jit(solution)/shard_map/ppermute | solution.py:148
  38.2 5.4 %collective-permute-start.17 = (s16[112,768]{1,0:T(8,128)(2,1)S(1)}, s16[112,768]{1,0:T(8,128)(2,1)S(1)}, u32[]{:S(2)}, u32[]{:S(2)}) collective-permute-start(s16[112,768]{1,0:T(8,128)(2,1)S(1)} %shard_map.147), channel_id=1, source_target_pairs={{0,4},{4,0},{8,12},{12,8},{1,5},{5,1},{9,13},{13,9},{2,6},{6,2},{1... | collective-permute-start | bytes 516104 | tf_op jit(solution)/shard_map/ppermute | solution.py:152
  39.5 7.9 %collective-permute-start.15 = (s16[128,768]{1,0:T(8,128)(2,1)S(1)}, s16[128,768]{1,0:T(8,128)(2,1)S(1)}, u32[]{:S(2)}, u32[]{:S(2)}) collective-permute-start(s16[128,768]{1,0:T(8,128)(2,1)S(1)} %collective-permute-done.8.refs_6_), channel_id=1, source_target_pairs={{0,2},{1,3},{2,0},{3,1},{4,6},{5,7},{6,4},{7,5},{8,10},{9,11},{10,... | collective-permute-start | bytes 589832 | tf_op jit(solution)/shard_map/ppermute | solution.py:144
  42.0 6.4 %collective-permute-start.14 = (s16[112,768]{1,0:T(8,128)(2,1)S(1)}, s16[112,768]{1,0:T(8,128)(2,1)S(1)}, u32[]{:S(2)}, u32[]{:S(2)}) collective-permute-start(s16[112,768]{1,0:T(8,128)(2,1)S(1)} %get-tuple-element.94), channel_id=1, source_target_pairs={{0,2},{1,3},{2,0},{3,1},{4,6},{5,7},{6,4},{7,5},{8,10},{9,11},{10,... | collective-permute-start | bytes 516104 | tf_op jit(solution)/shard_map/ppermute | solution.py:144
  44.0 8.1 %collective-permute-start.18 = (s16[112,768]{1,0:T(8,128)(2,1)S(1)}, s16[112,768]{1,0:T(8,128)(2,1)S(1)}, u32[]{:S(2)}, u32[]{:S(2)}) collective-permute-start(s16[112,768]{1,0:T(8,128)(2,1)S(1)} %shard_map.148), channel_id=1, source_target_pairs={{0,12},{4,8},{8,4},{12,0},{1,13},{5,9},{9,5},{13,1},{2,14},{6,10},... | collective-permute-start | bytes 516104 | tf_op jit(solution)/shard_map/ppermute | solution.py:152
  49.5 5.5 %collective-permute-start.16 = (s16[112,768]{1,0:T(8,128)(2,1)S(1)}, s16[112,768]{1,0:T(8,128)(2,1)S(1)}, u32[]{:S(2)}, u32[]{:S(2)}) collective-permute-start(s16[112,768]{1,0:T(8,128)(2,1)S(1)} %get-tuple-element.98), channel_id=1, source_target_pairs={{0,2},{1,3},{2,0},{3,1},{4,6},{5,7},{6,4},{7,5},{8,10},{9,11},{10,... | collective-permute-start | bytes 516104 | tf_op jit(solution)/shard_map/ppermute | solution.py:144
  51.1 5.5 %collective-permute-start.19 = (s16[112,768]{1,0:T(8,128)(2,1)S(1)}, s16[112,768]{1,0:T(8,128)(2,1)S(1)}, u32[]{:S(2)}, u32[]{:S(2)}) collective-permute-start(s16[112,768]{1,0:T(8,128)(2,1)S(1)} %shard_map.149), channel_id=1, source_target_pairs={{0,4},{4,0},{8,12},{12,8},{1,5},{5,1},{9,13},{13,9},{2,6},{6,2},{1... | collective-permute-start | bytes 516104 | tf_op jit(solution)/shard_map/ppermute | solution.py:152
  56.5 9.6 %copy-start = (f32[4,48,768]{2,1,0:T(8,128)S(1)}, f32[4,48,768]{2,1,0:T(8,128)}, u32[]{:S(2)}) copy-start(f32[4,48,768]{2,1,0:T(8,128)} %first.1) | copy-start | bytes 1769476
  56.5 9.6 %copy-start.1 = (f32[4,48,768]{2,1,0:T(8,128)S(1)}, f32[4,48,768]{2,1,0:T(8,128)}, u32[]{:S(2)}) copy-start(f32[4,48,768]{2,1,0:T(8,128)} %second.1) | copy-start | bytes 1769476
  57.1 5.5 %collective-permute-start.22 = (s16[112,768]{1,0:T(8,128)(2,1)S(1)}, s16[112,768]{1,0:T(8,128)(2,1)S(1)}, u32[]{:S(2)}, u32[]{:S(2)}) collective-permute-start(s16[112,768]{1,0:T(8,128)(2,1)S(1)} %get-tuple-element.106), channel_id=1, source_target_pairs={{0,2},{1,3},{2,0},{3,1},{4,6},{5,7},{6,4},{7,5},{8,10},{9,11},{10,... | collective-permute-start | bytes 516104 | tf_op jit(solution)/shard_map/ppermute | solution.py:144
  58.0 8.2 %collective-permute-start.21 = (s16[112,768]{1,0:T(8,128)(2,1)S(1)}, s16[112,768]{1,0:T(8,128)(2,1)S(1)}, u32[]{:S(2)}, u32[]{:S(2)}) collective-permute-start(s16[112,768]{1,0:T(8,128)(2,1)S(1)} %get-tuple-element.106), channel_id=1, source_target_pairs={{0,12},{4,8},{8,4},{12,0},{1,13},{5,9},{9,5},{13,1},{2,14},{6,10},... | collective-permute-start | bytes 516104 | tf_op jit(solution)/shard_map/ppermute | solution.py:152
  60.5 5.6 %collective-permute-start.28 = (f32[48,768]{1,0:T(8,128)S(1)}, f32[48,768]{1,0:T(8,128)S(1)}, u32[]{:S(2)}, u32[]{:S(2)}) collective-permute-start(f32[48,768]{1,0:T(8,128)S(1)} %constant_dynamic-slice_fusion), channel_id=1, source_target_pairs={{0,1},{1,0},{2,3},{3,2},{4,5},{5,4},{6,7},{7,6},{8,9},{9,8},{10,11... | collective-permute-start | bytes 442376 | tf_op jit(solution)/shard_map/ppermute | solution.py:140
  60.6 13.5 %collective-permute-start.27 = (s16[128,768]{1,0:T(8,128)(2,1)S(1)}, s16[128,768]{1,0:T(8,128)(2,1)S(1)}, u32[]{:S(2)}, u32[]{:S(2)}) collective-permute-start(s16[128,768]{1,0:T(8,128)(2,1)S(1)} %collective-permute-done.13.refs_4_), channel_id=1, source_target_pairs={{0,2},{1,3},{2,0},{3,1},{4,6},{5,7},{6,4},{7,5},{8,10},{9,11},{10,... | collective-permute-start | bytes 589832 | tf_op jit(solution)/shard_map/ppermute | solution.py:144
  61.9 8.0 %collective-permute-start.20 = (s16[112,768]{1,0:T(8,128)(2,1)S(1)}, s16[112,768]{1,0:T(8,128)(2,1)S(1)}, u32[]{:S(2)}, u32[]{:S(2)}) collective-permute-start(s16[112,768]{1,0:T(8,128)(2,1)S(1)} %get-tuple-element.106), channel_id=1, source_target_pairs={{0,4},{4,0},{8,12},{12,8},{1,5},{5,1},{9,13},{13,9},{2,6},{6,2},{1... | collective-permute-start | bytes 516104 | tf_op jit(solution)/shard_map/ppermute | solution.py:152
  66.1 6.6 %collective-permute-start.23 = (s16[112,768]{1,0:T(8,128)(2,1)S(1)}, s16[112,768]{1,0:T(8,128)(2,1)S(1)}, u32[]{:S(2)}, u32[]{:S(2)}) collective-permute-start(s16[112,768]{1,0:T(8,128)(2,1)S(1)} %collective-permute-done.21.three), channel_id=1, source_target_pairs={{0,4},{4,0},{8,12},{12,8},{1,5},{5,1},{9,13},{13,9},{2,6},{6,2},{1... | collective-permute-start | bytes 516104 | tf_op jit(solution)/shard_map/ppermute | solution.py:152
  68.0 8.8 %collective-permute-start.26 = (s16[112,768]{1,0:T(8,128)(2,1)S(1)}, s16[112,768]{1,0:T(8,128)(2,1)S(1)}, u32[]{:S(2)}, u32[]{:S(2)}) collective-permute-start(s16[112,768]{1,0:T(8,128)(2,1)S(1)} %collective-permute-done.21.three), channel_id=1, source_target_pairs={{0,2},{1,3},{2,0},{3,1},{4,6},{5,7},{6,4},{7,5},{8,10},{9,11},{10,... | collective-permute-start | bytes 516104 | tf_op jit(solution)/shard_map/ppermute | solution.py:144
  69.9 8.9 %collective-permute-start.24 = (s16[112,768]{1,0:T(8,128)(2,1)S(1)}, s16[112,768]{1,0:T(8,128)(2,1)S(1)}, u32[]{:S(2)}, u32[]{:S(2)}) collective-permute-start(s16[112,768]{1,0:T(8,128)(2,1)S(1)} %collective-permute-done.20.one), channel_id=1, source_target_pairs={{0,2},{1,3},{2,0},{3,1},{4,6},{5,7},{6,4},{7,5},{8,10},{9,11},{10,... | collective-permute-start | bytes 516104 | tf_op jit(solution)/shard_map/ppermute | solution.py:144
  72.7 7.9 %collective-permute-start.25 = (s16[112,768]{1,0:T(8,128)(2,1)S(1)}, s16[112,768]{1,0:T(8,128)(2,1)S(1)}, u32[]{:S(2)}, u32[]{:S(2)}) collective-permute-start(s16[112,768]{1,0:T(8,128)(2,1)S(1)} %collective-permute-done.23.two), channel_id=1, source_target_pairs={{0,2},{1,3},{2,0},{3,1},{4,6},{5,7},{6,4},{7,5},{8,10},{9,11},{10,... | collective-permute-start | bytes 516104 | tf_op jit(solution)/shard_map/ppermute | solution.py:144
  80.6 13.9 %copy-start.4 = (bf16[4,48,768]{2,1,0:T(8,128)(2,1)S(1)}, bf16[4,48,768]{2,1,0:T(8,128)(2,1)}, u32[]{:S(2)}) copy-start(bf16[4,48,768]{2,1,0:T(8,128)(2,1)} %weights.1) | copy-start | bytes 884740
  84.0 10.5 %collective-permute-start.29 = (f32[48,768]{1,0:T(8,128)S(1)}, f32[48,768]{1,0:T(8,128)S(1)}, u32[]{:S(2)}, u32[]{:S(2)}) collective-permute-start(f32[48,768]{1,0:T(8,128)S(1)} %get-tuple-element.123), channel_id=1, source_target_pairs={{0,1},{1,0},{2,3},{3,2},{4,5},{5,4},{6,7},{7,6},{8,9},{9,8},{10,11... | collective-permute-start | bytes 442376 | tf_op jit(solution)/shard_map/ppermute | solution.py:140
  95.2 6.0 %collective-permute-start.31 = (bf16[2,48,768]{2,1,0:T(8,128)(2,1)S(1)}, bf16[2,48,768]{2,1,0:T(8,128)(2,1)S(1)}, u32[]{:S(2)}, u32[]{:S(2)}) collective-permute-start(bf16[2,48,768]{2,1,0:T(8,128)(2,1)S(1)} %shard_map.155.near), channel_id=1, source_target_pairs={{0,16},{16,0},{1,17},{17,1},{2,18},{18,2},{3,19},{19,3},{4,20},{20... | collective-permute-start | bytes 442376 | tf_op jit(solution)/shard_map/ppermute | solution.py:148
  98.6 4.0 %collective-permute-start.30 = (f32[48,768]{1,0:T(8,128)S(1)}, f32[48,768]{1,0:T(8,128)S(1)}, u32[]{:S(2)}, u32[]{:S(2)}) collective-permute-start(f32[48,768]{1,0:T(8,128)S(1)} %get-tuple-element.126), channel_id=1, source_target_pairs={{0,1},{1,0},{2,3},{3,2},{4,5},{5,4},{6,7},{7,6},{8,9},{9,8},{10,11... | collective-permute-start | bytes 442376 | tf_op jit(solution)/shard_map/ppermute | solution.py:140
  100.6 1.9 %copy-start.2 = (f32[4,48,768]{2,1,0:T(8,128)S(1)}, f32[4,48,768]{2,1,0:T(8,128)}, u32[]{:S(2)}) copy-start(f32[4,48,768]{2,1,0:T(8,128)} %right.5) | copy-start | bytes 1769476
  100.7 1.9 %copy-start.3 = (f32[4,48,768]{2,1,0:T(8,128)S(1)}, f32[4,48,768]{2,1,0:T(8,128)}, u32[]{:S(2)}) copy-start(f32[4,48,768]{2,1,0:T(8,128)} %left.5) | copy-start | bytes 1769476
  100.7 1.9 %collective-permute-start.32 = (f32[48,768]{1,0:T(8,128)S(1)}, f32[48,768]{1,0:T(8,128)S(1)}, u32[]{:S(2)}, u32[]{:S(2)}) collective-permute-start(f32[48,768]{1,0:T(8,128)S(1)} %get-tuple-element.130), channel_id=1, source_target_pairs={{0,1},{1,0},{2,3},{3,2},{4,5},{5,4},{6,7},{7,6},{8,9},{9,8},{10,11... | collective-permute-start | bytes 442376 | tf_op jit(solution)/shard_map/ppermute | solution.py:140

commit v7 on v6

--- a/solution.py
+++ b/solution.py
@@ -639,9 +639,7 @@
                 (arrived, got_x[1], root_x[1], root_z[2])
             )
         if index == 3:
-            arrived, got_x[2], root_x[3] = lax.optimization_barrier(
-                (arrived, got_x[2], root_x[3])
-            )
+            arrived, root_x[3] = lax.optimization_barrier((arrived, root_x[3]))
         sent, keep = after_y(meta, arrived, mine, bits)
         got_x.append(to_x(sent))
         keeps.append(keep)

time: 104 us -> 103 us (level)
    ppermute x9, starting transfers between devices: 13.1 us -> 12.1 us  [to_z(): return lax.ppermute(value, 'tensor', [(i, i ^ bits) for i in range(4)])]
  transfers between devices with their start and end apart: 33 -> 33, of which waited for: 14 -> 13; matrix products, arithmetic and copies ran while one was open for 0% -> 0% of each run, Pallas kernels for 23% -> 23%
where the time goes in v7:
time: 103 us
  starting transfers between devices  36.3 us (35%)
  Pallas kernels  33.2 us (32%)
  waiting for transfers between devices  21.7 us (21%)
  blocking collectives  10.3 us (10%)
    pallas_call x19, Pallas kernels, call(): pl.pallas_call(body, out_shape=outs, in_specs=ins, out_specs=[VMEM_SPEC]...  29 us
    ppermute x12, starting transfers between devices, to_x(): return lax.ppermute(value, 'section', [(i, i ^ 2) for i in range(4)])  13.9 us
    ppermute x9, starting transfers between devices, to_z(): return lax.ppermute(value, 'tensor', [(i, i ^ bits) for i in range(4)])  12.1 us
    all_to_all x1, blocking collectives, two_planes(): sums = lax.all_to_all(sums, GROUP, 0, 0)  10.3 us
    ppermute x12, waiting for transfers between devices, to_x(): return lax.ppermute(value, 'section', [(i, i ^ 2) for i in range(4)])  9.87 us
    ppermute x9, waiting for transfers between devices, to_z(): return lax.ppermute(value, 'tensor', [(i, i ^ bits) for i in range(4)])  8.94 us
    ppermute x5, starting transfers between devices, to_y(): return lax.ppermute(value, 'shard', [(0, 1), (1, 0)])  8.53 us
    pallas_call x4, Pallas kernels, after_y(): pl.pallas_call(y_kernel, out_shape=[jax.ShapeDtypeStruct((coded_rows(rows...  4.16 us
  transfers between devices with their start and end apart: 33, of which 13 were waited for; matrix products, arithmetic and copies ran while one was open for 0% of the time, Pallas kernels for 23%

profile of v7, /device:TPU:0, one launch (start us, length us, event | category | flops | bytes accessed | tf_op | source)
XLA Modules:
  0.0 103.1 jit_solution(14496813815264103671)
XLA Ops:
  0.7 0.7 concatenate.3.meta
  1.4 3.3 %shard_map.137 = (bf16[2,512,768]{2,1,0:T(8,128)(2,1)S(1)}, bf16[2,512,768]{2,1,0:T(8,128)(2,1)S(1)}, f32[2,48,768]{2,1,0:T(8,128)S(1)}, bf16[2,512,768]{2,1,0:T(8,128)(2,1)S(1)}) custom-call(s32[12]{0:T(128)S(1)} %concatenate.3.meta, bf16[4,512,768]{2,1,0:T(8,128)(2,1)} %xin.3, bf16[4,512,768]{2,1,0:T(8,128)(2,1)} %dout.3, f32[4,48,768]{2,1,0:T(8,128)} %left.4, ...), custom_call_target="tpu_custom_call" | custom-call | flops 1000000000 | bytes 36000000 | tf_op jit(solution)/shard_map/pallas_call | solution.py:273
  4.7 0.5 collective-permute-start
  5.2 0.1 collective-permute-start.5
  5.3 0.4 collective-permute-start.3
  5.7 0.8 shard_map.138.own_ref
  6.5 1.7 %collective-permute-done.got = bf16[2,512,768]{2,1,0:T(8,128)(2,1)S(1)} collective-permute-done((bf16[2,512,768]{2,1,0:T(8,128)(2,1)S(1)}, bf16[2,512,768]{2,1,0:T(8,128)(2,1)S(1)}, u32[]{:S(2)}, u32[]{:S(2)}) %collective-permute-start) | collective-permute-done | bytes 1572896 | tf_op jit(solution)/shard_map/ppermute | solution.py:140
  8.2 2.4 %shard_map.139 = (s16[224,768]{1,0:T(8,128)(2,1)S(1)}, s16[224,768]{1,0:T(8,128)(2,1)S(1)}, s16[224,768]{1,0:T(8,128)(2,1)S(1)}, s16[224,768]{1,0:T(8,128)(2,1)S(1)}) custom-call(s32[12]{0:T(128)S(1)} %concatenate.3.meta, bf16[2,512,768]{2,1,0:T(8,128)(2,1)S(1)} %collective-permute-done.got, f32[768,768]{1,0:T(8,128)S(1)} %shard_map.138.own_ref), custom_call_target="tpu_custom_call" | custom-call | flops 1000000000 | bytes 36000000 | tf_op jit(solution)/shard_map/pallas_call | solution.py:273
  10.7 0.2 collective-permute-done.3.got
  10.9 2.9 %collective-permute-start.4 = (s16[224,768]{1,0:T(8,128)(2,1)S(1)}, s16[224,768]{1,0:T(8,128)(2,1)S(1)}, u32[]{:S(2)}, u32[]{:S(2)}) collective-permute-start(s16[224,768]{1,0:T(8,128)(2,1)S(1)} %get-tuple-element.76), channel_id=1, source_target_pairs={{0,16},{16,0},{1,17},{17,1},{2,18},{18,2},{3,19},{19,3},{4,20},{20... | collective-permute-start | bytes 1032200 | tf_op jit(solution)/shard_map/ppermute | solution.py:148
  13.8 1.7 %shard_map.140 = (f32[96,768]{1,0:T(8,128)S(1)}, s16[128,768]{1,0:T(8,128)(2,1)S(1)}) custom-call(s32[12]{0:T(128)S(1)} %concatenate.3.meta, f32[4,48,768]{2,1,0:T(8,128)} %left.4, f32[4,48,768]{2,1,0:T(8,128)} %right.4, f32[2,48,768]{2,1,0:T(8,128)S(1)} %collective-permute-done.3.got), custom_call_target="tpu_custom_call" | custom-call | flops 1000000000 | bytes 36000000 | tf_op jit(solution)/shard_map/pallas_call | solution.py:273
  15.5 1.6 %collective-permute-start.8 = (s16[128,768]{1,0:T(8,128)(2,1)S(1)}, s16[128,768]{1,0:T(8,128)(2,1)S(1)}, u32[]{:S(2)}, u32[]{:S(2)}) collective-permute-start(s16[128,768]{1,0:T(8,128)(2,1)S(1)} %get-tuple-element.85.refs_0_), channel_id=1, source_target_pairs={{0,4},{4,0},{8,12},{12,8},{1,5},{5,1},{9,13},{13,9},{2,6},{6,2},{1... | collective-permute-start | bytes 589832 | tf_op jit(solution)/shard_map/ppermute | solution.py:152
  17.1 2.5 %collective-permute-start.7 = (s16[128,768]{1,0:T(8,128)(2,1)S(1)}, s16[128,768]{1,0:T(8,128)(2,1)S(1)}, u32[]{:S(2)}, u32[]{:S(2)}) collective-permute-start(s16[128,768]{1,0:T(8,128)(2,1)S(1)} %get-tuple-element.85.refs_0_), channel_id=1, source_target_pairs={{0,12},{4,8},{8,4},{12,0},{1,13},{5,9},{9,5},{13,1},{2,14},{6,10},... | collective-permute-start | bytes 589832 | tf_op jit(solution)/shard_map/ppermute | solution.py:152
  19.6 0.5 collective-permute-start.2
  20.1 1.5 %collective-permute-start.9 = (s16[128,768]{1,0:T(8,128)(2,1)S(1)}, s16[128,768]{1,0:T(8,128)(2,1)S(1)}, u32[]{:S(2)}, u32[]{:S(2)}) collective-permute-start(s16[128,768]{1,0:T(8,128)(2,1)S(1)} %get-tuple-element.85.refs_0_), channel_id=1, source_target_pairs={{0,2},{1,3},{2,0},{3,1},{4,6},{5,7},{6,4},{7,5},{8,10},{9,11},{10,... | collective-permute-start | bytes 589832 | tf_op jit(solution)/shard_map/ppermute | solution.py:144
  21.6 3.1 %shard_map.141.own_ref = f32[768,768]{1,0:T(8,128)S(1)} custom-call(s32[12]{0:T(128)S(1)} %concatenate.3.meta, bf16[4,512,768]{2,1,0:T(8,128)(2,1)} %xin.3, bf16[4,512,768]{2,1,0:T(8,128)(2,1)} %dout.3), custom_call_target="tpu_custom_call" | custom-call | flops 1000000000 | bytes 36000000 | tf_op jit(solution)/shard_map/pallas_call | solution.py:273
  24.7 0.8 shard_map.142.mine
  25.5 1.0 %shard_map.143 = (s16[112,768]{1,0:T(8,128)(2,1)S(1)}, f32[96,768]{1,0:T(8,128)S(1)}) custom-call(s32[12]{0:T(128)S(1)} %concatenate.3.meta, s16[224,768]{1,0:T(8,128)(2,1)S(1)} %collective-permute-done.4.got, f32[768,768]{1,0:T(8,128)S(1)} %shard_map.142.mine), custom_call_target="tpu_custom_call" | custom-call | flops 1100000000 | bytes 39600000 | tf_op jit(solution)/shard_map/pallas_call | solution.py:369
  26.6 0.6 collective-permute-start.6
  27.2 1.5 %collective-permute-start.12 = (s16[224,768]{1,0:T(8,128)(2,1)S(1)}, s16[224,768]{1,0:T(8,128)(2,1)S(1)}, u32[]{:S(2)}, u32[]{:S(2)}) collective-permute-start(s16[224,768]{1,0:T(8,128)(2,1)S(1)} %get-tuple-element.93), channel_id=1, source_target_pairs={{0,16},{16,0},{1,17},{17,1},{2,18},{18,2},{3,19},{19,3},{4,20},{20... | collective-permute-start | bytes 1032200 | tf_op jit(solution)/shard_map/ppermute | solution.py:148
  28.7 1.5 %collective-permute-start.14 = (s16[128,768]{1,0:T(8,128)(2,1)S(1)}, s16[128,768]{1,0:T(8,128)(2,1)S(1)}, u32[]{:S(2)}, u32[]{:S(2)}) collective-permute-start(s16[128,768]{1,0:T(8,128)(2,1)S(1)} %collective-permute-done.8.refs_2_), channel_id=1, source_target_pairs={{0,2},{1,3},{2,0},{3,1},{4,6},{5,7},{6,4},{7,5},{8,10},{9,11},{10,... | collective-permute-start | bytes 589832 | tf_op jit(solution)/shard_map/ppermute | solution.py:144
  30.2 0.7 collective-permute-start.15
  30.9 3.0 %collective-permute-done.6.refs_0_ = s16[112,768]{1,0:T(8,128)(2,1)S(1)} collective-permute-done((s16[112,768]{1,0:T(8,128)(2,1)S(1)}, s16[112,768]{1,0:T(8,128)(2,1)S(1)}, u32[]{:S(2)}, u32[]{:S(2)}) %collective-permute-start.6) | collective-permute-done | bytes 172064 | tf_op jit(solution)/shard_map/ppermute | solution.py:144
  33.9 1.0 %shard_map.145 = (s16[112,768]{1,0:T(8,128)(2,1)S(1)}, f32[96,768]{1,0:T(8,128)S(1)}) custom-call(s32[12]{0:T(128)S(1)} %concatenate.3.meta, s16[224,768]{1,0:T(8,128)(2,1)S(1)} %collective-permute-done.2.got, f32[768,768]{1,0:T(8,128)S(1)} %shard_map.142.mine), custom_call_target="tpu_custom_call" | custom-call | flops 1100000000 | bytes 39600000 | tf_op jit(solution)/shard_map/pallas_call | solution.py:369
  35.0 2.0 %collective-permute-start.1 = (s16[224,768]{1,0:T(8,128)(2,1)S(1)}, s16[224,768]{1,0:T(8,128)(2,1)S(1)}, u32[]{:S(2)}, u32[]{:S(2)}) collective-permute-start(s16[224,768]{1,0:T(8,128)(2,1)S(1)} %get-tuple-element.72), channel_id=1, source_target_pairs={{0,16},{16,0},{1,17},{17,1},{2,18},{18,2},{3,19},{19,3},{4,20},{20... | collective-permute-start | bytes 1032200 | tf_op jit(solution)/shard_map/ppermute | solution.py:148
  37.0 0.2 shard_map.146
  37.3 0.9 collective-permute-done.12.got
  38.2 1.3 %collective-permute-start.16 = (s16[112,768]{1,0:T(8,128)(2,1)S(1)}, s16[112,768]{1,0:T(8,128)(2,1)S(1)}, u32[]{:S(2)}, u32[]{:S(2)}) collective-permute-start(s16[112,768]{1,0:T(8,128)(2,1)S(1)} %shard_map.146), channel_id=1, source_target_pairs={{0,4},{4,0},{8,12},{12,8},{1,5},{5,1},{9,13},{13,9},{2,6},{6,2},{1... | collective-permute-start | bytes 516104 | tf_op jit(solution)/shard_map/ppermute | solution.py:152
  39.5 1.5 %collective-permute-start.10 = (s16[128,768]{1,0:T(8,128)(2,1)S(1)}, s16[128,768]{1,0:T(8,128)(2,1)S(1)}, u32[]{:S(2)}, u32[]{:S(2)}) collective-permute-start(s16[128,768]{1,0:T(8,128)(2,1)S(1)} %collective-permute-done.7.refs_6_), channel_id=1, source_target_pairs={{0,2},{1,3},{2,0},{3,1},{4,6},{5,7},{6,4},{7,5},{8,10},{9,11},{10,... | collective-permute-start | bytes 589832 | tf_op jit(solution)/shard_map/ppermute | solution.py:144
  41.0 1.0 %shard_map.148 = (s16[112,768]{1,0:T(8,128)(2,1)S(1)}, f32[96,768]{1,0:T(8,128)S(1)}) custom-call(s32[12]{0:T(128)S(1)} %concatenate.3.meta, s16[224,768]{1,0:T(8,128)(2,1)S(1)} %collective-permute-done.12.got, f32[768,768]{1,0:T(8,128)S(1)} %shard_map.142.mine), custom_call_target="tpu_custom_call" | custom-call | flops 1100000000 | bytes 39600000 | tf_op jit(solution)/shard_map/pallas_call | solution.py:369
  42.0 0.6 collective-permute-start.18
  42.6 0.9 collective-permute-done.16.refs_1_
  43.6 0.4 shard_map.147
  44.0 3.4 %collective-permute-start.17 = (s16[112,768]{1,0:T(8,128)(2,1)S(1)}, s16[112,768]{1,0:T(8,128)(2,1)S(1)}, u32[]{:S(2)}, u32[]{:S(2)}) collective-permute-start(s16[112,768]{1,0:T(8,128)(2,1)S(1)} %shard_map.147), channel_id=1, source_target_pairs={{0,12},{4,8},{8,4},{12,0},{1,13},{5,9},{9,5},{13,1},{2,14},{6,10},... | collective-permute-start | bytes 516104 | tf_op jit(solution)/shard_map/ppermute | solution.py:152
  47.4 1.0 %shard_map.144 = (s16[112,768]{1,0:T(8,128)(2,1)S(1)}, f32[96,768]{1,0:T(8,128)S(1)}) custom-call(s32[12]{0:T(128)S(1)} %concatenate.3.meta, s16[224,768]{1,0:T(8,128)(2,1)S(1)} %collective-permute-done.1.got, f32[768,768]{1,0:T(8,128)S(1)} %shard_map.142.mine), custom_call_target="tpu_custom_call" | custom-call | flops 1100000000 | bytes 39600000 | tf_op jit(solution)/shard_map/pallas_call | solution.py:369
  48.5 1.6 %collective-permute-start.11 = (s16[112,768]{1,0:T(8,128)(2,1)S(1)}, s16[112,768]{1,0:T(8,128)(2,1)S(1)}, u32[]{:S(2)}, u32[]{:S(2)}) collective-permute-start(s16[112,768]{1,0:T(8,128)(2,1)S(1)} %get-tuple-element.90), channel_id=1, source_target_pairs={{0,2},{1,3},{2,0},{3,1},{4,6},{5,7},{6,4},{7,5},{8,10},{9,11},{10,... | collective-permute-start | bytes 516104 | tf_op jit(solution)/shard_map/ppermute | solution.py:144
  50.0 0.2 shard_map.149
  50.4 1.2 %collective-permute-done.17.far = s16[112,768]{1,0:T(8,128)(2,1)S(1)} collective-permute-done((s16[112,768]{1,0:T(8,128)(2,1)S(1)}, s16[112,768]{1,0:T(8,128)(2,1)S(1)}, u32[]{:S(2)}, u32[]{:S(2)}) %collective-permute-start.17) | collective-permute-done | bytes 172064 | tf_op jit(solution)/shard_map/ppermute | solution.py:152
  51.6 2.4 %collective-permute-done.11.got = s16[112,768]{1,0:T(8,128)(2,1)S(1)} collective-permute-done((s16[112,768]{1,0:T(8,128)(2,1)S(1)}, s16[112,768]{1,0:T(8,128)(2,1)S(1)}, u32[]{:S(2)}, u32[]{:S(2)}) %collective-permute-start.11) | collective-permute-done | bytes 172064 | tf_op jit(solution)/shard_map/ppermute | solution.py:144
  54.0 1.8 %collective-permute-done.19.near = s16[112,768]{1,0:T(8,128)(2,1)S(1)} collective-permute-done((s16[112,768]{1,0:T(8,128)(2,1)S(1)}, s16[112,768]{1,0:T(8,128)(2,1)S(1)}, u32[]{:S(2)}, u32[]{:S(2)}) %collective-permute-start.19) | collective-permute-done | bytes 172064 | tf_op jit(solution)/shard_map/ppermute | solution.py:152
  55.8 0.6 shard_map.150
  56.4 0.6 collective-permute-start.22
  57.0 2.4 %collective-permute-start.21 = (s16[112,768]{1,0:T(8,128)(2,1)S(1)}, s16[112,768]{1,0:T(8,128)(2,1)S(1)}, u32[]{:S(2)}, u32[]{:S(2)}) collective-permute-start(s16[112,768]{1,0:T(8,128)(2,1)S(1)} %get-tuple-element.104), channel_id=1, source_target_pairs={{0,12},{4,8},{8,4},{12,0},{1,13},{5,9},{9,5},{13,1},{2,14},{6,10},... | collective-permute-start | bytes 516104 | tf_op jit(solution)/shard_map/ppermute | solution.py:152
  59.5 1.6 %collective-permute-start.27 = (s16[128,768]{1,0:T(8,128)(2,1)S(1)}, s16[128,768]{1,0:T(8,128)(2,1)S(1)}, u32[]{:S(2)}, u32[]{:S(2)}) collective-permute-start(s16[128,768]{1,0:T(8,128)(2,1)S(1)} %collective-permute-done.15.refs_4_), channel_id=1, source_target_pairs={{0,2},{1,3},{2,0},{3,1},{4,6},{5,7},{6,4},{7,5},{8,10},{9,11},{10,... | collective-permute-start | bytes 589832 | tf_op jit(solution)/shard_map/ppermute | solution.py:144
  61.0 0.8 collective-permute-done.22.refs_0_
  61.8 3.1 %collective-permute-done.21.three = s16[112,768]{1,0:T(8,128)(2,1)S(1)} collective-permute-done((s16[112,768]{1,0:T(8,128)(2,1)S(1)}, s16[112,768]{1,0:T(8,128)(2,1)S(1)}, u32[]{:S(2)}, u32[]{:S(2)}) %collective-permute-start.21) | collective-permute-done | bytes 172064 | tf_op jit(solution)/shard_map/ppermute | solution.py:152
  65.0 1.9 %shard_map.153 = (f32[4,48,768]{2,1,0:T(8,128)}, f32[4,48,768]{2,1,0:T(8,128)}, f32[1,128]{1,0:T(1,128)S(1)}) custom-call(s32[12]{0:T(128)S(1)} %concatenate.3.meta, f32[96,768]{1,0:T(8,128)S(1)} %get-tuple-element.103.grad_ref.grad, f32[48,768]{1,0:T(8,128)S(1)} %collective-permute-done.28.got, f32[4,48,768]{2,1,0:T(8,128)S(1)} %copy-done, ...), custom_call_target="tpu_custom_call" | custom-call | flops 1000000000 | bytes 36000000 | tf_op jit(solution)/shard_map/pallas_call | solution.py:273
  66.9 2.4 %collective-permute-start.26 = (s16[112,768]{1,0:T(8,128)(2,1)S(1)}, s16[112,768]{1,0:T(8,128)(2,1)S(1)}, u32[]{:S(2)}, u32[]{:S(2)}) collective-permute-start(s16[112,768]{1,0:T(8,128)(2,1)S(1)} %collective-permute-done.21.three), channel_id=1, source_target_pairs={{0,2},{1,3},{2,0},{3,1},{4,6},{5,7},{6,4},{7,5},{8,10},{9,11},{10,... | collective-permute-start | bytes 516104 | tf_op jit(solution)/shard_map/ppermute | solution.py:144
  69.2 0.6 collective-permute-start.24
  69.9 1.9 %collective-permute-done.23.two = s16[112,768]{1,0:T(8,128)(2,1)S(1)} collective-permute-done((s16[112,768]{1,0:T(8,128)(2,1)S(1)}, s16[112,768]{1,0:T(8,128)(2,1)S(1)}, u32[]{:S(2)}, u32[]{:S(2)}) %collective-permute-start.23) | collective-permute-done | bytes 172064 | tf_op jit(solution)/shard_map/ppermute | solution.py:152
  71.7 1.5 %collective-permute-start.25 = (s16[112,768]{1,0:T(8,128)(2,1)S(1)}, s16[112,768]{1,0:T(8,128)(2,1)S(1)}, u32[]{:S(2)}, u32[]{:S(2)}) collective-permute-start(s16[112,768]{1,0:T(8,128)(2,1)S(1)} %collective-permute-done.23.two), channel_id=1, source_target_pairs={{0,2},{1,3},{2,0},{3,1},{4,6},{5,7},{6,4},{7,5},{8,10},{9,11},{10,... | collective-permute-start | bytes 516104 | tf_op jit(solution)/shard_map/ppermute | solution.py:144
  73.2 1.5 %shard_map.152 = (bf16[768,768]{1,0:T(8,128)(2,1)S(1)}, bf16[768,768]{1,0:T(8,128)(2,1)S(1)}) custom-call(s32[12]{0:T(128)S(1)} %concatenate.3.meta, s16[128,768]{1,0:T(8,128)(2,1)S(1)} %get-tuple-element.85.refs_0_, s16[128,768]{1,0:T(8,128)(2,1)S(1)} %collective-permute-done.9.refs_1_, s16[128,768]{1,0:T(8,128)(2,1)S(1)} %collective-permute-done.8.refs_2_, ...), custom_call_target="tpu_custom_call" | custom-call | flops 1000000000 | bytes 36000000 | tf_op jit(solution)/shard_map/pallas_call | solution.py:273
  74.7 1.1 %shard_map.151 = (bf16[768,768]{1,0:T(8,128)(2,1)S(1)}, bf16[768,768]{1,0:T(8,128)(2,1)S(1)}) custom-call(s32[12]{0:T(128)S(1)} %concatenate.3.meta, f32[96,768]{1,0:T(8,128)S(1)} %get-tuple-element.103.grad_ref.grad, s16[112,768]{1,0:T(8,128)(2,1)S(1)} %collective-permute-done.20.one, s16[112,768]{1,0:T(8,128)(2,1)S(1)} %collective-permute-done.23.two, ...), custom_call_target="tpu_custom_call" | custom-call | flops 1000000000 | bytes 36000000 | tf_op jit(solution)/shard_map/pallas_call | solution.py:273
  75.9 1.9 %collective-permute-done.24.refs_1_ = s16[112,768]{1,0:T(8,128)(2,1)S(1)} collective-permute-done((s16[112,768]{1,0:T(8,128)(2,1)S(1)}, s16[112,768]{1,0:T(8,128)(2,1)S(1)}, u32[]{:S(2)}, u32[]{:S(2)}) %collective-permute-start.24) | collective-permute-done | bytes 172064 | tf_op jit(solution)/shard_map/ppermute | solution.py:144
  77.8 1.8 %collective-permute-done.25.refs_2_ = s16[112,768]{1,0:T(8,128)(2,1)S(1)} collective-permute-done((s16[112,768]{1,0:T(8,128)(2,1)S(1)}, s16[112,768]{1,0:T(8,128)(2,1)S(1)}, u32[]{:S(2)}, u32[]{:S(2)}) %collective-permute-start.25) | collective-permute-done | bytes 172064 | tf_op jit(solution)/shard_map/ppermute | solution.py:144
  79.6 3.4 %shard_map.154 = (f32[48,768]{1,0:T(8,128)S(1)}, f32[48,768]{1,0:T(8,128)S(1)}, f32[1,128]{1,0:T(1,128)S(1)}, bf16[768,768]{1,0:T(8,128)(2,1)S(1)}, bf16[768,768]{1,0:T(8,128)(2,1)S(1)}) custom-call(s32[12]{0:T(128)S(1)} %concatenate.3.meta, bf16[768,768]{1,0:T(8,128)(2,1)S(1)} %get-tuple-element.106.high_in, ...), custom_call_target="tpu_custom_call" | custom-call | flops 4000000000 | bytes 144000000 | tf_op jit(solution)/shard_map/pallas_call | solution.py:273
  83.1 10.3 %all_to_all.5.sums = f32[16,1,128]{2,1,0:T(1,128)S(1)} all-to-all(f32[16,1,128]{2,1,0:T(1,128)S(1)} %broadcast_in_dim.9), channel_id=1, replica_groups=mesh['shard'=2,'tensor'=4,'section'=4] {'tensor','section'}, dimensions={0} | all-to-all | bytes 16384 | tf_op jit(solution)/shard_map/all_to_all | solution.py:708
  93.4 0.7 shard_map.155.near
  94.1 1.6 %collective-permute-start.31 = (bf16[2,48,768]{2,1,0:T(8,128)(2,1)S(1)}, bf16[2,48,768]{2,1,0:T(8,128)(2,1)S(1)}, u32[]{:S(2)}, u32[]{:S(2)}) collective-permute-start(bf16[2,48,768]{2,1,0:T(8,128)(2,1)S(1)} %shard_map.155.near), channel_id=1, source_target_pairs={{0,16},{16,0},{1,17},{17,1},{2,18},{18,2},{3,19},{19,3},{4,20},{20... | collective-permute-start | bytes 442376 | tf_op jit(solution)/shard_map/ppermute | solution.py:148
  95.7 1.8 %shard_map.156 = (f32[48,768]{1,0:T(8,128)S(1)}, f32[48,768]{1,0:T(8,128)S(1)}) custom-call(s32[12]{0:T(128)S(1)} %concatenate.3.meta, f32[96,768]{1,0:T(8,128)S(1)} %get-tuple-element.103.grad_ref.grad, bf16[768,768]{1,0:T(8,128)(2,1)S(1)} %get-tuple-element.122.high_ref, bf16[768,768]{1,0:T(8,128)(2,1)S(1)} %get-tuple-element.123.low_ref), custom_call_target="tpu_custom_call" | custom-call | flops 1400000000 | bytes 50400000 | tf_op jit(solution)/shard_map/pallas_call | solution.py:273
  97.6 2.0 %shard_map.158 = (f32[48,768]{1,0:T(8,128)S(1)}, f32[48,768]{1,0:T(8,128)S(1)}) custom-call(s32[12]{0:T(128)S(1)} %concatenate.3.meta, bf16[768,768]{1,0:T(8,128)(2,1)S(1)} %get-tuple-element.122.high_ref, bf16[768,768]{1,0:T(8,128)(2,1)S(1)} %get-tuple-element.123.low_ref), custom_call_target="tpu_custom_call" | custom-call | flops 1800000000 | bytes 64800000 | tf_op jit(solution)/shard_map/pallas_call | solution.py:273
  99.6 0.6 collective-permute-start.32
  100.1 1.3 %shard_map.157 = bf16[4,48,768]{2,1,0:T(8,128)(2,1)} custom-call(s32[12]{0:T(128)S(1)} %concatenate.3.meta, bf16[2,48,768]{2,1,0:T(8,128)(2,1)S(1)} %shard_map.155.near, bf16[2,48,768]{2,1,0:T(8,128)(2,1)S(1)} %collective-permute-done.31.mirror), custom_call_target="tpu_custom_call" | custom-call | flops 1000000000 | bytes 36000000 | tf_op jit(solution)/shard_map/pallas_call | solution.py:273
  101.5 1.7 %shard_map.159 = (f32[4,48,768]{2,1,0:T(8,128)}, f32[4,48,768]{2,1,0:T(8,128)}) custom-call(s32[12]{0:T(128)S(1)} %concatenate.3.meta, f32[48,768]{1,0:T(8,128)S(1)} %get-tuple-element.127.own_right, f32[48,768]{1,0:T(8,128)S(1)} %collective-permute-done.32.got_right, f32[48,768]{1,0:T(8,128)S(1)} %get-tuple-element.129.own_left, ...), custom_call_target="tpu_custom_call" | custom-call | flops 1000000000 | bytes 36000000 | tf_op jit(solution)/shard_map/pallas_call | solution.py:273
  (39 shorter events, 0.5 us)
Async XLA Ops:
  4.7 3.6 %collective-permute-start = (bf16[2,512,768]{2,1,0:T(8,128)(2,1)S(1)}, bf16[2,512,768]{2,1,0:T(8,128)(2,1)S(1)}, u32[]{:S(2)}, u32[]{:S(2)}) collective-permute-start(bf16[2,512,768]{2,1,0:T(8,128)(2,1)S(1)} %get-tuple-element.70), channel_id=1, source_target_pairs={{0,1},{1,0},{2,3},{3,2},{4,5},{5,4},{6,7},{7,6},{8,9},{9,8},{10,11... | collective-permute-start | bytes 4718600 | tf_op jit(solution)/shard_map/ppermute | solution.py:140
  5.2 14.9 %collective-permute-start.5 = (bf16[2,512,768]{2,1,0:T(8,128)(2,1)S(1)}, bf16[2,512,768]{2,1,0:T(8,128)(2,1)S(1)}, u32[]{:S(2)}, u32[]{:S(2)}) collective-permute-start(bf16[2,512,768]{2,1,0:T(8,128)(2,1)S(1)} %get-tuple-element.77), channel_id=1, source_target_pairs={{0,1},{1,0},{2,3},{3,2},{4,5},{5,4},{6,7},{7,6},{8,9},{9,8},{10,11... | collective-permute-start | bytes 4718600 | tf_op jit(solution)/shard_map/ppermute | solution.py:140
  5.3 5.6 %collective-permute-start.3 = (f32[2,48,768]{2,1,0:T(8,128)S(1)}, f32[2,48,768]{2,1,0:T(8,128)S(1)}, u32[]{:S(2)}, u32[]{:S(2)}) collective-permute-start(f32[2,48,768]{2,1,0:T(8,128)S(1)} %get-tuple-element.75), channel_id=1, source_target_pairs={{0,1},{1,0},{2,3},{3,2},{4,5},{5,4},{6,7},{7,6},{8,9},{9,8},{10,11... | collective-permute-start | bytes 884744 | tf_op jit(solution)/shard_map/ppermute | solution.py:140
  10.9 14.6 %collective-permute-start.4 = (s16[224,768]{1,0:T(8,128)(2,1)S(1)}, s16[224,768]{1,0:T(8,128)(2,1)S(1)}, u32[]{:S(2)}, u32[]{:S(2)}) collective-permute-start(s16[224,768]{1,0:T(8,128)(2,1)S(1)} %get-tuple-element.76), channel_id=1, source_target_pairs={{0,16},{16,0},{1,17},{17,1},{2,18},{18,2},{3,19},{19,3},{4,20},{20... | collective-permute-start | bytes 1032200 | tf_op jit(solution)/shard_map/ppermute | solution.py:148
  15.5 11.7 %collective-permute-start.8 = (s16[128,768]{1,0:T(8,128)(2,1)S(1)}, s16[128,768]{1,0:T(8,128)(2,1)S(1)}, u32[]{:S(2)}, u32[]{:S(2)}) collective-permute-start(s16[128,768]{1,0:T(8,128)(2,1)S(1)} %get-tuple-element.85.refs_0_), channel_id=1, source_target_pairs={{0,4},{4,0},{8,12},{12,8},{1,5},{5,1},{9,13},{13,9},{2,6},{6,2},{1... | collective-permute-start | bytes 589832 | tf_op jit(solution)/shard_map/ppermute | solution.py:152
  17.1 11.5 %collective-permute-start.7 = (s16[128,768]{1,0:T(8,128)(2,1)S(1)}, s16[128,768]{1,0:T(8,128)(2,1)S(1)}, u32[]{:S(2)}, u32[]{:S(2)}) collective-permute-start(s16[128,768]{1,0:T(8,128)(2,1)S(1)} %get-tuple-element.85.refs_0_), channel_id=1, source_target_pairs={{0,12},{4,8},{8,4},{12,0},{1,13},{5,9},{9,5},{13,1},{2,14},{6,10},... | collective-permute-start | bytes 589832 | tf_op jit(solution)/shard_map/ppermute | solution.py:152
  19.6 11.3 %collective-permute-start.2 = (s16[224,768]{1,0:T(8,128)(2,1)S(1)}, s16[224,768]{1,0:T(8,128)(2,1)S(1)}, u32[]{:S(2)}, u32[]{:S(2)}) collective-permute-start(s16[224,768]{1,0:T(8,128)(2,1)S(1)} %get-tuple-element.73), channel_id=1, source_target_pairs={{0,16},{16,0},{1,17},{17,1},{2,18},{18,2},{3,19},{19,3},{4,20},{20... | collective-permute-start | bytes 1032200 | tf_op jit(solution)/shard_map/ppermute | solution.py:148
  20.1 8.6 %collective-permute-start.9 = (s16[128,768]{1,0:T(8,128)(2,1)S(1)}, s16[128,768]{1,0:T(8,128)(2,1)S(1)}, u32[]{:S(2)}, u32[]{:S(2)}) collective-permute-start(s16[128,768]{1,0:T(8,128)(2,1)S(1)} %get-tuple-element.85.refs_0_), channel_id=1, source_target_pairs={{0,2},{1,3},{2,0},{3,1},{4,6},{5,7},{6,4},{7,5},{8,10},{9,11},{10,... | collective-permute-start | bytes 589832 | tf_op jit(solution)/shard_map/ppermute | solution.py:144
  26.6 7.3 %collective-permute-start.6 = (s16[112,768]{1,0:T(8,128)(2,1)S(1)}, s16[112,768]{1,0:T(8,128)(2,1)S(1)}, u32[]{:S(2)}, u32[]{:S(2)}) collective-permute-start(s16[112,768]{1,0:T(8,128)(2,1)S(1)} %get-tuple-element.83), channel_id=1, source_target_pairs={{0,2},{1,3},{2,0},{3,1},{4,6},{5,7},{6,4},{7,5},{8,10},{9,11},{10,... | collective-permute-start | bytes 516104 | tf_op jit(solution)/shard_map/ppermute | solution.py:144
  27.2 11.0 %collective-permute-start.12 = (s16[224,768]{1,0:T(8,128)(2,1)S(1)}, s16[224,768]{1,0:T(8,128)(2,1)S(1)}, u32[]{:S(2)}, u32[]{:S(2)}) collective-permute-start(s16[224,768]{1,0:T(8,128)(2,1)S(1)} %get-tuple-element.93), channel_id=1, source_target_pairs={{0,16},{16,0},{1,17},{17,1},{2,18},{18,2},{3,19},{19,3},{4,20},{20... | collective-permute-start | bytes 1032200 | tf_op jit(solution)/shard_map/ppermute | solution.py:148
  28.7 10.8 %collective-permute-start.14 = (s16[128,768]{1,0:T(8,128)(2,1)S(1)}, s16[128,768]{1,0:T(8,128)(2,1)S(1)}, u32[]{:S(2)}, u32[]{:S(2)}) collective-permute-start(s16[128,768]{1,0:T(8,128)(2,1)S(1)} %collective-permute-done.8.refs_2_), channel_id=1, source_target_pairs={{0,2},{1,3},{2,0},{3,1},{4,6},{5,7},{6,4},{7,5},{8,10},{9,11},{10,... | collective-permute-start | bytes 589832 | tf_op jit(solution)/shard_map/ppermute | solution.py:144
  30.2 10.8 %collective-permute-start.15 = (s16[128,768]{1,0:T(8,128)(2,1)S(1)}, s16[128,768]{1,0:T(8,128)(2,1)S(1)}, u32[]{:S(2)}, u32[]{:S(2)}) collective-permute-start(s16[128,768]{1,0:T(8,128)(2,1)S(1)} %collective-permute-done.7.refs_6_), channel_id=1, source_target_pairs={{0,4},{4,0},{8,12},{12,8},{1,5},{5,1},{9,13},{13,9},{2,6},{6,2},{1... | collective-permute-start | bytes 589832 | tf_op jit(solution)/shard_map/ppermute | solution.py:152
  34.9 6.1 %collective-permute-start.13 = (s16[112,768]{1,0:T(8,128)(2,1)S(1)}, s16[112,768]{1,0:T(8,128)(2,1)S(1)}, u32[]{:S(2)}, u32[]{:S(2)}) collective-permute-start(s16[112,768]{1,0:T(8,128)(2,1)S(1)} %get-tuple-element.94), channel_id=1, source_target_pairs={{0,2},{1,3},{2,0},{3,1},{4,6},{5,7},{6,4},{7,5},{8,10},{9,11},{10,... | collective-permute-start | bytes 516104 | tf_op jit(solution)/shard_map/ppermute | solution.py:144
  35.0 12.4 %collective-permute-start.1 = (s16[224,768]{1,0:T(8,128)(2,1)S(1)}, s16[224,768]{1,0:T(8,128)(2,1)S(1)}, u32[]{:S(2)}, u32[]{:S(2)}) collective-permute-start(s16[224,768]{1,0:T(8,128)(2,1)S(1)} %get-tuple-element.72), channel_id=1, source_target_pairs={{0,16},{16,0},{1,17},{17,1},{2,18},{18,2},{3,19},{19,3},{4,20},{20... | collective-permute-start | bytes 1032200 | tf_op jit(solution)/shard_map/ppermute | solution.py:148
  38.2 5.4 %collective-permute-start.16 = (s16[112,768]{1,0:T(8,128)(2,1)S(1)}, s16[112,768]{1,0:T(8,128)(2,1)S(1)}, u32[]{:S(2)}, u32[]{:S(2)}) collective-permute-start(s16[112,768]{1,0:T(8,128)(2,1)S(1)} %shard_map.146), channel_id=1, source_target_pairs={{0,4},{4,0},{8,12},{12,8},{1,5},{5,1},{9,13},{13,9},{2,6},{6,2},{1... | collective-permute-start | bytes 516104 | tf_op jit(solution)/shard_map/ppermute | solution.py:152
  39.5 7.9 %collective-permute-start.10 = (s16[128,768]{1,0:T(8,128)(2,1)S(1)}, s16[128,768]{1,0:T(8,128)(2,1)S(1)}, u32[]{:S(2)}, u32[]{:S(2)}) collective-permute-start(s16[128,768]{1,0:T(8,128)(2,1)S(1)} %collective-permute-done.7.refs_6_), channel_id=1, source_target_pairs={{0,2},{1,3},{2,0},{3,1},{4,6},{5,7},{6,4},{7,5},{8,10},{9,11},{10,... | collective-permute-start | bytes 589832 | tf_op jit(solution)/shard_map/ppermute | solution.py:144
  42.0 8.0 %collective-permute-start.18 = (s16[112,768]{1,0:T(8,128)(2,1)S(1)}, s16[112,768]{1,0:T(8,128)(2,1)S(1)}, u32[]{:S(2)}, u32[]{:S(2)}) collective-permute-start(s16[112,768]{1,0:T(8,128)(2,1)S(1)} %get-tuple-element.102), channel_id=1, source_target_pairs={{0,2},{1,3},{2,0},{3,1},{4,6},{5,7},{6,4},{7,5},{8,10},{9,11},{10,... | collective-permute-start | bytes 516104 | tf_op jit(solution)/shard_map/ppermute | solution.py:144
  44.0 7.6 %collective-permute-start.17 = (s16[112,768]{1,0:T(8,128)(2,1)S(1)}, s16[112,768]{1,0:T(8,128)(2,1)S(1)}, u32[]{:S(2)}, u32[]{:S(2)}) collective-permute-start(s16[112,768]{1,0:T(8,128)(2,1)S(1)} %shard_map.147), channel_id=1, source_target_pairs={{0,12},{4,8},{8,4},{12,0},{1,13},{5,9},{9,5},{13,1},{2,14},{6,10},... | collective-permute-start | bytes 516104 | tf_op jit(solution)/shard_map/ppermute | solution.py:152
  48.5 5.5 %collective-permute-start.11 = (s16[112,768]{1,0:T(8,128)(2,1)S(1)}, s16[112,768]{1,0:T(8,128)(2,1)S(1)}, u32[]{:S(2)}, u32[]{:S(2)}) collective-permute-start(s16[112,768]{1,0:T(8,128)(2,1)S(1)} %get-tuple-element.90), channel_id=1, source_target_pairs={{0,2},{1,3},{2,0},{3,1},{4,6},{5,7},{6,4},{7,5},{8,10},{9,11},{10,... | collective-permute-start | bytes 516104 | tf_op jit(solution)/shard_map/ppermute | solution.py:144
  50.3 5.5 %collective-permute-start.19 = (s16[112,768]{1,0:T(8,128)(2,1)S(1)}, s16[112,768]{1,0:T(8,128)(2,1)S(1)}, u32[]{:S(2)}, u32[]{:S(2)}) collective-permute-start(s16[112,768]{1,0:T(8,128)(2,1)S(1)} %shard_map.149), channel_id=1, source_target_pairs={{0,4},{4,0},{8,12},{12,8},{1,5},{5,1},{9,13},{13,9},{2,6},{6,2},{1... | collective-permute-start | bytes 516104 | tf_op jit(solution)/shard_map/ppermute | solution.py:152
  55.8 9.2 %copy-start = (f32[4,48,768]{2,1,0:T(8,128)S(1)}, f32[4,48,768]{2,1,0:T(8,128)}, u32[]{:S(2)}) copy-start(f32[4,48,768]{2,1,0:T(8,128)} %first.1) | copy-start | bytes 1769476
  55.8 9.2 %copy-start.1 = (f32[4,48,768]{2,1,0:T(8,128)S(1)}, f32[4,48,768]{2,1,0:T(8,128)}, u32[]{:S(2)}) copy-start(f32[4,48,768]{2,1,0:T(8,128)} %second.1) | copy-start | bytes 1769476
  56.4 5.5 %collective-permute-start.22 = (s16[112,768]{1,0:T(8,128)(2,1)S(1)}, s16[112,768]{1,0:T(8,128)(2,1)S(1)}, u32[]{:S(2)}, u32[]{:S(2)}) collective-permute-start(s16[112,768]{1,0:T(8,128)(2,1)S(1)} %get-tuple-element.104), channel_id=1, source_target_pairs={{0,2},{1,3},{2,0},{3,1},{4,6},{5,7},{6,4},{7,5},{8,10},{9,11},{10,... | collective-permute-start | bytes 516104 | tf_op jit(solution)/shard_map/ppermute | solution.py:144
  57.0 8.0 %collective-permute-start.21 = (s16[112,768]{1,0:T(8,128)(2,1)S(1)}, s16[112,768]{1,0:T(8,128)(2,1)S(1)}, u32[]{:S(2)}, u32[]{:S(2)}) collective-permute-start(s16[112,768]{1,0:T(8,128)(2,1)S(1)} %get-tuple-element.104), channel_id=1, source_target_pairs={{0,12},{4,8},{8,4},{12,0},{1,13},{5,9},{9,5},{13,1},{2,14},{6,10},... | collective-permute-start | bytes 516104 | tf_op jit(solution)/shard_map/ppermute | solution.py:152
  59.4 5.6 %collective-permute-start.28 = (f32[48,768]{1,0:T(8,128)S(1)}, f32[48,768]{1,0:T(8,128)S(1)}, u32[]{:S(2)}, u32[]{:S(2)}) collective-permute-start(f32[48,768]{1,0:T(8,128)S(1)} %constant_dynamic-slice_fusion), channel_id=1, source_target_pairs={{0,1},{1,0},{2,3},{3,2},{4,5},{5,4},{6,7},{7,6},{8,9},{9,8},{10,11... | collective-permute-start | bytes 442376 | tf_op jit(solution)/shard_map/ppermute | solution.py:140
  59.5 13.7 %collective-permute-start.27 = (s16[128,768]{1,0:T(8,128)(2,1)S(1)}, s16[128,768]{1,0:T(8,128)(2,1)S(1)}, u32[]{:S(2)}, u32[]{:S(2)}) collective-permute-start(s16[128,768]{1,0:T(8,128)(2,1)S(1)} %collective-permute-done.15.refs_4_), channel_id=1, source_target_pairs={{0,2},{1,3},{2,0},{3,1},{4,6},{5,7},{6,4},{7,5},{8,10},{9,11},{10,... | collective-permute-start | bytes 589832 | tf_op jit(solution)/shard_map/ppermute | solution.py:144
  61.0 8.2 %collective-permute-start.20 = (s16[112,768]{1,0:T(8,128)(2,1)S(1)}, s16[112,768]{1,0:T(8,128)(2,1)S(1)}, u32[]{:S(2)}, u32[]{:S(2)}) collective-permute-start(s16[112,768]{1,0:T(8,128)(2,1)S(1)} %get-tuple-element.104), channel_id=1, source_target_pairs={{0,4},{4,0},{8,12},{12,8},{1,5},{5,1},{9,13},{13,9},{2,6},{6,2},{1... | collective-permute-start | bytes 516104 | tf_op jit(solution)/shard_map/ppermute | solution.py:152
  65.0 6.8 %collective-permute-start.23 = (s16[112,768]{1,0:T(8,128)(2,1)S(1)}, s16[112,768]{1,0:T(8,128)(2,1)S(1)}, u32[]{:S(2)}, u32[]{:S(2)}) collective-permute-start(s16[112,768]{1,0:T(8,128)(2,1)S(1)} %collective-permute-done.21.three), channel_id=1, source_target_pairs={{0,4},{4,0},{8,12},{12,8},{1,5},{5,1},{9,13},{13,9},{2,6},{6,2},{1... | collective-permute-start | bytes 516104 | tf_op jit(solution)/shard_map/ppermute | solution.py:152
  66.9 9.0 %collective-permute-start.26 = (s16[112,768]{1,0:T(8,128)(2,1)S(1)}, s16[112,768]{1,0:T(8,128)(2,1)S(1)}, u32[]{:S(2)}, u32[]{:S(2)}) collective-permute-start(s16[112,768]{1,0:T(8,128)(2,1)S(1)} %collective-permute-done.21.three), channel_id=1, source_target_pairs={{0,2},{1,3},{2,0},{3,1},{4,6},{5,7},{6,4},{7,5},{8,10},{9,11},{10,... | collective-permute-start | bytes 516104 | tf_op jit(solution)/shard_map/ppermute | solution.py:144
  69.2 8.5 %collective-permute-start.24 = (s16[112,768]{1,0:T(8,128)(2,1)S(1)}, s16[112,768]{1,0:T(8,128)(2,1)S(1)}, u32[]{:S(2)}, u32[]{:S(2)}) collective-permute-start(s16[112,768]{1,0:T(8,128)(2,1)S(1)} %collective-permute-done.20.one), channel_id=1, source_target_pairs={{0,2},{1,3},{2,0},{3,1},{4,6},{5,7},{6,4},{7,5},{8,10},{9,11},{10,... | collective-permute-start | bytes 516104 | tf_op jit(solution)/shard_map/ppermute | solution.py:144
  71.7 7.9 %collective-permute-start.25 = (s16[112,768]{1,0:T(8,128)(2,1)S(1)}, s16[112,768]{1,0:T(8,128)(2,1)S(1)}, u32[]{:S(2)}, u32[]{:S(2)}) collective-permute-start(s16[112,768]{1,0:T(8,128)(2,1)S(1)} %collective-permute-done.23.two), channel_id=1, source_target_pairs={{0,2},{1,3},{2,0},{3,1},{4,6},{5,7},{6,4},{7,5},{8,10},{9,11},{10,... | collective-permute-start | bytes 516104 | tf_op jit(solution)/shard_map/ppermute | solution.py:144
  79.6 13.8 %copy-start.4 = (bf16[4,48,768]{2,1,0:T(8,128)(2,1)S(1)}, bf16[4,48,768]{2,1,0:T(8,128)(2,1)}, u32[]{:S(2)}) copy-start(bf16[4,48,768]{2,1,0:T(8,128)(2,1)} %weights.1) | copy-start | bytes 884740
  83.0 10.4 %collective-permute-start.29 = (f32[48,768]{1,0:T(8,128)S(1)}, f32[48,768]{1,0:T(8,128)S(1)}, u32[]{:S(2)}, u32[]{:S(2)}) collective-permute-start(f32[48,768]{1,0:T(8,128)S(1)} %get-tuple-element.121), channel_id=1, source_target_pairs={{0,1},{1,0},{2,3},{3,2},{4,5},{5,4},{6,7},{7,6},{8,9},{9,8},{10,11... | collective-permute-start | bytes 442376 | tf_op jit(solution)/shard_map/ppermute | solution.py:140
  94.1 6.0 %collective-permute-start.31 = (bf16[2,48,768]{2,1,0:T(8,128)(2,1)S(1)}, bf16[2,48,768]{2,1,0:T(8,128)(2,1)S(1)}, u32[]{:S(2)}, u32[]{:S(2)}) collective-permute-start(bf16[2,48,768]{2,1,0:T(8,128)(2,1)S(1)} %shard_map.155.near), channel_id=1, source_target_pairs={{0,16},{16,0},{1,17},{17,1},{2,18},{18,2},{3,19},{19,3},{4,20},{20... | collective-permute-start | bytes 442376 | tf_op jit(solution)/shard_map/ppermute | solution.py:148
  97.5 4.0 %collective-permute-start.30 = (f32[48,768]{1,0:T(8,128)S(1)}, f32[48,768]{1,0:T(8,128)S(1)}, u32[]{:S(2)}, u32[]{:S(2)}) collective-permute-start(f32[48,768]{1,0:T(8,128)S(1)} %get-tuple-element.124), channel_id=1, source_target_pairs={{0,1},{1,0},{2,3},{3,2},{4,5},{5,4},{6,7},{7,6},{8,9},{9,8},{10,11... | collective-permute-start | bytes 442376 | tf_op jit(solution)/shard_map/ppermute | solution.py:140
  99.6 1.9 %copy-start.2 = (f32[4,48,768]{2,1,0:T(8,128)S(1)}, f32[4,48,768]{2,1,0:T(8,128)}, u32[]{:S(2)}) copy-start(f32[4,48,768]{2,1,0:T(8,128)} %right.5) | copy-start | bytes 1769476
  99.6 1.9 %copy-start.3 = (f32[4,48,768]{2,1,0:T(8,128)S(1)}, f32[4,48,768]{2,1,0:T(8,128)}, u32[]{:S(2)}) copy-start(f32[4,48,768]{2,1,0:T(8,128)} %left.5) | copy-start | bytes 1769476
  99.6 1.9 %collective-permute-start.32 = (f32[48,768]{1,0:T(8,128)S(1)}, f32[48,768]{1,0:T(8,128)S(1)}, u32[]{:S(2)}, u32[]{:S(2)}) collective-permute-start(f32[48,768]{1,0:T(8,128)S(1)} %get-tuple-element.128), channel_id=1, source_target_pairs={{0,1},{1,0},{2,3},{3,2},{4,5},{5,4},{6,7},{7,6},{8,9},{9,8},{10,11... | collective-permute-start | bytes 442376 | tf_op jit(solution)/shard_map/ppermute | solution.py:140

commit v8 on v7

--- a/solution.py
+++ b/solution.py
@@ -265,7 +265,7 @@
 
 def work(micros):
     return pl.CostEstimate(
-        flops=int(micros * 10**9), transcendentals=0, bytes_accessed=int(micros * 36 * 10**6)
+        flops=int(micros * 15 * 10**8), transcendentals=0, bytes_accessed=int(micros * 36 * 10**6)
     )
 
 

time: 103 us -> 103 us (level)
  no operation moved by 1% of the time
where the time goes in v8:
time: 103 us
  starting transfers between devices  36.3 us (35%)
  Pallas kernels  33.2 us (32%)
  waiting for transfers between devices  21.7 us (21%)
  blocking collectives  10.3 us (10%)
    pallas_call x19, Pallas kernels, call(): pl.pallas_call(body, out_shape=outs, in_specs=ins, out_specs=[VMEM_SPEC]...  29 us
    ppermute x12, starting transfers between devices, to_x(): return lax.ppermute(value, 'section', [(i, i ^ 2) for i in range(4)])  13.9 us
    ppermute x9, starting transfers between devices, to_z(): return lax.ppermute(value, 'tensor', [(i, i ^ bits) for i in range(4)])  12.1 us
    all_to_all x1, blocking collectives, two_planes(): sums = lax.all_to_all(sums, GROUP, 0, 0)  10.3 us
    ppermute x12, waiting for transfers between devices, to_x(): return lax.ppermute(value, 'section', [(i, i ^ 2) for i in range(4)])  9.87 us
    ppermute x9, waiting for transfers between devices, to_z(): return lax.ppermute(value, 'tensor', [(i, i ^ bits) for i in range(4)])  8.94 us
    ppermute x5, starting transfers between devices, to_y(): return lax.ppermute(value, 'shard', [(0, 1), (1, 0)])  8.53 us
    pallas_call x4, Pallas kernels, after_y(): pl.pallas_call(y_kernel, out_shape=[jax.ShapeDtypeStruct((coded_rows(rows...  4.16 us
  transfers between devices with their start and end apart: 33, of which 13 were waited for; matrix products, arithmetic and copies ran while one was open for 0% of the time, Pallas kernels for 23%

profile of v8, /device:TPU:0, one launch (start us, length us, event | category | flops | bytes accessed | tf_op | source)
XLA Modules:
  0.0 103.2 jit_solution(4702337390805078468)
XLA Ops:
  0.7 0.7 concatenate.3.meta
  1.4 3.3 %shard_map.137 = (bf16[2,512,768]{2,1,0:T(8,128)(2,1)S(1)}, bf16[2,512,768]{2,1,0:T(8,128)(2,1)S(1)}, f32[2,48,768]{2,1,0:T(8,128)S(1)}, bf16[2,512,768]{2,1,0:T(8,128)(2,1)S(1)}) custom-call(s32[12]{0:T(128)S(1)} %concatenate.3.meta, bf16[4,512,768]{2,1,0:T(8,128)(2,1)} %xin.3, bf16[4,512,768]{2,1,0:T(8,128)(2,1)} %dout.3, f32[4,48,768]{2,1,0:T(8,128)} %left.4, ...), custom_call_target="tpu_custom_call" | custom-call | flops 1500000000 | bytes 36000000 | tf_op jit(solution)/shard_map/pallas_call | solution.py:273
  4.7 0.5 collective-permute-start
  5.2 0.1 collective-permute-start.5
  5.3 0.4 collective-permute-start.3
  5.7 0.8 shard_map.138.own_ref
  6.5 1.7 %collective-permute-done.got = bf16[2,512,768]{2,1,0:T(8,128)(2,1)S(1)} collective-permute-done((bf16[2,512,768]{2,1,0:T(8,128)(2,1)S(1)}, bf16[2,512,768]{2,1,0:T(8,128)(2,1)S(1)}, u32[]{:S(2)}, u32[]{:S(2)}) %collective-permute-start) | collective-permute-done | bytes 1572896 | tf_op jit(solution)/shard_map/ppermute | solution.py:140
  8.2 2.4 %shard_map.139 = (s16[224,768]{1,0:T(8,128)(2,1)S(1)}, s16[224,768]{1,0:T(8,128)(2,1)S(1)}, s16[224,768]{1,0:T(8,128)(2,1)S(1)}, s16[224,768]{1,0:T(8,128)(2,1)S(1)}) custom-call(s32[12]{0:T(128)S(1)} %concatenate.3.meta, bf16[2,512,768]{2,1,0:T(8,128)(2,1)S(1)} %collective-permute-done.got, f32[768,768]{1,0:T(8,128)S(1)} %shard_map.138.own_ref), custom_call_target="tpu_custom_call" | custom-call | flops 1500000000 | bytes 36000000 | tf_op jit(solution)/shard_map/pallas_call | solution.py:273
  10.7 0.2 collective-permute-done.3.got
  10.9 2.9 %collective-permute-start.4 = (s16[224,768]{1,0:T(8,128)(2,1)S(1)}, s16[224,768]{1,0:T(8,128)(2,1)S(1)}, u32[]{:S(2)}, u32[]{:S(2)}) collective-permute-start(s16[224,768]{1,0:T(8,128)(2,1)S(1)} %get-tuple-element.76), channel_id=1, source_target_pairs={{0,16},{16,0},{1,17},{17,1},{2,18},{18,2},{3,19},{19,3},{4,20},{20... | collective-permute-start | bytes 1032200 | tf_op jit(solution)/shard_map/ppermute | solution.py:148
  13.8 1.7 %shard_map.140 = (f32[96,768]{1,0:T(8,128)S(1)}, s16[128,768]{1,0:T(8,128)(2,1)S(1)}) custom-call(s32[12]{0:T(128)S(1)} %concatenate.3.meta, f32[4,48,768]{2,1,0:T(8,128)} %left.4, f32[4,48,768]{2,1,0:T(8,128)} %right.4, f32[2,48,768]{2,1,0:T(8,128)S(1)} %collective-permute-done.3.got), custom_call_target="tpu_custom_call" | custom-call | flops 1500000000 | bytes 36000000 | tf_op jit(solution)/shard_map/pallas_call | solution.py:273
  15.5 1.6 %collective-permute-start.8 = (s16[128,768]{1,0:T(8,128)(2,1)S(1)}, s16[128,768]{1,0:T(8,128)(2,1)S(1)}, u32[]{:S(2)}, u32[]{:S(2)}) collective-permute-start(s16[128,768]{1,0:T(8,128)(2,1)S(1)} %get-tuple-element.85.refs_0_), channel_id=1, source_target_pairs={{0,4},{4,0},{8,12},{12,8},{1,5},{5,1},{9,13},{13,9},{2,6},{6,2},{1... | collective-permute-start | bytes 589832 | tf_op jit(solution)/shard_map/ppermute | solution.py:152
  17.1 2.5 %collective-permute-start.7 = (s16[128,768]{1,0:T(8,128)(2,1)S(1)}, s16[128,768]{1,0:T(8,128)(2,1)S(1)}, u32[]{:S(2)}, u32[]{:S(2)}) collective-permute-start(s16[128,768]{1,0:T(8,128)(2,1)S(1)} %get-tuple-element.85.refs_0_), channel_id=1, source_target_pairs={{0,12},{4,8},{8,4},{12,0},{1,13},{5,9},{9,5},{13,1},{2,14},{6,10},... | collective-permute-start | bytes 589832 | tf_op jit(solution)/shard_map/ppermute | solution.py:152
  19.6 0.5 collective-permute-start.2
  20.1 1.5 %collective-permute-start.9 = (s16[128,768]{1,0:T(8,128)(2,1)S(1)}, s16[128,768]{1,0:T(8,128)(2,1)S(1)}, u32[]{:S(2)}, u32[]{:S(2)}) collective-permute-start(s16[128,768]{1,0:T(8,128)(2,1)S(1)} %get-tuple-element.85.refs_0_), channel_id=1, source_target_pairs={{0,2},{1,3},{2,0},{3,1},{4,6},{5,7},{6,4},{7,5},{8,10},{9,11},{10,... | collective-permute-start | bytes 589832 | tf_op jit(solution)/shard_map/ppermute | solution.py:144
  21.6 3.1 %shard_map.141.own_ref = f32[768,768]{1,0:T(8,128)S(1)} custom-call(s32[12]{0:T(128)S(1)} %concatenate.3.meta, bf16[4,512,768]{2,1,0:T(8,128)(2,1)} %xin.3, bf16[4,512,768]{2,1,0:T(8,128)(2,1)} %dout.3), custom_call_target="tpu_custom_call" | custom-call | flops 1500000000 | bytes 36000000 | tf_op jit(solution)/shard_map/pallas_call | solution.py:273
  24.7 0.8 shard_map.142.mine
  25.5 1.0 %shard_map.143 = (s16[112,768]{1,0:T(8,128)(2,1)S(1)}, f32[96,768]{1,0:T(8,128)S(1)}) custom-call(s32[12]{0:T(128)S(1)} %concatenate.3.meta, s16[224,768]{1,0:T(8,128)(2,1)S(1)} %collective-permute-done.4.got, f32[768,768]{1,0:T(8,128)S(1)} %shard_map.142.mine), custom_call_target="tpu_custom_call" | custom-call | flops 1650000000 | bytes 39600000 | tf_op jit(solution)/shard_map/pallas_call | solution.py:369
  26.6 0.6 collective-permute-start.6
  27.2 1.5 %collective-permute-start.12 = (s16[224,768]{1,0:T(8,128)(2,1)S(1)}, s16[224,768]{1,0:T(8,128)(2,1)S(1)}, u32[]{:S(2)}, u32[]{:S(2)}) collective-permute-start(s16[224,768]{1,0:T(8,128)(2,1)S(1)} %get-tuple-element.93), channel_id=1, source_target_pairs={{0,16},{16,0},{1,17},{17,1},{2,18},{18,2},{3,19},{19,3},{4,20},{20... | collective-permute-start | bytes 1032200 | tf_op jit(solution)/shard_map/ppermute | solution.py:148
  28.7 1.5 %collective-permute-start.14 = (s16[128,768]{1,0:T(8,128)(2,1)S(1)}, s16[128,768]{1,0:T(8,128)(2,1)S(1)}, u32[]{:S(2)}, u32[]{:S(2)}) collective-permute-start(s16[128,768]{1,0:T(8,128)(2,1)S(1)} %collective-permute-done.8.refs_2_), channel_id=1, source_target_pairs={{0,2},{1,3},{2,0},{3,1},{4,6},{5,7},{6,4},{7,5},{8,10},{9,11},{10,... | collective-permute-start | bytes 589832 | tf_op jit(solution)/shard_map/ppermute | solution.py:144
  30.2 0.7 collective-permute-start.15
  30.9 3.0 %collective-permute-done.6.refs_0_ = s16[112,768]{1,0:T(8,128)(2,1)S(1)} collective-permute-done((s16[112,768]{1,0:T(8,128)(2,1)S(1)}, s16[112,768]{1,0:T(8,128)(2,1)S(1)}, u32[]{:S(2)}, u32[]{:S(2)}) %collective-permute-start.6) | collective-permute-done | bytes 172064 | tf_op jit(solution)/shard_map/ppermute | solution.py:144
  33.9 1.0 %shard_map.145 = (s16[112,768]{1,0:T(8,128)(2,1)S(1)}, f32[96,768]{1,0:T(8,128)S(1)}) custom-call(s32[12]{0:T(128)S(1)} %concatenate.3.meta, s16[224,768]{1,0:T(8,128)(2,1)S(1)} %collective-permute-done.2.got, f32[768,768]{1,0:T(8,128)S(1)} %shard_map.142.mine), custom_call_target="tpu_custom_call" | custom-call | flops 1650000000 | bytes 39600000 | tf_op jit(solution)/shard_map/pallas_call | solution.py:369
  35.0 2.0 %collective-permute-start.1 = (s16[224,768]{1,0:T(8,128)(2,1)S(1)}, s16[224,768]{1,0:T(8,128)(2,1)S(1)}, u32[]{:S(2)}, u32[]{:S(2)}) collective-permute-start(s16[224,768]{1,0:T(8,128)(2,1)S(1)} %get-tuple-element.72), channel_id=1, source_target_pairs={{0,16},{16,0},{1,17},{17,1},{2,18},{18,2},{3,19},{19,3},{4,20},{20... | collective-permute-start | bytes 1032200 | tf_op jit(solution)/shard_map/ppermute | solution.py:148
  37.0 0.2 shard_map.146
  37.3 0.9 collective-permute-done.12.got
  38.2 1.3 %collective-permute-start.16 = (s16[112,768]{1,0:T(8,128)(2,1)S(1)}, s16[112,768]{1,0:T(8,128)(2,1)S(1)}, u32[]{:S(2)}, u32[]{:S(2)}) collective-permute-start(s16[112,768]{1,0:T(8,128)(2,1)S(1)} %shard_map.146), channel_id=1, source_target_pairs={{0,4},{4,0},{8,12},{12,8},{1,5},{5,1},{9,13},{13,9},{2,6},{6,2},{1... | collective-permute-start | bytes 516104 | tf_op jit(solution)/shard_map/ppermute | solution.py:152
  39.5 1.5 %collective-permute-start.10 = (s16[128,768]{1,0:T(8,128)(2,1)S(1)}, s16[128,768]{1,0:T(8,128)(2,1)S(1)}, u32[]{:S(2)}, u32[]{:S(2)}) collective-permute-start(s16[128,768]{1,0:T(8,128)(2,1)S(1)} %collective-permute-done.7.refs_6_), channel_id=1, source_target_pairs={{0,2},{1,3},{2,0},{3,1},{4,6},{5,7},{6,4},{7,5},{8,10},{9,11},{10,... | collective-permute-start | bytes 589832 | tf_op jit(solution)/shard_map/ppermute | solution.py:144
  41.0 1.0 %shard_map.148 = (s16[112,768]{1,0:T(8,128)(2,1)S(1)}, f32[96,768]{1,0:T(8,128)S(1)}) custom-call(s32[12]{0:T(128)S(1)} %concatenate.3.meta, s16[224,768]{1,0:T(8,128)(2,1)S(1)} %collective-permute-done.12.got, f32[768,768]{1,0:T(8,128)S(1)} %shard_map.142.mine), custom_call_target="tpu_custom_call" | custom-call | flops 1650000000 | bytes 39600000 | tf_op jit(solution)/shard_map/pallas_call | solution.py:369
  42.0 0.6 collective-permute-start.18
  42.6 0.9 collective-permute-done.16.refs_1_
  43.6 0.4 shard_map.147
  44.0 3.4 %collective-permute-start.17 = (s16[112,768]{1,0:T(8,128)(2,1)S(1)}, s16[112,768]{1,0:T(8,128)(2,1)S(1)}, u32[]{:S(2)}, u32[]{:S(2)}) collective-permute-start(s16[112,768]{1,0:T(8,128)(2,1)S(1)} %shard_map.147), channel_id=1, source_target_pairs={{0,12},{4,8},{8,4},{12,0},{1,13},{5,9},{9,5},{13,1},{2,14},{6,10},... | collective-permute-start | bytes 516104 | tf_op jit(solution)/shard_map/ppermute | solution.py:152
  47.4 1.0 %shard_map.144 = (s16[112,768]{1,0:T(8,128)(2,1)S(1)}, f32[96,768]{1,0:T(8,128)S(1)}) custom-call(s32[12]{0:T(128)S(1)} %concatenate.3.meta, s16[224,768]{1,0:T(8,128)(2,1)S(1)} %collective-permute-done.1.got, f32[768,768]{1,0:T(8,128)S(1)} %shard_map.142.mine), custom_call_target="tpu_custom_call" | custom-call | flops 1650000000 | bytes 39600000 | tf_op jit(solution)/shard_map/pallas_call | solution.py:369
  48.5 1.6 %collective-permute-start.11 = (s16[112,768]{1,0:T(8,128)(2,1)S(1)}, s16[112,768]{1,0:T(8,128)(2,1)S(1)}, u32[]{:S(2)}, u32[]{:S(2)}) collective-permute-start(s16[112,768]{1,0:T(8,128)(2,1)S(1)} %get-tuple-element.90), channel_id=1, source_target_pairs={{0,2},{1,3},{2,0},{3,1},{4,6},{5,7},{6,4},{7,5},{8,10},{9,11},{10,... | collective-permute-start | bytes 516104 | tf_op jit(solution)/shard_map/ppermute | solution.py:144
  50.0 0.2 shard_map.149
  50.4 1.2 %collective-permute-done.17.far = s16[112,768]{1,0:T(8,128)(2,1)S(1)} collective-permute-done((s16[112,768]{1,0:T(8,128)(2,1)S(1)}, s16[112,768]{1,0:T(8,128)(2,1)S(1)}, u32[]{:S(2)}, u32[]{:S(2)}) %collective-permute-start.17) | collective-permute-done | bytes 172064 | tf_op jit(solution)/shard_map/ppermute | solution.py:152
  51.6 2.4 %collective-permute-done.11.got = s16[112,768]{1,0:T(8,128)(2,1)S(1)} collective-permute-done((s16[112,768]{1,0:T(8,128)(2,1)S(1)}, s16[112,768]{1,0:T(8,128)(2,1)S(1)}, u32[]{:S(2)}, u32[]{:S(2)}) %collective-permute-start.11) | collective-permute-done | bytes 172064 | tf_op jit(solution)/shard_map/ppermute | solution.py:144
  54.0 1.8 %collective-permute-done.19.near = s16[112,768]{1,0:T(8,128)(2,1)S(1)} collective-permute-done((s16[112,768]{1,0:T(8,128)(2,1)S(1)}, s16[112,768]{1,0:T(8,128)(2,1)S(1)}, u32[]{:S(2)}, u32[]{:S(2)}) %collective-permute-start.19) | collective-permute-done | bytes 172064 | tf_op jit(solution)/shard_map/ppermute | solution.py:152
  55.8 0.6 shard_map.150
  56.4 0.6 collective-permute-start.22
  57.0 2.4 %collective-permute-start.21 = (s16[112,768]{1,0:T(8,128)(2,1)S(1)}, s16[112,768]{1,0:T(8,128)(2,1)S(1)}, u32[]{:S(2)}, u32[]{:S(2)}) collective-permute-start(s16[112,768]{1,0:T(8,128)(2,1)S(1)} %get-tuple-element.104), channel_id=1, source_target_pairs={{0,12},{4,8},{8,4},{12,0},{1,13},{5,9},{9,5},{13,1},{2,14},{6,10},... | collective-permute-start | bytes 516104 | tf_op jit(solution)/shard_map/ppermute | solution.py:152
  59.5 1.6 %collective-permute-start.27 = (s16[128,768]{1,0:T(8,128)(2,1)S(1)}, s16[128,768]{1,0:T(8,128)(2,1)S(1)}, u32[]{:S(2)}, u32[]{:S(2)}) collective-permute-start(s16[128,768]{1,0:T(8,128)(2,1)S(1)} %collective-permute-done.15.refs_4_), channel_id=1, source_target_pairs={{0,2},{1,3},{2,0},{3,1},{4,6},{5,7},{6,4},{7,5},{8,10},{9,11},{10,... | collective-permute-start | bytes 589832 | tf_op jit(solution)/shard_map/ppermute | solution.py:144
  61.0 0.8 collective-permute-done.22.refs_0_
  61.8 3.1 %collective-permute-done.21.three = s16[112,768]{1,0:T(8,128)(2,1)S(1)} collective-permute-done((s16[112,768]{1,0:T(8,128)(2,1)S(1)}, s16[112,768]{1,0:T(8,128)(2,1)S(1)}, u32[]{:S(2)}, u32[]{:S(2)}) %collective-permute-start.21) | collective-permute-done | bytes 172064 | tf_op jit(solution)/shard_map/ppermute | solution.py:152
  65.0 1.9 %shard_map.153 = (f32[4,48,768]{2,1,0:T(8,128)}, f32[4,48,768]{2,1,0:T(8,128)}, f32[1,128]{1,0:T(1,128)S(1)}) custom-call(s32[12]{0:T(128)S(1)} %concatenate.3.meta, f32[96,768]{1,0:T(8,128)S(1)} %get-tuple-element.103.grad_ref.grad, f32[48,768]{1,0:T(8,128)S(1)} %collective-permute-done.28.got, f32[4,48,768]{2,1,0:T(8,128)S(1)} %copy-done, ...), custom_call_target="tpu_custom_call" | custom-call | flops 1500000000 | bytes 36000000 | tf_op jit(solution)/shard_map/pallas_call | solution.py:273
  66.9 2.4 %collective-permute-start.26 = (s16[112,768]{1,0:T(8,128)(2,1)S(1)}, s16[112,768]{1,0:T(8,128)(2,1)S(1)}, u32[]{:S(2)}, u32[]{:S(2)}) collective-permute-start(s16[112,768]{1,0:T(8,128)(2,1)S(1)} %collective-permute-done.21.three), channel_id=1, source_target_pairs={{0,2},{1,3},{2,0},{3,1},{4,6},{5,7},{6,4},{7,5},{8,10},{9,11},{10,... | collective-permute-start | bytes 516104 | tf_op jit(solution)/shard_map/ppermute | solution.py:144
  69.2 0.6 collective-permute-start.24
  69.9 1.9 %collective-permute-done.23.two = s16[112,768]{1,0:T(8,128)(2,1)S(1)} collective-permute-done((s16[112,768]{1,0:T(8,128)(2,1)S(1)}, s16[112,768]{1,0:T(8,128)(2,1)S(1)}, u32[]{:S(2)}, u32[]{:S(2)}) %collective-permute-start.23) | collective-permute-done | bytes 172064 | tf_op jit(solution)/shard_map/ppermute | solution.py:152
  71.7 1.5 %collective-permute-start.25 = (s16[112,768]{1,0:T(8,128)(2,1)S(1)}, s16[112,768]{1,0:T(8,128)(2,1)S(1)}, u32[]{:S(2)}, u32[]{:S(2)}) collective-permute-start(s16[112,768]{1,0:T(8,128)(2,1)S(1)} %collective-permute-done.23.two), channel_id=1, source_target_pairs={{0,2},{1,3},{2,0},{3,1},{4,6},{5,7},{6,4},{7,5},{8,10},{9,11},{10,... | collective-permute-start | bytes 516104 | tf_op jit(solution)/shard_map/ppermute | solution.py:144
  73.2 1.5 %shard_map.152 = (bf16[768,768]{1,0:T(8,128)(2,1)S(1)}, bf16[768,768]{1,0:T(8,128)(2,1)S(1)}) custom-call(s32[12]{0:T(128)S(1)} %concatenate.3.meta, s16[128,768]{1,0:T(8,128)(2,1)S(1)} %get-tuple-element.85.refs_0_, s16[128,768]{1,0:T(8,128)(2,1)S(1)} %collective-permute-done.9.refs_1_, s16[128,768]{1,0:T(8,128)(2,1)S(1)} %collective-permute-done.8.refs_2_, ...), custom_call_target="tpu_custom_call" | custom-call | flops 1500000000 | bytes 36000000 | tf_op jit(solution)/shard_map/pallas_call | solution.py:273
  74.7 1.1 %shard_map.151 = (bf16[768,768]{1,0:T(8,128)(2,1)S(1)}, bf16[768,768]{1,0:T(8,128)(2,1)S(1)}) custom-call(s32[12]{0:T(128)S(1)} %concatenate.3.meta, f32[96,768]{1,0:T(8,128)S(1)} %get-tuple-element.103.grad_ref.grad, s16[112,768]{1,0:T(8,128)(2,1)S(1)} %collective-permute-done.20.one, s16[112,768]{1,0:T(8,128)(2,1)S(1)} %collective-permute-done.23.two, ...), custom_call_target="tpu_custom_call" | custom-call | flops 1500000000 | bytes 36000000 | tf_op jit(solution)/shard_map/pallas_call | solution.py:273
  75.9 1.9 %collective-permute-done.24.refs_1_ = s16[112,768]{1,0:T(8,128)(2,1)S(1)} collective-permute-done((s16[112,768]{1,0:T(8,128)(2,1)S(1)}, s16[112,768]{1,0:T(8,128)(2,1)S(1)}, u32[]{:S(2)}, u32[]{:S(2)}) %collective-permute-start.24) | collective-permute-done | bytes 172064 | tf_op jit(solution)/shard_map/ppermute | solution.py:144
  77.8 1.8 %collective-permute-done.25.refs_2_ = s16[112,768]{1,0:T(8,128)(2,1)S(1)} collective-permute-done((s16[112,768]{1,0:T(8,128)(2,1)S(1)}, s16[112,768]{1,0:T(8,128)(2,1)S(1)}, u32[]{:S(2)}, u32[]{:S(2)}) %collective-permute-start.25) | collective-permute-done | bytes 172064 | tf_op jit(solution)/shard_map/ppermute | solution.py:144
  79.6 3.4 %shard_map.154 = (f32[48,768]{1,0:T(8,128)S(1)}, f32[48,768]{1,0:T(8,128)S(1)}, f32[1,128]{1,0:T(1,128)S(1)}, bf16[768,768]{1,0:T(8,128)(2,1)S(1)}, bf16[768,768]{1,0:T(8,128)(2,1)S(1)}) custom-call(s32[12]{0:T(128)S(1)} %concatenate.3.meta, bf16[768,768]{1,0:T(8,128)(2,1)S(1)} %get-tuple-element.106.high_in, ...), custom_call_target="tpu_custom_call" | custom-call | flops 6000000000 | bytes 144000000 | tf_op jit(solution)/shard_map/pallas_call | solution.py:273
  83.1 10.3 %all_to_all.5.sums = f32[16,1,128]{2,1,0:T(1,128)S(1)} all-to-all(f32[16,1,128]{2,1,0:T(1,128)S(1)} %broadcast_in_dim.9), channel_id=1, replica_groups=mesh['shard'=2,'tensor'=4,'section'=4] {'tensor','section'}, dimensions={0} | all-to-all | bytes 16384 | tf_op jit(solution)/shard_map/all_to_all | solution.py:708
  93.4 0.7 shard_map.155.near
  94.1 1.6 %collective-permute-start.31 = (bf16[2,48,768]{2,1,0:T(8,128)(2,1)S(1)}, bf16[2,48,768]{2,1,0:T(8,128)(2,1)S(1)}, u32[]{:S(2)}, u32[]{:S(2)}) collective-permute-start(bf16[2,48,768]{2,1,0:T(8,128)(2,1)S(1)} %shard_map.155.near), channel_id=1, source_target_pairs={{0,16},{16,0},{1,17},{17,1},{2,18},{18,2},{3,19},{19,3},{4,20},{20... | collective-permute-start | bytes 442376 | tf_op jit(solution)/shard_map/ppermute | solution.py:148
  95.7 1.8 %shard_map.156 = (f32[48,768]{1,0:T(8,128)S(1)}, f32[48,768]{1,0:T(8,128)S(1)}) custom-call(s32[12]{0:T(128)S(1)} %concatenate.3.meta, f32[96,768]{1,0:T(8,128)S(1)} %get-tuple-element.103.grad_ref.grad, bf16[768,768]{1,0:T(8,128)(2,1)S(1)} %get-tuple-element.122.high_ref, bf16[768,768]{1,0:T(8,128)(2,1)S(1)} %get-tuple-element.123.low_ref), custom_call_target="tpu_custom_call" | custom-call | flops 2100000000 | bytes 50400000 | tf_op jit(solution)/shard_map/pallas_call | solution.py:273
  97.6 2.0 %shard_map.158 = (f32[48,768]{1,0:T(8,128)S(1)}, f32[48,768]{1,0:T(8,128)S(1)}) custom-call(s32[12]{0:T(128)S(1)} %concatenate.3.meta, bf16[768,768]{1,0:T(8,128)(2,1)S(1)} %get-tuple-element.122.high_ref, bf16[768,768]{1,0:T(8,128)(2,1)S(1)} %get-tuple-element.123.low_ref), custom_call_target="tpu_custom_call" | custom-call | flops 2700000000 | bytes 64800000 | tf_op jit(solution)/shard_map/pallas_call | solution.py:273
  99.6 0.6 collective-permute-start.32
  100.1 1.3 %shard_map.157 = bf16[4,48,768]{2,1,0:T(8,128)(2,1)} custom-call(s32[12]{0:T(128)S(1)} %concatenate.3.meta, bf16[2,48,768]{2,1,0:T(8,128)(2,1)S(1)} %shard_map.155.near, bf16[2,48,768]{2,1,0:T(8,128)(2,1)S(1)} %collective-permute-done.31.mirror), custom_call_target="tpu_custom_call" | custom-call | flops 1500000000 | bytes 36000000 | tf_op jit(solution)/shard_map/pallas_call | solution.py:273
  101.5 1.7 %shard_map.159 = (f32[4,48,768]{2,1,0:T(8,128)}, f32[4,48,768]{2,1,0:T(8,128)}) custom-call(s32[12]{0:T(128)S(1)} %concatenate.3.meta, f32[48,768]{1,0:T(8,128)S(1)} %get-tuple-element.127.own_right, f32[48,768]{1,0:T(8,128)S(1)} %collective-permute-done.32.got_right, f32[48,768]{1,0:T(8,128)S(1)} %get-tuple-element.129.own_left, ...), custom_call_target="tpu_custom_call" | custom-call | flops 1500000000 | bytes 36000000 | tf_op jit(solution)/shard_map/pallas_call | solution.py:273
  (39 shorter events, 0.5 us)
Async XLA Ops:
  4.7 3.6 %collective-permute-start = (bf16[2,512,768]{2,1,0:T(8,128)(2,1)S(1)}, bf16[2,512,768]{2,1,0:T(8,128)(2,1)S(1)}, u32[]{:S(2)}, u32[]{:S(2)}) collective-permute-start(bf16[2,512,768]{2,1,0:T(8,128)(2,1)S(1)} %get-tuple-element.70), channel_id=1, source_target_pairs={{0,1},{1,0},{2,3},{3,2},{4,5},{5,4},{6,7},{7,6},{8,9},{9,8},{10,11... | collective-permute-start | bytes 4718600 | tf_op jit(solution)/shard_map/ppermute | solution.py:140
  5.2 14.9 %collective-permute-start.5 = (bf16[2,512,768]{2,1,0:T(8,128)(2,1)S(1)}, bf16[2,512,768]{2,1,0:T(8,128)(2,1)S(1)}, u32[]{:S(2)}, u32[]{:S(2)}) collective-permute-start(bf16[2,512,768]{2,1,0:T(8,128)(2,1)S(1)} %get-tuple-element.77), channel_id=1, source_target_pairs={{0,1},{1,0},{2,3},{3,2},{4,5},{5,4},{6,7},{7,6},{8,9},{9,8},{10,11... | collective-permute-start | bytes 4718600 | tf_op jit(solution)/shard_map/ppermute | solution.py:140
  5.3 5.6 %collective-permute-start.3 = (f32[2,48,768]{2,1,0:T(8,128)S(1)}, f32[2,48,768]{2,1,0:T(8,128)S(1)}, u32[]{:S(2)}, u32[]{:S(2)}) collective-permute-start(f32[2,48,768]{2,1,0:T(8,128)S(1)} %get-tuple-element.75), channel_id=1, source_target_pairs={{0,1},{1,0},{2,3},{3,2},{4,5},{5,4},{6,7},{7,6},{8,9},{9,8},{10,11... | collective-permute-start | bytes 884744 | tf_op jit(solution)/shard_map/ppermute | solution.py:140
  10.9 14.6 %collective-permute-start.4 = (s16[224,768]{1,0:T(8,128)(2,1)S(1)}, s16[224,768]{1,0:T(8,128)(2,1)S(1)}, u32[]{:S(2)}, u32[]{:S(2)}) collective-permute-start(s16[224,768]{1,0:T(8,128)(2,1)S(1)} %get-tuple-element.76), channel_id=1, source_target_pairs={{0,16},{16,0},{1,17},{17,1},{2,18},{18,2},{3,19},{19,3},{4,20},{20... | collective-permute-start | bytes 1032200 | tf_op jit(solution)/shard_map/ppermute | solution.py:148
  15.5 11.7 %collective-permute-start.8 = (s16[128,768]{1,0:T(8,128)(2,1)S(1)}, s16[128,768]{1,0:T(8,128)(2,1)S(1)}, u32[]{:S(2)}, u32[]{:S(2)}) collective-permute-start(s16[128,768]{1,0:T(8,128)(2,1)S(1)} %get-tuple-element.85.refs_0_), channel_id=1, source_target_pairs={{0,4},{4,0},{8,12},{12,8},{1,5},{5,1},{9,13},{13,9},{2,6},{6,2},{1... | collective-permute-start | bytes 589832 | tf_op jit(solution)/shard_map/ppermute | solution.py:152
  17.1 11.5 %collective-permute-start.7 = (s16[128,768]{1,0:T(8,128)(2,1)S(1)}, s16[128,768]{1,0:T(8,128)(2,1)S(1)}, u32[]{:S(2)}, u32[]{:S(2)}) collective-permute-start(s16[128,768]{1,0:T(8,128)(2,1)S(1)} %get-tuple-element.85.refs_0_), channel_id=1, source_target_pairs={{0,12},{4,8},{8,4},{12,0},{1,13},{5,9},{9,5},{13,1},{2,14},{6,10},... | collective-permute-start | bytes 589832 | tf_op jit(solution)/shard_map/ppermute | solution.py:152
  19.6 11.3 %collective-permute-start.2 = (s16[224,768]{1,0:T(8,128)(2,1)S(1)}, s16[224,768]{1,0:T(8,128)(2,1)S(1)}, u32[]{:S(2)}, u32[]{:S(2)}) collective-permute-start(s16[224,768]{1,0:T(8,128)(2,1)S(1)} %get-tuple-element.73), channel_id=1, source_target_pairs={{0,16},{16,0},{1,17},{17,1},{2,18},{18,2},{3,19},{19,3},{4,20},{20... | collective-permute-start | bytes 1032200 | tf_op jit(solution)/shard_map/ppermute | solution.py:148
  20.1 8.6 %collective-permute-start.9 = (s16[128,768]{1,0:T(8,128)(2,1)S(1)}, s16[128,768]{1,0:T(8,128)(2,1)S(1)}, u32[]{:S(2)}, u32[]{:S(2)}) collective-permute-start(s16[128,768]{1,0:T(8,128)(2,1)S(1)} %get-tuple-element.85.refs_0_), channel_id=1, source_target_pairs={{0,2},{1,3},{2,0},{3,1},{4,6},{5,7},{6,4},{7,5},{8,10},{9,11},{10,... | collective-permute-start | bytes 589832 | tf_op jit(solution)/shard_map/ppermute | solution.py:144
  26.6 7.3 %collective-permute-start.6 = (s16[112,768]{1,0:T(8,128)(2,1)S(1)}, s16[112,768]{1,0:T(8,128)(2,1)S(1)}, u32[]{:S(2)}, u32[]{:S(2)}) collective-permute-start(s16[112,768]{1,0:T(8,128)(2,1)S(1)} %get-tuple-element.83), channel_id=1, source_target_pairs={{0,2},{1,3},{2,0},{3,1},{4,6},{5,7},{6,4},{7,5},{8,10},{9,11},{10,... | collective-permute-start | bytes 516104 | tf_op jit(solution)/shard_map/ppermute | solution.py:144
  27.2 11.0 %collective-permute-start.12 = (s16[224,768]{1,0:T(8,128)(2,1)S(1)}, s16[224,768]{1,0:T(8,128)(2,1)S(1)}, u32[]{:S(2)}, u32[]{:S(2)}) collective-permute-start(s16[224,768]{1,0:T(8,128)(2,1)S(1)} %get-tuple-element.93), channel_id=1, source_target_pairs={{0,16},{16,0},{1,17},{17,1},{2,18},{18,2},{3,19},{19,3},{4,20},{20... | collective-permute-start | bytes 1032200 | tf_op jit(solution)/shard_map/ppermute | solution.py:148
  28.7 10.8 %collective-permute-start.14 = (s16[128,768]{1,0:T(8,128)(2,1)S(1)}, s16[128,768]{1,0:T(8,128)(2,1)S(1)}, u32[]{:S(2)}, u32[]{:S(2)}) collective-permute-start(s16[128,768]{1,0:T(8,128)(2,1)S(1)} %collective-permute-done.8.refs_2_), channel_id=1, source_target_pairs={{0,2},{1,3},{2,0},{3,1},{4,6},{5,7},{6,4},{7,5},{8,10},{9,11},{10,... | collective-permute-start | bytes 589832 | tf_op jit(solution)/shard_map/ppermute | solution.py:144
  30.2 10.8 %collective-permute-start.15 = (s16[128,768]{1,0:T(8,128)(2,1)S(1)}, s16[128,768]{1,0:T(8,128)(2,1)S(1)}, u32[]{:S(2)}, u32[]{:S(2)}) collective-permute-start(s16[128,768]{1,0:T(8,128)(2,1)S(1)} %collective-permute-done.7.refs_6_), channel_id=1, source_target_pairs={{0,4},{4,0},{8,12},{12,8},{1,5},{5,1},{9,13},{13,9},{2,6},{6,2},{1... | collective-permute-start | bytes 589832 | tf_op jit(solution)/shard_map/ppermute | solution.py:152
  34.9 6.1 %collective-permute-start.13 = (s16[112,768]{1,0:T(8,128)(2,1)S(1)}, s16[112,768]{1,0:T(8,128)(2,1)S(1)}, u32[]{:S(2)}, u32[]{:S(2)}) collective-permute-start(s16[112,768]{1,0:T(8,128)(2,1)S(1)} %get-tuple-element.94), channel_id=1, source_target_pairs={{0,2},{1,3},{2,0},{3,1},{4,6},{5,7},{6,4},{7,5},{8,10},{9,11},{10,... | collective-permute-start | bytes 516104 | tf_op jit(solution)/shard_map/ppermute | solution.py:144
  35.0 12.4 %collective-permute-start.1 = (s16[224,768]{1,0:T(8,128)(2,1)S(1)}, s16[224,768]{1,0:T(8,128)(2,1)S(1)}, u32[]{:S(2)}, u32[]{:S(2)}) collective-permute-start(s16[224,768]{1,0:T(8,128)(2,1)S(1)} %get-tuple-element.72), channel_id=1, source_target_pairs={{0,16},{16,0},{1,17},{17,1},{2,18},{18,2},{3,19},{19,3},{4,20},{20... | collective-permute-start | bytes 1032200 | tf_op jit(solution)/shard_map/ppermute | solution.py:148
  38.2 5.4 %collective-permute-start.16 = (s16[112,768]{1,0:T(8,128)(2,1)S(1)}, s16[112,768]{1,0:T(8,128)(2,1)S(1)}, u32[]{:S(2)}, u32[]{:S(2)}) collective-permute-start(s16[112,768]{1,0:T(8,128)(2,1)S(1)} %shard_map.146), channel_id=1, source_target_pairs={{0,4},{4,0},{8,12},{12,8},{1,5},{5,1},{9,13},{13,9},{2,6},{6,2},{1... | collective-permute-start | bytes 516104 | tf_op jit(solution)/shard_map/ppermute | solution.py:152
  39.5 7.9 %collective-permute-start.10 = (s16[128,768]{1,0:T(8,128)(2,1)S(1)}, s16[128,768]{1,0:T(8,128)(2,1)S(1)}, u32[]{:S(2)}, u32[]{:S(2)}) collective-permute-start(s16[128,768]{1,0:T(8,128)(2,1)S(1)} %collective-permute-done.7.refs_6_), channel_id=1, source_target_pairs={{0,2},{1,3},{2,0},{3,1},{4,6},{5,7},{6,4},{7,5},{8,10},{9,11},{10,... | collective-permute-start | bytes 589832 | tf_op jit(solution)/shard_map/ppermute | solution.py:144
  42.0 8.0 %collective-permute-start.18 = (s16[112,768]{1,0:T(8,128)(2,1)S(1)}, s16[112,768]{1,0:T(8,128)(2,1)S(1)}, u32[]{:S(2)}, u32[]{:S(2)}) collective-permute-start(s16[112,768]{1,0:T(8,128)(2,1)S(1)} %get-tuple-element.102), channel_id=1, source_target_pairs={{0,2},{1,3},{2,0},{3,1},{4,6},{5,7},{6,4},{7,5},{8,10},{9,11},{10,... | collective-permute-start | bytes 516104 | tf_op jit(solution)/shard_map/ppermute | solution.py:144
  44.0 7.6 %collective-permute-start.17 = (s16[112,768]{1,0:T(8,128)(2,1)S(1)}, s16[112,768]{1,0:T(8,128)(2,1)S(1)}, u32[]{:S(2)}, u32[]{:S(2)}) collective-permute-start(s16[112,768]{1,0:T(8,128)(2,1)S(1)} %shard_map.147), channel_id=1, source_target_pairs={{0,12},{4,8},{8,4},{12,0},{1,13},{5,9},{9,5},{13,1},{2,14},{6,10},... | collective-permute-start | bytes 516104 | tf_op jit(solution)/shard_map/ppermute | solution.py:152
  48.5 5.5 %collective-permute-start.11 = (s16[112,768]{1,0:T(8,128)(2,1)S(1)}, s16[112,768]{1,0:T(8,128)(2,1)S(1)}, u32[]{:S(2)}, u32[]{:S(2)}) collective-permute-start(s16[112,768]{1,0:T(8,128)(2,1)S(1)} %get-tuple-element.90), channel_id=1, source_target_pairs={{0,2},{1,3},{2,0},{3,1},{4,6},{5,7},{6,4},{7,5},{8,10},{9,11},{10,... | collective-permute-start | bytes 516104 | tf_op jit(solution)/shard_map/ppermute | solution.py:144
  50.3 5.5 %collective-permute-start.19 = (s16[112,768]{1,0:T(8,128)(2,1)S(1)}, s16[112,768]{1,0:T(8,128)(2,1)S(1)}, u32[]{:S(2)}, u32[]{:S(2)}) collective-permute-start(s16[112,768]{1,0:T(8,128)(2,1)S(1)} %shard_map.149), channel_id=1, source_target_pairs={{0,4},{4,0},{8,12},{12,8},{1,5},{5,1},{9,13},{13,9},{2,6},{6,2},{1... | collective-permute-start | bytes 516104 | tf_op jit(solution)/shard_map/ppermute | solution.py:152
  55.8 9.2 %copy-start = (f32[4,48,768]{2,1,0:T(8,128)S(1)}, f32[4,48,768]{2,1,0:T(8,128)}, u32[]{:S(2)}) copy-start(f32[4,48,768]{2,1,0:T(8,128)} %first.1) | copy-start | bytes 1769476
  55.8 9.2 %copy-start.1 = (f32[4,48,768]{2,1,0:T(8,128)S(1)}, f32[4,48,768]{2,1,0:T(8,128)}, u32[]{:S(2)}) copy-start(f32[4,48,768]{2,1,0:T(8,128)} %second.1) | copy-start | bytes 1769476
  56.4 5.5 %collective-permute-start.22 = (s16[112,768]{1,0:T(8,128)(2,1)S(1)}, s16[112,768]{1,0:T(8,128)(2,1)S(1)}, u32[]{:S(2)}, u32[]{:S(2)}) collective-permute-start(s16[112,768]{1,0:T(8,128)(2,1)S(1)} %get-tuple-element.104), channel_id=1, source_target_pairs={{0,2},{1,3},{2,0},{3,1},{4,6},{5,7},{6,4},{7,5},{8,10},{9,11},{10,... | collective-permute-start | bytes 516104 | tf_op jit(solution)/shard_map/ppermute | solution.py:144
  57.0 8.0 %collective-permute-start.21 = (s16[112,768]{1,0:T(8,128)(2,1)S(1)}, s16[112,768]{1,0:T(8,128)(2,1)S(1)}, u32[]{:S(2)}, u32[]{:S(2)}) collective-permute-start(s16[112,768]{1,0:T(8,128)(2,1)S(1)} %get-tuple-element.104), channel_id=1, source_target_pairs={{0,12},{4,8},{8,4},{12,0},{1,13},{5,9},{9,5},{13,1},{2,14},{6,10},... | collective-permute-start | bytes 516104 | tf_op jit(solution)/shard_map/ppermute | solution.py:152
  59.4 5.6 %collective-permute-start.28 = (f32[48,768]{1,0:T(8,128)S(1)}, f32[48,768]{1,0:T(8,128)S(1)}, u32[]{:S(2)}, u32[]{:S(2)}) collective-permute-start(f32[48,768]{1,0:T(8,128)S(1)} %constant_dynamic-slice_fusion), channel_id=1, source_target_pairs={{0,1},{1,0},{2,3},{3,2},{4,5},{5,4},{6,7},{7,6},{8,9},{9,8},{10,11... | collective-permute-start | bytes 442376 | tf_op jit(solution)/shard_map/ppermute | solution.py:140
  59.5 13.7 %collective-permute-start.27 = (s16[128,768]{1,0:T(8,128)(2,1)S(1)}, s16[128,768]{1,0:T(8,128)(2,1)S(1)}, u32[]{:S(2)}, u32[]{:S(2)}) collective-permute-start(s16[128,768]{1,0:T(8,128)(2,1)S(1)} %collective-permute-done.15.refs_4_), channel_id=1, source_target_pairs={{0,2},{1,3},{2,0},{3,1},{4,6},{5,7},{6,4},{7,5},{8,10},{9,11},{10,... | collective-permute-start | bytes 589832 | tf_op jit(solution)/shard_map/ppermute | solution.py:144
  61.0 8.2 %collective-permute-start.20 = (s16[112,768]{1,0:T(8,128)(2,1)S(1)}, s16[112,768]{1,0:T(8,128)(2,1)S(1)}, u32[]{:S(2)}, u32[]{:S(2)}) collective-permute-start(s16[112,768]{1,0:T(8,128)(2,1)S(1)} %get-tuple-element.104), channel_id=1, source_target_pairs={{0,4},{4,0},{8,12},{12,8},{1,5},{5,1},{9,13},{13,9},{2,6},{6,2},{1... | collective-permute-start | bytes 516104 | tf_op jit(solution)/shard_map/ppermute | solution.py:152
  65.0 6.8 %collective-permute-start.23 = (s16[112,768]{1,0:T(8,128)(2,1)S(1)}, s16[112,768]{1,0:T(8,128)(2,1)S(1)}, u32[]{:S(2)}, u32[]{:S(2)}) collective-permute-start(s16[112,768]{1,0:T(8,128)(2,1)S(1)} %collective-permute-done.21.three), channel_id=1, source_target_pairs={{0,4},{4,0},{8,12},{12,8},{1,5},{5,1},{9,13},{13,9},{2,6},{6,2},{1... | collective-permute-start | bytes 516104 | tf_op jit(solution)/shard_map/ppermute | solution.py:152
  66.9 9.0 %collective-permute-start.26 = (s16[112,768]{1,0:T(8,128)(2,1)S(1)}, s16[112,768]{1,0:T(8,128)(2,1)S(1)}, u32[]{:S(2)}, u32[]{:S(2)}) collective-permute-start(s16[112,768]{1,0:T(8,128)(2,1)S(1)} %collective-permute-done.21.three), channel_id=1, source_target_pairs={{0,2},{1,3},{2,0},{3,1},{4,6},{5,7},{6,4},{7,5},{8,10},{9,11},{10,... | collective-permute-start | bytes 516104 | tf_op jit(solution)/shard_map/ppermute | solution.py:144
  69.2 8.5 %collective-permute-start.24 = (s16[112,768]{1,0:T(8,128)(2,1)S(1)}, s16[112,768]{1,0:T(8,128)(2,1)S(1)}, u32[]{:S(2)}, u32[]{:S(2)}) collective-permute-start(s16[112,768]{1,0:T(8,128)(2,1)S(1)} %collective-permute-done.20.one), channel_id=1, source_target_pairs={{0,2},{1,3},{2,0},{3,1},{4,6},{5,7},{6,4},{7,5},{8,10},{9,11},{10,... | collective-permute-start | bytes 516104 | tf_op jit(solution)/shard_map/ppermute | solution.py:144
  71.7 7.9 %collective-permute-start.25 = (s16[112,768]{1,0:T(8,128)(2,1)S(1)}, s16[112,768]{1,0:T(8,128)(2,1)S(1)}, u32[]{:S(2)}, u32[]{:S(2)}) collective-permute-start(s16[112,768]{1,0:T(8,128)(2,1)S(1)} %collective-permute-done.23.two), channel_id=1, source_target_pairs={{0,2},{1,3},{2,0},{3,1},{4,6},{5,7},{6,4},{7,5},{8,10},{9,11},{10,... | collective-permute-start | bytes 516104 | tf_op jit(solution)/shard_map/ppermute | solution.py:144
  79.6 13.8 %copy-start.4 = (bf16[4,48,768]{2,1,0:T(8,128)(2,1)S(1)}, bf16[4,48,768]{2,1,0:T(8,128)(2,1)}, u32[]{:S(2)}) copy-start(bf16[4,48,768]{2,1,0:T(8,128)(2,1)} %weights.1) | copy-start | bytes 884740
  83.0 10.4 %collective-permute-start.29 = (f32[48,768]{1,0:T(8,128)S(1)}, f32[48,768]{1,0:T(8,128)S(1)}, u32[]{:S(2)}, u32[]{:S(2)}) collective-permute-start(f32[48,768]{1,0:T(8,128)S(1)} %get-tuple-element.121), channel_id=1, source_target_pairs={{0,1},{1,0},{2,3},{3,2},{4,5},{5,4},{6,7},{7,6},{8,9},{9,8},{10,11... | collective-permute-start | bytes 442376 | tf_op jit(solution)/shard_map/ppermute | solution.py:140
  94.1 6.0 %collective-permute-start.31 = (bf16[2,48,768]{2,1,0:T(8,128)(2,1)S(1)}, bf16[2,48,768]{2,1,0:T(8,128)(2,1)S(1)}, u32[]{:S(2)}, u32[]{:S(2)}) collective-permute-start(bf16[2,48,768]{2,1,0:T(8,128)(2,1)S(1)} %shard_map.155.near), channel_id=1, source_target_pairs={{0,16},{16,0},{1,17},{17,1},{2,18},{18,2},{3,19},{19,3},{4,20},{20... | collective-permute-start | bytes 442376 | tf_op jit(solution)/shard_map/ppermute | solution.py:148
  97.5 4.0 %collective-permute-start.30 = (f32[48,768]{1,0:T(8,128)S(1)}, f32[48,768]{1,0:T(8,128)S(1)}, u32[]{:S(2)}, u32[]{:S(2)}) collective-permute-start(f32[48,768]{1,0:T(8,128)S(1)} %get-tuple-element.124), channel_id=1, source_target_pairs={{0,1},{1,0},{2,3},{3,2},{4,5},{5,4},{6,7},{7,6},{8,9},{9,8},{10,11... | collective-permute-start | bytes 442376 | tf_op jit(solution)/shard_map/ppermute | solution.py:140
  99.6 1.9 %copy-start.2 = (f32[4,48,768]{2,1,0:T(8,128)S(1)}, f32[4,48,768]{2,1,0:T(8,128)}, u32[]{:S(2)}) copy-start(f32[4,48,768]{2,1,0:T(8,128)} %right.5) | copy-start | bytes 1769476
  99.6 1.9 %copy-start.3 = (f32[4,48,768]{2,1,0:T(8,128)S(1)}, f32[4,48,768]{2,1,0:T(8,128)}, u32[]{:S(2)}) copy-start(f32[4,48,768]{2,1,0:T(8,128)} %left.5) | copy-start | bytes 1769476
  99.6 1.9 %collective-permute-start.32 = (f32[48,768]{1,0:T(8,128)S(1)}, f32[48,768]{1,0:T(8,128)S(1)}, u32[]{:S(2)}, u32[]{:S(2)}) collective-permute-start(f32[48,768]{1,0:T(8,128)S(1)} %get-tuple-element.128), channel_id=1, source_target_pairs={{0,1},{1,0},{2,3},{3,2},{4,5},{5,4},{6,7},{7,6},{8,9},{9,8},{10,11... | collective-permute-start | bytes 442376 | tf_op jit(solution)/shard_map/ppermute | solution.py:140
